TPU v7x, 32 devices: a whole 2x2x4 slice. The times are simulated.
32 devices in a mesh: dp: 16 (over z, x, core), blk: 2 (over y).
Axes of the slice: x: 2, y: 2, z: 4, core: 2. Of those that a mesh axis runs over, the one named last changes fastest.
Arguments:
- tokens: bfloat16 [32, 1024, 1024], P('dp', 'blk'), may hold values from -6 to 6
- cotangent: bfloat16 [32, 1024, 1024], P('dp', 'blk'), may hold values from -6 to 6
- doc_lengths: int32 [32, 4], P('dp'), may hold values from 0 to 1024, as said below
- norm1_gain: float32 [1024], replicated, may hold values from 0.5 to 1.5
- norm1_shift: float32 [1024], replicated, may hold values from -1.75 to 1.75
- qkv_weight: bfloat16 [1024, 3072], replicated, may hold values from -0.1875 to 0.1875
- query_bias: float32 [1024], replicated, may hold values from -3 to 3
- value_bias: float32 [1024], replicated, may hold values from -3 to 3
- head_scales: float32 [16], replicated, may hold values from 0.5 to 1.5
- out_weight: bfloat16 [1024, 1024], replicated, may hold values from -0.1875 to 0.1875
- out_bias: float32 [1024], replicated, may hold values from -3 to 3
- attn_gain: float32 [1024], replicated, may hold values from 0.5 to 1.5
- attn_shift: float32 [1024], replicated, may hold values from -1.75 to 1.75
- norm2_gain: float32 [1024], replicated, may hold values from 0.5 to 1.5
- norm2_shift: float32 [1024], replicated, may hold values from -1.75 to 1.75
- fc1_weight: bfloat16 [1024, 4096], replicated, may hold values from -0.1875 to 0.1875
- fc1_bias: float32 [4096], replicated, may hold values from -3 to 3
- mid_gain: float32 [4096], replicated, may hold values from 0.5 to 1.5
- mid_shift: float32 [4096], replicated, may hold values from -1.75 to 1.75
- fc2_weight: bfloat16 [4096, 1024], replicated, may hold values from -0.09375 to 0.09375
- fc2_bias: float32 [1024], replicated, may hold values from -1.75 to 1.75
Outputs:
- output: float32 [32, 1024, 1024], P('dp', 'blk')
- tokens_grad: float32 [32, 1024, 1024], P('dp', 'blk')
- norm1_gain_grad: float32 [1024], replicated
- norm1_shift_grad: float32 [1024], replicated
- qkv_weight_grad: float32 [1024, 3072], P('dp', 'blk')
- query_bias_grad: float32 [1024], replicated
- value_bias_grad: float32 [1024], replicated
- head_scales_grad: float32 [16], replicated
- out_weight_grad: float32 [1024, 1024], P('dp', 'blk')
- out_bias_grad: float32 [1024], replicated
- attn_gain_grad: float32 [1024], replicated
- attn_shift_grad: float32 [1024], replicated
- norm2_gain_grad: float32 [1024], replicated
- norm2_shift_grad: float32 [1024], replicated
- fc1_weight_grad: float32 [1024, 4096], P('dp', 'blk')
- fc1_bias_grad: float32 [4096], replicated
- mid_gain_grad: float32 [4096], replicated
- mid_shift_grad: float32 [4096], replicated
- fc2_weight_grad: float32 [4096, 1024], P('dp', 'blk')
- fc2_bias_grad: float32 [1024], replicated
Inputs may be any that keep to these rules, and one draw needn't show every extreme that they name: `doc_lengths`: each row's 4 entries are document lengths in order (0 for an empty slot), each 0, 256, 512 or 1024, summing to 1024. In each aligned block of 2 rows (the rows of one index of dp) one row is a single document of 1024 positions.
All inputs are finite; a program needn't handle non-finite values.
Results may differ from a plain program's by a relative error of at most 0.02.
Values may be sent and summed in bfloat16 or wider, within the bound.
A program may use at most 320 MiB of HBM per device.

v0:
```python
from functools import partial

import jax
import jax.numpy as jnp
from jax import lax
from jax.sharding import PartitionSpec as P

eps = 1e-05
masked_score = -1e30


def norm_forward(values, gain, shift):
    average = jnp.mean(values, axis=-1, keepdims=True)
    centered = values - average
    inverse = lax.rsqrt(jnp.mean(centered * centered, axis=-1, keepdims=True) + eps)
    normed = centered * inverse
    return (normed * gain + shift, normed, inverse)


def norm_backward(grad_y, normed, inverse, gain):
    scaled = grad_y * gain
    grad_in = inverse * (
        scaled
        - jnp.mean(scaled, axis=-1, keepdims=True)
        - normed * jnp.mean(scaled * normed, axis=-1, keepdims=True)
    )
    return (grad_in, jnp.sum(grad_y * normed, axis=(0, 1)), jnp.sum(grad_y, axis=(0, 1)))


def local(
    tokens,
    cotangent,
    doc_lengths,
    norm1_gain,
    norm1_shift,
    qkv_weight,
    query_bias,
    value_bias,
    head_scales,
    out_weight,
    out_bias,
    attn_gain,
    attn_shift,
    norm2_gain,
    norm2_shift,
    fc1_weight,
    fc1_bias,
    mid_gain,
    mid_shift,
    fc2_weight,
    fc2_bias,
):
    f32 = jnp.float32
    bf16 = jnp.bfloat16
    batch_size, local_len, model_width = tokens.shape
    head_count = head_scales.shape[0]
    head_dim = model_width // head_count
    score_scale = head_dim ** (-0.5)
    row_len = local_len * lax.axis_size("blk")
    row_first = lax.axis_index("blk") * local_len
    query_pos = row_first + jnp.arange(local_len, dtype=jnp.int32)
    doc_ends = jnp.cumsum(doc_lengths, axis=1, dtype=jnp.int32)
    starts = jnp.max(
        jnp.where(doc_ends[:, None, :] <= query_pos[None, :, None], doc_ends[:, None, :], 0), axis=2
    )
    lowest = jnp.min(starts[:, 0])
    query_last = row_first + local_len - 1
    inputs = tokens.astype(f32)
    attn_norm, unit_one, inverse_one = norm_forward(inputs, norm1_gain, norm1_shift)
    attn_in = attn_norm.astype(bf16)
    projected = jnp.dot(attn_in, qkv_weight, preferred_element_type=f32)
    queries = (
        (projected[..., :model_width] + query_bias)
        .astype(bf16)
        .reshape(batch_size, local_len, head_count, head_dim)
    )
    keys_low = projected[..., model_width : 2 * model_width].astype(bf16)
    values_low = (projected[..., 2 * model_width :] + value_bias).astype(bf16)

    def block_scores(key_piece, offset):
        key_len = key_piece.shape[1]
        keys_head = key_piece.reshape(batch_size, key_len, head_count, head_dim)
        raw_scores = (
            jnp.einsum("bqhd,bkhd->bhqk", queries, keys_head, preferred_element_type=f32)
            * score_scale
        )
        key_pos = offset + jnp.arange(key_len, dtype=jnp.int32)
        allowed = (key_pos[None, None, :] <= query_pos[None, :, None]) & (
            key_pos[None, None, :] >= starts[:, :, None]
        )
        return (jnp.where(allowed[:, None], raw_scores, masked_score), keys_head)

    def is_live(offset, key_len):
        return (offset <= query_last) & (offset + key_len - 1 >= lowest)

    def attend_slab(running, key_piece, value_piece, offset):
        key_len = key_piece.shape[1]

        def attend_compute(state):
            running_max, running_sum, weighted = state
            scores, keys_head = block_scores(key_piece, offset)
            new_max = jnp.maximum(running_max, jnp.max(scores, axis=3))
            rescale = jnp.exp(running_max - new_max)
            weights = jnp.exp(scores - new_max[..., None])
            values_head = value_piece.reshape(batch_size, key_len, head_count, head_dim)
            update = jnp.einsum(
                "bhqk,bkhd->bqhd", weights.astype(bf16), values_head, preferred_element_type=f32
            )
            rescale_t = jnp.transpose(rescale, (0, 2, 1))[..., None]
            return (
                new_max,
                running_sum * rescale + jnp.sum(weights, axis=3),
                weighted * rescale_t + update,
            )

        return lax.cond(is_live(offset, key_len), attend_compute, lambda state: state, running)

    start_state = (
        jnp.full((batch_size, head_count, local_len), masked_score, f32),
        jnp.zeros((batch_size, head_count, local_len), f32),
        jnp.zeros((batch_size, local_len, head_count, head_dim), f32),
    )
    key_piece = lax.all_gather(keys_low, "blk", axis=1, tiled=True)
    value_piece = lax.all_gather(values_low, "blk", axis=1, tiled=True)
    turns = key_piece.shape[1] // local_len

    def one_turn(index, state):
        begin = index * local_len
        key_slab = lax.dynamic_slice_in_dim(key_piece, begin, local_len, 1)
        value_slab = lax.dynamic_slice_in_dim(value_piece, begin, local_len, 1)
        return attend_slab(state, key_slab, value_slab, begin)

    running_max, running_sum, weighted = lax.fori_loop(0, turns, one_turn, start_state)
    attended = weighted / jnp.transpose(running_sum, (0, 2, 1))[..., None]
    log_total = running_max + jnp.log(running_sum)
    heads_out = (
        (attended * head_scales[:, None]).reshape(batch_size, local_len, model_width).astype(bf16)
    )
    projection = jnp.dot(heads_out, out_weight, preferred_element_type=f32) + out_bias
    branch, unit_attn, inverse_attn = norm_forward(projection, attn_gain, attn_shift)
    middle = inputs + branch
    ffn_norm, unit_two, inverse_two = norm_forward(middle, norm2_gain, norm2_shift)
    ffn_in = ffn_norm.astype(bf16)
    hidden = jnp.dot(ffn_in, fc1_weight, preferred_element_type=f32) + fc1_bias
    activated, gelu_grad = jax.vjp(partial(jax.nn.gelu, approximate=False), hidden)
    mid_norm, unit_mid, inverse_mid = norm_forward(activated, mid_gain, mid_shift)
    mid_out = mid_norm.astype(bf16)
    output = middle + jnp.dot(mid_out, fc2_weight, preferred_element_type=f32) + fc2_bias
    grad_output = cotangent.astype(f32)
    fc2_weight_grad = jnp.einsum("bcf,bcd->fd", mid_out, cotangent, preferred_element_type=f32)
    fc2_bias_grad = jnp.sum(grad_output, axis=(0, 1))
    grad_mid = jnp.einsum("bcd,fd->bcf", cotangent, fc2_weight, preferred_element_type=f32)
    grad_act, mid_gain_grad, mid_shift_grad = norm_backward(
        grad_mid, unit_mid, inverse_mid, mid_gain
    )
    grad_hidden = gelu_grad(grad_act)[0].astype(bf16)
    fc1_weight_grad = jnp.einsum("bcd,bcf->df", ffn_in, grad_hidden, preferred_element_type=f32)
    fc1_bias_grad = jnp.sum(grad_hidden.astype(f32), axis=(0, 1))
    grad_ffn_in = jnp.einsum("bcf,df->bcd", grad_hidden, fc1_weight, preferred_element_type=f32)
    grad_two, norm2_gain_grad, norm2_shift_grad = norm_backward(
        grad_ffn_in, unit_two, inverse_two, norm2_gain
    )
    grad_middle = grad_output + grad_two
    grad_proj_f, attn_gain_grad, attn_shift_grad = norm_backward(
        grad_middle, unit_attn, inverse_attn, attn_gain
    )
    grad_projection = grad_proj_f.astype(bf16)
    out_weight_grad = jnp.einsum(
        "bcd,bce->de", heads_out, grad_projection, preferred_element_type=f32
    )
    out_bias_grad = jnp.sum(grad_projection.astype(f32), axis=(0, 1))
    grad_heads = jnp.einsum(
        "bce,de->bcd", grad_projection, out_weight, preferred_element_type=f32
    ).reshape(batch_size, local_len, head_count, head_dim)
    head_scales_grad = jnp.sum(grad_heads * attended, axis=(0, 1, 3))
    grad_attended = (grad_heads * head_scales[:, None]).astype(bf16)
    row_dot = jnp.transpose(jnp.sum(grad_attended.astype(f32) * attended, axis=3), (0, 2, 1))

    def back_slab(running, key_piece, value_piece, offset):
        key_len = key_piece.shape[1]

        def back_compute(state):
            grad_queries, kv_buffer = state
            scores, keys_head = block_scores(key_piece, offset)
            attn_probs = jnp.exp(scores - log_total[..., None])
            values_head = value_piece.reshape(batch_size, key_len, head_count, head_dim)
            grad_probs = jnp.einsum(
                "bqhd,bkhd->bhqk", grad_attended, values_head, preferred_element_type=f32
            )
            grad_scores = (attn_probs * (grad_probs - row_dot[..., None])).astype(bf16)
            grad_queries = (
                grad_queries
                + jnp.einsum("bhqk,bkhd->bqhd", grad_scores, keys_head, preferred_element_type=f32)
                * score_scale
            )
            grad_keys = (
                jnp.einsum("bhqk,bqhd->bkhd", grad_scores, queries, preferred_element_type=f32)
                * score_scale
            )
            grad_values = jnp.einsum(
                "bhqk,bqhd->bkhd",
                attn_probs.astype(bf16),
                grad_attended,
                preferred_element_type=f32,
            )
            addition = jnp.concatenate(
                [
                    grad_keys.reshape(batch_size, key_len, model_width),
                    grad_values.reshape(batch_size, key_len, model_width),
                ],
                axis=2,
            )
            previous = lax.dynamic_slice_in_dim(kv_buffer, offset, key_len, 1)
            return (
                grad_queries,
                lax.dynamic_update_slice_in_dim(kv_buffer, previous + addition, offset, 1),
            )

        return lax.cond(is_live(offset, key_len), back_compute, lambda state: state, running)

    back_state = (
        jnp.zeros((batch_size, local_len, head_count, head_dim), f32),
        jnp.zeros((batch_size, row_len, 2 * model_width), f32),
    )
    attend_key_piece = lax.all_gather(keys_low, "blk", axis=1, tiled=True)
    attend_value_piece = lax.all_gather(values_low, "blk", axis=1, tiled=True)
    turns = attend_key_piece.shape[1] // local_len

    def one_turn(index, state):
        begin = index * local_len
        key_slab = lax.dynamic_slice_in_dim(attend_key_piece, begin, local_len, 1)
        value_slab = lax.dynamic_slice_in_dim(attend_value_piece, begin, local_len, 1)
        return back_slab(state, key_slab, value_slab, begin)

    grad_queries, kv_buffer = lax.fori_loop(0, turns, one_turn, back_state)
    grad_kv = lax.psum_scatter(
        kv_buffer.astype(jnp.bfloat16), "blk", scatter_dimension=1, tiled=True
    ).astype(jnp.float32)
    grad_qkv = jnp.concatenate(
        [grad_queries.reshape(batch_size, local_len, model_width), grad_kv], axis=2
    ).astype(bf16)
    qkv_weight_grad = jnp.einsum("bcd,bce->de", attn_in, grad_qkv, preferred_element_type=f32)
    query_bias_grad = jnp.sum(grad_qkv[..., :model_width].astype(f32), axis=(0, 1))
    value_bias_grad = jnp.sum(grad_qkv[..., 2 * model_width :].astype(f32), axis=(0, 1))
    grad_attn_in = jnp.einsum("bce,de->bcd", grad_qkv, qkv_weight, preferred_element_type=f32)
    grad_one, norm1_gain_grad, norm1_shift_grad = norm_backward(
        grad_attn_in, unit_one, inverse_one, norm1_gain
    )
    tokens_grad = grad_middle + grad_one
    matrix_grads = (qkv_weight_grad, out_weight_grad, fc1_weight_grad, fc2_weight_grad)
    reduced = (
        lax.psum_scatter(
            matrix_grads[0].astype(jnp.bfloat16), "dp", scatter_dimension=0, tiled=True
        ).astype(jnp.float32),
        lax.psum_scatter(
            matrix_grads[1].astype(jnp.bfloat16), "dp", scatter_dimension=0, tiled=True
        ).astype(jnp.float32),
        lax.psum_scatter(
            matrix_grads[2].astype(jnp.bfloat16), "dp", scatter_dimension=0, tiled=True
        ).astype(jnp.float32),
        lax.psum_scatter(
            matrix_grads[3].astype(jnp.bfloat16), "dp", scatter_dimension=0, tiled=True
        ).astype(jnp.float32),
    )
    reduced = (
        lax.psum_scatter(
            reduced[0].astype(jnp.bfloat16), "blk", scatter_dimension=1, tiled=True
        ).astype(jnp.float32),
        lax.psum_scatter(
            reduced[1].astype(jnp.bfloat16), "blk", scatter_dimension=1, tiled=True
        ).astype(jnp.float32),
        lax.psum_scatter(
            reduced[2].astype(jnp.bfloat16), "blk", scatter_dimension=1, tiled=True
        ).astype(jnp.float32),
        lax.psum_scatter(
            reduced[3].astype(jnp.bfloat16), "blk", scatter_dimension=1, tiled=True
        ).astype(jnp.float32),
    )
    small_sums = lax.psum(
        (
            norm1_gain_grad,
            norm1_shift_grad,
            query_bias_grad,
            value_bias_grad,
            head_scales_grad,
            out_bias_grad,
            attn_gain_grad,
            attn_shift_grad,
            norm2_gain_grad,
            norm2_shift_grad,
            fc1_bias_grad,
            mid_gain_grad,
            mid_shift_grad,
            fc2_bias_grad,
        ),
        ("dp", "blk"),
    )
    return (
        output,
        tokens_grad,
        small_sums[0],
        small_sums[1],
        reduced[0],
        small_sums[2],
        small_sums[3],
        small_sums[4],
        reduced[1],
        small_sums[5],
        small_sums[6],
        small_sums[7],
        small_sums[8],
        small_sums[9],
        reduced[2],
        small_sums[10],
        small_sums[11],
        small_sums[12],
        reduced[3],
        small_sums[13],
    )


def solution(mesh):
    placed = (
        P("dp", "blk", None),
        P("dp", "blk", None),
        P("dp", None),
        P(),
        P(),
        P(),
        P(),
        P(),
        P(),
        P(),
        P(),
        P(),
        P(),
        P(),
        P(),
        P(),
        P(),
        P(),
        P(),
        P(),
        P(),
    )
    return jax.shard_map(
        local,
        mesh=mesh,
        in_specs=placed,
        out_specs=(
            P("dp", "blk", None),
            P("dp", "blk", None),
            P(),
            P(),
            P("dp", "blk"),
            P(),
            P(),
            P(),
            P("dp", "blk"),
            P(),
            P(),
            P(),
            P(),
            P(),
            P("dp", "blk"),
            P(),
            P(),
            P(),
            P("dp", "blk"),
            P(),
        ),
        check_vma=False,
    )
```

profile of v0, /device:TPU:0, one launch (start us, length us, event | category | flops | bytes accessed | tf_op | source)
XLA Modules:
  0.0 1123.7 jit_solution(9375756112477163833)
XLA Ops:
  37.2 50.2 %all-gather.5.cloned.1.call-done = bf16[2,1024,1024]{2,1,0:T(8,128)(2,1)} async-done(((bf16[2,512,1024]{2,1,0:T(8,128)(2,1)}), bf16[2,1024,1024]{2,1,0:T(8,128)(2,1)}) %all-gather.5.cloned.1.call-update) | async-done | bytes 4194320 | tf_op jit(solution)/shard_map/all_gather | solution.py:124
  93.6 52.7 %all-gather.3.cloned.1.call-done = bf16[2,1024,1024]{2,1,0:T(8,128)(2,1)} async-done(((bf16[2,512,1024]{2,1,0:T(8,128)(2,1)}), bf16[2,1024,1024]{2,1,0:T(8,128)(2,1)}) %all-gather.3.cloned.1.call-update) | async-done | bytes 4194320 | tf_op jit(solution)/shard_map/all_gather | solution.py:123
  155.0 52.4 %while.42 = (s32[]{:T(128)}, f32[2,16,512]{2,1,0:T(8,128)S(1)}, f32[2,16,512]{2,1,0:T(8,128)S(1)}, f32[2,512,16,64]{1,3,2,0:T(8,128)}, s32[]{:T(128)}, /*index=5...) while((s32[]{:T(128)}, f32[2,16,512]{2,1,0:T(8,128)S(1)}, ...), condition=%wide.region_10.11_spmd.clone, body=%wide.region_5.10_spmd.clone.sunk | while | flops 2243216384 | bytes 135809408 | solution.py:133
  155.7 50.8 %conditional.6 = ((f32[2,16,512]{2,1,0:T(8,128)S(1)}, f32[2,16,512]{2,1,0:T(8,128)S(1)}, f32[2,512,16,64]{1,3,2,0:T(8,128)})) conditional(s32[]{:T(128)} %convert_element_type.236, (f32[2,16,512]{2,1,0:T(8,128)S(1)}, f32[2,16,512]{2,1,0:T(8,128)S(1)}, f32[2,512,16,64]{1,3,2,0:T(8,128)}) %tuple.184, (s32[]{:T(128)}, s32[]{:T(128)}, ...), branch_computations={%region_6.6_spmd, %region_7.9_spmd} | conditional | flops 2243216384 | bytes 135807072 | solution.py:116
  160.5 13.4 %fusion.6 = (f32[2,16,512]{2,1,0:T(8,128)S(1)}, f32[2,16,512,512]{3,2,1,0:T(8,128)}) fusion(pred[2,512,512]{1,2,0:T(8,128)(4,1)S(1)} %compare_and_fusion, bf16[2,512,16,64]{1,3,2,0:T(8,128)(2,1)S(1)} %bitcast.115, bf16[2,512,16,64]{1,3,2,0:T(8,128)(2,1)S(1)} %copy-done.2), kind=kOutput, calls=%fused_computation.6 | convolution fusion | flops 1098891264 | bytes 38338560 | tf_op jit(solution)/shard_map/while/body/eval_jaxpr/cond/branch_1_fun/bqhd,bkhd->bhqk/dot_general | solution.py:84
  173.9 18.4 %bitcast_add_fusion = f32[2,512,16,64]{1,3,2,0:T(8,128)} fusion(f32[2,512,16,64]{1,3,2,0:T(8,128)} %get-tuple-element.987, bf16[2,512,16,64]{1,3,2,0:T(8,128)(2,1)} %bitcast.117, f32[2,16,512,512]{3,2,1,0:T(8,128)} %get-tuple-element.1296, f32[2,16,512]{2,1,0:T(8,128)S(1)} %get-tuple-element.1475, pred[2,512,512]{1,2,0:T(8,128)(4,1)S(1)} %compare_and_fusion, ...), kind=kOutput, calls=%fused_computation.9 | convolution fusion | flops 1109393408 | bytes 44695552 | tf_op jit(solution)/shard_map/while/body/eval_jaxpr/cond/branch_1_fun/bhqk,bkhd->bqhd/dot_general | solution.py:106
  192.3 14.2 %fusion.5 = f32[2,16,512]{2,1,0:T(8,128)S(1)} fusion(f32[2,16,512,512]{3,2,1,0:T(8,128)} %get-tuple-element.1296, f32[2,16,512]{2,1,0:T(8,128)S(1)} %get-tuple-element.1475, pred[2,512,512]{1,2,0:T(8,128)(4,1)S(1)} %compare_and_fusion), kind=kLoop, calls=%fused_computation.5 | loop fusion | flops 33538048 | bytes 34209792 | tf_op jit(solution)/shard_map/while/body/eval_jaxpr/cond/branch_1_fun/reduce_sum | solution.py:112
  220.4 24.5 %fusion.60 = (u8[512,4096]{1,0:T(8,128)(4,1)}, u8[512,4096]{1,0:T(8,128)(4,1)}, f32[2,512,4096]{2,1,0:T(8,128)}) fusion(f32[4096]{0:T(1024)S(1)} %copy-done.31, bf16[1024,4096]{1,0:T(8,128)(2,1)} %param.44, f32[2,512,1024]{2,1,0:T(8,128)} %copy-done.11, f32[1024]{0:T(1024)S(1)} %copy-done.54, f32[1024]{0:T(1024)S(1)} %copy-done.46, ...), kind=kOutput, calls=%fused_computation.127 | convolution fusion | flops 8649703424 | bytes 33587200 | tf_op jit(solution)/shard_map/dot_general | solution.py:144
  244.9 46.6 %fusion.71 = (f32[2,512]{1,0:T(2,128)S(1)}, f32[2,512,4096]{2,1,0:T(8,128)}, f32[2,512,4096]{2,1,0:T(8,128)}) fusion(f32[2,512,4096]{2,1,0:T(8,128)} %get-tuple-element.1310, f32[4096]{0:T(1024)S(1)} %copy-done.31, u8[512,4096]{1,0:T(8,128)(4,1)} %get-tuple-element.1202, u8[512,4096]{1,0:T(8,128)(4,1)} %get-tuple-element.1201), kind=kLoop, calls=%fused_computation.161 | loop fusion | flops 297794560 | bytes 54546432 | tf_op jit(solution)/shard_map/reduce_sum | solution.py:13
  299.1 21.6 %multiply_reduce_fusion = (f32[4096]{0:T(1024)}, f32[2,512]{1,0:T(2,128)S(1)}, f32[2,512]{1,0:T(2,128)S(1)}, f32[4096]{0:T(1024)}, f32[2,512,4096]{2,1,0:T(8,128)}) fusion(f32[2,512,4096]{2,1,0:T(8,128)} %get-tuple-element.1291, f32[2,512]{1,0:T(2,128)S(1)} %add_rsqrt_fusion, f32[2,512]{1,0:T(2,128)S(1)} %broadcast_multiply_fusion.2, ...), kind=kOutput, calls=%fused_computation.50 | convolution fusion | flops 8627673088 | bytes 44105728 | tf_op jit(solution)/shard_map/bcd,fd->bcf/dot_general | solution.py:152
  320.8 28.4 %convert_reduce_fusion = (f32[4096]{0:T(1024)}, bf16[2,512,4096]{2,1,0:T(8,128)(2,1)}) fusion(f32[2,512,4096]{2,1,0:T(8,128)} %get-tuple-element.1292, f32[2,512]{1,0:T(2,128)S(1)} %get-tuple-element.1314, f32[2,512,4096]{2,1,0:T(8,128)} %get-tuple-element.1291, f32[2,512]{1,0:T(2,128)S(1)} %broadcast_multiply_fusion.2, ...), kind=kLoop, calls=%fused_computation.51 | loop fusion | flops 100659200 | bytes 75563008 | tf_op jit(solution)/shard_map/reduce_sum | solution.py:158
  349.2 15.6 %multiply_reduce_fusion.4 = (f32[1024]{0:T(1024)}, f32[2,512]{1,0:T(2,128)S(1)}, f32[2,512]{1,0:T(2,128)S(1)}, f32[1024]{0:T(1024)}, f32[2,512,1024]{2,1,0:T(8,128)S(1)}) fusion(f32[2,512,1024]{2,1,0:T(8,128)S(1)} %copy-done.12, f32[2,512]{1,0:T(2,128)S(1)} %add_rsqrt_fusion.1, f32[2,512]{1,0:T(2,128)S(1)} %broadcast_multiply_fusion.9, ...), kind=kOutput, calls=%fused_computation.110 | convolution fusion | flops 8599367680 | bytes 25194496 | tf_op jit(solution)/shard_map/bcf,df->bcd/dot_general | solution.py:159
  377.2 19.5 %bitcast_convert_fusion = bf16[4096,1024]{1,0:T(8,128)(2,1)} fusion(bf16[2,512,1024]{2,1,0:T(8,128)(2,1)} %param.30, f32[2,512,4096]{2,1,0:T(8,128)} %get-tuple-element.1291, f32[4096]{0:T(1024)S(1)} %copy-done.52, f32[4096]{0:T(1024)S(1)} %copy-done.41, f32[2,512]{1,0:T(2,128)S(1)} %add_rsqrt_fusion, f32[2,512]{1,0:T(2,128)S(1)} %broadcast_multiply_fusion.2), kind=kOutput, calls=%fused_computation.48 | convolution fusion | flops 8615100416 | bytes 27303936 | tf_op jit(solution)/shard_map/bcf,bcd->fd/dot_general | solution.py:150
  396.8 15.3 %bitcast_convert_fusion.1 = bf16[1024,4096]{1,0:T(8,128)(2,1)} fusion(bf16[2,512,4096]{2,1,0:T(8,128)(2,1)} %get-tuple-element.1283, f32[2,512,1024]{2,1,0:T(8,128)} %copy-done.11, f32[1024]{0:T(1024)S(1)} %copy-done.54, f32[1024]{0:T(1024)S(1)} %copy-done.46, f32[2,512]{1,0:T(2,128)S(1)} %add_rsqrt_fusion.1, f32[2,512]{1,0:T(2,128)S(1)} %broadcast_multiply_fusion.9), kind=kOutput, calls=%fused_computation.49 | convolution fusion | flops 8599371776 | bytes 20987904 | tf_op jit(solution)/shard_map/bcd,bcf->df/dot_general | solution.py:157
  430.9 90.2 %while.43 = (s32[]{:T(128)}, f32[2,512,16,64]{1,3,2,0:T(8,128)}, f32[2,1024,2048]{1,2,0:T(8,128)}, s32[]{:T(128)}, s32[]{:T(128)}, /*index=5*/s32[2,512]{1,0:T(2...) while((s32[]{:T(128)}, f32[2,512,16,64]{1,3,2,0:T(8,128)}, ...), condition=%wide.region_27.28_spmd.clone, body=%wide.region_24.27_spmd.clone.sunk | while | flops 5461246976 | bytes 277039584 | solution.py:235
  431.9 88.4 %conditional.7 = ((f32[2,512,16,64]{1,3,2,0:T(8,128)}, f32[2,1024,2048]{1,2,0:T(8,128)})) conditional(s32[]{:T(128)} %convert_element_type.237, (f32[2,512,16,64]{1,3,2,0:T(8,128)}, f32[2,1024,2048]{1,2,0:T(8,128)}) %tuple.187, (s32[]{:T(128)}, s32[]{:T(128)}, s32[2,512]{1,0:T(2,128)S(1)}, bf16[2,1024,1024]{1,2,0:T(8,128)(2,1)}, ...), branch_computations={%region_25.25_spmd, %region_26.26_spmd} | conditional | flops 5461246976 | bytes 277037248 | solution.py:219
  435.2 13.8 %fusion.74 = f32[2,16,512,512]{3,2,1,0:T(8,128)} fusion(bf16[2,512,16,64]{1,3,2,0:T(8,128)(2,1)S(1)} %bitcast.113, bf16[2,512,16,64]{1,3,2,0:T(8,128)(2,1)S(1)} %get-tuple-element.1009), kind=kOutput, calls=%fused_computation.163 | convolution fusion | flops 1073741824 | bytes 37748736 | tf_op jit(solution)/shard_map/while/body/eval_jaxpr/cond/branch_1_fun/bqhd,bkhd->bhqk/dot_general | solution.py:84
  449.0 19.9 %fusion.15 = bf16[2,16,512,512]{2,3,1,0:T(8,128)(2,1)} fusion(f32[2,16,512,512]{3,2,1,0:T(8,128)} %fusion.74, bf16[2,512,16,64]{1,3,2,0:T(8,128)(2,1)S(1)} %bitcast.118, bf16[2,512,16,64]{1,3,2,0:T(8,128)(2,1)S(1)} %copy-done.26, f32[2,16,512]{2,1,0:T(8,128)S(1)} %get-tuple-element.1013, f32[2,16,512]{2,1,0:T(8,128)S(1)} %get-tuple-element.1010, ...), kind=kOutput, calls=%fused_computation.22 | convolution fusion | flops 1124073472 | bytes 55181312 | tf_op jit(solution)/shard_map/while/body/eval_jaxpr/cond/branch_1_fun/bqhd,bkhd->bhqk/dot_general | solution.py:187
  468.9 10.9 convolution_multiply_fusion
  479.8 16.6 %fusion.19 = f32[2,16,512,64]{2,3,1,0:T(8,128)} fusion(bf16[2,512,16,64]{1,3,2,0:T(8,128)(2,1)} %get-tuple-element.1012, f32[2,16,512,512]{3,2,1,0:T(8,128)} %fusion.74, f32[2,16,512]{2,1,0:T(8,128)S(1)} %get-tuple-element.1010, pred[2,512,512]{1,2,0:T(8,128)(4,1)S(1)} %compare_and_fusion.1), kind=kOutput, calls=%fused_computation.27 | convolution fusion | flops 1107296256 | bytes 40435712 | tf_op jit(solution)/shard_map/while/body/eval_jaxpr/cond/branch_1_fun/bhqk,bqhd->bkhd/dot_general | solution.py:200
  496.4 11.7 %fusion.22 = f32[2,1024,2048]{1,2,0:T(8,128)} fusion(f32[2,1024,2048]{1,2,0:T(8,128)} %get-tuple-element.1014, s32[]{:T(128)S(6)} %select_n.46, f32[2,512,1024]{1,2,0:T(8,128)} %bitcast.116, f32[2,512,1024]{1,2,0:T(8,128)} %bitcast.112), kind=kLoop, calls=%fused_computation.30 | loop fusion | flops 4194304 | bytes 25165828 | tf_op jit(solution)/shard_map/while/body/eval_jaxpr/cond/branch_1_fun/dynamic_update_slice | solution.py:216
  508.1 10.2 bitcast_add_fusion.1
  521.2 13.7 %copy.86 = bf16[2,1024,2048]{2,1,0:T(8,128)(2,1)} copy(f32[2,1024,2048]{1,2,0:T(8,128)} %get-tuple-element.1060) | data formatting | bytes 25165824 | tf_op jit(solution)/shard_map/while | solution.py:235
  535.7 62.0 %reduce-scatter.24.cloned.1.call-done = bf16[256,1024]{1,0:T(8,128)(2,1)} async-done(((bf16[4096,1024]{1,0:T(8,128)(2,1)}), bf16[256,1024]{1,0:T(8,128)(2,1)}) %reduce-scatter.24.cloned.1.call-update) | async-done | bytes 524304 | tf_op jit(solution)/shard_map/reduce_scatter | solution.py:261
  606.3 100.4 %reduce-scatter.20.cloned.1.call-done = bf16[64,4096]{1,0:T(8,128)(2,1)} async-done(((bf16[1024,4096]{1,0:T(8,128)(2,1)}), bf16[64,4096]{1,0:T(8,128)(2,1)}) %reduce-scatter.20.cloned.1.call-update) | async-done | bytes 524304 | tf_op jit(solution)/shard_map/reduce_scatter | solution.py:258
  706.7 101.2 %reduce-scatter.10.cloned.1.call-done = bf16[2,512,2048]{2,1,0:T(8,128)(2,1)} async-done(((bf16[2,1024,2048]{2,1,0:T(8,128)(2,1)}), bf16[2,512,2048]{2,1,0:T(8,128)(2,1)}) %reduce-scatter.10.cloned.1.call-update) | async-done | bytes 4194320 | tf_op jit(solution)/shard_map/reduce_scatter | solution.py:236
  808.0 12.0 %bitcast_convert_fusion.2 = bf16[1024,3072]{1,0:T(8,128)(2,1)} fusion(bf16[2,512,2048]{2,1,0:T(8,128)(2,1)} %reduce-scatter.10.cloned.1.call-done, bf16[2,512,1024]{2,1,0:T(8,128)(2,1)} %copy.87, bf16[2,512,1024]{2,1,0:T(8,128)(2,1)S(1)} %copy-done.16, f32[1024]{0:T(1024)S(1)} %copy-done.56, f32[1024]{0:T(1024)S(1)} %copy-done.48, ...), kind=kOutput, calls=%fused_computation.71 | convolution fusion | flops 6464471040 | bytes 14696448 | tf_op jit(solution)/shard_map/bcd,bce->de/dot_general | solution.py:242
  820.8 16.8 %add_add_fusion = f32[2,512,1024]{2,1,0:T(8,128)} fusion(f32[2,512,1024]{2,1,0:T(8,128)} %copy-done.11, bf16[4096,1024]{1,0:T(8,128)(2,1)} %param.48, f32[1024]{0:T(1024)S(1)} %copy-done.57, f32[2,512,4096]{2,1,0:T(8,128)} %get-tuple-element.1291, f32[4096]{0:T(1024)S(1)} %copy-done.53, f32[4096]{0:T(1024)S(1)} %copy-done.42, f32[2,512]{1,0:T(2,128)S(1)} %copy-done.40, ...), kind=kOutput, calls=%fused_computation.121 | convolution fusion | flops 8613003264 | bytes 33599488 | tf_op jit(solution)/shard_map/dot_general | solution.py:148
  840.9 13.3 %reduce-scatter.22.cloned.1.call-done = bf16[64,2048]{1,0:T(8,128)(2,1)} async-done(((bf16[64,4096]{1,0:T(8,128)(2,1)}), bf16[64,2048]{1,0:T(8,128)(2,1)}) %reduce-scatter.22.cloned.1.call-update) | async-done | bytes 262160 | tf_op jit(solution)/shard_map/reduce_scatter | solution.py:272
  856.0 87.3 %reduce-scatter.12.cloned.1.call-done = bf16[64,3072]{1,0:T(8,128)(2,1)} async-done(((bf16[1024,3072]{1,0:T(8,128)(2,1)}), bf16[64,3072]{1,0:T(8,128)(2,1)}) %reduce-scatter.12.cloned.1.call-update) | async-done | bytes 393232 | tf_op jit(solution)/shard_map/reduce_scatter | solution.py:252
  943.3 13.9 %fusion.55 = (f32[1024]{0:T(1024)}, f32[2,512]{1,0:T(2,128)S(1)}, f32[2,512]{1,0:T(2,128)S(1)}, f32[1024]{0:T(1024)}, f32[2,512,1024]{2,1,0:T(8,128)}) fusion(bf16[2,512,1024]{2,1,0:T(8,128)(2,1)S(1)} %copy-done.16, f32[2,512]{1,0:T(2,128)S(1)} %copy-done.38, f32[2,512]{1,0:T(2,128)S(1)} %copy-done.34, f32[1024]{0:T(1024)S(1)} %copy-done.48, ...), kind=kOutput, calls=%fused_computation.102 | convolution fusion | flops 6465515520 | bytes 18903040 | tf_op jit(solution)/shard_map/bce,de->bcd/dot_general | solution.py:245
  966.2 132.7 %all-reduce.3.cloned.1.call-done = (f32[1024]{0:T(1024)}, f32[1024]{0:T(1024)}, f32[1024]{0:T(1024)}, f32[1024]{0:T(1024)}, f32[16]{0:T(128)}, /*index=5*/f32[10...) async-done(((f32[1024]{0:T(1024)}, f32[1024]{0:T(1024)}, ...) | async-done | bytes 90192 | tf_op jit(solution)/shard_map/psum | solution.py:279
  (227 shorter events, 148.5 us)
Async XLA Ops:
  7.2 203.4 %copy-start = (bf16[1024,1024]{1,0:T(8,128)(2,1)S(1)}, bf16[1024,1024]{1,0:T(8,128)(2,1)}, u32[]{:S(2)}) copy-start(bf16[1024,1024]{1,0:T(8,128)(2,1)} %param.38) | copy-start | bytes 6291460
  7.2 80.1 %all-gather.5.cloned.1.call-start = ((), (), s32[]{:S(2)}) async-start(), calls=%async_computation.10 | async-start | bytes 6291456 | tf_op jit(solution)/shard_map/all_gather | solution.py:124
  12.3 9.1 copy-start.43
  12.3 9.1 copy-start.44
  27.7 118.5 %all-gather.3.cloned.1.call-start = ((), (), s32[]{:S(2)}) async-start(), calls=%async_computation.9 | async-start | bytes 6291456 | tf_op jit(solution)/shard_map/all_gather | solution.py:123
  31.7 503.3 %reduce-scatter.16.cloned.1.call-start = ((), (), s32[]{:S(2)}) async-start(), calls=%async_computation.14 | async-start | bytes 2228224 | tf_op jit(solution)/shard_map/reduce_scatter | solution.py:255
  155.0 52.4 %copy-start.49 = (f32[16]{0:T(128)S(1)}, f32[16]{0:T(128)}, u32[]{:S(2)}) copy-start(f32[16]{0:T(128)} %param.37) | copy-start | bytes 196
  291.5 85.7 %copy-start.35 = (f32[2,512]{1,0:T(2,128)}, f32[2,512]{1,0:T(2,128)S(1)}, u32[]{:S(2)}) copy-start(f32[2,512]{1,0:T(2,128)S(1)} %broadcast_multiply_fusion.2) | copy-start | bytes 12292
  299.1 78.1 %copy-start.39 = (f32[2,512]{1,0:T(2,128)}, f32[2,512]{1,0:T(2,128)S(1)}, u32[]{:S(2)}) copy-start(f32[2,512]{1,0:T(2,128)S(1)} %add_rsqrt_fusion) | copy-start | bytes 12292
  320.8 28.5 %copy-start.12 = (f32[2,512,1024]{2,1,0:T(8,128)S(1)}, f32[2,512,1024]{2,1,0:T(8,128)}, u32[]{:S(2)}) copy-start(f32[2,512,1024]{2,1,0:T(8,128)} %copy-done.11) | copy-start | bytes 12582916
  349.2 15.6 %copy-start.9 = (f32[2,512,1024]{2,1,0:T(8,128)S(1)}, f32[2,512,1024]{2,1,0:T(8,128)}, u32[]{:S(2)}) copy-start(f32[2,512,1024]{2,1,0:T(8,128)} %copy-done.8) | copy-start | bytes 12582916
  349.2 15.6 %copy-start.22 = (bf16[2,512,1024]{2,1,0:T(8,128)(2,1)S(1)}, bf16[2,512,1024]{2,1,0:T(8,128)(2,1)}, u32[]{:S(2)}) copy-start(bf16[2,512,1024]{2,1,0:T(8,128)(2,1)} %param.30) | copy-start | bytes 6291460
  377.2 220.5 %reduce-scatter.24.cloned.1.call-start = ((), (), s32[]{:S(2)}) async-start(), calls=%async_computation.18 | async-start | bytes 8912896 | tf_op jit(solution)/shard_map/reduce_scatter | solution.py:261
  396.7 309.9 %reduce-scatter.20.cloned.1.call-start = ((), (), s32[]{:S(2)}) async-start(), calls=%async_computation.16 | async-start | bytes 8912896 | tf_op jit(solution)/shard_map/reduce_scatter | solution.py:258
  412.1 395.9 %reduce-scatter.10.cloned.1.call-start = ((), (), s32[]{:S(2)}) async-start(), calls=%async_computation.11 | async-start | bytes 12582912 | tf_op jit(solution)/shard_map/reduce_scatter | solution.py:236
  435.2 13.8 %copy-start.4 = (bf16[2,512,1024]{1,2,0:T(8,128)(2,1)}, bf16[2,512,1024]{1,2,0:T(8,128)(2,1)S(1)}, u32[]{:S(2)}) copy-start(bf16[2,512,1024]{1,2,0:T(8,128)(2,1)S(1)} %get-tuple-element.1304) | copy-start | bytes 6291460 | tf_op jit(solution)/shard_map/while/body/eval_jaxpr/cond
  435.2 13.8 %copy-start.26 = (bf16[2,512,16,64]{1,3,2,0:T(8,128)(2,1)S(1)}, bf16[2,512,16,64]{1,3,2,0:T(8,128)(2,1)}, u32[]{:S(2)}) copy-start(bf16[2,512,16,64]{1,3,2,0:T(8,128)(2,1)} %get-tuple-element.1012) | copy-start | bytes 6291460 | tf_op jit(solution)/shard_map/while/body/eval_jaxpr/cond
  496.4 11.7 %copy-start.5 = (bf16[2,512,1024]{1,2,0:T(8,128)(2,1)S(1)}, bf16[2,512,1024]{1,2,0:T(8,128)(2,1)}, u32[]{:S(2)}) copy-start(bf16[2,512,1024]{1,2,0:T(8,128)(2,1)} %copy-done.4) | copy-start | bytes 6291460 | tf_op jit(solution)/shard_map/while/body/eval_jaxpr/cond
  496.4 11.7 %copy-start.6 = (f32[2,512,16,64]{1,3,2,0:T(8,128)S(1)}, f32[2,512,16,64]{1,3,2,0:T(8,128)}, u32[]{:S(2)}) copy-start(f32[2,512,16,64]{1,3,2,0:T(8,128)} %get-tuple-element.1004) | copy-start | bytes 12582916 | tf_op jit(solution)/shard_map/while/body/eval_jaxpr/cond
  534.9 302.7 %reduce-scatter.18.cloned.1.call-start = ((), (), s32[]{:S(2)}) async-start(), calls=%async_computation.15 | async-start | bytes 196608 | tf_op jit(solution)/shard_map/reduce_scatter | solution.py:269
  535.7 303.4 %reduce-scatter.26.cloned.1.call-start = ((), (), s32[]{:S(2)}) async-start(), calls=%async_computation.19 | async-start | bytes 786432 | tf_op jit(solution)/shard_map/reduce_scatter | solution.py:275
  597.7 256.5 %reduce-scatter.22.cloned.1.call-start = ((), (), s32[]{:S(2)}) async-start(), calls=%async_computation.17 | async-start | bytes 786432 | tf_op jit(solution)/shard_map/reduce_scatter | solution.py:272
  597.8 210.2 %copy-start.16 = (bf16[2,512,1024]{2,1,0:T(8,128)(2,1)S(1)}, bf16[2,512,1024]{2,1,0:T(8,128)(2,1)}, u32[]{:S(2)}) copy-start(bf16[2,512,1024]{2,1,0:T(8,128)(2,1)} %param.29) | copy-start | bytes 6291460
  597.8 210.2 %copy-start.34 = (f32[2,512]{1,0:T(2,128)S(1)}, f32[2,512]{1,0:T(2,128)}, u32[]{:S(2)}) copy-start(f32[2,512]{1,0:T(2,128)} %copy-done.33) | copy-start | bytes 12292
  597.8 210.2 %copy-start.38 = (f32[2,512]{1,0:T(2,128)S(1)}, f32[2,512]{1,0:T(2,128)}, u32[]{:S(2)}) copy-start(f32[2,512]{1,0:T(2,128)} %copy-done.37) | copy-start | bytes 12292
  597.8 210.2 %copy-start.48 = (f32[1024]{0:T(1024)S(1)}, f32[1024]{0:T(1024)}, u32[]{:S(2)}) copy-start(f32[1024]{0:T(1024)} %param.32) | copy-start | bytes 12292
  597.8 210.2 %copy-start.56 = (f32[1024]{0:T(1024)S(1)}, f32[1024]{0:T(1024)}, u32[]{:S(2)}) copy-start(f32[1024]{0:T(1024)} %param.33) | copy-start | bytes 12292
  706.7 236.6 %reduce-scatter.12.cloned.1.call-start = ((), (), s32[]{:S(2)}) async-start(), calls=%async_computation.12 | async-start | bytes 6684672 | tf_op jit(solution)/shard_map/reduce_scatter | solution.py:252
  820.0 144.4 %reduce-scatter.14.cloned.1.call-start = ((), (), s32[]{:S(2)}) async-start(), calls=%async_computation.13 | async-start | bytes 589824 | tf_op jit(solution)/shard_map/reduce_scatter | solution.py:266
  943.2 155.6 %all-reduce.3.cloned.1.call-start = ((), (), s32[]{:S(2)}) async-start(), calls=%async_computation.20 | async-start | bytes 181248 | tf_op jit(solution)/shard_map/psum | solution.py:279
  943.3 13.9 %copy-start.27 = (bf16[2,512,2048]{2,1,0:T(8,128)(2,1)S(1)}, bf16[2,512,2048]{2,1,0:T(8,128)(2,1)}, u32[]{:S(2)}) copy-start(bf16[2,512,2048]{2,1,0:T(8,128)(2,1)} %reduce-scatter.10.cloned.1.call-done) | copy-start | bytes 12582916
  958.2 158.5 %copy-start.1 = (bf16[1024,1024]{1,0:T(8,128)(2,1)S(1)}, bf16[1024,1024]{1,0:T(8,128)(2,1)}, u32[]{:S(2)}) copy-start(bf16[1024,1024]{1,0:T(8,128)(2,1)} %param.38) | copy-start | bytes 6291460
  (38 other events, 118.7 us)
Sparse Core Ops, SparseCore 0:
  27.9 59.4 all-gather.4
  89.5 56.7 all-gather.2
  377.3 112.3 reduce-scatter.15
  494.2 103.4 reduce-scatter.23
  602.1 104.4 reduce-scatter.19
  708.9 99.0 reduce-scatter.9
  810.2 10.2 reduce-scatter.17
  822.7 14.5 reduce-scatter.25
  839.6 14.5 reduce-scatter.21
  858.0 85.2 reduce-scatter.11
  945.6 12.2 reduce-scatter.13
  965.9 132.9 all-reduce.2
where the time goes:
time: 1130 us; the launch traced here: 1120 us
  waiting for transfers between devices  601 us (53%)
  matrix products  262 us (23%)
  other arithmetic  154 us (14%)
  local copies, waits for them, and re-layouts  88 us (8%)
  between operations  15.1 us (1%)
    psum x1, waiting for transfers between devices, local(): lax.psum((norm1_gain_grad, norm1_shift_grad, query_bias_grad, value_bias_...  133 us
    reduce_scatter x1, waiting for transfers between devices, local(): lax.psum_scatter(kv_buffer.astype(jnp.bfloat16), 'blk', scatter_dimension...  101 us
    reduce_scatter x1, waiting for transfers between devices, local(): lax.psum_scatter(matrix_grads[2].astype(jnp.bfloat16), 'dp', scatter_dime...  100 us
    reduce_scatter x1, waiting for transfers between devices, local(): lax.psum_scatter(matrix_grads[0].astype(jnp.bfloat16), 'dp', scatter_dime...  87.3 us
    reduce_scatter x1, waiting for transfers between devices, local(): lax.psum_scatter(matrix_grads[3].astype(jnp.bfloat16), 'dp', scatter_dime...  62 us
    all_gather x1, waiting for transfers between devices, local(): key_piece = lax.all_gather(keys_low, 'blk', axis=1, tiled=True)  52.7 us
    reduce_sum x3, other arithmetic, norm_forward(): average = jnp.mean(values, axis=-1, keepdims=True)  50.2 us
    all_gather x1, waiting for transfers between devices, local(): value_piece = lax.all_gather(values_low, 'blk', axis=1, tiled=True)  50.2 us
  transfers between devices with their start and end apart: 12, of which 8 were waited for; matrix products, arithmetic and copies ran while one was open for 21% of the time, Pallas kernels for 0%

commit v1 on v0

--- a/solution.py
+++ b/solution.py
@@ -3,10 +3,488 @@
 import jax
 import jax.numpy as jnp
 from jax import lax
+from jax.experimental import pallas as pl
+from jax.experimental.pallas import tpu as pltpu
 from jax.sharding import PartitionSpec as P
 
+f32 = jnp.float32
+bf16 = jnp.bfloat16
 eps = 1e-05
 masked_score = -1e30
+LANES = 128
+NT = (((1,), (1,)), ((), ()))
+NN = (((1,), (0,)), ((), ()))
+TN = (((0,), (0,)), ((), ()))
+
+
+def mm(a, b, dims=NN):
+    return lax.dot_general(a, b, dims, preferred_element_type=f32)
+
+
+def fold(x):
+    total = x[:, :LANES]
+    for c in range(LANES, x.shape[1], LANES):
+        total = total + x[:, c : c + LANES]
+    return total
+
+
+def row_mean(x):
+    return jnp.sum(fold(x), axis=1, keepdims=True) * (1.0 / x.shape[1])
+
+
+def row_sum(x):
+    return jnp.sum(x, axis=0, keepdims=True)
+
+
+def norm_unit(v):
+    centered = v - row_mean(v)
+    inverse = lax.rsqrt(row_mean(centered * centered) + eps)
+    return centered * inverse, inverse
+
+
+def norm_back(grad_y, unit, inverse, gain):
+    e = grad_y * gain
+    return inverse * (e - row_mean(e) - unit * row_mean(e * unit))
+
+
+def params(mib=None, **more):
+    return pltpu.CompilerParams(vmem_limit_bytes=(mib or 60) * 2**20, **more)
+
+
+def whole(shape):
+    return pl.BlockSpec(shape, lambda *_: (0,) * len(shape), pipeline_mode=pl.Buffered(1))
+
+
+def qkv_body(scale, tok, gain, shift, w, qb, vb, *refs):
+    attn_in, qkv = refs[-2:]
+    unit, _ = norm_unit(tok[...].astype(f32))
+    x = (unit * gain[...] + shift[...]).astype(bf16)
+    attn_in[...] = x
+    d = x.shape[1]
+    q = (mm(x, w[:, :d]) + qb[...]).astype(bf16)
+    qkv[:, :d] = (q.astype(f32) * scale).astype(bf16)
+    qkv[:, d : 2 * d] = mm(x, w[:, d : 2 * d]).astype(bf16)
+    qkv[:, 2 * d :] = (mm(x, w[:, 2 * d :]) + vb[...]).astype(bf16)
+
+
+def project_qkv(tok, gain, shift, w, qb, vb, scale, slot, total, earlier=(), tb=256):
+    n, d = tok.shape
+    first = slot * (n // tb)
+    held = pl.BlockSpec(memory_space=pl.ANY)
+    return pl.pallas_call(
+        partial(qkv_body, scale),
+        name="project_qkv",
+        grid=(n // tb,),
+        in_specs=[pl.BlockSpec((tb, d), lambda i: (i, 0))]
+        + [whole(a.shape) for a in (gain, shift, w, qb, vb)]
+        + [held] * len(earlier),
+        out_specs=[
+            pl.BlockSpec((tb, d), lambda i: (first + i, 0)),
+            pl.BlockSpec((tb, 3 * d), lambda i: (first + i, 0)),
+        ],
+        out_shape=[
+            jax.ShapeDtypeStruct((total, d), bf16),
+            jax.ShapeDtypeStruct((total, 3 * d), bf16),
+        ],
+        input_output_aliases={6 + k: k for k in range(len(earlier))},
+        compiler_params=params(),
+        cost_estimate=pl.CostEstimate(
+            flops=2 * n * d * 3 * d, bytes_accessed=6 * d * d + 10 * n * d, transcendentals=n
+        ),
+    )(tok, gain, shift, w, qb, vb, *earlier)
+
+
+def half_slot(own, half):
+    return own if half == 0 else 1 - own
+
+
+def pick(ref, own, block, size):
+    half, sub = divmod(block, 2)
+    return ref[half_slot(own, half), sub * size : (sub + 1) * size, :]
+
+
+def head_mask(size):
+    return lax.broadcasted_iota(jnp.int32, (size, LANES), 1) < LANES // 2
+
+
+def block_penalty(tab, i, j):
+    return jnp.where(tab[1 + 4 * i + j] > 0, 0.0, masked_score).astype(f32)
+
+
+def attend_body(tab, q, k, v, head_scale, heads_out, lse):
+    size = q.shape[1] // 2
+    own = tab[0]
+    low = head_mask(size)
+    causal = lax.broadcasted_iota(jnp.int32, (size, size), 0) >= lax.broadcasted_iota(
+        jnp.int32, (size, size), 1
+    )
+    lane = lax.broadcasted_iota(jnp.int32, (size, LANES), 1)
+    for i in range(4):
+        qi = pick(q, own, i, size)
+        outs = []
+        logs = []
+        for h in range(2):
+            qm = jnp.where(low if h == 0 else ~low, qi, 0).astype(bf16)
+            parts = []
+            for j in range(i + 1):
+                s = mm(qm, pick(k, own, j, size), NT)
+                parts.append(
+                    jnp.where(causal, s, masked_score) if j == i else s + block_penalty(tab, i, j)
+                )
+            top = parts[0]
+            for s in parts[1:]:
+                top = jnp.maximum(top, s)
+            top = jnp.max(top, axis=1, keepdims=True)
+            total = None
+            out = None
+            for j, s in enumerate(parts):
+                p = jnp.exp(s - top)
+                part_sum = fold(p)
+                total = part_sum if total is None else total + part_sum
+                part_out = mm(p.astype(bf16), pick(v, own, j, size))
+                out = part_out if out is None else out + part_out
+            total = jnp.sum(total, axis=1, keepdims=True)
+            outs.append(out * (1.0 / total))
+            logs.append(top + jnp.log(total))
+        both = jnp.where(low, outs[0], outs[1]) * head_scale[...]
+        half, sub = divmod(i, 2)
+        heads_out[half_slot(own, half), sub * size : (sub + 1) * size, :] = both.astype(bf16)
+        columns = jnp.where(lane == 0, logs[0], logs[1])
+        lse[0, i] = jnp.transpose(columns)[:8]
+
+
+def attend(tab, qkv, head_scale_row):
+    _, half_len, wide = qkv.shape
+    d = wide // 3
+    pairs = d // LANES
+    size = half_len // 2
+
+    def lanes(first):
+        return pl.BlockSpec((2, half_len, LANES), lambda p, t: (0, 0, first + p))
+
+    flops = 16 * half_len * half_len * pairs * LANES
+    return pl.pallas_call(
+        attend_body,
+        name="attend",
+        grid_spec=pltpu.PrefetchScalarGridSpec(
+            num_scalar_prefetch=1,
+            grid=(pairs,),
+            in_specs=[
+                lanes(0),
+                lanes(pairs),
+                lanes(2 * pairs),
+                pl.BlockSpec((1, LANES), lambda p, t: (0, p)),
+            ],
+            out_specs=[
+                lanes(0),
+                pl.BlockSpec((1, 4, 8, size), lambda p, t: (p, 0, 0, 0)),
+            ],
+        ),
+        out_shape=[
+            jax.ShapeDtypeStruct((2, half_len, d), bf16),
+            jax.ShapeDtypeStruct((pairs, 4, 8, size), f32),
+        ],
+        compiler_params=params(),
+        cost_estimate=pl.CostEstimate(
+            flops=flops * 4, bytes_accessed=8 * half_len * wide, transcendentals=8 * half_len * half_len * pairs
+        ),
+    )(tab, qkv, qkv, qkv, head_scale_row)
+
+
+def attend_back_body(
+    scale, tab, q, k, v, heads_out, d_out, inv_scale, lse, dq, dk, dv, dots, dq_acc
+):
+    size = q.shape[1] // 2
+    own = tab[0]
+    low = head_mask(size)
+    masks = (low, ~low)
+    causal = lax.broadcasted_iota(jnp.int32, (size, size), 0) <= lax.broadcasted_iota(
+        jnp.int32, (size, size), 1
+    )
+    pick_rows = (
+        lax.broadcasted_iota(jnp.int32, (8, LANES), 1) // (LANES // 2)
+        == lax.broadcasted_iota(jnp.int32, (8, LANES), 0)
+    ).astype(f32)
+    qs, gs, deltas = {}, {}, []
+    for i in range(4):
+        qi = pick(q, own, i, size)
+        gi = pick(d_out, own, i, size)
+        for h in range(2):
+            qs[i, h] = jnp.where(masks[h], qi, 0).astype(bf16)
+            gs[i, h] = jnp.where(masks[h], gi, 0).astype(bf16)
+        product = gi.astype(f32) * pick(heads_out, own, i, size).astype(f32) * inv_scale[...]
+        delta = lax.dot_general(
+            pick_rows, product, NT, preferred_element_type=f32, precision=lax.Precision.HIGHEST
+        )
+        deltas.append(delta)
+        dots[0, i] = delta
+        dq_acc[i] = jnp.zeros((size, LANES), f32)
+    for j in range(4):
+        kj = pick(k, own, j, size)
+        vj = pick(v, own, j, size)
+        dk_j = jnp.zeros((size, LANES), f32)
+        dv_j = jnp.zeros((size, LANES), f32)
+        for h in range(2):
+            km = jnp.where(masks[h], kj, 0).astype(bf16)
+            for i in range(j, 4):
+                logs = lse[0, i, h : h + 1, :]
+                if i > j:
+                    logs = logs - block_penalty(tab, i, j)
+                s = mm(kj, qs[i, h], NT)
+                if i == j:
+                    s = jnp.where(causal, s, masked_score)
+                p = jnp.exp(s - logs)
+                gp = mm(vj, gs[i, h], NT)
+                ds = (p * (gp - deltas[i][h : h + 1, :])).astype(bf16)
+                dv_j = dv_j + mm(p.astype(bf16), gs[i, h])
+                dk_j = dk_j + mm(ds, qs[i, h])
+                dq_acc[i] += mm(ds, km, TN)
+        half, sub = divmod(j, 2)
+        where = (half_slot(own, half), slice(sub * size, (sub + 1) * size))
+        dk[where[0], where[1], :] = dk_j.astype(bf16)
+        dv[where[0], where[1], :] = dv_j.astype(bf16)
+    for i in range(4):
+        half, sub = divmod(i, 2)
+        dq[half_slot(own, half), sub * size : (sub + 1) * size, :] = (dq_acc[i] * scale).astype(bf16)
+
+
+def attend_back(tab, qkv, heads_out, d_out, inv_scale_row, lse, scale):
+    _, half_len, wide = qkv.shape
+    d = wide // 3
+    pairs = d // LANES
+    size = half_len // 2
+
+    def lanes(first):
+        return pl.BlockSpec((2, half_len, LANES), lambda p, t: (0, 0, first + p))
+
+    small = pl.BlockSpec((1, 4, 8, size), lambda p, t: (p, 0, 0, 0))
+    flops = 16 * half_len * half_len * pairs * LANES
+    return pl.pallas_call(
+        partial(attend_back_body, scale),
+        name="attend_back",
+        grid_spec=pltpu.PrefetchScalarGridSpec(
+            num_scalar_prefetch=1,
+            grid=(pairs,),
+            in_specs=[
+                lanes(0),
+                lanes(pairs),
+                lanes(2 * pairs),
+                lanes(0),
+                lanes(0),
+                pl.BlockSpec((1, LANES), lambda p, t: (0, p)),
+                small,
+            ],
+            out_specs=[lanes(0), lanes(0), lanes(0), small],
+            scratch_shapes=[pltpu.VMEM((4, size, LANES), f32)],
+        ),
+        out_shape=[jax.ShapeDtypeStruct((2, half_len, d), bf16)] * 3
+        + [jax.ShapeDtypeStruct((pairs, 4, 8, size), f32)],
+        compiler_params=params(),
+        cost_estimate=pl.CostEstimate(
+            flops=flops * 10, bytes_accessed=16 * half_len * wide, transcendentals=8 * half_len * half_len * pairs
+        ),
+    )(tab, qkv, qkv, qkv, heads_out, d_out, inv_scale_row, lse)
+
+
+def gelu_parts(v):
+    a = jnp.abs(v)
+    t = 1.0 / (1.0 + (0.3275911 * 0.7071067811865476) * a)
+    bell = jnp.exp(v * v * -0.5)
+    poly = ((((1.061405429 * t - 1.453152027) * t + 1.421413741) * t - 0.284496736) * t + 0.254829592) * t
+    tail = (0.5 * poly) * bell
+    cdf = jnp.where(v < 0, tail, 1.0 - tail)
+    return v * cdf, cdf + v * (bell * 0.3989422804014327)
+
+
+def middle_body(
+    ho, tok, cot, out_w, w1, w2, vec, vec4,
+    output, grad_middle, ffn_in, mid_out, grad_hidden, grad_proj, d_out, sums, sums4,
+    act, slope, back,
+):
+    step = pl.program_id(0)
+    d = ho.shape[1]
+    ff = w1.shape[1]
+    fc = 512
+    chunks = ff // fc
+
+    @pl.when(step == 0)
+    def _():
+        sums[...] = jnp.zeros_like(sums)
+        sums4[...] = jnp.zeros_like(sums4)
+
+    def v(r):
+        return vec[r : r + 1, :]
+
+    tokens = tok[...].astype(f32)
+    projection = mm(ho[...], out_w[...]) + v(0)
+    unit_attn, inverse_attn = norm_unit(projection)
+    middle = tokens + (unit_attn * v(1) + v(2))
+    unit_two, inverse_two = norm_unit(middle)
+    x = (unit_two * v(3) + v(4)).astype(bf16)
+    ffn_in[...] = x
+    g = cot[...]
+    tb = x.shape[0]
+    zero = jnp.zeros((tb, LANES), f32)
+
+    def span(c):
+        return pl.ds(pl.multiple_of(c * fc, fc), fc)
+
+    def one(c, total):
+        s = span(c)
+        h = mm(x, w1[:, s]) + vec4[0:1, s]
+        back[:, s] = mm(g, w2[s, :], NT)
+        a, b = gelu_parts(h)
+        act[:, s] = a
+        slope[:, s] = b
+        return total + fold(a)
+
+    total = lax.fori_loop(0, chunks, one, zero)
+    mean = jnp.sum(total, axis=1, keepdims=True) * (1.0 / ff)
+
+    def two(c, total):
+        a = act[:, span(c)] - mean
+        return total + fold(a * a)
+
+    total = lax.fori_loop(0, chunks, two, zero)
+    inverse = lax.rsqrt(jnp.sum(total, axis=1, keepdims=True) * (1.0 / ff) + eps)
+
+    def three(c, carry):
+        acc, sum_e, sum_eu = carry
+        s = span(c)
+        u = (act[:, s] - mean) * inverse
+        act[:, s] = u
+        gain = vec4[1:2, s]
+        m = (u * gain + vec4[2:3, s]).astype(bf16)
+        mid_out[:, s] = m
+        gm = back[:, s]
+        sums4[1:2, s] += row_sum(gm * u)
+        sums4[2:3, s] += row_sum(gm)
+        e = gm * gain
+        return acc + mm(m, w2[s, :]), sum_e + fold(e), sum_eu + fold(e * u)
+
+    acc, sum_e, sum_eu = lax.fori_loop(
+        0, chunks, three, (jnp.zeros((tb, d), f32), zero, zero)
+    )
+    output[...] = middle + acc + v(5)
+    mean_e = jnp.sum(sum_e, axis=1, keepdims=True) * (1.0 / ff)
+    mean_eu = jnp.sum(sum_eu, axis=1, keepdims=True) * (1.0 / ff)
+
+    def four(c, acc):
+        s = span(c)
+        e = back[:, s] * vec4[1:2, s]
+        grad_act = inverse * (e - mean_e - act[:, s] * mean_eu)
+        gh = (grad_act * slope[:, s]).astype(bf16)
+        grad_hidden[:, s] = gh
+        sums4[0:1, s] += row_sum(gh.astype(f32))
+        return acc + mm(gh, w1[:, s], NT)
+
+    grad_ffn_in = lax.fori_loop(0, chunks, four, jnp.zeros((tb, d), f32))
+    gout = g.astype(f32)
+    sums[5:6, :] += row_sum(gout)
+    sums[3:4, :] += row_sum(grad_ffn_in * unit_two)
+    sums[4:5, :] += row_sum(grad_ffn_in)
+    gmid = gout + norm_back(grad_ffn_in, unit_two, inverse_two, v(3))
+    grad_middle[...] = gmid
+    sums[1:2, :] += row_sum(gmid * unit_attn)
+    sums[2:3, :] += row_sum(gmid)
+    gp = norm_back(gmid, unit_attn, inverse_attn, v(1)).astype(bf16)
+    grad_proj[...] = gp
+    sums[0:1, :] += row_sum(gp.astype(f32))
+    d_out[...] = (mm(gp, out_w[...], NT) * v(6)).astype(bf16)
+
+
+def middle_pass(ho, tok, cot, out_w, w1, w2, vec, vec4, tb=256):
+    n, d = ho.shape
+    ff = w1.shape[1]
+    rows = pl.BlockSpec((tb, d), lambda i: (i, 0))
+    wide = pl.BlockSpec((tb, ff), lambda i: (i, 0))
+    return pl.pallas_call(
+        middle_body,
+        name="middle_pass",
+        grid=(n // tb,),
+        in_specs=[rows, rows, rows] + [whole(a.shape) for a in (out_w, w1, w2, vec, vec4)],
+        out_specs=[rows, rows, rows, wide, wide, rows, rows, whole((8, d)), whole((8, ff))],
+        out_shape=[
+            jax.ShapeDtypeStruct((n, d), f32),
+            jax.ShapeDtypeStruct((n, d), f32),
+            jax.ShapeDtypeStruct((n, d), bf16),
+            jax.ShapeDtypeStruct((n, ff), bf16),
+            jax.ShapeDtypeStruct((n, ff), bf16),
+            jax.ShapeDtypeStruct((n, d), bf16),
+            jax.ShapeDtypeStruct((n, d), bf16),
+            jax.ShapeDtypeStruct((8, d), f32),
+            jax.ShapeDtypeStruct((8, ff), f32),
+        ],
+        scratch_shapes=[pltpu.VMEM((tb, ff), f32)] * 3,
+        compiler_params=params(),
+        cost_estimate=pl.CostEstimate(
+            flops=8 * n * d * ff + 4 * n * d * d,
+            bytes_accessed=4 * d * ff + 2 * d * d + 4 * n * ff + 20 * n * d,
+            transcendentals=2 * n * ff,
+        ),
+    )(ho, tok, cot, out_w, w1, w2, vec, vec4)
+
+
+def first_back_body(dq, dk, dv, w, tok, grad_middle, gain, tokens_grad, sums):
+    @pl.when(pl.program_id(0) == 0)
+    def _():
+        sums[...] = jnp.zeros_like(sums)
+
+    d = dq.shape[1]
+    grad = mm(dq[...], w[:, :d], NT) + mm(dk[...], w[:, d : 2 * d], NT) + mm(dv[...], w[:, 2 * d :], NT)
+    unit, inverse = norm_unit(tok[...].astype(f32))
+    sums[0:1, :] += row_sum(grad * unit)
+    sums[1:2, :] += row_sum(grad)
+    sums[2:3, :] += row_sum(dq[...].astype(f32))
+    sums[3:4, :] += row_sum(dv[...].astype(f32))
+    tokens_grad[...] = grad_middle[...] + norm_back(grad, unit, inverse, gain[...])
+
+
+def first_back(dq, dk, dv, w, tok, grad_middle, gain, tb=256):
+    n, d = dq.shape
+    rows = pl.BlockSpec((tb, d), lambda i: (i, 0))
+    return pl.pallas_call(
+        first_back_body,
+        name="first_back",
+        grid=(n // tb,),
+        in_specs=[rows, rows, rows, whole(w.shape), rows, rows, whole(gain.shape)],
+        out_specs=[rows, whole((8, d))],
+        out_shape=[jax.ShapeDtypeStruct((n, d), f32), jax.ShapeDtypeStruct((8, d), f32)],
+        compiler_params=params(),
+        cost_estimate=pl.CostEstimate(
+            flops=6 * n * d * d, bytes_accessed=6 * d * d + 16 * n * d, transcendentals=n
+        ),
+    )(dq, dk, dv, w, tok, grad_middle, gain)
+
+
+def weight_grad_body(a, b, out):
+    out[...] = mm(a[...], b[...], TN).astype(bf16)
+
+
+def weight_grad(a, b, tm=512, tn=1024):
+    t, m = a.shape
+    n = b.shape[1]
+    return pl.pallas_call(
+        weight_grad_body,
+        name="weight_grad",
+        grid=(m // tm, n // tn),
+        in_specs=[
+            pl.BlockSpec((t, tm), lambda i, j: (0, i)),
+            pl.BlockSpec((t, tn), lambda i, j: (0, j)),
+        ],
+        out_specs=pl.BlockSpec((tm, tn), lambda i, j: (i, j)),
+        out_shape=jax.ShapeDtypeStruct((m, n), bf16),
+        compiler_params=params(),
+        cost_estimate=pl.CostEstimate(
+            flops=2 * t * m * n, bytes_accessed=2 * (t * m + t * n + m * n), transcendentals=0
+        ),
+    )(a, b)
+
+
+def running_sums(lengths):
+    count = lengths.shape[1]
+    upto = jnp.arange(count)[:, None] >= jnp.arange(count)[None, :]
+    return jnp.sum(jnp.where(upto[None], lengths[:, None, :], 0), axis=2).astype(jnp.int32)
 
 
 def norm_forward(values, gain, shift):
@@ -27,7 +505,7 @@
     return (grad_in, jnp.sum(grad_y * normed, axis=(0, 1)), jnp.sum(grad_y, axis=(0, 1)))
 
 
-def local(
+def local_general(
     tokens,
     cotangent,
     doc_lengths,
@@ -59,7 +537,7 @@
     row_len = local_len * lax.axis_size("blk")
     row_first = lax.axis_index("blk") * local_len
     query_pos = row_first + jnp.arange(local_len, dtype=jnp.int32)
-    doc_ends = jnp.cumsum(doc_lengths, axis=1, dtype=jnp.int32)
+    doc_ends = running_sums(doc_lengths)
     starts = jnp.max(
         jnp.where(doc_ends[:, None, :] <= query_pos[None, :, None], doc_ends[:, None, :], 0), axis=2
     )
@@ -319,7 +797,137 @@
     )
 
 
+swap = ((0, 1), (1, 0))
+
+
+def exchange(x):
+    return lax.ppermute(x, "blk", swap)
+
+
+def local_rows(
+    tokens,
+    cotangent,
+    doc_lengths,
+    norm1_gain,
+    norm1_shift,
+    qkv_weight,
+    query_bias,
+    value_bias,
+    head_scales,
+    out_weight,
+    out_bias,
+    attn_gain,
+    attn_shift,
+    norm2_gain,
+    norm2_shift,
+    fc1_weight,
+    fc1_bias,
+    mid_gain,
+    mid_shift,
+    fc2_weight,
+    fc2_bias,
+):
+    _, half_len, d = tokens.shape
+    ff = fc1_weight.shape[1]
+    heads = head_scales.shape[0]
+    head_dim = d // heads
+    scale = head_dim**-0.5
+    n = 2 * half_len
+    b = lax.axis_index("blk")
+
+    def split(x):
+        return (
+            lax.dynamic_index_in_dim(x, b, 0, keepdims=False),
+            lax.dynamic_index_in_dim(x, 1 - b, 0, keepdims=False),
+        )
+
+    def assemble(x):
+        kept = x[:half_len]
+        back = exchange(x[half_len:].astype(bf16)).astype(f32)
+        return jnp.where(b == 0, jnp.stack([kept, back]), jnp.stack([back, kept]))
+
+    tok_own, tok_other = split(tokens)
+    cot_own, cot_other = split(cotangent)
+    tok_in = exchange(tok_other)
+    cot_in = exchange(cot_other)
+
+    lengths = lax.dynamic_slice_in_dim(doc_lengths, b, 1, 0)
+    ends = running_sums(lengths)[0]
+    firsts = (half_len // 2) * jnp.arange(4, dtype=jnp.int32)
+    starts = jnp.max(jnp.where(ends[None, :] <= firsts[:, None], ends[None, :], 0), axis=1)
+    allowed = (firsts[None, :] >= starts[:, None]).astype(jnp.int32)
+    tab = jnp.concatenate([b.astype(jnp.int32)[None], allowed.reshape(16)])
+
+    def line(x):
+        return x.reshape(1, -1)
+
+    scale_row = jnp.broadcast_to(head_scales[:, None], (heads, head_dim)).reshape(1, d)
+    vec = jnp.stack(
+        [out_bias, attn_gain, attn_shift, norm2_gain, norm2_shift, fc2_bias, scale_row[0], out_bias]
+    )
+    vec4 = jnp.stack([fc1_bias, mid_gain, mid_shift, fc1_bias])
+
+    first_args = (line(norm1_gain), line(norm1_shift), qkv_weight, line(query_bias), line(value_bias))
+    early = project_qkv(tok_own, *first_args, scale, 0, n)
+    attn_in, qkv = project_qkv(tok_in, *first_args, scale, 1, n, early)
+    qkv = qkv.reshape(2, half_len, 3 * d)
+    tok = jnp.concatenate([tok_own, tok_in])
+    cot = jnp.concatenate([cot_own, cot_in])
+    heads_out, logs = attend(tab, qkv, scale_row)
+    output, grad_middle, ffn_in, mid_out, grad_hidden, grad_proj, d_out, sums, sums4 = middle_pass(
+        heads_out.reshape(n, d), tok, cot, out_weight, fc1_weight, fc2_weight, vec, vec4
+    )
+    output = assemble(output)
+    fc2_weight_grad = weight_grad(mid_out, cot)
+    fc1_weight_grad = weight_grad(ffn_in, grad_hidden)
+    out_weight_grad = weight_grad(heads_out.reshape(n, d), grad_proj)
+    dq, dk, dv, dots = attend_back(
+        tab, qkv, heads_out, d_out.reshape(2, half_len, d), 1.0 / scale_row, logs, scale
+    )
+    dq, dk, dv = (x.reshape(n, d) for x in (dq, dk, dv))
+    qkv_weight_grad = jnp.concatenate([weight_grad(attn_in, x) for x in (dq, dk, dv)], axis=1)
+    tokens_grad, first_sums = first_back(
+        dq, dk, dv, qkv_weight, tok, grad_middle, line(norm1_gain)
+    )
+    tokens_grad = assemble(tokens_grad)
+    head_scales_grad = jnp.sum(dots[:, :, :2, :], axis=(1, 3)).reshape(heads) / head_scales
+
+    def scatter(x):
+        x = lax.psum_scatter(x, "dp", scatter_dimension=0, tiled=True)
+        return lax.psum_scatter(x, "blk", scatter_dimension=1, tiled=True).astype(f32)
+
+    small = lax.psum(
+        (first_sums, sums, sums4, head_scales_grad),
+        ("dp", "blk"),
+    )
+    first_sums, sums, sums4, head_scales_grad = small
+    return (
+        output,
+        tokens_grad,
+        first_sums[0],
+        first_sums[1],
+        scatter(qkv_weight_grad),
+        first_sums[2],
+        first_sums[3],
+        head_scales_grad,
+        scatter(out_weight_grad),
+        sums[0],
+        sums[1],
+        sums[2],
+        sums[3],
+        sums[4],
+        scatter(fc1_weight_grad),
+        sums4[0],
+        sums4[1],
+        sums4[2],
+        scatter(fc2_weight_grad),
+        sums[5],
+    )
+
+
 def solution(mesh):
+    rows_fit = mesh.shape["blk"] == 2
+    local = local_rows if rows_fit else local_general
     placed = (
         P("dp", "blk", None),
         P("dp", "blk", None),

time: 1130 us -> 667 us (0.59)
  waiting for transfers between devices: 601 us -> 318 us
  Pallas kernels: 0 us -> 281 us
  matrix products: 262 us -> 0 us
  other arithmetic: 154 us -> 27.2 us
  local copies, waits for them, and re-layouts: 88 us -> 17.4 us
    pallas_call x0 -> x12, Pallas kernels: none -> 281 us  [the longest x1 110 us: middle_pass(): pl.pallas_call(middle_body, name='middle_pass', grid=(n // tb,), in_specs...]
    dot_general x19 -> x0, matrix products: 262 us -> none  [the longest x2 27.1 us: block_scores(): jnp.einsum('bqhd,bkhd->bhqk', queries, keys_head, preferred_element_type=...]
    reduce_scatter x9 -> x8, waiting for transfers between devices: 364 us -> 243 us  [the longest x4 243 us: scatter(): x = lax.psum_scatter(x, 'dp', scatter_dimension=0, tiled=True)]
    reduce_sum x14 -> x2, other arithmetic: 120 us -> 1.22 us  [the longest x1 1.1 us: local_rows(): jnp.sum(dots[:, :, :2, :], axis=(1, 3)).reshape(heads) / head_scales]
    all_gather x2 -> x0, waiting for transfers between devices: 103 us -> none  [the longest x1 52.7 us: local(): key_piece = lax.all_gather(keys_low, 'blk', axis=1, tiled=True)]
    psum x1 -> x2, waiting for transfers between devices: 133 us -> 62.6 us  [local_rows(): small = lax.psum((first_sums, sums, sums4, head_scales_grad), ('dp', 'blk'))]
    unnamed x120 -> x43, local copies, waits for them, and re-layouts: 40.7 us -> 0.61 us
    while x1 -> x0, local copies, waits for them, and re-layouts: 13.7 us -> none  [local(): grad_queries, kv_buffer = lax.fori_loop(0, turns, one_turn, back_state)]
  transfers between devices with their start and end apart: 12 -> 14, of which waited for: 8 -> 5; matrix products, arithmetic and copies ran while one was open for 21% -> 5% of each run, Pallas kernels for 0% -> 25%
where the time goes in v1:
time: 667 us; the launch traced here: 666 us
  waiting for transfers between devices  318 us (48%)
  Pallas kernels  281 us (42%)
  other arithmetic  27.2 us (4%)
  local copies, waits for them, and re-layouts  17.4 us (3%)
  between operations  15.9 us (2%)
    reduce_scatter x4, waiting for transfers between devices, scatter(): x = lax.psum_scatter(x, 'dp', scatter_dimension=0, tiled=True)  243 us
    pallas_call x1, Pallas kernels, middle_pass(): pl.pallas_call(middle_body, name='middle_pass', grid=(n // tb,), in_specs...  110 us
    psum x2, waiting for transfers between devices, local_rows(): small = lax.psum((first_sums, sums, sums4, head_scales_grad), ('dp', 'blk'))  62.6 us
    pallas_call x1, Pallas kernels, attend_back(): pl.pallas_call(partial(attend_back_body, scale), name='attend_back', grid...  55.9 us
    pallas_call x6, Pallas kernels, weight_grad(): pl.pallas_call(weight_grad_body, name='weight_grad', grid=(m // tm, n //...  52.9 us
    pallas_call x1, Pallas kernels, attend(): pl.pallas_call(attend_body, name='attend', grid_spec=pltpu.PrefetchScalar...  29.7 us
    pallas_call x2, Pallas kernels, project_qkv(): pl.pallas_call(partial(qkv_body, scale), name='project_qkv', grid=(n // t...  16.9 us
    pallas_call x1, Pallas kernels, first_back(): pl.pallas_call(first_back_body, name='first_back', grid=(n // tb,), in_sp...  15.8 us
  transfers between devices with their start and end apart: 14, of which 5 were waited for; matrix products, arithmetic and copies ran while one was open for 5% of the time, Pallas kernels for 25%

profile of v1, /device:TPU:0, one launch (start us, length us, event | category | flops | bytes accessed | tf_op | source)
XLA Modules:
  0.0 665.6 jit_solution(2644793335829288218)
XLA Ops:
  8.2 3.2 dynamic-slice_bitcast_fusion.2
  11.3 3.0 collective-permute-start
  18.0 8.5 %project_qkv.2 = (bf16[1024,1024]{1,0:T(8,128)(2,1)}, bf16[1024,3072]{1,0:T(8,128)(2,1)}) custom-call(bf16[512,1024]{1,0:T(8,128)(2,1)} %get-tuple-element.67.tok, f32[1,1024]{1,0:T(1,128)} %bitcast.73, f32[1,1024]{1,0:T(1,128)} %bitcast.67, bf16[1024,3072]{1,0:T(8,128)(2,1)} %w.5, f32[1,1024]{1,0:T(1,128)} %bitcast.69, f32[1,1024]{1,0:T(1,128)} %bitcast.71), custom_call_target="tpu_custom_call" | custom-call | flops 3221225472 | bytes 11534336 | tf_op jit(solution)/shard_map/project_qkv/pallas_call | solution.py:74
  27.2 11.3 %collective-permute-done.tok = bf16[512,1024]{1,0:T(8,128)(2,1)S(1)} collective-permute-done((bf16[512,1024]{1,0:T(8,128)(2,1)}, bf16[512,1024]{1,0:T(8,128)(2,1)S(1)}, u32[]{:S(2)}, u32[]{:S(2)}) %collective-permute-start) | collective-permute-done | bytes 1048608 | tf_op jit(solution)/shard_map/ppermute | solution.py:804
  38.5 1.7 pad_maximum_fusion.1.tok
  40.2 8.4 %project_qkv.3 = (bf16[1024,1024]{1,0:T(8,128)(2,1)}, bf16[1024,3072]{1,0:T(8,128)(2,1)}) custom-call(bf16[512,1024]{1,0:T(8,128)(2,1)} %copy-done.3, f32[1,1024]{1,0:T(1,128)} %bitcast.74, f32[1,1024]{1,0:T(1,128)} %bitcast.68, bf16[1024,3072]{1,0:T(8,128)(2,1)} %w.5, f32[1,1024]{1,0:T(1,128)} %bitcast.70, ...), custom_call_target="tpu_custom_call", output_to_operand_aliasing={{0}: (6, {}), {1}: (7, {})} | custom-call | flops 3221225472 | bytes 11534336 | tf_op jit(solution)/shard_map/project_qkv/pallas_call | solution.py:74
  48.6 29.7 %attend.1 = (bf16[2,512,1024]{2,1,0:T(8,128)(2,1)}, f32[8,4,8,256]{3,2,1,0:T(8,128)}) custom-call(s32[17]{0:T(128)} %pad_add_fusion.tab, bf16[2,512,3072]{2,1,0:T(8,128)(2,1)} %bitcast.53, bf16[2,512,3072]{2,1,0:T(8,128)(2,1)} %bitcast.54, bf16[2,512,3072]{2,1,0:T(8,128)(2,1)} %bitcast.55, f32[1,1024]{1,0:T(1,128)} %copy-done.9), custom_call_target="tpu_custom_call" | custom-call | flops 17179869184 | bytes 12582912 | tf_op jit(solution)/shard_map/attend/pallas_call | solution.py:166
  78.3 2.8 pad_maximum_fusion.2.cot.b
  81.2 110.2 %middle_pass.1 = (f32[1024,1024]{1,0:T(8,128)}, f32[1024,1024]{1,0:T(8,128)}, bf16[1024,1024]{1,0:T(8,128)(2,1)}, bf16[1024,4096]{1,0:T(8,128)(2,1)}, bf16[1024,...) custom-call(bf16[1024,1024]{1,0:T(8,128)(2,1)} %bitcast.97, ...), custom_call_target="tpu_custom_call" | custom-call | flops 38654705664 | bytes 56623104 | tf_op jit(solution)/shard_map/middle_pass/pallas_call | solution.py:401
  191.3 5.5 weight_grad.9
  196.9 55.9 %attend_back.1 = (bf16[2,512,1024]{2,1,0:T(8,128)(2,1)}, bf16[2,512,1024]{2,1,0:T(8,128)(2,1)}, bf16[2,512,1024]{2,1,0:T(8,128)(2,1)}, f32[8,4,8,256]{3,2,1,0:T(8,128)}) custom-call(s32[17]{0:T(128)} %pad_add_fusion.tab, bf16[2,512,3072]{2,1,0:T(8,128)(2,1)} %bitcast.56, bf16[2,512,3072]{2,1,0:T(8,128)(2,1)} %bitcast.57, bf16[2,512,3072]{2,1,0:T(8,128)(2,1)} %bitcast.58, ...), custom_call_target="tpu_custom_call" | custom-call | flops 42949672960 | bytes 25165824 | tf_op jit(solution)/shard_map/attend_back/pallas_call | solution.py:262
  252.8 5.5 weight_grad.8
  258.3 5.5 weight_grad.7
  263.8 5.6 weight_grad.6
  269.4 5.4 pad_maximum_fusion
  274.8 14.6 %weight_grad.11 = bf16[4096,1024]{1,0:T(8,128)(2,1)} custom-call(bf16[1024,4096]{1,0:T(8,128)(2,1)} %get-tuple-element.61.a, bf16[1024,1024]{1,0:T(8,128)(2,1)} %pad_maximum_fusion.2.cot.b), custom_call_target="tpu_custom_call" | custom-call | flops 8589934592 | bytes 18874368 | tf_op jit(solution)/shard_map/weight_grad/pallas_call | solution.py:467
  291.2 15.8 %first_back.1 = (f32[1024,1024]{1,0:T(8,128)}, f32[8,1024]{1,0:T(8,128)}) custom-call(bf16[1024,1024]{1,0:T(8,128)(2,1)} %bitcast.92, bf16[1024,1024]{1,0:T(8,128)(2,1)} %bitcast.94, bf16[1024,1024]{1,0:T(8,128)(2,1)} %bitcast.96, bf16[1024,3072]{1,0:T(8,128)(2,1)} %w.5, bf16[1024,1024]{1,0:T(8,128)(2,1)} %pad_maximum_fusion.1.tok, ...), custom_call_target="tpu_custom_call" | custom-call | flops 6442450944 | bytes 23068672 | tf_op jit(solution)/shard_map/first_back/pallas_call | solution.py:446
  307.1 16.2 %weight_grad.10 = bf16[1024,4096]{1,0:T(8,128)(2,1)} custom-call(bf16[1024,1024]{1,0:T(8,128)(2,1)} %get-tuple-element.58.a, bf16[1024,4096]{1,0:T(8,128)(2,1)} %get-tuple-element.59.b), custom_call_target="tpu_custom_call" | custom-call | flops 8589934592 | bytes 18874368 | tf_op jit(solution)/shard_map/weight_grad/pallas_call | solution.py:467
  324.6 37.6 %reduce-scatter.9.cloned.1.call-done = bf16[64,3072]{1,0:T(8,128)(2,1)} async-done(((bf16[1024,3072]{1,0:T(8,128)(2,1)}), bf16[64,3072]{1,0:T(8,128)(2,1)}) %reduce-scatter.9.cloned.1.call-update) | async-done | bytes 393232 | tf_op jit(solution)/shard_map/reduce_scatter | solution.py:896
  362.2 108.6 %reduce-scatter.21.cloned.1.call-done = bf16[256,1024]{1,0:T(8,128)(2,1)} async-done(((bf16[4096,1024]{1,0:T(8,128)(2,1)}), bf16[256,1024]{1,0:T(8,128)(2,1)}) %reduce-scatter.21.cloned.1.call-update) | async-done | bytes 524304 | tf_op jit(solution)/shard_map/reduce_scatter | solution.py:896
  470.9 2.9 slice.94
  473.8 3.2 slice.95
  480.8 1.8 fusion.2
  482.6 97.2 %reduce-scatter.17.cloned.1.call-done = bf16[64,4096]{1,0:T(8,128)(2,1)} async-done(((bf16[1024,4096]{1,0:T(8,128)(2,1)}), bf16[64,4096]{1,0:T(8,128)(2,1)}) %reduce-scatter.17.cloned.1.call-update) | async-done | bytes 524304 | tf_op jit(solution)/shard_map/reduce_scatter | solution.py:896
  579.8 62.6 %all-reduce.4.cloned.1.call-done = f32[8,4096]{1,0:T(8,128)} async-done(((f32[8,4096]{1,0:T(8,128)}), f32[8,4096]{1,0:T(8,128)}) %all-reduce.4.cloned.1.call-update) | async-done | bytes 131088 | tf_op jit(solution)/shard_map/psum | solution.py:899
  642.4 1.8 fusion.1
  645.7 2.5 maximum_select_fusion
  648.4 2.5 maximum_select_fusion.1
  650.9 1.5 convert_element_type.26
  652.4 1.7 convert_element_type.25
  654.1 1.8 convert_element_type.28
  655.9 1.8 convert_element_type.27
  (95 shorter events, 13.6 us)
Async XLA Ops:
  8.0 7.4 %copy-start = (s32[2,4]{1,0:T(2,128)S(1)}, s32[2,4]{1,0:T(2,128)}, u32[]{:S(2)}) copy-start(s32[2,4]{1,0:T(2,128)} %param.23) | copy-start | bytes 100
  8.0 316.0 %reduce-scatter.13.cloned.1.call-start = ((), (), s32[]{:S(2)}) async-start(), calls=%async_computation.10 | async-start | bytes 2228224 | tf_op jit(solution)/shard_map/reduce_scatter | solution.py:896
  8.1 6.2 copy-start.7
  8.1 7.8 %copy-start.19 = (f32[16]{0:T(128)S(1)}, f32[16]{0:T(128)}, u32[]{:S(2)}) copy-start(f32[16]{0:T(128)} %param.29) | copy-start | bytes 196
  8.1 8.0 %copy-start.13 = (f32[1024]{0:T(1024)S(1)}, f32[1024]{0:T(1024)}, u32[]{:S(2)}) copy-start(f32[1024]{0:T(1024)} %param.31) | copy-start | bytes 12292
  8.1 8.0 %copy-start.14 = (f32[1024]{0:T(1024)S(1)}, f32[1024]{0:T(1024)}, u32[]{:S(2)}) copy-start(f32[1024]{0:T(1024)} %param.32) | copy-start | bytes 12292
  8.1 8.0 %copy-start.15 = (f32[1024]{0:T(1024)S(1)}, f32[1024]{0:T(1024)}, u32[]{:S(2)}) copy-start(f32[1024]{0:T(1024)} %param.33) | copy-start | bytes 12292
  8.1 8.0 %copy-start.16 = (f32[1024]{0:T(1024)S(1)}, f32[1024]{0:T(1024)}, u32[]{:S(2)}) copy-start(f32[1024]{0:T(1024)} %param.34) | copy-start | bytes 12292
  8.2 8.0 %copy-start.17 = (f32[1024]{0:T(1024)S(1)}, f32[1024]{0:T(1024)}, u32[]{:S(2)}) copy-start(f32[1024]{0:T(1024)} %param.35) | copy-start | bytes 12292
  8.2 8.0 %copy-start.18 = (f32[1024]{0:T(1024)S(1)}, f32[1024]{0:T(1024)}, u32[]{:S(2)}) copy-start(f32[1024]{0:T(1024)} %param.41) | copy-start | bytes 12292
  11.3 27.2 %collective-permute-start = (bf16[512,1024]{1,0:T(8,128)(2,1)}, bf16[512,1024]{1,0:T(8,128)(2,1)S(1)}, u32[]{:S(2)}, u32[]{:S(2)}) collective-permute-start(bf16[512,1024]{1,0:T(8,128)(2,1)} %get-tuple-element.68), channel_id=1, source_target_pairs={{0,1},{1,0},{2,3},{3,2},{4,5},{5,4},{6,7},{7,6},{8,9},{9,8},{10,11... | collective-permute-start | bytes 3145736 | tf_op jit(solution)/shard_map/ppermute | solution.py:804
  15.5 62.9 %collective-permute-start.1 = (bf16[512,1024]{1,0:T(8,128)(2,1)}, bf16[512,1024]{1,0:T(8,128)(2,1)}, u32[]{:S(2)}, u32[]{:S(2)}) collective-permute-start(bf16[512,1024]{1,0:T(8,128)(2,1)} %get-tuple-element.66), channel_id=1, source_target_pairs={{0,1},{1,0},{2,3},{3,2},{4,5},{5,4},{6,7},{7,6},{8,9},{9,8},{10,11... | collective-permute-start | bytes 3145736 | tf_op jit(solution)/shard_map/ppermute | solution.py:804
  16.1 10.4 %copy-start.9 = (f32[1,1024]{1,0:T(1,128)}, f32[1,1024]{1,0:T(1,128)S(1)}, u32[]{:S(2)}) copy-start(f32[1,1024]{1,0:T(1,128)S(1)} %reshape.160.head_scale) | copy-start | bytes 12292
  18.0 8.5 %copy-start.10 = (f32[4096]{0:T(1024)S(1)}, f32[4096]{0:T(1024)}, u32[]{:S(2)}) copy-start(f32[4096]{0:T(1024)} %param.37) | copy-start | bytes 49156
  18.0 8.5 %copy-start.11 = (f32[4096]{0:T(1024)S(1)}, f32[4096]{0:T(1024)}, u32[]{:S(2)}) copy-start(f32[4096]{0:T(1024)} %param.39) | copy-start | bytes 49156
  18.0 8.5 %copy-start.12 = (f32[4096]{0:T(1024)S(1)}, f32[4096]{0:T(1024)}, u32[]{:S(2)}) copy-start(f32[4096]{0:T(1024)} %param.38) | copy-start | bytes 49156
  18.0 20.5 %copy-start.4 = (bf16[512,1024]{1,0:T(8,128)(2,1)S(1)}, bf16[512,1024]{1,0:T(8,128)(2,1)}, u32[]{:S(2)}) copy-start(bf16[512,1024]{1,0:T(8,128)(2,1)} %get-tuple-element.67.tok) | copy-start | bytes 3145732
  196.8 165.3 %reduce-scatter.9.cloned.1.call-start = ((), (), s32[]{:S(2)}) async-start(), calls=%async_computation.8 | async-start | bytes 6684672 | tf_op jit(solution)/shard_map/reduce_scatter | solution.py:896
  274.8 196.1 %reduce-scatter.21.cloned.1.call-start = ((), (), s32[]{:S(2)}) async-start(), calls=%async_computation.15 | async-start | bytes 8912896 | tf_op jit(solution)/shard_map/reduce_scatter | solution.py:896
  289.5 191.4 %all-reduce.6.cloned.1.call-start = ((), (), s32[]{:S(2)}) async-start(), calls=%async_computation.17 | async-start | bytes 132096 | tf_op jit(solution)/shard_map/psum | solution.py:899
  307.1 272.7 %reduce-scatter.17.cloned.1.call-start = ((), (), s32[]{:S(2)}) async-start(), calls=%async_computation.12 | async-start | bytes 8912896 | tf_op jit(solution)/shard_map/reduce_scatter | solution.py:896
  323.4 319.0 %all-reduce.4.cloned.1.call-start = ((), (), s32[]{:S(2)}) async-start(), calls=%async_computation.14 | async-start | bytes 262144 | tf_op jit(solution)/shard_map/psum | solution.py:899
  323.9 326.9 %reduce-scatter.15.cloned.1.call-start = ((), (), s32[]{:S(2)}) async-start(), calls=%async_computation.11 | async-start | bytes 196608 | tf_op jit(solution)/shard_map/reduce_scatter | solution.py:897
  324.5 327.8 %reduce-scatter.11.cloned.1.call-start = ((), (), s32[]{:S(2)}) async-start(), calls=%async_computation.9 | async-start | bytes 589824 | tf_op jit(solution)/shard_map/reduce_scatter | solution.py:897
  362.2 291.9 %reduce-scatter.23.cloned.1.call-start = ((), (), s32[]{:S(2)}) async-start(), calls=%async_computation.16 | async-start | bytes 786432 | tf_op jit(solution)/shard_map/reduce_scatter | solution.py:897
  470.8 185.0 %reduce-scatter.19.cloned.1.call-start = ((), (), s32[]{:S(2)}) async-start(), calls=%async_computation.13 | async-start | bytes 786432 | tf_op jit(solution)/shard_map/reduce_scatter | solution.py:897
  470.9 8.2 %copy-start.6 = (f32[1024,1024]{1,0:T(8,128)S(1)}, f32[1024,1024]{1,0:T(8,128)}, u32[]{:S(2)}) copy-start(f32[1024,1024]{1,0:T(8,128)} %get-tuple-element.52) | copy-start | bytes 12582916
  470.9 8.5 %copy-start.5 = (f32[1024,1024]{1,0:T(8,128)S(1)}, f32[1024,1024]{1,0:T(8,128)}, u32[]{:S(2)}) copy-start(f32[1024,1024]{1,0:T(8,128)} %get-tuple-element.45) | copy-start | bytes 12582916
  477.1 167.1 %collective-permute-start.2 = (bf16[512,1024]{1,0:T(8,128)(2,1)}, bf16[512,1024]{1,0:T(8,128)(2,1)}, u32[]{:S(2)}, u32[]{:S(2)}) collective-permute-start(bf16[512,1024]{1,0:T(8,128)(2,1)} %slice.95), channel_id=1, source_target_pairs={{0,1},{1,0},{2,3},{3,2},{4,5},{5,4},{6,7},{7,6},{8,9},{9,8},{10,11... | collective-permute-start | bytes 3145736 | tf_op jit(solution)/shard_map/ppermute | solution.py:804
  478.5 169.6 %collective-permute-start.3 = (bf16[512,1024]{1,0:T(8,128)(2,1)}, bf16[512,1024]{1,0:T(8,128)(2,1)S(1)}, u32[]{:S(2)}, u32[]{:S(2)}) collective-permute-start(bf16[512,1024]{1,0:T(8,128)(2,1)} %slice.94), channel_id=1, source_target_pairs={{0,1},{1,0},{2,3},{3,2},{4,5},{5,4},{6,7},{7,6},{8,9},{9,8},{10,11... | collective-permute-start | bytes 3145736 | tf_op jit(solution)/shard_map/ppermute | solution.py:804
  648.2 10.0 %copy-start.1 = (s32[2,4]{1,0:T(2,128)S(1)}, s32[2,4]{1,0:T(2,128)}, u32[]{:S(2)}) copy-start(s32[2,4]{1,0:T(2,128)} %param.23) | copy-start | bytes 100
  648.4 9.3 %copy-start.20 = (f32[16]{0:T(128)S(1)}, f32[16]{0:T(128)}, u32[]{:S(2)}) copy-start(f32[16]{0:T(128)} %get-tuple-element.93) | copy-start | bytes 196
  (3 other events, 10.6 us)
Sparse Core Ops, SparseCore 0:
  197.0 63.3 reduce-scatter.12
  274.9 87.2 reduce-scatter.8
  366.2 104.5 reduce-scatter.20
  474.7 104.9 reduce-scatter.16
  581.8 9.9 reduce-scatter.14
  593.9 13.1 reduce-scatter.10
  609.5 14.5 reduce-scatter.22
  626.3 14.5 reduce-scatter.18
Sparse Core Ops, SparseCore 1:
  307.2 170.1 all-reduce.5
  484.3 158.1 all-reduce.3

commit v2 on v1

--- a/solution.py
+++ b/solution.py
@@ -55,11 +55,22 @@
     return pl.BlockSpec(shape, lambda *_: (0,) * len(shape), pipeline_mode=pl.Buffered(1))
 
 
+def core_split(x):
+    low = lax.broadcasted_iota(jnp.int32, (x.shape[0], LANES), 1) < LANES // 2
+    even, odd = [], []
+    for c in range(0, x.shape[1], 2 * LANES):
+        a = x[:, c : c + LANES].astype(f32)
+        b = x[:, c + LANES : c + 2 * LANES].astype(f32)
+        even.append(jnp.where(low, a, pltpu.roll(b, LANES // 2, 1)))
+        odd.append(jnp.where(low, pltpu.roll(a, LANES // 2, 1), b))
+    return (jnp.concatenate(y, axis=1).astype(bf16) for y in (even, odd))
+
+
 def qkv_body(scale, tok, gain, shift, w, qb, vb, *refs):
     attn_in, qkv = refs[-2:]
     unit, _ = norm_unit(tok[...].astype(f32))
     x = (unit * gain[...] + shift[...]).astype(bf16)
-    attn_in[...] = x
+    attn_in[0], attn_in[1] = core_split(x)
     d = x.shape[1]
     q = (mm(x, w[:, :d]) + qb[...]).astype(bf16)
     qkv[:, :d] = (q.astype(f32) * scale).astype(bf16)
@@ -79,11 +90,11 @@
         + [whole(a.shape) for a in (gain, shift, w, qb, vb)]
         + [held] * len(earlier),
         out_specs=[
-            pl.BlockSpec((tb, d), lambda i: (first + i, 0)),
+            pl.BlockSpec((2, tb, d // 2), lambda i: (0, first + i, 0)),
             pl.BlockSpec((tb, 3 * d), lambda i: (first + i, 0)),
         ],
         out_shape=[
-            jax.ShapeDtypeStruct((total, d), bf16),
+            jax.ShapeDtypeStruct((2, total, d // 2), bf16),
             jax.ShapeDtypeStruct((total, 3 * d), bf16),
         ],
         input_output_aliases={6 + k: k for k in range(len(earlier))},
@@ -192,7 +203,7 @@
 
 
 def attend_back_body(
-    scale, tab, q, k, v, heads_out, d_out, inv_scale, lse, dq, dk, dv, dots, dq_acc
+    scale, tab, q, k, v, heads_out, d_out, inv_scale, lse, dqkv, dots, dq_acc
 ):
     size = q.shape[1] // 2
     own = tab[0]
@@ -241,23 +252,26 @@
                 dq_acc[i] += mm(ds, km, TN)
         half, sub = divmod(j, 2)
         where = (half_slot(own, half), slice(sub * size, (sub + 1) * size))
-        dk[where[0], where[1], :] = dk_j.astype(bf16)
-        dv[where[0], where[1], :] = dv_j.astype(bf16)
+        dqkv[1, where[0], where[1], :] = dk_j.astype(bf16)
+        dqkv[2, where[0], where[1], :] = dv_j.astype(bf16)
     for i in range(4):
         half, sub = divmod(i, 2)
-        dq[half_slot(own, half), sub * size : (sub + 1) * size, :] = (dq_acc[i] * scale).astype(bf16)
-
-
-def attend_back(tab, qkv, heads_out, d_out, inv_scale_row, lse, scale):
+        dqkv[0, half_slot(own, half), sub * size : (sub + 1) * size, :] = (dq_acc[i] * scale).astype(bf16)
+
+
+def attend_back(tab, qkv, heads_out, d_out, inv_scale_row, lse, scale, group):
     _, half_len, wide = qkv.shape
     d = wide // 3
-    pairs = d // LANES
+    every = d // LANES
+    pairs = every // 2
     size = half_len // 2
 
+    def pair(p):
+        return p + 2 * (p // 2) + 2 * group
+
     def lanes(first):
-        return pl.BlockSpec((2, half_len, LANES), lambda p, t: (0, 0, first + p))
-
-    small = pl.BlockSpec((1, 4, 8, size), lambda p, t: (p, 0, 0, 0))
+        return pl.BlockSpec((2, half_len, LANES), lambda p, t: (0, 0, first + pair(p)))
+
     flops = 16 * half_len * half_len * pairs * LANES
     return pl.pallas_call(
         partial(attend_back_body, scale),
@@ -267,21 +281,26 @@
             grid=(pairs,),
             in_specs=[
                 lanes(0),
-                lanes(pairs),
-                lanes(2 * pairs),
+                lanes(every),
+                lanes(2 * every),
                 lanes(0),
                 lanes(0),
-                pl.BlockSpec((1, LANES), lambda p, t: (0, p)),
-                small,
+                pl.BlockSpec((1, LANES), lambda p, t: (0, pair(p))),
+                pl.BlockSpec((1, 4, 8, size), lambda p, t: (pair(p), 0, 0, 0)),
             ],
-            out_specs=[lanes(0), lanes(0), lanes(0), small],
+            out_specs=[
+                pl.BlockSpec((3, 2, half_len, LANES), lambda p, t: (0, 0, 0, p)),
+                pl.BlockSpec((1, 4, 8, size), lambda p, t: (p, 0, 0, 0)),
+            ],
             scratch_shapes=[pltpu.VMEM((4, size, LANES), f32)],
         ),
-        out_shape=[jax.ShapeDtypeStruct((2, half_len, d), bf16)] * 3
-        + [jax.ShapeDtypeStruct((pairs, 4, 8, size), f32)],
+        out_shape=[
+            jax.ShapeDtypeStruct((3, 2, half_len, d // 2), bf16),
+            jax.ShapeDtypeStruct((pairs, 4, 8, size), f32),
+        ],
         compiler_params=params(),
         cost_estimate=pl.CostEstimate(
-            flops=flops * 10, bytes_accessed=16 * half_len * wide, transcendentals=8 * half_len * half_len * pairs
+            flops=flops * 10, bytes_accessed=8 * half_len * wide, transcendentals=8 * half_len * half_len * pairs
         ),
     )(tab, qkv, qkv, qkv, heads_out, d_out, inv_scale_row, lse)
 
@@ -298,7 +317,7 @@
 
 def middle_body(
     ho, tok, cot, out_w, w1, w2, vec, vec4,
-    output, grad_middle, ffn_in, mid_out, grad_hidden, grad_proj, d_out, sums, sums4,
+    output, grad_middle, ffn_in, heads_in, mid_out, grad_hidden, grad_proj, d_out, sums, sums4,
     act, slope, back,
 ):
     step = pl.program_id(0)
@@ -321,7 +340,8 @@
     middle = tokens + (unit_attn * v(1) + v(2))
     unit_two, inverse_two = norm_unit(middle)
     x = (unit_two * v(3) + v(4)).astype(bf16)
-    ffn_in[...] = x
+    ffn_in[0], ffn_in[1] = core_split(x)
+    heads_in[0], heads_in[1] = core_split(ho[...])
     g = cot[...]
     tb = x.shape[0]
     zero = jnp.zeros((tb, LANES), f32)
@@ -398,16 +418,18 @@
     ff = w1.shape[1]
     rows = pl.BlockSpec((tb, d), lambda i: (i, 0))
     wide = pl.BlockSpec((tb, ff), lambda i: (i, 0))
+    split = pl.BlockSpec((2, tb, d // 2), lambda i: (0, i, 0))
     return pl.pallas_call(
         middle_body,
         name="middle_pass",
         grid=(n // tb,),
         in_specs=[rows, rows, rows] + [whole(a.shape) for a in (out_w, w1, w2, vec, vec4)],
-        out_specs=[rows, rows, rows, wide, wide, rows, rows, whole((8, d)), whole((8, ff))],
+        out_specs=[rows, rows, split, split, wide, wide, rows, rows, whole((8, d)), whole((8, ff))],
         out_shape=[
             jax.ShapeDtypeStruct((n, d), f32),
             jax.ShapeDtypeStruct((n, d), f32),
-            jax.ShapeDtypeStruct((n, d), bf16),
+            jax.ShapeDtypeStruct((2, n, d // 2), bf16),
+            jax.ShapeDtypeStruct((2, n, d // 2), bf16),
             jax.ShapeDtypeStruct((n, ff), bf16),
             jax.ShapeDtypeStruct((n, ff), bf16),
             jax.ShapeDtypeStruct((n, d), bf16),
@@ -425,60 +447,105 @@
     )(ho, tok, cot, out_w, w1, w2, vec, vec4)
 
 
-def first_back_body(dq, dk, dv, w, tok, grad_middle, gain, tokens_grad, sums):
+def first_back_body(even, odd, w, tok, grad_middle, gain, tokens_grad, sums):
     @pl.when(pl.program_id(0) == 0)
     def _():
         sums[...] = jnp.zeros_like(sums)
 
-    d = dq.shape[1]
-    grad = mm(dq[...], w[:, :d], NT) + mm(dk[...], w[:, d : 2 * d], NT) + mm(dv[...], w[:, 2 * d :], NT)
+    d = w.shape[0]
+    run = d // 4
+    grad = None
+    for part in range(3):
+        for r in range(4):
+            piece = (even, odd)[r % 2][part, :, (r // 2) * run : (r // 2 + 1) * run]
+            here = r * run
+            term = mm(piece, w[:, part * d + here : part * d + here + run], NT)
+            grad = term if grad is None else grad + term
+            if part != 1:
+                at = 2 + part // 2
+                sums[at : at + 1, here : here + run] += row_sum(piece.astype(f32))
     unit, inverse = norm_unit(tok[...].astype(f32))
     sums[0:1, :] += row_sum(grad * unit)
     sums[1:2, :] += row_sum(grad)
-    sums[2:3, :] += row_sum(dq[...].astype(f32))
-    sums[3:4, :] += row_sum(dv[...].astype(f32))
-    tokens_grad[...] = grad_middle[...] + norm_back(grad, unit, inverse, gain[...])
-
-
-def first_back(dq, dk, dv, w, tok, grad_middle, gain, tb=256):
-    n, d = dq.shape
-    rows = pl.BlockSpec((tb, d), lambda i: (i, 0))
+    whole_grad = grad_middle[...] + norm_back(grad, unit, inverse, gain[...])
+    tokens_grad[...] = whole_grad.astype(tokens_grad.dtype)
+
+
+def first_back(even, odd, w, tok, grad_middle, gain, slot, kind, tb=256):
+    d = w.shape[0]
+    n = even.shape[1] // 2
+    first = slot * (n // tb)
+    rows = pl.BlockSpec((tb, d), lambda i: (first + i, 0))
+    half = pl.BlockSpec((3, tb, d // 2), lambda i: (0, first + i, 0))
     return pl.pallas_call(
         first_back_body,
         name="first_back",
         grid=(n // tb,),
-        in_specs=[rows, rows, rows, whole(w.shape), rows, rows, whole(gain.shape)],
-        out_specs=[rows, whole((8, d))],
-        out_shape=[jax.ShapeDtypeStruct((n, d), f32), jax.ShapeDtypeStruct((8, d), f32)],
+        in_specs=[half, half, whole(w.shape), rows, rows, whole(gain.shape)],
+        out_specs=[pl.BlockSpec((tb, d), lambda i: (i, 0)), whole((8, d))],
+        out_shape=[jax.ShapeDtypeStruct((n, d), kind), jax.ShapeDtypeStruct((8, d), f32)],
         compiler_params=params(),
         cost_estimate=pl.CostEstimate(
             flops=6 * n * d * d, bytes_accessed=6 * d * d + 16 * n * d, transcendentals=n
         ),
-    )(dq, dk, dv, w, tok, grad_middle, gain)
-
-
-def weight_grad_body(a, b, out):
-    out[...] = mm(a[...], b[...], TN).astype(bf16)
-
-
-def weight_grad(a, b, tm=512, tn=1024):
-    t, m = a.shape
-    n = b.shape[1]
+    )(even, odd, w, tok, grad_middle, gain)
+
+
+def after(x, *others):
+    return lax.optimization_barrier((x,) + others)[0]
+
+
+def weight_grad_body(a_lead, b_lead, tab, a, b, *refs):
+    lhs = a[0] if a_lead else a[...]
+    rhs = b[0] if b_lead else b[...]
+    total = mm(lhs, rhs, TN)
+    if len(refs) == 1:
+        refs[0][0] = total.astype(bf16)
+        return
+    received, send, keep = refs
+    total = (total + received[0].astype(f32)).astype(bf16)
+
+    @pl.when(pl.program_id(0) == 0)
+    def _():
+        send[...] = total
+
+    @pl.when(pl.program_id(0) == 1)
+    def _():
+        keep[...] = total
+
+
+def weight_grad(tab, a, b, a_block, b_block, out_block, shape, steps, received=None):
+    flops = 2 * a.shape[-2] * 2 * shape[0] * shape[1]
+    out_index = out_block[1]
+    moved = 2 * (a.size + b.size) + 4 * shape[0] * shape[1]
+    common = dict(
+        name="weight_grad",
+        compiler_params=params(),
+        cost_estimate=pl.CostEstimate(flops=flops, bytes_accessed=moved, transcendentals=0),
+    )
+    part = pl.BlockSpec((1,) + out_block[0], lambda s, i, t: (s,) + out_index(i))
+    in_specs = [pl.BlockSpec(*a_block), pl.BlockSpec(*b_block)]
+    args = [tab, a, b]
+    if received is None:
+        out_specs = part
+        out_shape = jax.ShapeDtypeStruct((2,) + shape, bf16)
+    else:
+        in_specs.append(part)
+        args.append(received)
+        last = steps - 1
+        out_specs = [
+            pl.BlockSpec(out_block[0], lambda s, i, t: out_index(jnp.where(s == 0, i, last))),
+            pl.BlockSpec(out_block[0], lambda s, i, t: out_index(jnp.where(s == 0, 0, i))),
+        ]
+        out_shape = [jax.ShapeDtypeStruct(shape, bf16)] * 2
     return pl.pallas_call(
-        weight_grad_body,
-        name="weight_grad",
-        grid=(m // tm, n // tn),
-        in_specs=[
-            pl.BlockSpec((t, tm), lambda i, j: (0, i)),
-            pl.BlockSpec((t, tn), lambda i, j: (0, j)),
-        ],
-        out_specs=pl.BlockSpec((tm, tn), lambda i, j: (i, j)),
-        out_shape=jax.ShapeDtypeStruct((m, n), bf16),
-        compiler_params=params(),
-        cost_estimate=pl.CostEstimate(
-            flops=2 * t * m * n, bytes_accessed=2 * (t * m + t * n + m * n), transcendentals=0
+        partial(weight_grad_body, len(a_block[0]) == 3, len(b_block[0]) == 3),
+        grid_spec=pltpu.PrefetchScalarGridSpec(
+            num_scalar_prefetch=1, grid=(2, steps), in_specs=in_specs, out_specs=out_specs
         ),
-    )(a, b)
+        out_shape=out_shape,
+        **common,
+    )(*args)
 
 
 def running_sums(lengths):
@@ -804,6 +871,10 @@
     return lax.ppermute(x, "blk", swap)
 
 
+def flip(x, bit):
+    return lax.ppermute(x, "dp", [(i, i ^ bit) for i in range(16)])
+
+
 def local_rows(
     tokens,
     cotangent,
@@ -841,9 +912,8 @@
             lax.dynamic_index_in_dim(x, 1 - b, 0, keepdims=False),
         )
 
-    def assemble(x):
-        kept = x[:half_len]
-        back = exchange(x[half_len:].astype(bf16)).astype(f32)
+    def assemble(kept, sent):
+        back = exchange(sent).astype(f32)
         return jnp.where(b == 0, jnp.stack([kept, back]), jnp.stack([back, kept]))
 
     tok_own, tok_other = split(tokens)
@@ -874,59 +944,158 @@
     tok = jnp.concatenate([tok_own, tok_in])
     cot = jnp.concatenate([cot_own, cot_in])
     heads_out, logs = attend(tab, qkv, scale_row)
-    output, grad_middle, ffn_in, mid_out, grad_hidden, grad_proj, d_out, sums, sums4 = middle_pass(
+    output, grad_middle, ffn_in, heads_in, mid_out, grad_hidden, grad_proj, d_out, sums, sums4 = middle_pass(
         heads_out.reshape(n, d), tok, cot, out_weight, fc1_weight, fc2_weight, vec, vec4
     )
-    output = assemble(output)
-    fc2_weight_grad = weight_grad(mid_out, cot)
-    fc1_weight_grad = weight_grad(ffn_in, grad_hidden)
-    out_weight_grad = weight_grad(heads_out.reshape(n, d), grad_proj)
-    dq, dk, dv, dots = attend_back(
-        tab, qkv, heads_out, d_out.reshape(2, half_len, d), 1.0 / scale_row, logs, scale
-    )
-    dq, dk, dv = (x.reshape(n, d) for x in (dq, dk, dv))
-    qkv_weight_grad = jnp.concatenate([weight_grad(attn_in, x) for x in (dq, dk, dv)], axis=1)
-    tokens_grad, first_sums = first_back(
-        dq, dk, dv, qkv_weight, tok, grad_middle, line(norm1_gain)
-    )
-    tokens_grad = assemble(tokens_grad)
-    head_scales_grad = jnp.sum(dots[:, :, :2, :], axis=(1, 3)).reshape(heads) / head_scales
-
-    def scatter(x):
-        x = lax.psum_scatter(x, "dp", scatter_dimension=0, tiled=True)
-        return lax.psum_scatter(x, "blk", scatter_dimension=1, tiled=True).astype(f32)
-
-    small = lax.psum(
-        (first_sums, sums, sums4, head_scales_grad),
-        ("dp", "blk"),
-    )
-    first_sums, sums, sums4, head_scales_grad = small
+    output = assemble(output[:half_len], output[half_len:].astype(bf16))
+    dp = lax.axis_index("dp").astype(jnp.int32)
+    core, x, y = dp % 2, (dp // 2) % 2, b.astype(jnp.int32)
+    z = dp // 4
+    theirs = jnp.stack([1 - core, x, y])
+    mine = jnp.stack([core, x, y])
+
+    def part_of(s, t, at):
+        return jnp.where(s == 0, 1 - t[at], t[at])
+
+    tall = ff // 16
+    tall_how = (
+        ((n, tall), lambda s, i, t: (0, (i * 2 + part_of(s, t, 1)) * 2 + t[0])),
+        ((n, d), lambda s, i, t: (0, 0)),
+        ((tall, d), lambda i: (i, 0)),
+        (4 * tall, d),
+        4,
+    )
+
+    def flat_how(width):
+        tn = d // 2
+        steps = width // (2 * tn)
+        return (
+            ((1, n, d // 2), lambda s, i, t: (t[0], 0, 0)),
+            ((n, tn), lambda s, i, t: (0, part_of(s, t, 2) * steps + i)),
+            ((d // 2, tn), lambda i: (0, i)),
+            (d // 2, steps * tn),
+            steps,
+        )
+
+    run = d // 4
+    qkv_how = (
+        ((1, n, d // 2), lambda s, i, t: (t[0], 0, 0)),
+        (
+            (1, n, run),
+            lambda s, i, t: ((part_of(s, t, 2) * 3 + i) // 2, 0, (part_of(s, t, 2) * 3 + i) % 2),
+        ),
+        ((d // 2, run), lambda i: (0, i)),
+        (d // 2, 3 * run),
+        3,
+    )
+
+    def z_stage(parts):
+        total = lax.dynamic_index_in_dim(parts, z, 0, keepdims=False).astype(f32)
+        for k in (1, 2, 3):
+            total = total + flip(lax.dynamic_index_in_dim(parts, z ^ k, 0, keepdims=False), 4 * k).astype(f32)
+        return total
+
+    def along_y(send, keep):
+        total = (keep.astype(f32) + flip(send, 2).astype(f32)).astype(bf16).reshape(4, -1, d)
+        return (
+            lax.dynamic_slice_in_dim(total, (1 - y) * (d // 2), d // 2, 2),
+            lax.dynamic_slice_in_dim(total, y * (d // 2), d // 2, 2),
+        )
+
+    def along_x(send, keep):
+        total = keep.astype(f32) + exchange(send).astype(f32)
+        total = total.astype(bf16).reshape(4, 2, d // 16, -1)
+        return (
+            lax.dynamic_index_in_dim(total, 1 - x, 1, keepdims=False),
+            lax.dynamic_index_in_dim(total, x, 1, keepdims=False),
+        )
+
+    def end_y(send, keep):
+        return z_stage((keep.astype(f32) + exchange(send).astype(f32)).astype(bf16))
+
+    def end_x(send, keep):
+        return z_stage((keep.astype(f32) + flip(send, 2).astype(f32)).astype(bf16))
+
+    flat4, flat1 = flat_how(ff), flat_how(d)
+    fc2_theirs = weight_grad(theirs, mid_out, cot, *tall_how)
+    ffn_in = after(ffn_in, fc2_theirs)
+    fc1_theirs = weight_grad(theirs, ffn_in, grad_hidden, *flat4)
+    heads_in = after(heads_in, fc1_theirs)
+    out_theirs = weight_grad(theirs, heads_in, grad_proj, *flat1)
+    mid_out = after(mid_out, out_theirs)
+    fc2_parts = weight_grad(mine, mid_out, cot, *tall_how, flip(fc2_theirs, 1))
+    ffn_in = after(ffn_in, *fc2_parts)
+    fc1_parts = weight_grad(mine, ffn_in, grad_hidden, *flat4, flip(fc1_theirs, 1))
+    heads_in = after(heads_in, *fc1_parts)
+    out_parts = weight_grad(mine, heads_in, grad_proj, *flat1, flip(out_theirs, 1))
+    d_out = after(d_out, *out_parts).reshape(2, half_len, d)
+    back_args = (1.0 / scale_row, logs, scale)
+    even, dots_even = attend_back(tab, qkv, heads_out, d_out, *back_args, 0)
+    even = even.reshape(3, n, d // 2)
+    fc2_parts = along_y(fc2_parts[0], after(fc2_parts[1], even))
+    fc1_parts = along_x(fc1_parts[0], after(fc1_parts[1], even))
+    out_parts = along_x(out_parts[0], after(out_parts[1], even))
+    even_theirs = weight_grad(theirs, attn_in, even, *qkv_how)
+    d_out = after(d_out, even_theirs, *fc2_parts, *fc1_parts, *out_parts)
+    odd, dots_odd = attend_back(tab, qkv, heads_out, d_out, *back_args, 1)
+    odd = odd.reshape(3, n, d // 2)
+    odd_theirs = weight_grad(theirs, attn_in, odd, *qkv_how)
+    attn_in = after(attn_in, odd_theirs)
+    even_parts = weight_grad(mine, attn_in, even, *qkv_how, flip(even_theirs, 1))
+    first_rest = (odd, qkv_weight, tok, grad_middle, line(norm1_gain))
+    grad_sent, sums_sent = first_back(after(even, *even_parts), *first_rest, 1, bf16)
+    attn_in = after(attn_in, grad_sent)
+    odd_parts = weight_grad(mine, attn_in, odd, *qkv_how, flip(odd_theirs, 1))
+    grad_kept, sums_kept = first_back(after(even, *odd_parts), *first_rest, 0, f32)
+    fc2_weight_grad = end_y(fc2_parts[0], after(fc2_parts[1], odd))
+    fc1_weight_grad = end_x(fc1_parts[0], after(fc1_parts[1], odd))
+    out_weight_grad = end_x(out_parts[0], after(out_parts[1], odd))
+    even_parts = along_x(even_parts[0], after(even_parts[1], grad_kept))
+    odd_parts = along_x(odd_parts[0], after(odd_parts[1], grad_kept))
+    even_grad, odd_grad = end_x(*even_parts), end_x(*odd_parts)
+    qkv_weight_grad = jnp.stack(
+        [even_grad.reshape(-1, 3, run), odd_grad.reshape(-1, 3, run)], axis=2
+    ).reshape(-1, 6 * run)
+    first_sums = sums_sent + sums_kept
+    tokens_grad = assemble(grad_kept, grad_sent)
+    dots = jnp.stack([dots_even.reshape(2, 2, 4, 8, -1), dots_odd.reshape(2, 2, 4, 8, -1)], axis=1)
+    head_scales_grad = jnp.sum(dots[..., :2, :], axis=(3, 5)).reshape(heads) / head_scales
+    head_scales_grad = jnp.pad(head_scales_grad, (0, d - heads))
+
+    def everywhere(v):
+        for move in (partial(flip, bit=1), partial(flip, bit=2), exchange, partial(flip, bit=4), partial(flip, bit=8)):
+            v = v + move(v)
+        return v
+
+    sums = everywhere(jnp.concatenate([sums.reshape(8, d), sums4.reshape(8 * ff // d, d)[: 3 * ff // d]]))
+    sums4 = sums[8:].reshape(3, ff)
+    first_sums = everywhere(jnp.concatenate([first_sums[:4], head_scales_grad[None]]))
     return (
         output,
         tokens_grad,
         first_sums[0],
         first_sums[1],
-        scatter(qkv_weight_grad),
+        qkv_weight_grad,
         first_sums[2],
         first_sums[3],
-        head_scales_grad,
-        scatter(out_weight_grad),
+        first_sums[4, :heads],
+        out_weight_grad,
         sums[0],
         sums[1],
         sums[2],
         sums[3],
         sums[4],
-        scatter(fc1_weight_grad),
+        fc1_weight_grad,
         sums4[0],
         sums4[1],
         sums4[2],
-        scatter(fc2_weight_grad),
+        fc2_weight_grad,
         sums[5],
     )
 
 
 def solution(mesh):
-    rows_fit = mesh.shape["blk"] == 2
+    rows_fit = dict(mesh.shape) == {"dp": 16, "blk": 2}
     local = local_rows if rows_fit else local_general
     placed = (
         P("dp", "blk", None),

time: 667 us -> 557 us (0.84)
  waiting for transfers between devices: 318 us -> 124 us
  Pallas kernels: 281 us -> 324 us
  starting transfers between devices: 5.4 us -> 47.5 us
  between operations: 15.9 us -> 1.47 us
    reduce_scatter x8 -> x0, waiting for transfers between devices: 243 us -> none  [the longest x4 243 us: scatter(): x = lax.psum_scatter(x, 'dp', scatter_dimension=0, tiled=True)]
    ppermute x4 -> x11, waiting for transfers between devices: 11.3 us -> 78.5 us  [exchange(): return lax.ppermute(x, 'blk', swap)]
    psum x2 -> x0, waiting for transfers between devices: 62.6 us -> none  [local_rows(): small = lax.psum((first_sums, sums, sums4, head_scales_grad), ('dp', 'blk'))]
    ppermute x0 -> x33, waiting for transfers between devices: none -> 45.5 us  [flip(): return lax.ppermute(x, 'dp', [(i, i ^ bit) for i in range(16)])]
    ppermute x0 -> x33, starting transfers between devices: none -> 35.3 us  [flip(): return lax.ppermute(x, 'dp', [(i, i ^ bit) for i in range(16)])]
    pallas_call x6 -> x10, Pallas kernels: 52.9 us -> 86.3 us  [weight_grad(): pl.pallas_call(partial(weight_grad_body, len(a_block[0]) == 3, len(b_bloc...]
    ppermute x4 -> x11, starting transfers between devices: 5 us -> 12.3 us  [exchange(): return lax.ppermute(x, 'blk', swap)]
    pallas_call x1 -> x2, Pallas kernels: 55.9 us -> 59.3 us  [attend_back(): pl.pallas_call(partial(attend_back_body, scale), name='attend_back', grid...]
  transfers between devices with their start and end apart: 14 -> 44, of which waited for: 5 -> 16; matrix products, arithmetic and copies ran while one was open for 5% -> 8% of each run, Pallas kernels for 25% -> 37%
where the time goes in v2:
time: 557 us; the launch traced here: 549 us
  Pallas kernels  324 us (58%)
  waiting for transfers between devices  124 us (22%)
  starting transfers between devices  47.5 us (9%)
  other arithmetic  30 us (5%)
  local copies, waits for them, and re-layouts  21.5 us (4%)
    pallas_call x1, Pallas kernels, middle_pass(): pl.pallas_call(middle_body, name='middle_pass', grid=(n // tb,), in_specs...  113 us
    pallas_call x10, Pallas kernels, weight_grad(): pl.pallas_call(partial(weight_grad_body, len(a_block[0]) == 3, len(b_bloc...  86.3 us
    ppermute x11, waiting for transfers between devices, exchange(): return lax.ppermute(x, 'blk', swap)  78.5 us
    pallas_call x2, Pallas kernels, attend_back(): pl.pallas_call(partial(attend_back_body, scale), name='attend_back', grid...  59.3 us
    ppermute x33, waiting for transfers between devices, flip(): return lax.ppermute(x, 'dp', [(i, i ^ bit) for i in range(16)])  45.5 us
    ppermute x33, starting transfers between devices, flip(): return lax.ppermute(x, 'dp', [(i, i ^ bit) for i in range(16)])  35.3 us
    pallas_call x1, Pallas kernels, attend(): pl.pallas_call(attend_body, name='attend', grid_spec=pltpu.PrefetchScalar...  29.6 us
    pallas_call x2, Pallas kernels, first_back(): pl.pallas_call(first_back_body, name='first_back', grid=(n // tb,), in_sp...  19 us
  transfers between devices with their start and end apart: 44, of which 16 were waited for; matrix products, arithmetic and copies ran while one was open for 8% of the time, Pallas kernels for 37%

profile of v2, /device:TPU:0, one launch (start us, length us, event | category | flops | bytes accessed | tf_op | source)
XLA Modules:
  0.0 549.0 jit_solution(4542936485323367292)
XLA Ops:
  0.7 3.2 dynamic-slice_bitcast_fusion.4
  3.9 3.0 collective-permute-start
  10.7 8.8 %project_qkv.2 = (bf16[2,1024,512]{2,1,0:T(8,128)(2,1)}, bf16[1024,3072]{1,0:T(8,128)(2,1)}) custom-call(bf16[512,1024]{1,0:T(8,128)(2,1)} %get-tuple-element.132.tok, f32[1,1024]{1,0:T(1,128)} %bitcast.168, f32[1,1024]{1,0:T(1,128)} %bitcast.180, bf16[1024,3072]{1,0:T(8,128)(2,1)} %w.7, f32[1,1024]{1,0:T(1,128)} %bitcast.182, f32[1,1024]{1,0:T(1,128)} %bitcast.184), custom_call_target="tpu_custom_call" | custom-call | flops 3221225472 | bytes 11534336 | tf_op jit(solution)/shard_map/project_qkv/pallas_call | solution.py:85
  20.2 10.9 %collective-permute-done.tok = bf16[512,1024]{1,0:T(8,128)(2,1)S(1)} collective-permute-done((bf16[512,1024]{1,0:T(8,128)(2,1)}, bf16[512,1024]{1,0:T(8,128)(2,1)S(1)}, u32[]{:S(2)}, u32[]{:S(2)}) %collective-permute-start) | collective-permute-done | bytes 1048608 | tf_op jit(solution)/shard_map/ppermute | solution.py:871
  32.9 8.7 %project_qkv.3 = (bf16[2,1024,512]{2,1,0:T(8,128)(2,1)}, bf16[1024,3072]{1,0:T(8,128)(2,1)}) custom-call(bf16[512,1024]{1,0:T(8,128)(2,1)} %copy-done.3, f32[1,1024]{1,0:T(1,128)} %bitcast.169, f32[1,1024]{1,0:T(1,128)} %bitcast.181, bf16[1024,3072]{1,0:T(8,128)(2,1)} %w.7, f32[1,1024]{1,0:T(1,128)} %bitcast.183, ...), custom_call_target="tpu_custom_call", output_to_operand_aliasing={{0}: (6, {}), {1}: (7, {})} | custom-call | flops 3221225472 | bytes 11534336 | tf_op jit(solution)/shard_map/project_qkv/pallas_call | solution.py:85
  41.6 29.6 %attend.1 = (bf16[2,512,1024]{2,1,0:T(8,128)(2,1)}, f32[8,4,8,256]{3,2,1,0:T(8,128)}) custom-call(s32[17]{0:T(128)} %pad_add_fusion.tab, bf16[2,512,3072]{2,1,0:T(8,128)(2,1)} %bitcast.151, bf16[2,512,3072]{2,1,0:T(8,128)(2,1)} %bitcast.152, bf16[2,512,3072]{2,1,0:T(8,128)(2,1)} %bitcast.153, f32[1,1024]{1,0:T(1,128)} %copy-done.16), custom_call_target="tpu_custom_call" | custom-call | flops 17179869184 | bytes 12582912 | tf_op jit(solution)/shard_map/attend/pallas_call | solution.py:177
  74.0 112.7 %middle_pass.1 = (f32[1024,1024]{1,0:T(8,128)}, f32[1024,1024]{1,0:T(8,128)}, bf16[2,1024,512]{2,1,0:T(8,128)(2,1)}, bf16[2,1024,512]{2,1,0:T(8,128)(2,1)}, bf16...) custom-call(bf16[1024,1024]{1,0:T(8,128)(2,1)} %bitcast.201, ...), custom_call_target="tpu_custom_call" | custom-call | flops 38654705664 | bytes 56623104 | tf_op jit(solution)/shard_map/middle_pass/pallas_call | solution.py:422
  186.7 10.9 %weight_grad.10 = bf16[2,1024,1024]{2,1,0:T(8,128)(2,1)} custom-call(s32[3]{0:T(128)} %add_add_fusion.1.tab, bf16[1024,4096]{1,0:T(8,128)(2,1)} %get-tuple-element.86.a, bf16[1024,1024]{1,0:T(8,128)(2,1)} %pad_maximum_fusion.1.cot.b), custom_call_target="tpu_custom_call" | custom-call | flops 4294967296 | bytes 14680064 | tf_op jit(solution)/shard_map/weight_grad/pallas_call | solution.py:541
  197.6 11.4 %weight_grad.11 = bf16[2,512,2048]{2,1,0:T(8,128)(2,1)} custom-call(s32[3]{0:T(128)} %add_add_fusion.1.tab, bf16[2,1024,512]{2,1,0:T(8,128)(2,1)} %get-tuple-element.89.a, bf16[1024,4096]{1,0:T(8,128)(2,1)} %get-tuple-element.83.b), custom_call_target="tpu_custom_call" | custom-call | flops 4294967296 | bytes 14680064 | tf_op jit(solution)/shard_map/weight_grad/pallas_call | solution.py:541
  209.7 6.6 %collective-permute-done.31 = f32[20,1024]{1,0:T(8,128)S(1)} collective-permute-done((f32[20,1024]{1,0:T(8,128)S(1)}, f32[20,1024]{1,0:T(8,128)S(1)}, u32[]{:S(2)}, u32[]{:S(2)}) %collective-permute-start.31) | collective-permute-done | bytes 81952 | tf_op jit(solution)/shard_map/ppermute | solution.py:875
  231.7 2.9 collective-permute-start.35
  234.6 4.5 weight_grad.12
  241.0 10.0 %collective-permute-done.2 = bf16[512,1024]{1,0:T(8,128)(2,1)S(1)} collective-permute-done((bf16[512,1024]{1,0:T(8,128)(2,1)}, bf16[512,1024]{1,0:T(8,128)(2,1)S(1)}, u32[]{:S(2)}, u32[]{:S(2)}) %collective-permute-start.2) | collective-permute-done | bytes 1048608 | tf_op jit(solution)/shard_map/ppermute | solution.py:871
  253.9 12.0 %weight_grad.13 = (bf16[1024,1024]{1,0:T(8,128)(2,1)}, bf16[1024,1024]{1,0:T(8,128)(2,1)}) custom-call(s32[3]{0:T(128)} %add_add_fusion.tab, bf16[1024,4096]{1,0:T(8,128)(2,1)} %get-tuple-element.86.a, bf16[1024,1024]{1,0:T(8,128)(2,1)} %pad_maximum_fusion.1.cot.b, bf16[2,1024,1024]{2,1,0:T(8,128)(2,1)} %collective-permute-done.3.refs_0_), custom_call_target="tpu_custom_call" | custom-call | flops 4294967296 | bytes 14680064 | tf_op jit(solution)/shard_map/weight_grad/pallas_call | solution.py:541
  267.4 12.3 %weight_grad.14 = (bf16[512,2048]{1,0:T(8,128)(2,1)}, bf16[512,2048]{1,0:T(8,128)(2,1)}) custom-call(s32[3]{0:T(128)} %add_add_fusion.tab, bf16[2,1024,512]{2,1,0:T(8,128)(2,1)} %get-tuple-element.89.a, bf16[1024,4096]{1,0:T(8,128)(2,1)} %get-tuple-element.83.b, bf16[2,512,2048]{2,1,0:T(8,128)(2,1)} %collective-permute-done.4.refs_0_), custom_call_target="tpu_custom_call" | custom-call | flops 4294967296 | bytes 14680064 | tf_op jit(solution)/shard_map/weight_grad/pallas_call | solution.py:541
  280.2 5.0 weight_grad.15
  286.7 29.8 %attend_back.2 = (bf16[3,2,512,512]{3,2,1,0:T(8,128)(2,1)}, f32[4,4,8,256]{3,2,1,0:T(8,128)}) custom-call(s32[17]{0:T(128)} %pad_add_fusion.tab, bf16[2,512,3072]{2,1,0:T(8,128)(2,1)} %bitcast.154, bf16[2,512,3072]{2,1,0:T(8,128)(2,1)} %bitcast.155, bf16[2,512,3072]{2,1,0:T(8,128)(2,1)} %bitcast.156, bf16[2,512,1024]{2,1,0:T(8,128)(2,1)} %get-tuple-element.76.heads_out, ...), custom_call_target="tpu_custom_call" | custom-call | flops 21474836480 | bytes 12582912 | tf_op jit(solution)/shard_map/attend_back/pallas_call | solution.py:276
  316.6 7.5 %weight_grad.16 = bf16[2,512,768]{2,1,0:T(8,128)(2,1)} custom-call(s32[3]{0:T(128)} %add_add_fusion.1.tab, bf16[2,1024,512]{2,1,0:T(8,128)(2,1)} %get-tuple-element.110.a, bf16[3,1024,512]{2,1,0:T(8,128)(2,1)} %bitcast.141), custom_call_target="tpu_custom_call" | custom-call | flops 1610612736 | bytes 6815744 | tf_op jit(solution)/shard_map/weight_grad/pallas_call | solution.py:541
  324.0 12.5 %collective-permute-done.8 = bf16[512,512]{1,0:T(8,128)(2,1)S(1)} collective-permute-done((bf16[512,512]{1,0:T(8,128)(2,1)}, bf16[512,512]{1,0:T(8,128)(2,1)S(1)}, u32[]{:S(2)}, u32[]{:S(2)}) %collective-permute-start.8) | collective-permute-done | bytes 524320 | tf_op jit(solution)/shard_map/ppermute | solution.py:871
  346.6 29.5 %attend_back.3 = (bf16[3,2,512,512]{3,2,1,0:T(8,128)(2,1)}, f32[4,4,8,256]{3,2,1,0:T(8,128)}) custom-call(s32[17]{0:T(128)} %pad_add_fusion.tab, bf16[2,512,3072]{2,1,0:T(8,128)(2,1)} %bitcast.157, bf16[2,512,3072]{2,1,0:T(8,128)(2,1)} %bitcast.158, bf16[2,512,3072]{2,1,0:T(8,128)(2,1)} %bitcast.159, bf16[2,512,1024]{2,1,0:T(8,128)(2,1)} %get-tuple-element.76.heads_out, ...), custom_call_target="tpu_custom_call" | custom-call | flops 21474836480 | bytes 12582912 | tf_op jit(solution)/shard_map/attend_back/pallas_call | solution.py:276
  382.0 7.3 %weight_grad.17 = bf16[2,512,768]{2,1,0:T(8,128)(2,1)} custom-call(s32[3]{0:T(128)} %add_add_fusion.1.tab, bf16[2,1024,512]{2,1,0:T(8,128)(2,1)} %get-tuple-element.110.a, bf16[3,1024,512]{2,1,0:T(8,128)(2,1)} %bitcast.145), custom_call_target="tpu_custom_call" | custom-call | flops 1610612736 | bytes 6815744 | tf_op jit(solution)/shard_map/weight_grad/pallas_call | solution.py:541
  389.4 7.7 %weight_grad.18 = (bf16[512,768]{1,0:T(8,128)(2,1)}, bf16[512,768]{1,0:T(8,128)(2,1)}) custom-call(s32[3]{0:T(128)} %add_add_fusion.tab, bf16[2,1024,512]{2,1,0:T(8,128)(2,1)} %get-tuple-element.110.a, bf16[3,1024,512]{2,1,0:T(8,128)(2,1)} %bitcast.142, bf16[2,512,768]{2,1,0:T(8,128)(2,1)} %collective-permute-done.9.refs_0_), custom_call_target="tpu_custom_call" | custom-call | flops 1610612736 | bytes 6815744 | tf_op jit(solution)/shard_map/weight_grad/pallas_call | solution.py:541
  397.1 9.3 %first_back.2 = (bf16[512,1024]{1,0:T(8,128)(2,1)}, f32[8,1024]{1,0:T(8,128)}) custom-call(bf16[3,1024,512]{2,1,0:T(8,128)(2,1)} %bitcast.143, bf16[3,1024,512]{2,1,0:T(8,128)(2,1)} %bitcast.146, bf16[1024,3072]{1,0:T(8,128)(2,1)} %w.7, bf16[1024,1024]{1,0:T(8,128)(2,1)} %pad_maximum_fusion.tok, f32[1024,1024]{1,0:T(8,128)} %get-tuple-element.108.grad_middle, ...), custom_call_target="tpu_custom_call" | custom-call | flops 3221225472 | bytes 14680064 | tf_op jit(solution)/shard_map/first_back/pallas_call | solution.py:480
  420.0 29.4 %collective-permute-done.11 = bf16[512,1024]{1,0:T(8,128)(2,1)S(1)} collective-permute-done((bf16[512,1024]{1,0:T(8,128)(2,1)}, bf16[512,1024]{1,0:T(8,128)(2,1)S(1)}, u32[]{:S(2)}, u32[]{:S(2)}) %collective-permute-start.11) | collective-permute-done | bytes 1048608 | tf_op jit(solution)/shard_map/ppermute | solution.py:871
  453.2 7.7 %weight_grad.19 = (bf16[512,768]{1,0:T(8,128)(2,1)}, bf16[512,768]{1,0:T(8,128)(2,1)}) custom-call(s32[3]{0:T(128)} %add_add_fusion.tab, bf16[2,1024,512]{2,1,0:T(8,128)(2,1)} %get-tuple-element.110.a, bf16[3,1024,512]{2,1,0:T(8,128)(2,1)} %bitcast.147, bf16[2,512,768]{2,1,0:T(8,128)(2,1)} %collective-permute-done.10.refs_0_), custom_call_target="tpu_custom_call" | custom-call | flops 1610612736 | bytes 6815744 | tf_op jit(solution)/shard_map/weight_grad/pallas_call | solution.py:541
  460.9 9.7 %first_back.3 = (f32[512,1024]{1,0:T(8,128)}, f32[8,1024]{1,0:T(8,128)}) custom-call(bf16[3,1024,512]{2,1,0:T(8,128)(2,1)} %bitcast.144, bf16[3,1024,512]{2,1,0:T(8,128)(2,1)} %bitcast.148, bf16[1024,3072]{1,0:T(8,128)(2,1)} %w.7, bf16[1024,1024]{1,0:T(8,128)(2,1)} %pad_maximum_fusion.tok, f32[1024,1024]{1,0:T(8,128)} %get-tuple-element.108.grad_middle, ...), custom_call_target="tpu_custom_call" | custom-call | flops 3221225472 | bytes 14680064 | tf_op jit(solution)/shard_map/first_back/pallas_call | solution.py:480
  477.1 5.6 %collective-permute-done.43 = bf16[256,512]{1,0:T(8,128)(2,1)S(1)} collective-permute-done((bf16[256,512]{1,0:T(8,128)(2,1)S(1)}, bf16[256,512]{1,0:T(8,128)(2,1)S(1)}, u32[]{:S(2)}, u32[]{:S(2)}) %collective-permute-start.43) | collective-permute-done | bytes 262176 | tf_op jit(solution)/shard_map/ppermute | solution.py:875
  482.7 13.8 %collective-permute-done.42 = bf16[256,512]{1,0:T(8,128)(2,1)S(1)} collective-permute-done((bf16[256,512]{1,0:T(8,128)(2,1)S(1)}, bf16[256,512]{1,0:T(8,128)(2,1)S(1)}, u32[]{:S(2)}, u32[]{:S(2)}) %collective-permute-start.42) | collective-permute-done | bytes 262176 | tf_op jit(solution)/shard_map/ppermute | solution.py:875
  501.9 15.6 %collective-permute-done.14 = f32[5,1024]{1,0:T(8,128)S(1)} collective-permute-done((f32[5,1024]{1,0:T(8,128)S(1)}, f32[5,1024]{1,0:T(8,128)S(1)}, u32[]{:S(2)}, u32[]{:S(2)}) %collective-permute-start.14) | collective-permute-done | bytes 20512 | tf_op jit(solution)/shard_map/ppermute | solution.py:871
  518.1 3.3 collective-permute-done.15
  539.0 2.9 collective-permute-done.20
  543.5 3.6 collective-permute-done.25
  (221 shorter events, 99.7 us)
Async XLA Ops:
  3.9 27.2 %collective-permute-start = (bf16[512,1024]{1,0:T(8,128)(2,1)}, bf16[512,1024]{1,0:T(8,128)(2,1)S(1)}, u32[]{:S(2)}, u32[]{:S(2)}) collective-permute-start(bf16[512,1024]{1,0:T(8,128)(2,1)} %get-tuple-element.133), channel_id=1, source_target_pairs={{0,1},{1,0},{2,3},{3,2},{4,5},{5,4},{6,7},{7,6},{8,9},{9,8},{10,11... | collective-permute-start | bytes 3145736 | tf_op jit(solution)/shard_map/ppermute | solution.py:871
  8.1 63.1 %collective-permute-start.1 = (bf16[512,1024]{1,0:T(8,128)(2,1)}, bf16[512,1024]{1,0:T(8,128)(2,1)}, u32[]{:S(2)}, u32[]{:S(2)}) collective-permute-start(bf16[512,1024]{1,0:T(8,128)(2,1)} %get-tuple-element.131), channel_id=1, source_target_pairs={{0,1},{1,0},{2,3},{3,2},{4,5},{5,4},{6,7},{7,6},{8,9},{9,8},{10,11... | collective-permute-start | bytes 3145736 | tf_op jit(solution)/shard_map/ppermute | solution.py:871
  197.6 56.3 %collective-permute-start.3 = (bf16[2,1024,1024]{2,1,0:T(8,128)(2,1)}, bf16[2,1024,1024]{2,1,0:T(8,128)(2,1)}, u32[]{:S(2)}, u32[]{:S(2)}) collective-permute-start(bf16[2,1024,1024]{2,1,0:T(8,128)(2,1)} %weight_grad.10), channel_id=1, source_target_pairs={{0,2},{2,0},{4,6},{6,4},{8,10},{10,8},{12,14},{14,12},{16,18},{18,... | collective-permute-start | bytes 12582920 | tf_op jit(solution)/shard_map/ppermute | solution.py:875
  209.0 58.4 %collective-permute-start.4 = (bf16[2,512,2048]{2,1,0:T(8,128)(2,1)}, bf16[2,512,2048]{2,1,0:T(8,128)(2,1)}, u32[]{:S(2)}, u32[]{:S(2)}) collective-permute-start(bf16[2,512,2048]{2,1,0:T(8,128)(2,1)} %weight_grad.11), channel_id=1, source_target_pairs={{0,2},{2,0},{4,6},{6,4},{8,10},{10,8},{12,14},{14,12},{16,18},{18,... | collective-permute-start | bytes 12582920 | tf_op jit(solution)/shard_map/ppermute | solution.py:875
  226.7 24.3 %collective-permute-start.2 = (bf16[512,1024]{1,0:T(8,128)(2,1)}, bf16[512,1024]{1,0:T(8,128)(2,1)S(1)}, u32[]{:S(2)}, u32[]{:S(2)}) collective-permute-start(bf16[512,1024]{1,0:T(8,128)(2,1)} %slice.113), channel_id=1, source_target_pairs={{0,1},{1,0},{2,3},{3,2},{4,5},{5,4},{6,7},{7,6},{8,9},{9,8},{10,11... | collective-permute-start | bytes 3145736 | tf_op jit(solution)/shard_map/ppermute | solution.py:871
  239.1 41.1 %collective-permute-start.5 = (bf16[2,512,512]{2,1,0:T(8,128)(2,1)}, bf16[2,512,512]{2,1,0:T(8,128)(2,1)}, u32[]{:S(2)}, u32[]{:S(2)}) collective-permute-start(bf16[2,512,512]{2,1,0:T(8,128)(2,1)} %weight_grad.12), channel_id=1, source_target_pairs={{0,2},{2,0},{4,6},{6,4},{8,10},{10,8},{12,14},{14,12},{16,18},{18,... | collective-permute-start | bytes 3145736 | tf_op jit(solution)/shard_map/ppermute | solution.py:875
  265.9 74.1 %collective-permute-start.6 = (bf16[1024,1024]{1,0:T(8,128)(2,1)}, bf16[1024,1024]{1,0:T(8,128)(2,1)}, u32[]{:S(2)}, u32[]{:S(2)}) collective-permute-start(bf16[1024,1024]{1,0:T(8,128)(2,1)} %get-tuple-element.87), channel_id=1, source_target_pairs={{0,4},{2,6},{4,0},{6,2},{8,12},{10,14},{12,8},{14,10},{16,20},{18,... | collective-permute-start | bytes 6291464 | tf_op jit(solution)/shard_map/ppermute | solution.py:875
  279.7 58.2 %collective-permute-start.7 = (bf16[512,2048]{1,0:T(8,128)(2,1)}, bf16[512,2048]{1,0:T(8,128)(2,1)S(1)}, u32[]{:S(2)}, u32[]{:S(2)}) collective-permute-start(bf16[512,2048]{1,0:T(8,128)(2,1)} %get-tuple-element.90), channel_id=1, source_target_pairs={{0,1},{1,0},{2,3},{3,2},{4,5},{5,4},{6,7},{7,6},{8,9},{9,8},{10,11... | collective-permute-start | bytes 6291464 | tf_op jit(solution)/shard_map/ppermute | solution.py:871
  285.2 51.3 %collective-permute-start.8 = (bf16[512,512]{1,0:T(8,128)(2,1)}, bf16[512,512]{1,0:T(8,128)(2,1)S(1)}, u32[]{:S(2)}, u32[]{:S(2)}) collective-permute-start(bf16[512,512]{1,0:T(8,128)(2,1)} %get-tuple-element.93), channel_id=1, source_target_pairs={{0,1},{1,0},{2,3},{3,2},{4,5},{5,4},{6,7},{7,6},{8,9},{9,8},{10,11... | collective-permute-start | bytes 1572872 | tf_op jit(solution)/shard_map/ppermute | solution.py:871
  324.0 65.2 %collective-permute-start.9 = (bf16[2,512,768]{2,1,0:T(8,128)(2,1)}, bf16[2,512,768]{2,1,0:T(8,128)(2,1)}, u32[]{:S(2)}, u32[]{:S(2)}) collective-permute-start(bf16[2,512,768]{2,1,0:T(8,128)(2,1)} %weight_grad.16), channel_id=1, source_target_pairs={{0,2},{2,0},{4,6},{6,4},{8,10},{10,8},{12,14},{14,12},{16,18},{18,... | collective-permute-start | bytes 4718600 | tf_op jit(solution)/shard_map/ppermute | solution.py:875
  337.4 38.7 %collective-permute-start.27 = (bf16[4,64,512]{2,1,0:T(8,128)(2,1)}, bf16[4,64,512]{2,1,0:T(8,128)(2,1)}, u32[]{:S(2)}, u32[]{:S(2)}) collective-permute-start(bf16[4,64,512]{2,1,0:T(8,128)(2,1)} %get-tuple-element.141), channel_id=1, source_target_pairs={{0,4},{2,6},{4,0},{6,2},{8,12},{10,14},{12,8},{14,10},{16,20},{18,... | collective-permute-start | bytes 786440 | tf_op jit(solution)/shard_map/ppermute | solution.py:875
  344.6 70.2 %collective-permute-start.40 = (bf16[4,256,512]{2,1,0:T(8,128)(2,1)}, bf16[4,256,512]{2,1,0:T(8,128)(2,1)S(1)}, u32[]{:S(2)}, u32[]{:S(2)}) collective-permute-start(bf16[4,256,512]{2,1,0:T(8,128)(2,1)} %get-tuple-element.129), channel_id=1, source_target_pairs={{0,1},{1,0},{2,3},{3,2},{4,5},{5,4},{6,7},{7,6},{8,9},{9,8},{10,11... | collective-permute-start | bytes 3145736 | tf_op jit(solution)/shard_map/ppermute | solution.py:871
  345.5 64.9 %collective-permute-start.36 = (bf16[4,64,2048]{2,1,0:T(8,128)(2,1)}, bf16[4,64,2048]{2,1,0:T(8,128)(2,1)}, u32[]{:S(2)}, u32[]{:S(2)}) collective-permute-start(bf16[4,64,2048]{2,1,0:T(8,128)(2,1)} %get-tuple-element.127), channel_id=1, source_target_pairs={{0,4},{2,6},{4,0},{6,2},{8,12},{10,14},{12,8},{14,10},{16,20},{18,... | collective-permute-start | bytes 3145736 | tf_op jit(solution)/shard_map/ppermute | solution.py:875
  377.9 28.8 %collective-permute-start.28 = (bf16[64,512]{1,0:T(8,128)(2,1)S(1)}, bf16[64,512]{1,0:T(8,128)(2,1)S(1)}, u32[]{:S(2)}, u32[]{:S(2)}) collective-permute-start(bf16[64,512]{1,0:T(8,128)(2,1)S(1)} %get-tuple-element.148), channel_id=1, source_target_pairs={{0,8},{2,10},{4,12},{6,14},{8,0},{10,2},{12,4},{14,6},{16,24},{18,... | collective-permute-start | bytes 196616 | tf_op jit(solution)/shard_map/ppermute | solution.py:875
  379.5 27.3 %collective-permute-start.30 = (bf16[64,512]{1,0:T(8,128)(2,1)S(1)}, bf16[64,512]{1,0:T(8,128)(2,1)S(1)}, u32[]{:S(2)}, u32[]{:S(2)}) collective-permute-start(bf16[64,512]{1,0:T(8,128)(2,1)S(1)} %get-tuple-element.149), channel_id=1, source_target_pairs={{0,24},{2,26},{4,28},{6,30},{8,16},{10,18},{12,20},{14,22},{16,8},... | collective-permute-start | bytes 196616 | tf_op jit(solution)/shard_map/ppermute | solution.py:875
  389.3 19.1 %collective-permute-start.29 = (bf16[64,512]{1,0:T(8,128)(2,1)S(1)}, bf16[64,512]{1,0:T(8,128)(2,1)S(1)}, u32[]{:S(2)}, u32[]{:S(2)}) collective-permute-start(bf16[64,512]{1,0:T(8,128)(2,1)S(1)} %get-tuple-element.150), channel_id=1, source_target_pairs={{0,16},{2,18},{4,20},{6,22},{8,24},{10,26},{12,28},{14,30},{16,0},... | collective-permute-start | bytes 196616 | tf_op jit(solution)/shard_map/ppermute | solution.py:875
  406.7 45.8 %collective-permute-start.10 = (bf16[2,512,768]{2,1,0:T(8,128)(2,1)}, bf16[2,512,768]{2,1,0:T(8,128)(2,1)}, u32[]{:S(2)}, u32[]{:S(2)}) collective-permute-start(bf16[2,512,768]{2,1,0:T(8,128)(2,1)} %weight_grad.17), channel_id=1, source_target_pairs={{0,2},{2,0},{4,6},{6,4},{8,10},{10,8},{12,14},{14,12},{16,18},{18,... | collective-permute-start | bytes 4718600 | tf_op jit(solution)/shard_map/ppermute | solution.py:875
  406.8 93.8 %collective-permute-start.17 = (bf16[512,768]{1,0:T(8,128)(2,1)}, bf16[512,768]{1,0:T(8,128)(2,1)}, u32[]{:S(2)}, u32[]{:S(2)}) collective-permute-start(bf16[512,768]{1,0:T(8,128)(2,1)} %get-tuple-element.105), channel_id=1, source_target_pairs={{0,1},{1,0},{2,3},{3,2},{4,5},{5,4},{6,7},{7,6},{8,9},{9,8},{10,11... | collective-permute-start | bytes 2359304 | tf_op jit(solution)/shard_map/ppermute | solution.py:871
  408.4 41.1 %collective-permute-start.11 = (bf16[512,1024]{1,0:T(8,128)(2,1)}, bf16[512,1024]{1,0:T(8,128)(2,1)S(1)}, u32[]{:S(2)}, u32[]{:S(2)}) collective-permute-start(bf16[512,1024]{1,0:T(8,128)(2,1)} %get-tuple-element.109), channel_id=1, source_target_pairs={{0,1},{1,0},{2,3},{3,2},{4,5},{5,4},{6,7},{7,6},{8,9},{9,8},{10,11... | collective-permute-start | bytes 3145736 | tf_op jit(solution)/shard_map/ppermute | solution.py:871
  413.0 58.5 %collective-permute-start.37 = (bf16[64,2048]{1,0:T(8,128)(2,1)}, bf16[64,2048]{1,0:T(8,128)(2,1)}, u32[]{:S(2)}, u32[]{:S(2)}) collective-permute-start(bf16[64,2048]{1,0:T(8,128)(2,1)} %get-tuple-element.137), channel_id=1, source_target_pairs={{0,8},{2,10},{4,12},{6,14},{8,0},{10,2},{12,4},{14,6},{16,24},{18,... | collective-permute-start | bytes 786440 | tf_op jit(solution)/shard_map/ppermute | solution.py:875
  415.9 56.7 %collective-permute-start.39 = (bf16[64,2048]{1,0:T(8,128)(2,1)}, bf16[64,2048]{1,0:T(8,128)(2,1)}, u32[]{:S(2)}, u32[]{:S(2)}) collective-permute-start(bf16[64,2048]{1,0:T(8,128)(2,1)} %get-tuple-element.138), channel_id=1, source_target_pairs={{0,24},{2,26},{4,28},{6,30},{8,16},{10,18},{12,20},{14,22},{16,8},... | collective-permute-start | bytes 786440 | tf_op jit(solution)/shard_map/ppermute | solution.py:875
  449.4 25.0 %collective-permute-start.38 = (bf16[64,2048]{1,0:T(8,128)(2,1)}, bf16[64,2048]{1,0:T(8,128)(2,1)}, u32[]{:S(2)}, u32[]{:S(2)}) collective-permute-start(bf16[64,2048]{1,0:T(8,128)(2,1)} %get-tuple-element.139), channel_id=1, source_target_pairs={{0,16},{2,18},{4,20},{6,22},{8,24},{10,26},{12,28},{14,30},{16,0},... | collective-permute-start | bytes 786440 | tf_op jit(solution)/shard_map/ppermute | solution.py:875
  452.5 24.7 %collective-permute-start.41 = (bf16[256,512]{1,0:T(8,128)(2,1)S(1)}, bf16[256,512]{1,0:T(8,128)(2,1)}, u32[]{:S(2)}, u32[]{:S(2)}) collective-permute-start(bf16[256,512]{1,0:T(8,128)(2,1)S(1)} %get-tuple-element.134), channel_id=1, source_target_pairs={{0,8},{2,10},{4,12},{6,14},{8,0},{10,2},{12,4},{14,6},{16,24},{18,... | collective-permute-start | bytes 786440 | tf_op jit(solution)/shard_map/ppermute | solution.py:875
  471.6 11.2 %collective-permute-start.43 = (bf16[256,512]{1,0:T(8,128)(2,1)S(1)}, bf16[256,512]{1,0:T(8,128)(2,1)S(1)}, u32[]{:S(2)}, u32[]{:S(2)}) collective-permute-start(bf16[256,512]{1,0:T(8,128)(2,1)S(1)} %get-tuple-element.135), channel_id=1, source_target_pairs={{0,24},{2,26},{4,28},{6,30},{8,16},{10,18},{12,20},{14,22},{16,8},... | collective-permute-start | bytes 786440 | tf_op jit(solution)/shard_map/ppermute | solution.py:875
  472.5 24.0 %collective-permute-start.42 = (bf16[256,512]{1,0:T(8,128)(2,1)S(1)}, bf16[256,512]{1,0:T(8,128)(2,1)S(1)}, u32[]{:S(2)}, u32[]{:S(2)}) collective-permute-start(bf16[256,512]{1,0:T(8,128)(2,1)S(1)} %get-tuple-element.136), channel_id=1, source_target_pairs={{0,16},{2,18},{4,20},{6,22},{8,24},{10,26},{12,28},{14,30},{16,0},... | collective-permute-start | bytes 786440 | tf_op jit(solution)/shard_map/ppermute | solution.py:875
  476.5 23.4 %collective-permute-start.13 = (f32[5,1024]{1,0:T(8,128)S(1)}, f32[5,1024]{1,0:T(8,128)S(1)}, u32[]{:S(2)}, u32[]{:S(2)}) collective-permute-start(f32[5,1024]{1,0:T(8,128)S(1)} %fusion.14), channel_id=1, source_target_pairs={{0,4},{2,6},{4,0},{6,2},{8,12},{10,14},{12,8},{14,10},{16,20},{18,... | collective-permute-start | bytes 61448 | tf_op jit(solution)/shard_map/ppermute | solution.py:875
  498.4 28.4 %collective-permute-start.22 = (bf16[512,768]{1,0:T(8,128)(2,1)S(1)}, bf16[512,768]{1,0:T(8,128)(2,1)S(1)}, u32[]{:S(2)}, u32[]{:S(2)}) collective-permute-start(bf16[512,768]{1,0:T(8,128)(2,1)S(1)} %copy-done.32), channel_id=1, source_target_pairs={{0,1},{1,0},{2,3},{3,2},{4,5},{5,4},{6,7},{7,6},{8,9},{9,8},{10,11... | collective-permute-start | bytes 2359304 | tf_op jit(solution)/shard_map/ppermute | solution.py:871
  499.9 17.5 %collective-permute-start.14 = (f32[5,1024]{1,0:T(8,128)S(1)}, f32[5,1024]{1,0:T(8,128)S(1)}, u32[]{:S(2)}, u32[]{:S(2)}) collective-permute-start(f32[5,1024]{1,0:T(8,128)S(1)} %add.197), channel_id=1, source_target_pairs={{0,1},{1,0},{2,3},{3,2},{4,5},{5,4},{6,7},{7,6},{8,9},{9,8},{10,11... | collective-permute-start | bytes 61448 | tf_op jit(solution)/shard_map/ppermute | solution.py:871
  517.5 10.7 %collective-permute-start.18 = (bf16[4,64,768]{2,1,0:T(8,128)(2,1)S(1)}, bf16[4,64,768]{2,1,0:T(8,128)(2,1)S(1)}, u32[]{:S(2)}, u32[]{:S(2)}) collective-permute-start(bf16[4,64,768]{2,1,0:T(8,128)(2,1)S(1)} %dynamic-slice_bitcast_fusion.7), channel_id=1, source_target_pairs={{0,4},{2,6},{4,0},{6,2},{8,12},{10,14},{12,8},{14,10},{16,20},{18,... | collective-permute-start | bytes 1179656 | tf_op jit(solution)/shard_map/ppermute | solution.py:875
  528.4 10.6 %collective-permute-start.19 = (bf16[64,768]{1,0:T(8,128)(2,1)S(1)}, bf16[64,768]{1,0:T(8,128)(2,1)S(1)}, u32[]{:S(2)}, u32[]{:S(2)}) collective-permute-start(bf16[64,768]{1,0:T(8,128)(2,1)S(1)} %get-tuple-element.142), channel_id=1, source_target_pairs={{0,8},{2,10},{4,12},{6,14},{8,0},{10,2},{12,4},{14,6},{16,24},{18,... | collective-permute-start | bytes 294920 | tf_op jit(solution)/shard_map/ppermute | solution.py:875
  530.1 8.8 %collective-permute-start.21 = (bf16[64,768]{1,0:T(8,128)(2,1)S(1)}, bf16[64,768]{1,0:T(8,128)(2,1)S(1)}, u32[]{:S(2)}, u32[]{:S(2)}) collective-permute-start(bf16[64,768]{1,0:T(8,128)(2,1)S(1)} %get-tuple-element.143), channel_id=1, source_target_pairs={{0,24},{2,26},{4,28},{6,30},{8,16},{10,18},{12,20},{14,22},{16,8},... | collective-permute-start | bytes 294920 | tf_op jit(solution)/shard_map/ppermute | solution.py:875
  532.2 9.6 %collective-permute-start.20 = (bf16[64,768]{1,0:T(8,128)(2,1)S(1)}, bf16[64,768]{1,0:T(8,128)(2,1)S(1)}, u32[]{:S(2)}, u32[]{:S(2)}) collective-permute-start(bf16[64,768]{1,0:T(8,128)(2,1)S(1)} %get-tuple-element.144), channel_id=1, source_target_pairs={{0,16},{2,18},{4,20},{6,22},{8,24},{10,26},{12,28},{14,30},{16,0},... | collective-permute-start | bytes 294920 | tf_op jit(solution)/shard_map/ppermute | solution.py:875
  (45 other events, 398.4 us)

commit v3 on v2

--- a/solution.py
+++ b/solution.py
@@ -66,33 +66,61 @@
     return (jnp.concatenate(y, axis=1).astype(bf16) for y in (even, odd))
 
 
-def qkv_body(scale, tok, gain, shift, w, qb, vb, *refs):
-    attn_in, qkv = refs[-2:]
-    unit, _ = norm_unit(tok[...].astype(f32))
-    x = (unit * gain[...] + shift[...]).astype(bf16)
-    attn_in[0], attn_in[1] = core_split(x)
-    d = x.shape[1]
-    q = (mm(x, w[:, :d]) + qb[...]).astype(bf16)
-    qkv[:, :d] = (q.astype(f32) * scale).astype(bf16)
-    qkv[:, d : 2 * d] = mm(x, w[:, d : 2 * d]).astype(bf16)
-    qkv[:, 2 * d :] = (mm(x, w[:, 2 * d :]) + vb[...]).astype(bf16)
-
-
-def project_qkv(tok, gain, shift, w, qb, vb, scale, slot, total, earlier=(), tb=256):
-    n, d = tok.shape
-    first = slot * (n // tb)
+def qkv_body(scale, at, tok, gain, shift, w, bias, *refs):
+    attn_in, qkv, x, ws, sems = refs[-5:]
+    step = pl.program_id(0)
+    steps, d, cols = ws.shape
+    half = cols // 2
+
+    def fetch(k, h):
+        columns = pl.ds(pl.multiple_of(k * cols + h * half, half), half)
+        return pltpu.make_async_copy(
+            w.at[:, columns], ws.at[k, :, pl.ds(h * half, half)], sems.at[k, h]
+        )
+
+    @pl.when(step == 0)
+    def _():
+        for k in range(steps):
+            for h in range(2):
+                fetch(k, h).start()
+        unit, _ = norm_unit(tok[0].astype(f32))
+        here = (unit * gain[...] + shift[...]).astype(bf16)
+        x[...] = here
+        attn_in[0], attn_in[1] = core_split(here)
+
+    for h in range(2):
+        fetch(step, h).wait()
+    total = (mm(x[...], ws[step]) + bias[...]).astype(bf16)
+    qkv[...] = (total.astype(f32) * jnp.where(step == 0, scale, 1.0)).astype(bf16)
+
+
+def project_qkv(at, tok, gain, shift, w, bias, scale, slot, total, earlier=()):
+    _, n, d = tok.shape
     held = pl.BlockSpec(memory_space=pl.ANY)
     return pl.pallas_call(
         partial(qkv_body, scale),
         name="project_qkv",
-        grid=(n // tb,),
-        in_specs=[pl.BlockSpec((tb, d), lambda i: (i, 0))]
-        + [whole(a.shape) for a in (gain, shift, w, qb, vb)]
-        + [held] * len(earlier),
-        out_specs=[
-            pl.BlockSpec((2, tb, d // 2), lambda i: (0, first + i, 0)),
-            pl.BlockSpec((tb, 3 * d), lambda i: (first + i, 0)),
-        ],
+        grid_spec=pltpu.PrefetchScalarGridSpec(
+            num_scalar_prefetch=1,
+            grid=(3,),
+            in_specs=[
+                pl.BlockSpec((1, n, d), lambda i, at: (at[0], 0, 0), pipeline_mode=pl.Buffered(1)),
+                whole(gain.shape),
+                whole(shift.shape),
+                held,
+                pl.BlockSpec((1, d), lambda i, at: (0, i)),
+            ]
+            + [held] * len(earlier),
+            out_specs=[
+                pl.BlockSpec((2, n, d // 2), lambda i, at: (0, slot, 0)),
+                pl.BlockSpec((n, d), lambda i, at: (slot, i)),
+            ],
+            scratch_shapes=[
+                pltpu.VMEM((n, d), bf16),
+                pltpu.VMEM((3, d, d), bf16),
+                pltpu.SemaphoreType.DMA((3, 2)),
+            ],
+        ),
         out_shape=[
             jax.ShapeDtypeStruct((2, total, d // 2), bf16),
             jax.ShapeDtypeStruct((total, 3 * d), bf16),
@@ -102,7 +130,7 @@
         cost_estimate=pl.CostEstimate(
             flops=2 * n * d * 3 * d, bytes_accessed=6 * d * d + 10 * n * d, transcendentals=n
         ),
-    )(tok, gain, shift, w, qb, vb, *earlier)
+    )(at, tok, gain, shift, w, bias, *earlier)
 
 
 def half_slot(own, half):
@@ -122,45 +150,48 @@
     return jnp.where(tab[1 + 4 * i + j] > 0, 0.0, masked_score).astype(f32)
 
 
-def attend_body(tab, q, k, v, head_scale, heads_out, lse):
+def stack_heads(x, low):
+    zero = jnp.zeros_like(x)
+    return jnp.concatenate([jnp.where(low, x, zero), jnp.where(low, zero, x)], axis=0)
+
+
+def place(ref, own, *targets):
+    half = ref.shape[1]
+    for h in range(2):
+        targets[0][h * half : (h + 1) * half, :] = ref[half_slot(own, h)]
+
+
+def attend_body(tab, q, k, v, head_scale, heads_out, lse, kp, vp):
     size = q.shape[1] // 2
     own = tab[0]
     low = head_mask(size)
-    causal = lax.broadcasted_iota(jnp.int32, (size, size), 0) >= lax.broadcasted_iota(
-        jnp.int32, (size, size), 1
+    causal = lax.broadcasted_iota(jnp.int32, (2 * size, size), 0) % size >= lax.broadcasted_iota(
+        jnp.int32, (2 * size, size), 1
     )
     lane = lax.broadcasted_iota(jnp.int32, (size, LANES), 1)
+    place(k, own, kp)
+    place(v, own, vp)
     for i in range(4):
-        qi = pick(q, own, i, size)
-        outs = []
-        logs = []
-        for h in range(2):
-            qm = jnp.where(low if h == 0 else ~low, qi, 0).astype(bf16)
-            parts = []
-            for j in range(i + 1):
-                s = mm(qm, pick(k, own, j, size), NT)
-                parts.append(
-                    jnp.where(causal, s, masked_score) if j == i else s + block_penalty(tab, i, j)
-                )
-            top = parts[0]
-            for s in parts[1:]:
-                top = jnp.maximum(top, s)
-            top = jnp.max(top, axis=1, keepdims=True)
-            total = None
-            out = None
-            for j, s in enumerate(parts):
-                p = jnp.exp(s - top)
-                part_sum = fold(p)
-                total = part_sum if total is None else total + part_sum
-                part_out = mm(p.astype(bf16), pick(v, own, j, size))
-                out = part_out if out is None else out + part_out
-            total = jnp.sum(total, axis=1, keepdims=True)
-            outs.append(out * (1.0 / total))
-            logs.append(top + jnp.log(total))
-        both = jnp.where(low, outs[0], outs[1]) * head_scale[...]
+        width = (i + 1) * size
+        s = mm(stack_heads(pick(q, own, i, size), low), kp[:width, :], NT)
+        parts = [s[:, j * size : (j + 1) * size] + block_penalty(tab, i, j) for j in range(i)]
+        parts.append(jnp.where(causal, s[:, i * size :], masked_score))
+        top = parts[0]
+        for part in parts[1:]:
+            top = jnp.maximum(top, part)
+        top = jnp.max(top, axis=1, keepdims=True)
+        parts = [jnp.exp(part - top) for part in parts]
+        total = fold(parts[0])
+        for part in parts[1:]:
+            total = total + fold(part)
+        total = jnp.sum(total, axis=1, keepdims=True)
+        p = jnp.concatenate([part.astype(bf16) for part in parts], axis=1)
+        out = mm(p, vp[:width, :]) * (1.0 / total)
+        both = jnp.where(low, out[:size], out[size:]) * head_scale[...]
         half, sub = divmod(i, 2)
         heads_out[half_slot(own, half), sub * size : (sub + 1) * size, :] = both.astype(bf16)
-        columns = jnp.where(lane == 0, logs[0], logs[1])
+        logs = top + jnp.log(total)
+        columns = jnp.where(lane == 0, logs[:size], logs[size:])
         lse[0, i] = jnp.transpose(columns)[:8]
 
 
@@ -190,6 +221,7 @@
                 lanes(0),
                 pl.BlockSpec((1, 4, 8, size), lambda p, t: (p, 0, 0, 0)),
             ],
+            scratch_shapes=[pltpu.VMEM((2 * half_len, LANES), bf16)] * 2,
         ),
         out_shape=[
             jax.ShapeDtypeStruct((2, half_len, d), bf16),
@@ -203,60 +235,64 @@
 
 
 def attend_back_body(
-    scale, tab, q, k, v, heads_out, d_out, inv_scale, lse, dqkv, dots, dq_acc
+    scale, tab, q, k, v, heads_out, d_out, inv_scale, lse, dqkv, dots, kp, vp, dk, dv
 ):
     size = q.shape[1] // 2
     own = tab[0]
     low = head_mask(size)
-    masks = (low, ~low)
-    causal = lax.broadcasted_iota(jnp.int32, (size, size), 0) <= lax.broadcasted_iota(
-        jnp.int32, (size, size), 1
-    )
-    pick_rows = (
-        lax.broadcasted_iota(jnp.int32, (8, LANES), 1) // (LANES // 2)
-        == lax.broadcasted_iota(jnp.int32, (8, LANES), 0)
-    ).astype(f32)
-    qs, gs, deltas = {}, {}, []
-    for i in range(4):
-        qi = pick(q, own, i, size)
+    causal = lax.broadcasted_iota(jnp.int32, (2 * size, size), 0) % size >= lax.broadcasted_iota(
+        jnp.int32, (2 * size, size), 1
+    )
+    place(k, own, kp)
+    place(v, own, vp)
+    dots[...] = jnp.zeros_like(dots)
+    for i in range(3, -1, -1):
+        width = (i + 1) * size
+        q2 = stack_heads(pick(q, own, i, size), low)
         gi = pick(d_out, own, i, size)
-        for h in range(2):
-            qs[i, h] = jnp.where(masks[h], qi, 0).astype(bf16)
-            gs[i, h] = jnp.where(masks[h], gi, 0).astype(bf16)
+        g2 = stack_heads(gi, low)
         product = gi.astype(f32) * pick(heads_out, own, i, size).astype(f32) * inv_scale[...]
-        delta = lax.dot_general(
-            pick_rows, product, NT, preferred_element_type=f32, precision=lax.Precision.HIGHEST
+        dots[0, 0:1, :] += row_sum(product)
+        zero = jnp.zeros_like(product)
+        delta = jnp.concatenate(
+            [
+                jnp.sum(jnp.where(low, product, zero), axis=1, keepdims=True),
+                jnp.sum(jnp.where(low, zero, product), axis=1, keepdims=True),
+            ],
+            axis=0,
         )
-        deltas.append(delta)
-        dots[0, i] = delta
-        dq_acc[i] = jnp.zeros((size, LANES), f32)
-    for j in range(4):
-        kj = pick(k, own, j, size)
-        vj = pick(v, own, j, size)
-        dk_j = jnp.zeros((size, LANES), f32)
-        dv_j = jnp.zeros((size, LANES), f32)
-        for h in range(2):
-            km = jnp.where(masks[h], kj, 0).astype(bf16)
-            for i in range(j, 4):
-                logs = lse[0, i, h : h + 1, :]
-                if i > j:
-                    logs = logs - block_penalty(tab, i, j)
-                s = mm(kj, qs[i, h], NT)
-                if i == j:
-                    s = jnp.where(causal, s, masked_score)
-                p = jnp.exp(s - logs)
-                gp = mm(vj, gs[i, h], NT)
-                ds = (p * (gp - deltas[i][h : h + 1, :])).astype(bf16)
-                dv_j = dv_j + mm(p.astype(bf16), gs[i, h])
-                dk_j = dk_j + mm(ds, qs[i, h])
-                dq_acc[i] += mm(ds, km, TN)
-        half, sub = divmod(j, 2)
-        where = (half_slot(own, half), slice(sub * size, (sub + 1) * size))
-        dqkv[1, where[0], where[1], :] = dk_j.astype(bf16)
-        dqkv[2, where[0], where[1], :] = dv_j.astype(bf16)
-    for i in range(4):
+        columns = jnp.transpose(lse[0, i])
+        logs = jnp.concatenate([columns[:, 0:1], columns[:, 1:2]], axis=0)
+        s = mm(q2, kp[:width, :], NT)
+        g = mm(g2, vp[:width, :], NT)
+        ps, ds = [], []
+        for j in range(i + 1):
+            here = slice(j * size, (j + 1) * size)
+            if j < i:
+                p = jnp.exp(s[:, here] - (logs - block_penalty(tab, i, j)))
+            else:
+                p = jnp.exp(jnp.where(causal, s[:, here], masked_score) - logs)
+            ps.append(p.astype(bf16))
+            ds.append((p * (g[:, here] - delta)).astype(bf16))
+        p = jnp.concatenate(ps, axis=1)
+        d = jnp.concatenate(ds, axis=1)
+        dv_part = mm(p, g2, TN)
+        dk_part = mm(d, q2, TN)
+        if i == 3:
+            dv[...] = dv_part
+            dk[...] = dk_part
+        else:
+            dv[:width, :] += dv_part
+            dk[:width, :] += dk_part
+        dq = mm(d, kp[:width, :]) * scale
         half, sub = divmod(i, 2)
-        dqkv[0, half_slot(own, half), sub * size : (sub + 1) * size, :] = (dq_acc[i] * scale).astype(bf16)
+        dqkv[0, half_slot(own, half), sub * size : (sub + 1) * size, :] = jnp.where(
+            low, dq[:size], dq[size:]
+        ).astype(bf16)
+    for half in range(2):
+        here = slice(half * 2 * size, (half + 1) * 2 * size)
+        dqkv[1, half_slot(own, half)] = dk[here, :].astype(bf16)
+        dqkv[2, half_slot(own, half)] = dv[here, :].astype(bf16)
 
 
 def attend_back(tab, qkv, heads_out, d_out, inv_scale_row, lse, scale, group):
@@ -290,13 +326,14 @@
             ],
             out_specs=[
                 pl.BlockSpec((3, 2, half_len, LANES), lambda p, t: (0, 0, 0, p)),
-                pl.BlockSpec((1, 4, 8, size), lambda p, t: (p, 0, 0, 0)),
+                pl.BlockSpec((1, 8, LANES), lambda p, t: (p, 0, 0)),
             ],
-            scratch_shapes=[pltpu.VMEM((4, size, LANES), f32)],
+            scratch_shapes=[pltpu.VMEM((2 * half_len, LANES), bf16)] * 2
+            + [pltpu.VMEM((2 * half_len, LANES), f32)] * 2,
         ),
         out_shape=[
             jax.ShapeDtypeStruct((3, 2, half_len, d // 2), bf16),
-            jax.ShapeDtypeStruct((pairs, 4, 8, size), f32),
+            jax.ShapeDtypeStruct((pairs, 8, LANES), f32),
         ],
         compiler_params=params(),
         cost_estimate=pl.CostEstimate(
@@ -316,138 +353,237 @@
 
 
 def middle_body(
-    ho, tok, cot, out_w, w1, w2, vec, vec4,
-    output, grad_middle, ffn_in, heads_in, mid_out, grad_hidden, grad_proj, d_out, sums, sums4,
-    act, slope, back,
+    at, ho, tok, cot, out_w, w1, w2, vec, vec4, *refs
 ):
+    (
+        output, grad_middle, sums, sums4, ffn_in, heads_in, mid_out, grad_hidden, grad_proj, d_out,
+        act, slope, back, acc, unit_b, stats, total, total_u, w1s, w2s, sems,
+    ) = refs[-21:]
+    ho, tok, cot, d_out = (ref.at[0] for ref in (ho, tok, cot, d_out))
+    output = output.at[0] if len(output.shape) == 3 else output
     step = pl.program_id(0)
-    d = ho.shape[1]
-    ff = w1.shape[1]
-    fc = 512
-    chunks = ff // fc
+    n, d = ho.shape
+    chunks, _, fc = w1s.shape
+    ff = fc * chunks
+    c = step % chunks
+    ahead = 2
+
+    def fetch(k):
+        columns = pl.ds(pl.multiple_of(k * fc, fc), fc)
+        return (
+            pltpu.make_async_copy(w1.at[:, columns], w1s.at[k], sems.at[0, k]),
+            pltpu.make_async_copy(w2.at[columns, :], w2s.at[k], sems.at[1, k]),
+        )
+    strip = 128
+    strips = n // strip
+
+    def v(r):
+        return vec[r : r + 1, :]
+
+    def rows(t):
+        return pl.ds(pl.multiple_of(t * strip, strip), strip)
 
     @pl.when(step == 0)
     def _():
+        for k in range(ahead):
+            for copy in fetch(k):
+                copy.start()
         sums[...] = jnp.zeros_like(sums)
-        sums4[...] = jnp.zeros_like(sums4)
-
-    def v(r):
-        return vec[r : r + 1, :]
-
-    tokens = tok[...].astype(f32)
-    projection = mm(ho[...], out_w[...]) + v(0)
-    unit_attn, inverse_attn = norm_unit(projection)
-    middle = tokens + (unit_attn * v(1) + v(2))
-    unit_two, inverse_two = norm_unit(middle)
-    x = (unit_two * v(3) + v(4)).astype(bf16)
-    ffn_in[0], ffn_in[1] = core_split(x)
-    heads_in[0], heads_in[1] = core_split(ho[...])
-    g = cot[...]
-    tb = x.shape[0]
-    zero = jnp.zeros((tb, LANES), f32)
-
-    def span(c):
-        return pl.ds(pl.multiple_of(c * fc, fc), fc)
-
-    def one(c, total):
-        s = span(c)
-        h = mm(x, w1[:, s]) + vec4[0:1, s]
-        back[:, s] = mm(g, w2[s, :], NT)
+        acc[...] = mm(ho[...], out_w[...])
+
+        def one(t, _):
+            r = rows(t)
+            unit_attn, inverse_attn = norm_unit(acc[r, :] + v(0))
+            middle = tok[r, :].astype(f32) + (unit_attn * v(1) + v(2))
+            unit_two, inverse_two = norm_unit(middle)
+            x = (unit_two * v(3) + v(4)).astype(bf16)
+            grad_middle[r, :] = unit_attn
+            unit_b[r, :] = unit_two
+            stats[r, 0:1] = inverse_attn
+            stats[r, 1:2] = inverse_two
+            acc[r, :] = middle + v(5)
+            d_out[r, :] = x
+            ffn_in[0, r, :], ffn_in[1, r, :] = core_split(x)
+            heads_in[0, r, :], heads_in[1, r, :] = core_split(ho[r, :])
+            return 0
+
+        lax.fori_loop(0, strips, one, 0)
+
+    @pl.when(step < chunks - ahead)
+    def _():
+        for copy in fetch(step + ahead):
+            copy.start()
+
+    @pl.when(step < chunks)
+    def _():
+        for copy in fetch(step):
+            copy.wait()
+        h = mm(d_out[...], w1s[c]) + vec4[0:1, :]
+        back[c] = mm(cot[...], w2s[c], NT).astype(back.dtype)
         a, b = gelu_parts(h)
-        act[:, s] = a
-        slope[:, s] = b
-        return total + fold(a)
-
-    total = lax.fori_loop(0, chunks, one, zero)
-    mean = jnp.sum(total, axis=1, keepdims=True) * (1.0 / ff)
-
-    def two(c, total):
-        a = act[:, span(c)] - mean
-        return total + fold(a * a)
-
-    total = lax.fori_loop(0, chunks, two, zero)
-    inverse = lax.rsqrt(jnp.sum(total, axis=1, keepdims=True) * (1.0 / ff) + eps)
-
-    def three(c, carry):
-        acc, sum_e, sum_eu = carry
-        s = span(c)
-        u = (act[:, s] - mean) * inverse
-        act[:, s] = u
-        gain = vec4[1:2, s]
-        m = (u * gain + vec4[2:3, s]).astype(bf16)
-        mid_out[:, s] = m
-        gm = back[:, s]
-        sums4[1:2, s] += row_sum(gm * u)
-        sums4[2:3, s] += row_sum(gm)
-        e = gm * gain
-        return acc + mm(m, w2[s, :]), sum_e + fold(e), sum_eu + fold(e * u)
-
-    acc, sum_e, sum_eu = lax.fori_loop(
-        0, chunks, three, (jnp.zeros((tb, d), f32), zero, zero)
-    )
-    output[...] = middle + acc + v(5)
-    mean_e = jnp.sum(sum_e, axis=1, keepdims=True) * (1.0 / ff)
-    mean_eu = jnp.sum(sum_eu, axis=1, keepdims=True) * (1.0 / ff)
-
-    def four(c, acc):
-        s = span(c)
-        e = back[:, s] * vec4[1:2, s]
-        grad_act = inverse * (e - mean_e - act[:, s] * mean_eu)
-        gh = (grad_act * slope[:, s]).astype(bf16)
-        grad_hidden[:, s] = gh
-        sums4[0:1, s] += row_sum(gh.astype(f32))
-        return acc + mm(gh, w1[:, s], NT)
-
-    grad_ffn_in = lax.fori_loop(0, chunks, four, jnp.zeros((tb, d), f32))
-    gout = g.astype(f32)
-    sums[5:6, :] += row_sum(gout)
-    sums[3:4, :] += row_sum(grad_ffn_in * unit_two)
-    sums[4:5, :] += row_sum(grad_ffn_in)
-    gmid = gout + norm_back(grad_ffn_in, unit_two, inverse_two, v(3))
-    grad_middle[...] = gmid
-    sums[1:2, :] += row_sum(gmid * unit_attn)
-    sums[2:3, :] += row_sum(gmid)
-    gp = norm_back(gmid, unit_attn, inverse_attn, v(1)).astype(bf16)
-    grad_proj[...] = gp
-    sums[0:1, :] += row_sum(gp.astype(f32))
-    d_out[...] = (mm(gp, out_w[...], NT) * v(6)).astype(bf16)
-
-
-def middle_pass(ho, tok, cot, out_w, w1, w2, vec, vec4, tb=256):
-    n, d = ho.shape
+        act[c] = a
+        slope[c] = b.astype(slope.dtype)
+
+    @pl.when(step == 0)
+    def _():
+        total[...] = jnp.zeros_like(total)
+
+    @pl.when(step < chunks)
+    def _():
+        total[...] += fold(act[c])
+
+    @pl.when(step == chunks)
+    def _():
+        mean = jnp.sum(total[...], axis=1, keepdims=True) * (1.0 / ff)
+
+        def one(k, t):
+            centered = act[k] - mean
+            return t + fold(centered * centered)
+
+        square = lax.fori_loop(0, chunks, one, jnp.zeros_like(total))
+        stats[:, 2:3] = mean
+        stats[:, 3:4] = lax.rsqrt(jnp.sum(square, axis=1, keepdims=True) * (1.0 / ff) + eps)
+        total[...] = jnp.zeros_like(total)
+        total_u[...] = jnp.zeros_like(total_u)
+
+    here = pl.ds(pl.multiple_of(c * fc, fc), fc)
+
+    @pl.when((step >= chunks) & (step < 2 * chunks))
+    def _():
+        u = (act[c] - stats[:, 2:3]) * stats[:, 3:4]
+        act[c] = u
+        gain = vec4[1:2, :]
+        m = (u * gain + vec4[2:3, :]).astype(bf16)
+        mid_out[...] = m
+        acc[...] += mm(m, w2s[c])
+        gm = back[c].astype(f32)
+        gmu = gm * u
+        sums4[1:2, here] = row_sum(gmu)
+        sums4[2:3, here] = row_sum(gm)
+        total[...] += fold(gm * gain)
+        total_u[...] += fold(gmu * gain)
+
+    @pl.when(step == 2 * chunks)
+    def _():
+        stats[:, 4:5] = jnp.sum(total[...], axis=1, keepdims=True) * (1.0 / ff)
+        stats[:, 5:6] = jnp.sum(total_u[...], axis=1, keepdims=True) * (1.0 / ff)
+        output[...] = acc[...].astype(output.dtype)
+        acc[...] = jnp.zeros_like(acc)
+
+    @pl.when(step >= 2 * chunks)
+    def _():
+        e = back[c].astype(f32) * vec4[1:2, :]
+        grad_act = stats[:, 3:4] * (e - stats[:, 4:5] - act[c] * stats[:, 5:6])
+        gh = (grad_act * slope[c].astype(f32)).astype(bf16)
+        grad_hidden[...] = gh
+        sums4[0:1, here] = row_sum(gh.astype(f32))
+        acc[...] += mm(gh, w1s[c], NT)
+
+    @pl.when(step == 3 * chunks - 1)
+    def _():
+        def one(t, _):
+            r = rows(t)
+            grad_ffn_in = acc[r, :]
+            unit_two = unit_b[r, :]
+            unit_attn = grad_middle[r, :]
+            gout = cot[r, :].astype(f32)
+            sums[5:6, :] += row_sum(gout)
+            sums[3:4, :] += row_sum(grad_ffn_in * unit_two)
+            sums[4:5, :] += row_sum(grad_ffn_in)
+            gmid = gout + norm_back(grad_ffn_in, unit_two, stats[r, 1:2], v(3))
+            grad_middle[r, :] = gmid
+            sums[1:2, :] += row_sum(gmid * unit_attn)
+            sums[2:3, :] += row_sum(gmid)
+            gp = norm_back(gmid, unit_attn, stats[r, 0:1], v(1)).astype(bf16)
+            grad_proj[r, :] = gp
+            sums[0:1, :] += row_sum(gp.astype(f32))
+            return 0
+
+        lax.fori_loop(0, strips, one, 0)
+        d_out[...] = (mm(grad_proj[...], out_w[...], NT) * v(6)).astype(bf16)
+
+
+def middle_pass(at, ho, tok, cot, out_w, w1, w2, vec, vec4, slot, last_part, earlier=(), fc=1024):
+    _, n, d = ho.shape
     ff = w1.shape[1]
-    rows = pl.BlockSpec((tb, d), lambda i: (i, 0))
-    wide = pl.BlockSpec((tb, ff), lambda i: (i, 0))
-    split = pl.BlockSpec((2, tb, d // 2), lambda i: (0, i, 0))
+    chunks = ff // fc
+    last = chunks - 1
+    rows = whole((n, d))
+    held = pl.BlockSpec(memory_space=pl.ANY)
+
+    def once(shape, index):
+        return pl.BlockSpec(shape, index, pipeline_mode=pl.Buffered(1))
+
+    in_place = once((1, n, d), lambda t, at: (at[0], 0, 0))
+    in_slot = once((1, n, d), lambda t, at: (slot, 0, 0))
+    split = once((2, n, d // 2), lambda t, at: (0, slot, 0))
+    kind = f32 if last_part else bf16
     return pl.pallas_call(
         middle_body,
         name="middle_pass",
-        grid=(n // tb,),
-        in_specs=[rows, rows, rows] + [whole(a.shape) for a in (out_w, w1, w2, vec, vec4)],
-        out_specs=[rows, rows, split, split, wide, wide, rows, rows, whole((8, d)), whole((8, ff))],
+        grid_spec=pltpu.PrefetchScalarGridSpec(
+            num_scalar_prefetch=1,
+            grid=(3 * chunks,),
+            in_specs=[
+                in_slot,
+                in_place,
+                in_place,
+                whole(out_w.shape),
+                held,
+                held,
+                whole(vec.shape),
+                pl.BlockSpec((vec4.shape[0], fc), lambda t, at: (0, t % chunks)),
+            ]
+            + [held] * len(earlier),
+            out_specs=[
+                in_place if last_part else rows,
+                rows,
+                whole((8, d)),
+                whole((8, ff)),
+                split,
+                split,
+                pl.BlockSpec((n, fc), lambda t, at: (slot, jnp.clip(t - chunks, 0, last))),
+                pl.BlockSpec((n, fc), lambda t, at: (slot, jnp.clip(t - 2 * chunks, 0, last))),
+                once((n, d), lambda t, at: (slot, 0)),
+                in_slot,
+            ],
+            scratch_shapes=[
+                pltpu.VMEM((chunks, n, fc), f32),
+                pltpu.VMEM((chunks, n, fc), bf16),
+                pltpu.VMEM((chunks, n, fc), bf16),
+                pltpu.VMEM((n, d), f32),
+                pltpu.VMEM((n, d), f32),
+                pltpu.VMEM((n, LANES), f32),
+                pltpu.VMEM((n, LANES), f32),
+                pltpu.VMEM((n, LANES), f32),
+                pltpu.VMEM((chunks, d, fc), bf16),
+                pltpu.VMEM((chunks, fc, d), bf16),
+                pltpu.SemaphoreType.DMA((2, chunks)),
+            ],
+        ),
         out_shape=[
+            jax.ShapeDtypeStruct((2, n, d) if last_part else (n, d), kind),
             jax.ShapeDtypeStruct((n, d), f32),
-            jax.ShapeDtypeStruct((n, d), f32),
-            jax.ShapeDtypeStruct((2, n, d // 2), bf16),
-            jax.ShapeDtypeStruct((2, n, d // 2), bf16),
-            jax.ShapeDtypeStruct((n, ff), bf16),
-            jax.ShapeDtypeStruct((n, ff), bf16),
-            jax.ShapeDtypeStruct((n, d), bf16),
-            jax.ShapeDtypeStruct((n, d), bf16),
             jax.ShapeDtypeStruct((8, d), f32),
             jax.ShapeDtypeStruct((8, ff), f32),
+            jax.ShapeDtypeStruct((2, 2 * n, d // 2), bf16),
+            jax.ShapeDtypeStruct((2, 2 * n, d // 2), bf16),
+            jax.ShapeDtypeStruct((2 * n, ff), bf16),
+            jax.ShapeDtypeStruct((2 * n, ff), bf16),
+            jax.ShapeDtypeStruct((2 * n, d), bf16),
+            jax.ShapeDtypeStruct((2, n, d), bf16),
         ],
-        scratch_shapes=[pltpu.VMEM((tb, ff), f32)] * 3,
-        compiler_params=params(),
+        input_output_aliases={9 + k: 4 + k for k in range(len(earlier))},
+        compiler_params=params(62),
         cost_estimate=pl.CostEstimate(
             flops=8 * n * d * ff + 4 * n * d * d,
             bytes_accessed=4 * d * ff + 2 * d * d + 4 * n * ff + 20 * n * d,
             transcendentals=2 * n * ff,
         ),
-    )(ho, tok, cot, out_w, w1, w2, vec, vec4)
-
-
-def first_back_body(even, odd, w, tok, grad_middle, gain, tokens_grad, sums):
+    )(at, ho, tok, cot, out_w, w1, w2, vec, vec4, *earlier)
+
+
+def first_back_body(at, even, odd, w, tok, grad_middle, gain, tokens_grad, sums):
     @pl.when(pl.program_id(0) == 0)
     def _():
         sums[...] = jnp.zeros_like(sums)
@@ -464,45 +600,58 @@
             if part != 1:
                 at = 2 + part // 2
                 sums[at : at + 1, here : here + run] += row_sum(piece.astype(f32))
-    unit, inverse = norm_unit(tok[...].astype(f32))
+    unit, inverse = norm_unit(tok[0].astype(f32))
     sums[0:1, :] += row_sum(grad * unit)
     sums[1:2, :] += row_sum(grad)
     whole_grad = grad_middle[...] + norm_back(grad, unit, inverse, gain[...])
-    tokens_grad[...] = whole_grad.astype(tokens_grad.dtype)
-
-
-def first_back(even, odd, w, tok, grad_middle, gain, slot, kind, tb=256):
+    if len(tokens_grad.shape) == 3:
+        tokens_grad[0] = whole_grad
+    else:
+        tokens_grad[...] = whole_grad.astype(tokens_grad.dtype)
+
+
+def first_back(at, even, odd, w, tok, grad_middle, gain, slot, last_part, tb=256):
     d = w.shape[0]
     n = even.shape[1] // 2
     first = slot * (n // tb)
-    rows = pl.BlockSpec((tb, d), lambda i: (first + i, 0))
-    half = pl.BlockSpec((3, tb, d // 2), lambda i: (0, first + i, 0))
+    half = pl.BlockSpec((3, tb, d // 2), lambda i, at: (0, first + i, 0))
+    rows = pl.BlockSpec((tb, d), lambda i, at: (i, 0))
+    in_place = pl.BlockSpec((1, tb, d), lambda i, at: (at[0], i, 0))
     return pl.pallas_call(
         first_back_body,
         name="first_back",
-        grid=(n // tb,),
-        in_specs=[half, half, whole(w.shape), rows, rows, whole(gain.shape)],
-        out_specs=[pl.BlockSpec((tb, d), lambda i: (i, 0)), whole((8, d))],
-        out_shape=[jax.ShapeDtypeStruct((n, d), kind), jax.ShapeDtypeStruct((8, d), f32)],
+        grid_spec=pltpu.PrefetchScalarGridSpec(
+            num_scalar_prefetch=1,
+            grid=(n // tb,),
+            in_specs=[half, half, whole(w.shape), in_place, rows, whole(gain.shape)],
+            out_specs=[in_place if last_part else rows, whole((8, d))],
+        ),
+        out_shape=[
+            jax.ShapeDtypeStruct((2, n, d), f32) if last_part else jax.ShapeDtypeStruct((n, d), bf16),
+            jax.ShapeDtypeStruct((8, d), f32),
+        ],
         compiler_params=params(),
         cost_estimate=pl.CostEstimate(
             flops=6 * n * d * d, bytes_accessed=6 * d * d + 16 * n * d, transcendentals=n
         ),
-    )(even, odd, w, tok, grad_middle, gain)
+    )(at, even, odd, w, tok, grad_middle, gain)
 
 
 def after(x, *others):
     return lax.optimization_barrier((x,) + others)[0]
 
 
-def weight_grad_body(a_lead, b_lead, tab, a, b, *refs):
-    lhs = a[0] if a_lead else a[...]
-    rhs = b[0] if b_lead else b[...]
-    total = mm(lhs, rhs, TN)
-    if len(refs) == 1:
-        refs[0][0] = total.astype(bf16)
+def weight_grad_body(a_count, b_count, halves, received_too, tab, *refs):
+    def joined(parts, axis=1):
+        parts = [x[0] if len(x.shape) == 3 else x[...] for x in parts]
+        return parts[0] if len(parts) == 1 else jnp.concatenate(parts, axis=axis)
+
+    rhs = joined(refs[a_count : a_count + b_count], 0 if halves else 1)
+    total = mm(joined(refs[:a_count]), rhs, TN)
+    if not received_too:
+        refs[-1][0] = total.astype(bf16)
         return
-    received, send, keep = refs
+    received, send, keep = refs[-3:]
     total = (total + received[0].astype(f32)).astype(bf16)
 
     @pl.when(pl.program_id(0) == 0)
@@ -514,18 +663,15 @@
         keep[...] = total
 
 
-def weight_grad(tab, a, b, a_block, b_block, out_block, shape, steps, received=None):
+def weight_grad(tab, a, b, a_blocks, b_blocks, out_block, shape, steps, received=None):
     flops = 2 * a.shape[-2] * 2 * shape[0] * shape[1]
     out_index = out_block[1]
-    moved = 2 * (a.size + b.size) + 4 * shape[0] * shape[1]
-    common = dict(
-        name="weight_grad",
-        compiler_params=params(),
-        cost_estimate=pl.CostEstimate(flops=flops, bytes_accessed=moved, transcendentals=0),
-    )
+    halves = isinstance(b, tuple)
+    bs = b if halves else (b,) * len(b_blocks)
+    moved = 2 * (a.size + bs[0].size) + 4 * shape[0] * shape[1]
     part = pl.BlockSpec((1,) + out_block[0], lambda s, i, t: (s,) + out_index(i))
-    in_specs = [pl.BlockSpec(*a_block), pl.BlockSpec(*b_block)]
-    args = [tab, a, b]
+    in_specs = [pl.BlockSpec(*spec) for spec in (*a_blocks, *b_blocks)]
+    args = [tab] + [a] * len(a_blocks) + list(bs)
     if received is None:
         out_specs = part
         out_shape = jax.ShapeDtypeStruct((2,) + shape, bf16)
@@ -539,13 +685,73 @@
         ]
         out_shape = [jax.ShapeDtypeStruct(shape, bf16)] * 2
     return pl.pallas_call(
-        partial(weight_grad_body, len(a_block[0]) == 3, len(b_block[0]) == 3),
+        partial(weight_grad_body, len(a_blocks), len(b_blocks), halves, received is not None),
+        name="weight_grad",
         grid_spec=pltpu.PrefetchScalarGridSpec(
             num_scalar_prefetch=1, grid=(2, steps), in_specs=in_specs, out_specs=out_specs
         ),
         out_shape=out_shape,
-        **common,
+        compiler_params=params(),
+        cost_estimate=pl.CostEstimate(flops=flops, bytes_accessed=moved, transcendentals=0),
     )(*args)
+
+
+def part_of(s, t, at):
+    return jnp.where(s == 0, 1 - t[at], t[at])
+
+
+def tall_how(n, d, ff):
+    tall = ff // 16
+
+    def run(k):
+        return ((n, tall), lambda s, i, t: (0, ((2 * i + k) * 2 + part_of(s, t, 1)) * 2 + t[0]))
+
+    return (
+        [run(0), run(1)],
+        [
+            ((1, n // 2, d), lambda s, i, t: (t[2], 0, 0)),
+            ((1, n // 2, d), lambda s, i, t: (0, 0, 0)),
+        ],
+        ((2 * tall, d), lambda i: (i, 0)),
+        (4 * tall, d),
+        2,
+    )
+
+
+def flat_how(n, d, width):
+    tn = d // 2
+    count = 2 if width > 2 * d else 1
+    steps = width // (2 * tn * count)
+
+    def columns(k):
+        return ((n, tn), lambda s, i, t: (0, (part_of(s, t, 2) * steps + i) * count + k))
+
+    return (
+        [((1, n, d // 2), lambda s, i, t: (t[0], 0, 0))],
+        [columns(k) for k in range(count)],
+        ((d // 2, tn * count), lambda i: (0, i)),
+        (d // 2, steps * tn * count),
+        steps,
+    )
+
+
+def qkv_how(n, d):
+    run = d // 4
+
+    def columns(k):
+        def index(s, i, t):
+            at = part_of(s, t, 2) * 3 + k
+            return at // 2, 0, at % 2
+
+        return ((1, n, run), index)
+
+    return (
+        [((1, n, d // 2), lambda s, i, t: (t[0], 0, 0))],
+        [columns(k) for k in range(3)],
+        ((d // 2, 3 * run), lambda i: (0, 0)),
+        (d // 2, 3 * run),
+        1,
+    )
 
 
 def running_sums(lengths):
@@ -904,90 +1110,53 @@
     head_dim = d // heads
     scale = head_dim**-0.5
     n = 2 * half_len
-    b = lax.axis_index("blk")
-
-    def split(x):
-        return (
-            lax.dynamic_index_in_dim(x, b, 0, keepdims=False),
-            lax.dynamic_index_in_dim(x, 1 - b, 0, keepdims=False),
-        )
-
-    def assemble(kept, sent):
-        back = exchange(sent).astype(f32)
-        return jnp.where(b == 0, jnp.stack([kept, back]), jnp.stack([back, kept]))
-
-    tok_own, tok_other = split(tokens)
-    cot_own, cot_other = split(cotangent)
-    tok_in = exchange(tok_other)
-    cot_in = exchange(cot_other)
+    b = lax.axis_index("blk").astype(jnp.int32)
+    dp = lax.axis_index("dp").astype(jnp.int32)
+    core, x, z, y = dp % 2, (dp // 2) % 2, dp // 4, b
+
+    tok_in = exchange(lax.dynamic_slice_in_dim(tokens, 1 - b, 1, 0))
+    cot_in = exchange(lax.dynamic_slice_in_dim(cotangent, 1 - b, 1, 0))
+    kept_at = b[None]
+    sent_at = jnp.zeros((1,), jnp.int32)
 
     lengths = lax.dynamic_slice_in_dim(doc_lengths, b, 1, 0)
     ends = running_sums(lengths)[0]
     firsts = (half_len // 2) * jnp.arange(4, dtype=jnp.int32)
     starts = jnp.max(jnp.where(ends[None, :] <= firsts[:, None], ends[None, :], 0), axis=1)
     allowed = (firsts[None, :] >= starts[:, None]).astype(jnp.int32)
-    tab = jnp.concatenate([b.astype(jnp.int32)[None], allowed.reshape(16)])
-
-    def line(x):
-        return x.reshape(1, -1)
+    tab = jnp.concatenate([b[None], allowed.reshape(16)])
+    theirs = jnp.stack([1 - core, x, y])
+    mine = jnp.stack([core, x, y])
+
+    def line(v):
+        return v.reshape(1, -1)
 
     scale_row = jnp.broadcast_to(head_scales[:, None], (heads, head_dim)).reshape(1, d)
     vec = jnp.stack(
         [out_bias, attn_gain, attn_shift, norm2_gain, norm2_shift, fc2_bias, scale_row[0], out_bias]
     )
     vec4 = jnp.stack([fc1_bias, mid_gain, mid_shift, fc1_bias])
-
-    first_args = (line(norm1_gain), line(norm1_shift), qkv_weight, line(query_bias), line(value_bias))
-    early = project_qkv(tok_own, *first_args, scale, 0, n)
-    attn_in, qkv = project_qkv(tok_in, *first_args, scale, 1, n, early)
+    qkv_bias = jnp.concatenate([query_bias, jnp.zeros_like(query_bias), value_bias])
+
+    first_args = (line(norm1_gain), line(norm1_shift), qkv_weight, line(qkv_bias), scale)
+    early = project_qkv(kept_at, tokens, *first_args, 0, n)
+    attn_in, qkv = project_qkv(sent_at, tok_in, *first_args, 1, n, early)
     qkv = qkv.reshape(2, half_len, 3 * d)
-    tok = jnp.concatenate([tok_own, tok_in])
-    cot = jnp.concatenate([cot_own, cot_in])
     heads_out, logs = attend(tab, qkv, scale_row)
-    output, grad_middle, ffn_in, heads_in, mid_out, grad_hidden, grad_proj, d_out, sums, sums4 = middle_pass(
-        heads_out.reshape(n, d), tok, cot, out_weight, fc1_weight, fc2_weight, vec, vec4
-    )
-    output = assemble(output[:half_len], output[half_len:].astype(bf16))
-    dp = lax.axis_index("dp").astype(jnp.int32)
-    core, x, y = dp % 2, (dp // 2) % 2, b.astype(jnp.int32)
-    z = dp // 4
-    theirs = jnp.stack([1 - core, x, y])
-    mine = jnp.stack([core, x, y])
-
-    def part_of(s, t, at):
-        return jnp.where(s == 0, 1 - t[at], t[at])
-
-    tall = ff // 16
-    tall_how = (
-        ((n, tall), lambda s, i, t: (0, (i * 2 + part_of(s, t, 1)) * 2 + t[0])),
-        ((n, d), lambda s, i, t: (0, 0)),
-        ((tall, d), lambda i: (i, 0)),
-        (4 * tall, d),
-        4,
-    )
-
-    def flat_how(width):
-        tn = d // 2
-        steps = width // (2 * tn)
-        return (
-            ((1, n, d // 2), lambda s, i, t: (t[0], 0, 0)),
-            ((n, tn), lambda s, i, t: (0, part_of(s, t, 2) * steps + i)),
-            ((d // 2, tn), lambda i: (0, i)),
-            (d // 2, steps * tn),
-            steps,
-        )
-
-    run = d // 4
-    qkv_how = (
-        ((1, n, d // 2), lambda s, i, t: (t[0], 0, 0)),
-        (
-            (1, n, run),
-            lambda s, i, t: ((part_of(s, t, 2) * 3 + i) // 2, 0, (part_of(s, t, 2) * 3 + i) % 2),
-        ),
-        ((d // 2, run), lambda i: (0, i)),
-        (d // 2, 3 * run),
-        3,
-    )
+
+    weights = (out_weight, fc1_weight, fc2_weight, vec, vec4)
+    out_sent, mid_sent, *more = middle_pass(sent_at, heads_out, tok_in, cot_in, *weights, 1, False)
+    sums, sums4, *earlier = more
+    out_back = exchange(out_sent)
+    output, mid_kept, *more = middle_pass(
+        kept_at, heads_out, tokens, cotangent, *weights, 0, True, earlier
+    )
+    sums = sums + more[0]
+    sums4 = sums4 + more[1]
+    ffn_in, heads_in, mid_out, grad_hidden, grad_proj, d_out = more[2:]
+
+    def fill(kept, back):
+        return lax.dynamic_update_slice_in_dim(kept, back.astype(f32)[None], 1 - b, 0)
 
     def z_stage(parts):
         total = lax.dynamic_index_in_dim(parts, z, 0, keepdims=False).astype(f32)
@@ -995,81 +1164,95 @@
             total = total + flip(lax.dynamic_index_in_dim(parts, z ^ k, 0, keepdims=False), 4 * k).astype(f32)
         return total
 
-    def along_y(send, keep):
-        total = (keep.astype(f32) + flip(send, 2).astype(f32)).astype(bf16).reshape(4, -1, d)
-        return (
-            lax.dynamic_slice_in_dim(total, (1 - y) * (d // 2), d // 2, 2),
-            lax.dynamic_slice_in_dim(total, y * (d // 2), d // 2, 2),
-        )
-
-    def along_x(send, keep):
-        total = keep.astype(f32) + exchange(send).astype(f32)
-        total = total.astype(bf16).reshape(4, 2, d // 16, -1)
+    def rows_by_x(total):
+        total = total.astype(bf16).reshape(4, 2, -1, total.shape[1])
         return (
             lax.dynamic_index_in_dim(total, 1 - x, 1, keepdims=False),
             lax.dynamic_index_in_dim(total, x, 1, keepdims=False),
         )
 
-    def end_y(send, keep):
-        return z_stage((keep.astype(f32) + exchange(send).astype(f32)).astype(bf16))
-
-    def end_x(send, keep):
-        return z_stage((keep.astype(f32) + flip(send, 2).astype(f32)).astype(bf16))
-
-    flat4, flat1 = flat_how(ff), flat_how(d)
-    fc2_theirs = weight_grad(theirs, mid_out, cot, *tall_how)
+    def columns_by_y(total):
+        total = total.astype(bf16)
+        total = total.reshape(4, -1, total.shape[-1])
+        width = total.shape[2] // 2
+        return (
+            lax.dynamic_slice_in_dim(total, (1 - y) * width, width, 2),
+            lax.dynamic_slice_in_dim(total, y * width, width, 2),
+        )
+
+    def add_x(send, keep):
+        return keep.astype(f32) + flip(send, 2).astype(f32)
+
+    def add_y(send, keep):
+        return keep.astype(f32) + exchange(send).astype(f32)
+
+    tall, flat4, flat1, qkv3 = (
+        tall_how(n, d, ff), flat_how(n, d, ff), flat_how(n, d, d), qkv_how(n, d)
+    )
+    cots = (cotangent, cot_in)
+    fc2_theirs = weight_grad(theirs, mid_out, cots, *tall)
     ffn_in = after(ffn_in, fc2_theirs)
     fc1_theirs = weight_grad(theirs, ffn_in, grad_hidden, *flat4)
-    heads_in = after(heads_in, fc1_theirs)
+    mid_out = after(mid_out, fc1_theirs)
+    fc2_parts = weight_grad(mine, mid_out, cots, *tall, flip(fc2_theirs, 1))
+    heads_in = after(heads_in, *fc2_parts)
     out_theirs = weight_grad(theirs, heads_in, grad_proj, *flat1)
-    mid_out = after(mid_out, out_theirs)
-    fc2_parts = weight_grad(mine, mid_out, cot, *tall_how, flip(fc2_theirs, 1))
-    ffn_in = after(ffn_in, *fc2_parts)
+    ffn_in = after(ffn_in, out_theirs)
     fc1_parts = weight_grad(mine, ffn_in, grad_hidden, *flat4, flip(fc1_theirs, 1))
-    heads_in = after(heads_in, *fc1_parts)
-    out_parts = weight_grad(mine, heads_in, grad_proj, *flat1, flip(out_theirs, 1))
-    d_out = after(d_out, *out_parts).reshape(2, half_len, d)
+
+    sums = jnp.concatenate([sums, sums4.reshape(8 * ff // d, d)[: 3 * ff // d]])
+    steps = (
+        (partial(flip, bit=1), fc2_theirs),
+        (partial(flip, bit=2), fc1_theirs),
+        (exchange, fc2_parts[0]),
+        (partial(flip, bit=4), fc1_parts[0]),
+    )
+    for move, done in steps:
+        sums = after(sums, done) + move(sums)
+
+    d_out = after(d_out, *fc1_parts)
     back_args = (1.0 / scale_row, logs, scale)
     even, dots_even = attend_back(tab, qkv, heads_out, d_out, *back_args, 0)
     even = even.reshape(3, n, d // 2)
-    fc2_parts = along_y(fc2_parts[0], after(fc2_parts[1], even))
-    fc1_parts = along_x(fc1_parts[0], after(fc1_parts[1], even))
-    out_parts = along_x(out_parts[0], after(out_parts[1], even))
-    even_theirs = weight_grad(theirs, attn_in, even, *qkv_how)
-    d_out = after(d_out, even_theirs, *fc2_parts, *fc1_parts, *out_parts)
+    sums = after(sums, even) + flip(sums, 8)
+    output = fill(after(output, even), out_back)
+    out_parts = weight_grad(mine, after(heads_in, even), grad_proj, *flat1, flip(out_theirs, 1))
+    even_theirs = weight_grad(theirs, after(attn_in, *out_parts), even, *qkv3)
+    fc2_parts = columns_by_y(add_x(fc2_parts[0], after(fc2_parts[1], even_theirs)))
+    fc1_parts = rows_by_x(add_y(fc1_parts[0], after(fc1_parts[1], even_theirs)))
+    d_out = after(d_out, even_theirs, *fc2_parts, *fc1_parts)
     odd, dots_odd = attend_back(tab, qkv, heads_out, d_out, *back_args, 1)
     odd = odd.reshape(3, n, d // 2)
-    odd_theirs = weight_grad(theirs, attn_in, odd, *qkv_how)
+    odd_theirs = weight_grad(theirs, attn_in, odd, *qkv3)
     attn_in = after(attn_in, odd_theirs)
-    even_parts = weight_grad(mine, attn_in, even, *qkv_how, flip(even_theirs, 1))
-    first_rest = (odd, qkv_weight, tok, grad_middle, line(norm1_gain))
-    grad_sent, sums_sent = first_back(after(even, *even_parts), *first_rest, 1, bf16)
-    attn_in = after(attn_in, grad_sent)
-    odd_parts = weight_grad(mine, attn_in, odd, *qkv_how, flip(odd_theirs, 1))
-    grad_kept, sums_kept = first_back(after(even, *odd_parts), *first_rest, 0, f32)
-    fc2_weight_grad = end_y(fc2_parts[0], after(fc2_parts[1], odd))
-    fc1_weight_grad = end_x(fc1_parts[0], after(fc1_parts[1], odd))
-    out_weight_grad = end_x(out_parts[0], after(out_parts[1], odd))
-    even_parts = along_x(even_parts[0], after(even_parts[1], grad_kept))
-    odd_parts = along_x(odd_parts[0], after(odd_parts[1], grad_kept))
-    even_grad, odd_grad = end_x(*even_parts), end_x(*odd_parts)
+    even_parts = weight_grad(mine, attn_in, even, *qkv3, flip(even_theirs, 1))
+    grad_sent, sums_sent = first_back(
+        sent_at, after(even, *even_parts), odd, qkv_weight, tok_in, mid_sent, line(norm1_gain), 1, False
+    )
+    grad_back = exchange(grad_sent)
+    odd_parts = weight_grad(mine, after(attn_in, grad_sent), odd, *qkv3, flip(odd_theirs, 1))
+    tokens_grad, sums_kept = first_back(
+        kept_at, after(even, *odd_parts), odd, qkv_weight, tokens, mid_kept, line(norm1_gain), 0, True
+    )
+    fc2_weight_grad = z_stage(add_y(fc2_parts[0], after(fc2_parts[1], grad_sent)).astype(bf16))
+    fc1_weight_grad = z_stage(add_x(fc1_parts[0], after(fc1_parts[1], grad_sent)).astype(bf16))
+    out_parts = rows_by_x(add_y(out_parts[0], after(out_parts[1], odd)))
+    out_weight_grad = z_stage(add_x(out_parts[0], after(out_parts[1], grad_sent)).astype(bf16))
+    even_parts = rows_by_x(add_y(even_parts[0], after(even_parts[1], tokens_grad)))
+    odd_parts = rows_by_x(add_y(odd_parts[0], after(odd_parts[1], tokens_grad)))
+    even_grad, odd_grad = (z_stage(add_x(*parts).astype(bf16)) for parts in (even_parts, odd_parts))
+    run = d // 4
     qkv_weight_grad = jnp.stack(
         [even_grad.reshape(-1, 3, run), odd_grad.reshape(-1, 3, run)], axis=2
     ).reshape(-1, 6 * run)
-    first_sums = sums_sent + sums_kept
-    tokens_grad = assemble(grad_kept, grad_sent)
-    dots = jnp.stack([dots_even.reshape(2, 2, 4, 8, -1), dots_odd.reshape(2, 2, 4, 8, -1)], axis=1)
-    head_scales_grad = jnp.sum(dots[..., :2, :], axis=(3, 5)).reshape(heads) / head_scales
+    tokens_grad = fill(tokens_grad, grad_back)
+    dots = jnp.stack([dots_even[:, 0].reshape(2, 4, head_dim), dots_odd[:, 0].reshape(2, 4, head_dim)], axis=1)
+    head_scales_grad = jnp.sum(dots, axis=3).reshape(heads) / head_scales
     head_scales_grad = jnp.pad(head_scales_grad, (0, d - heads))
-
-    def everywhere(v):
-        for move in (partial(flip, bit=1), partial(flip, bit=2), exchange, partial(flip, bit=4), partial(flip, bit=8)):
-            v = v + move(v)
-        return v
-
-    sums = everywhere(jnp.concatenate([sums.reshape(8, d), sums4.reshape(8 * ff // d, d)[: 3 * ff // d]]))
+    first_sums = jnp.concatenate([(sums_sent + sums_kept)[:4], head_scales_grad[None]])
+    for move in (partial(flip, bit=1), partial(flip, bit=2), exchange, partial(flip, bit=4), partial(flip, bit=8)):
+        first_sums = first_sums + move(first_sums)
     sums4 = sums[8:].reshape(3, ff)
-    first_sums = everywhere(jnp.concatenate([first_sums[:4], head_scales_grad[None]]))
     return (
         output,
         tokens_grad,

time: 557 us -> 462 us (0.83)
  Pallas kernels: 324 us -> 277 us
  waiting for transfers between devices: 124 us -> 78.7 us
  starting transfers between devices: 47.5 us -> 60.9 us
  local copies, waits for them, and re-layouts: 21.5 us -> 14.1 us
  other arithmetic: 30 us -> 22.7 us
    ppermute x11, waiting for transfers between devices: 78.5 us -> 40.8 us  [exchange(): return lax.ppermute(x, 'blk', swap)]
    pallas_call x15 -> x16, Pallas kernels: 235 us -> 213 us  [the longest x2 102 us: middle_pass(): pl.pallas_call(middle_body, name='middle_pass', grid_spec=pltpu.PrefetchS...]
    pallas_call x2, Pallas kernels: 59.3 us -> 39.1 us  [attend_back(): pl.pallas_call(partial(attend_back_body, scale), name='attend_back', grid...]
    ppermute x33, starting transfers between devices: 35.3 us -> 46.3 us  [flip(): return lax.ppermute(x, 'dp', [(i, i ^ bit) for i in range(16)])]
    ppermute x33, waiting for transfers between devices: 45.5 us -> 37.9 us  [flip(): return lax.ppermute(x, 'dp', [(i, i ^ bit) for i in range(16)])]
    squeeze x6 -> x4, local copies, waits for them, and re-layouts: 6.34 us -> 0.35 us  [the longest x2 0.29 us: rows_by_x(): lax.dynamic_index_in_dim(total, x, 1, keepdims=False)]
  transfers between devices with their start and end apart: 44 -> 44, of which waited for: 16 -> 16; matrix products, arithmetic and copies ran while one was open for 8% -> 7% of each run, Pallas kernels for 37% -> 37%
where the time goes in v3:
time: 462 us; the launch traced here: 455 us
  Pallas kernels  277 us (60%)
  waiting for transfers between devices  78.7 us (17%)
  starting transfers between devices  60.9 us (13%)
  other arithmetic  22.7 us (5%)
  local copies, waits for them, and re-layouts  14.1 us (3%)
    pallas_call x2, Pallas kernels, middle_pass(): pl.pallas_call(middle_body, name='middle_pass', grid_spec=pltpu.PrefetchS...  102 us
    pallas_call x10, Pallas kernels, weight_grad(): pl.pallas_call(partial(weight_grad_body, len(a_blocks), len(b_blocks), ha...  74.5 us
    ppermute x33, starting transfers between devices, flip(): return lax.ppermute(x, 'dp', [(i, i ^ bit) for i in range(16)])  46.3 us
    ppermute x11, waiting for transfers between devices, exchange(): return lax.ppermute(x, 'blk', swap)  40.8 us
    pallas_call x2, Pallas kernels, attend_back(): pl.pallas_call(partial(attend_back_body, scale), name='attend_back', grid...  39.1 us
    ppermute x33, waiting for transfers between devices, flip(): return lax.ppermute(x, 'dp', [(i, i ^ bit) for i in range(16)])  37.9 us
    pallas_call x1, Pallas kernels, attend(): pl.pallas_call(attend_body, name='attend', grid_spec=pltpu.PrefetchScalar...  25 us
    pallas_call x2, Pallas kernels, first_back(): pl.pallas_call(first_back_body, name='first_back', grid_spec=pltpu.Prefet...  19 us
  transfers between devices with their start and end apart: 44, of which 16 were waited for; matrix products, arithmetic and copies ran while one was open for 7% of the time, Pallas kernels for 37%

profile of v3, /device:TPU:0, one launch (start us, length us, event | category | flops | bytes accessed | tf_op | source)
XLA Modules:
  0.0 455.2 jit_solution(5982030832319364760)
XLA Ops:
  2.2 3.0 collective-permute-start
  8.8 8.9 %project_qkv.2 = (bf16[2,1024,512]{2,1,0:T(8,128)(2,1)}, bf16[1024,3072]{1,0:T(8,128)(2,1)}) custom-call(s32[1]{0:T(128)} %bitcast.at, bf16[2,512,1024]{2,1,0:T(8,128)(2,1)} %tok.5, f32[1,1024]{1,0:T(1,128)} %bitcast.161, f32[1,1024]{1,0:T(1,128)} %bitcast.171, bf16[1024,3072]{1,0:T(8,128)(2,1)} %w.7, f32[1,3072]{1,0:T(1,128)} %bitcast.157), custom_call_target="tpu_custom_call" | custom-call | flops 3221225472 | bytes 11534336 | tf_op jit(solution)/shard_map/project_qkv/pallas_call | solution.py:100
  18.5 10.7 %collective-permute-done.tok = bf16[1,512,1024]{2,1,0:T(8,128)(2,1)S(1)} collective-permute-done((bf16[1,512,1024]{2,1,0:T(8,128)(2,1)S(1)}, bf16[1,512,1024]{2,1,0:T(8,128)(2,1)S(1)}, u32[]{:S(2)}, u32[]{:S(2)}) %collective-permute-start) | collective-permute-done | bytes 1048608 | tf_op jit(solution)/shard_map/ppermute | solution.py:1077
  30.3 8.9 %project_qkv.3 = (bf16[2,1024,512]{2,1,0:T(8,128)(2,1)}, bf16[1024,3072]{1,0:T(8,128)(2,1)}) custom-call(s32[1]{0:T(128)} %constant.128.clone.1.at, bf16[1,512,1024]{2,1,0:T(8,128)(2,1)} %copy-done.3, f32[1,1024]{1,0:T(1,128)} %bitcast.162, f32[1,1024]{1,0:T(1,128)} %bitcast.172, ...), custom_call_target="tpu_custom_call", output_to_operand_aliasing={{0}: (6, {}), {1}: (7, {})} | custom-call | flops 3221225472 | bytes 11534336 | tf_op jit(solution)/shard_map/project_qkv/pallas_call | solution.py:100
  39.1 25.0 %attend.1 = (bf16[2,512,1024]{2,1,0:T(8,128)(2,1)}, f32[8,4,8,256]{3,2,1,0:T(8,128)}) custom-call(s32[17]{0:T(128)} %pad_add_fusion.tab, bf16[2,512,3072]{2,1,0:T(8,128)(2,1)} %bitcast.143, bf16[2,512,3072]{2,1,0:T(8,128)(2,1)} %bitcast.144, bf16[2,512,3072]{2,1,0:T(8,128)(2,1)} %bitcast.145, f32[1,1024]{1,0:T(1,128)} %copy-done.10), custom_call_target="tpu_custom_call" | custom-call | flops 17179869184 | bytes 12582912 | tf_op jit(solution)/shard_map/attend/pallas_call | solution.py:208
  64.1 50.6 %middle_pass.2 = (bf16[512,1024]{1,0:T(8,128)(2,1)}, f32[512,1024]{1,0:T(8,128)}, f32[8,1024]{1,0:T(8,128)}, f32[8,4096]{1,0:T(8,128)}, bf16[2,1024,512]{2,1,0:T...) custom-call(s32[1]{0:T(128)} %constant.128.clone.1.at, ...), custom_call_target="tpu_custom_call" | custom-call | flops 19327352832 | bytes 37748736 | tf_op jit(solution)/shard_map/middle_pass/pallas_call | solution.py:521
  114.7 51.1 %middle_pass.3 = (f32[2,512,1024]{2,1,0:T(8,128)}, f32[512,1024]{1,0:T(8,128)}, f32[8,1024]{1,0:T(8,128)}, f32[8,4096]{1,0:T(8,128)}, bf16[2,1024,512]{2,1,0:T(8...) custom-call(s32[1]{0:T(128)} %bitcast.at, ...), custom_call_target="tpu_custom_call", output_to_operand_aliasing={{4}: (9, {}), {5}: (10, {}), {6}: (11, {}), {7}: (12, {}), ... | custom-call | flops 19327352832 | bytes 37748736 | tf_op jit(solution)/shard_map/middle_pass/pallas_call | solution.py:521
  165.9 9.1 %weight_grad.10 = bf16[2,1024,1024]{2,1,0:T(8,128)(2,1)} custom-call(s32[3]{0:T(128)} %add_add_fusion.1.tab, bf16[1024,4096]{1,0:T(8,128)(2,1)} %get-tuple-element.107.refs_0_.refs_1_, bf16[1024,4096]{1,0:T(8,128)(2,1)} %get-tuple-element.107.refs_0_.refs_1_, bf16[2,512,1024]{2,1,0:T(8,128)(2,1)} %refs_2_.3, ...), custom_call_target="tpu_custom_call" | custom-call | flops 4294967296 | bytes 14680064 | tf_op jit(solution)/shard_map/weight_grad/pallas_call | solution.py:687
  175.0 9.8 %weight_grad.11 = bf16[2,512,2048]{2,1,0:T(8,128)(2,1)} custom-call(s32[3]{0:T(128)} %add_add_fusion.1.tab, bf16[2,1024,512]{2,1,0:T(8,128)(2,1)} %get-tuple-element.112.refs_0_, bf16[1024,4096]{1,0:T(8,128)(2,1)} %get-tuple-element.106.refs_1_.refs_2_, bf16[1024,4096]{1,0:T(8,128)(2,1)} %get-tuple-element.106.refs_1_.refs_2_), custom_call_target="tpu_custom_call" | custom-call | flops 4294967296 | bytes 14680064 | tf_op jit(solution)/shard_map/weight_grad/pallas_call | solution.py:687
  186.2 6.0 %collective-permute-done.31 = f32[20,1024]{1,0:T(8,128)S(1)} collective-permute-done((f32[20,1024]{1,0:T(8,128)S(1)}, f32[20,1024]{1,0:T(8,128)S(1)}, u32[]{:S(2)}, u32[]{:S(2)}) %collective-permute-start.31) | collective-permute-done | bytes 81952 | tf_op jit(solution)/shard_map/ppermute | solution.py:1081
  199.2 10.6 %weight_grad.12 = (bf16[1024,1024]{1,0:T(8,128)(2,1)}, bf16[1024,1024]{1,0:T(8,128)(2,1)}) custom-call(s32[3]{0:T(128)} %add_add_fusion.tab, bf16[1024,4096]{1,0:T(8,128)(2,1)} %get-tuple-element.107.refs_0_.refs_1_, bf16[1024,4096]{1,0:T(8,128)(2,1)} %get-tuple-element.107.refs_0_.refs_1_, bf16[2,512,1024]{2,1,0:T(8,128)(2,1)} %refs_2_.3, ...), custom_call_target="tpu_custom_call" | custom-call | flops 4294967296 | bytes 14680064 | tf_op jit(solution)/shard_map/weight_grad/pallas_call | solution.py:687
  209.9 4.5 weight_grad.13
  215.9 11.1 %weight_grad.14 = (bf16[512,2048]{1,0:T(8,128)(2,1)}, bf16[512,2048]{1,0:T(8,128)(2,1)}) custom-call(s32[3]{0:T(128)} %add_add_fusion.tab, bf16[2,1024,512]{2,1,0:T(8,128)(2,1)} %get-tuple-element.112.refs_0_, bf16[1024,4096]{1,0:T(8,128)(2,1)} %get-tuple-element.106.refs_1_.refs_2_, bf16[1024,4096]{1,0:T(8,128)(2,1)} %get-tuple-element.106.refs_1_.refs_2_, ...), custom_call_target="tpu_custom_call" | custom-call | flops 4294967296 | bytes 14680064 | tf_op jit(solution)/shard_map/weight_grad/pallas_call | solution.py:687
  229.2 19.5 %attend_back.2 = (bf16[3,2,512,512]{3,2,1,0:T(8,128)(2,1)}, f32[4,8,128]{2,1,0:T(8,128)}) custom-call(s32[17]{0:T(128)} %pad_add_fusion.tab, bf16[2,512,3072]{2,1,0:T(8,128)(2,1)} %bitcast.146, bf16[2,512,3072]{2,1,0:T(8,128)(2,1)} %bitcast.147, bf16[2,512,3072]{2,1,0:T(8,128)(2,1)} %bitcast.148, bf16[2,512,1024]{2,1,0:T(8,128)(2,1)} %get-tuple-element.93.ho.heads_out, ...), custom_call_target="tpu_custom_call" | custom-call | flops 21474836480 | bytes 12582912 | tf_op jit(solution)/shard_map/attend_back/pallas_call | solution.py:312
  253.8 3.8 collective-permute-done.35
  259.3 5.0 %weight_grad.15 = (bf16[512,512]{1,0:T(8,128)(2,1)}, bf16[512,512]{1,0:T(8,128)(2,1)}) custom-call(s32[3]{0:T(128)} %add_add_fusion.tab, bf16[2,1024,512]{2,1,0:T(8,128)(2,1)} %get-tuple-element.121.refs_0_, bf16[1024,1024]{1,0:T(8,128)(2,1)} %get-tuple-element.111.refs_1_, bf16[2,512,512]{2,1,0:T(8,128)(2,1)} %copy-done.6), custom_call_target="tpu_custom_call" | custom-call | flops 1073741824 | bytes 5242880 | tf_op jit(solution)/shard_map/weight_grad/pallas_call | solution.py:687
  264.3 6.0 %weight_grad.16 = bf16[2,512,768]{2,1,0:T(8,128)(2,1)} custom-call(s32[3]{0:T(128)} %add_add_fusion.1.tab, bf16[2,1024,512]{2,1,0:T(8,128)(2,1)} %get-tuple-element.135.refs_0_, bf16[3,1024,512]{2,1,0:T(8,128)(2,1)} %bitcast.125, bf16[3,1024,512]{2,1,0:T(8,128)(2,1)} %bitcast.126, bf16[3,1024,512]{2,1,0:T(8,128)(2,1)} %bitcast.127), custom_call_target="tpu_custom_call" | custom-call | flops 1610612736 | bytes 6815744 | tf_op jit(solution)/shard_map/weight_grad/pallas_call | solution.py:687
  271.9 3.9 collective-permute-done.7
  283.5 19.5 %attend_back.3 = (bf16[3,2,512,512]{3,2,1,0:T(8,128)(2,1)}, f32[4,8,128]{2,1,0:T(8,128)}) custom-call(s32[17]{0:T(128)} %pad_add_fusion.tab, bf16[2,512,3072]{2,1,0:T(8,128)(2,1)} %bitcast.149, bf16[2,512,3072]{2,1,0:T(8,128)(2,1)} %bitcast.150, bf16[2,512,3072]{2,1,0:T(8,128)(2,1)} %bitcast.151, bf16[2,512,1024]{2,1,0:T(8,128)(2,1)} %get-tuple-element.93.ho.heads_out, ...), custom_call_target="tpu_custom_call" | custom-call | flops 21474836480 | bytes 12582912 | tf_op jit(solution)/shard_map/attend_back/pallas_call | solution.py:312
  303.1 5.8 %weight_grad.17 = bf16[2,512,768]{2,1,0:T(8,128)(2,1)} custom-call(s32[3]{0:T(128)} %add_add_fusion.1.tab, bf16[2,1024,512]{2,1,0:T(8,128)(2,1)} %get-tuple-element.135.refs_0_, bf16[3,1024,512]{2,1,0:T(8,128)(2,1)} %bitcast.133, bf16[3,1024,512]{2,1,0:T(8,128)(2,1)} %bitcast.134, bf16[3,1024,512]{2,1,0:T(8,128)(2,1)} %bitcast.135), custom_call_target="tpu_custom_call" | custom-call | flops 1610612736 | bytes 6815744 | tf_op jit(solution)/shard_map/weight_grad/pallas_call | solution.py:687
  311.0 6.3 %weight_grad.18 = (bf16[512,768]{1,0:T(8,128)(2,1)}, bf16[512,768]{1,0:T(8,128)(2,1)}) custom-call(s32[3]{0:T(128)} %add_add_fusion.tab, bf16[2,1024,512]{2,1,0:T(8,128)(2,1)} %get-tuple-element.135.refs_0_, bf16[3,1024,512]{2,1,0:T(8,128)(2,1)} %bitcast.128, bf16[3,1024,512]{2,1,0:T(8,128)(2,1)} %bitcast.129, bf16[3,1024,512]{2,1,0:T(8,128)(2,1)} %bitcast.130, ...), custom_call_target="tpu_custom_call" | custom-call | flops 1610612736 | bytes 6815744 | tf_op jit(solution)/shard_map/weight_grad/pallas_call | solution.py:687
  317.3 9.5 %first_back.2 = (bf16[512,1024]{1,0:T(8,128)(2,1)}, f32[8,1024]{1,0:T(8,128)}) custom-call(s32[1]{0:T(128)} %constant.128.clone.1.at, bf16[3,1024,512]{2,1,0:T(8,128)(2,1)} %bitcast.131, bf16[3,1024,512]{2,1,0:T(8,128)(2,1)} %bitcast.136, bf16[1024,3072]{1,0:T(8,128)(2,1)} %w.7, bf16[1,512,1024]{2,1,0:T(8,128)(2,1)} %copy-done.3, ...), custom_call_target="tpu_custom_call" | custom-call | flops 3221225472 | bytes 14680064 | tf_op jit(solution)/shard_map/first_back/pallas_call | solution.py:620
  343.7 3.3 collective-permute-start.38
  347.0 9.7 %collective-permute-done.40 = bf16[4,256,512]{2,1,0:T(8,128)(2,1)} collective-permute-done((bf16[4,256,512]{2,1,0:T(8,128)(2,1)}, bf16[4,256,512]{2,1,0:T(8,128)(2,1)}, u32[]{:S(2)}, u32[]{:S(2)}) %collective-permute-start.40) | collective-permute-done | bytes 1048608 | tf_op jit(solution)/shard_map/ppermute | solution.py:1077
  360.8 6.3 %weight_grad.19 = (bf16[512,768]{1,0:T(8,128)(2,1)}, bf16[512,768]{1,0:T(8,128)(2,1)}) custom-call(s32[3]{0:T(128)} %add_add_fusion.tab, bf16[2,1024,512]{2,1,0:T(8,128)(2,1)} %get-tuple-element.135.refs_0_, bf16[3,1024,512]{2,1,0:T(8,128)(2,1)} %bitcast.137, bf16[3,1024,512]{2,1,0:T(8,128)(2,1)} %bitcast.138, bf16[3,1024,512]{2,1,0:T(8,128)(2,1)} %bitcast.139, ...), custom_call_target="tpu_custom_call" | custom-call | flops 1610612736 | bytes 6815744 | tf_op jit(solution)/shard_map/weight_grad/pallas_call | solution.py:687
  367.1 9.5 %first_back.3 = (f32[2,512,1024]{2,1,0:T(8,128)}, f32[8,1024]{1,0:T(8,128)}) custom-call(s32[1]{0:T(128)} %bitcast.at, bf16[3,1024,512]{2,1,0:T(8,128)(2,1)} %bitcast.132, bf16[3,1024,512]{2,1,0:T(8,128)(2,1)} %bitcast.140, bf16[1024,3072]{1,0:T(8,128)(2,1)} %w.7, bf16[2,512,1024]{2,1,0:T(8,128)(2,1)} %tok.5, f32[512,1024]{1,0:T(8,128)} %get-tuple-element.139.grad_middle, ...), custom_call_target="tpu_custom_call" | custom-call | flops 3221225472 | bytes 14680064 | tf_op jit(solution)/shard_map/first_back/pallas_call | solution.py:620
  384.5 5.9 %collective-permute-done.41 = bf16[256,512]{1,0:T(8,128)(2,1)S(1)} collective-permute-done((bf16[256,512]{1,0:T(8,128)(2,1)S(1)}, bf16[256,512]{1,0:T(8,128)(2,1)S(1)}, u32[]{:S(2)}, u32[]{:S(2)}) %collective-permute-start.41) | collective-permute-done | bytes 262176 | tf_op jit(solution)/shard_map/ppermute | solution.py:1081
  391.7 8.4 %collective-permute-done.42 = bf16[256,512]{1,0:T(8,128)(2,1)S(1)} collective-permute-done((bf16[256,512]{1,0:T(8,128)(2,1)S(1)}, bf16[256,512]{1,0:T(8,128)(2,1)S(1)}, u32[]{:S(2)}, u32[]{:S(2)}) %collective-permute-start.42) | collective-permute-done | bytes 262176 | tf_op jit(solution)/shard_map/ppermute | solution.py:1081
  404.4 16.5 %collective-permute-done.13 = f32[5,1024]{1,0:T(8,128)S(1)} collective-permute-done((f32[5,1024]{1,0:T(8,128)S(1)}, f32[5,1024]{1,0:T(8,128)S(1)}, u32[]{:S(2)}, u32[]{:S(2)}) %collective-permute-start.13) | collective-permute-done | bytes 20512 | tf_op jit(solution)/shard_map/ppermute | solution.py:1077
  420.9 4.6 %collective-permute-start.14 = (f32[5,1024]{1,0:T(8,128)S(1)}, f32[5,1024]{1,0:T(8,128)S(1)}, u32[]{:S(2)}, u32[]{:S(2)}) collective-permute-start(f32[5,1024]{1,0:T(8,128)S(1)} %add.202), channel_id=1, source_target_pairs={{0,8},{2,10},{4,12},{6,14},{8,0},{10,2},{12,4},{14,6},{16,24},{18,... | collective-permute-start | bytes 61448 | tf_op jit(solution)/shard_map/ppermute | solution.py:1081
  438.8 2.9 collective-permute-start.20
  449.7 3.4 collective-permute-done.24
  (224 shorter events, 94.4 us)
Async XLA Ops:
  2.2 27.0 %collective-permute-start = (bf16[1,512,1024]{2,1,0:T(8,128)(2,1)S(1)}, bf16[1,512,1024]{2,1,0:T(8,128)(2,1)S(1)}, u32[]{:S(2)}, u32[]{:S(2)}) collective-permute-start(bf16[1,512,1024]{2,1,0:T(8,128)(2,1)S(1)} %constant_dynamic-slice_fusion.3), channel_id=1, source_target_pairs={{0,1},{1,0},{2,3},{3,2},{4,5},{5,4},{6,7},{7,6},{8,9},{9,8},{10,11... | collective-permute-start | bytes 3145736 | tf_op jit(solution)/shard_map/ppermute | solution.py:1077
  5.3 58.8 %collective-permute-start.1 = (bf16[1,512,1024]{2,1,0:T(8,128)(2,1)S(1)}, bf16[1,512,1024]{2,1,0:T(8,128)(2,1)}, u32[]{:S(2)}, u32[]{:S(2)}) collective-permute-start(bf16[1,512,1024]{2,1,0:T(8,128)(2,1)S(1)} %constant_dynamic-slice_fusion.2), channel_id=1, source_target_pairs={{0,1},{1,0},{2,3},{3,2},{4,5},{5,4},{6,7},{7,6},{8,9},{9,8},{10,11... | collective-permute-start | bytes 3145736 | tf_op jit(solution)/shard_map/ppermute | solution.py:1077
  175.0 24.3 %collective-permute-start.2 = (bf16[2,1024,1024]{2,1,0:T(8,128)(2,1)}, bf16[2,1024,1024]{2,1,0:T(8,128)(2,1)}, u32[]{:S(2)}, u32[]{:S(2)}) collective-permute-start(bf16[2,1024,1024]{2,1,0:T(8,128)(2,1)} %weight_grad.10), channel_id=1, source_target_pairs={{0,2},{2,0},{4,6},{6,4},{8,10},{10,8},{12,14},{14,12},{16,18},{18,... | collective-permute-start | bytes 12582920 | tf_op jit(solution)/shard_map/ppermute | solution.py:1081
  184.9 31.0 %collective-permute-start.3 = (bf16[2,512,2048]{2,1,0:T(8,128)(2,1)}, bf16[2,512,2048]{2,1,0:T(8,128)(2,1)}, u32[]{:S(2)}, u32[]{:S(2)}) collective-permute-start(bf16[2,512,2048]{2,1,0:T(8,128)(2,1)} %weight_grad.11), channel_id=1, source_target_pairs={{0,2},{2,0},{4,6},{6,4},{8,10},{10,8},{12,14},{14,12},{16,18},{18,... | collective-permute-start | bytes 12582920 | tf_op jit(solution)/shard_map/ppermute | solution.py:1081
  194.9 53.8 %collective-permute-start.4 = (bf16[512,1024]{1,0:T(8,128)(2,1)S(1)}, bf16[512,1024]{1,0:T(8,128)(2,1)S(1)}, u32[]{:S(2)}, u32[]{:S(2)}) collective-permute-start(bf16[512,1024]{1,0:T(8,128)(2,1)S(1)} %copy-done.32), channel_id=1, source_target_pairs={{0,1},{1,0},{2,3},{3,2},{4,5},{5,4},{6,7},{7,6},{8,9},{9,8},{10,11... | collective-permute-start | bytes 3145736 | tf_op jit(solution)/shard_map/ppermute | solution.py:1077
  197.4 30.1 %collective-permute-start.33 = (f32[20,1024]{1,0:T(8,128)S(1)}, f32[20,1024]{1,0:T(8,128)S(1)}, u32[]{:S(2)}, u32[]{:S(2)}) collective-permute-start(f32[20,1024]{1,0:T(8,128)S(1)} %add.227), channel_id=1, source_target_pairs={{0,1},{1,0},{2,3},{3,2},{4,5},{5,4},{6,7},{7,6},{8,9},{9,8},{10,11... | collective-permute-start | bytes 245768 | tf_op jit(solution)/shard_map/ppermute | solution.py:1077
  214.4 43.9 %collective-permute-start.5 = (bf16[2,512,512]{2,1,0:T(8,128)(2,1)}, bf16[2,512,512]{2,1,0:T(8,128)(2,1)S(1)}, u32[]{:S(2)}, u32[]{:S(2)}) collective-permute-start(bf16[2,512,512]{2,1,0:T(8,128)(2,1)} %weight_grad.13), channel_id=1, source_target_pairs={{0,2},{2,0},{4,6},{6,4},{8,10},{10,8},{12,14},{14,12},{16,18},{18,... | collective-permute-start | bytes 3145736 | tf_op jit(solution)/shard_map/ppermute | solution.py:1081
  214.4 64.6 %collective-permute-start.6 = (bf16[1024,1024]{1,0:T(8,128)(2,1)}, bf16[1024,1024]{1,0:T(8,128)(2,1)}, u32[]{:S(2)}, u32[]{:S(2)}) collective-permute-start(bf16[1024,1024]{1,0:T(8,128)(2,1)} %get-tuple-element.108), channel_id=1, source_target_pairs={{0,4},{2,6},{4,0},{6,2},{8,12},{10,14},{12,8},{14,10},{16,20},{18,... | collective-permute-start | bytes 6291464 | tf_op jit(solution)/shard_map/ppermute | solution.py:1081
  227.0 48.8 %collective-permute-start.7 = (bf16[512,2048]{1,0:T(8,128)(2,1)}, bf16[512,2048]{1,0:T(8,128)(2,1)}, u32[]{:S(2)}, u32[]{:S(2)}) collective-permute-start(bf16[512,2048]{1,0:T(8,128)(2,1)} %get-tuple-element.113), channel_id=1, source_target_pairs={{0,1},{1,0},{2,3},{3,2},{4,5},{5,4},{6,7},{7,6},{8,9},{9,8},{10,11... | collective-permute-start | bytes 6291464 | tf_op jit(solution)/shard_map/ppermute | solution.py:1077
  227.5 22.8 %collective-permute-start.34 = (f32[20,1024]{1,0:T(8,128)S(1)}, f32[20,1024]{1,0:T(8,128)S(1)}, u32[]{:S(2)}, u32[]{:S(2)}) collective-permute-start(f32[20,1024]{1,0:T(8,128)S(1)} %add.228), channel_id=1, source_target_pairs={{0,8},{2,10},{4,12},{6,14},{8,0},{10,2},{12,4},{14,6},{16,24},{18,... | collective-permute-start | bytes 245768 | tf_op jit(solution)/shard_map/ppermute | solution.py:1081
  270.3 40.7 %collective-permute-start.8 = (bf16[2,512,768]{2,1,0:T(8,128)(2,1)}, bf16[2,512,768]{2,1,0:T(8,128)(2,1)}, u32[]{:S(2)}, u32[]{:S(2)}) collective-permute-start(bf16[2,512,768]{2,1,0:T(8,128)(2,1)} %weight_grad.16), channel_id=1, source_target_pairs={{0,2},{2,0},{4,6},{6,4},{8,10},{10,8},{12,14},{14,12},{16,18},{18,... | collective-permute-start | bytes 4718600 | tf_op jit(solution)/shard_map/ppermute | solution.py:1081
  270.3 38.5 %collective-permute-start.26 = (bf16[512,512]{1,0:T(8,128)(2,1)}, bf16[512,512]{1,0:T(8,128)(2,1)}, u32[]{:S(2)}, u32[]{:S(2)}) collective-permute-start(bf16[512,512]{1,0:T(8,128)(2,1)} %get-tuple-element.122), channel_id=1, source_target_pairs={{0,1},{1,0},{2,3},{3,2},{4,5},{5,4},{6,7},{7,6},{8,9},{9,8},{10,11... | collective-permute-start | bytes 1572872 | tf_op jit(solution)/shard_map/ppermute | solution.py:1077
  278.4 62.9 %collective-permute-start.36 = (bf16[4,64,2048]{2,1,0:T(8,128)(2,1)S(1)}, bf16[4,64,2048]{2,1,0:T(8,128)(2,1)}, u32[]{:S(2)}, u32[]{:S(2)}) collective-permute-start(bf16[4,64,2048]{2,1,0:T(8,128)(2,1)S(1)} %get-tuple-element.161), channel_id=1, source_target_pairs={{0,4},{2,6},{4,0},{6,2},{8,12},{10,14},{12,8},{14,10},{16,20},{18,... | collective-permute-start | bytes 3145736 | tf_op jit(solution)/shard_map/ppermute | solution.py:1081
  308.8 51.9 %collective-permute-start.9 = (bf16[2,512,768]{2,1,0:T(8,128)(2,1)}, bf16[2,512,768]{2,1,0:T(8,128)(2,1)}, u32[]{:S(2)}, u32[]{:S(2)}) collective-permute-start(bf16[2,512,768]{2,1,0:T(8,128)(2,1)} %weight_grad.17), channel_id=1, source_target_pairs={{0,2},{2,0},{4,6},{6,4},{8,10},{10,8},{12,14},{14,12},{16,18},{18,... | collective-permute-start | bytes 4718600 | tf_op jit(solution)/shard_map/ppermute | solution.py:1081
  310.1 16.7 %collective-permute-start.27 = (bf16[4,64,512]{2,1,0:T(8,128)(2,1)S(1)}, bf16[4,64,512]{2,1,0:T(8,128)(2,1)S(1)}, u32[]{:S(2)}, u32[]{:S(2)}) collective-permute-start(bf16[4,64,512]{2,1,0:T(8,128)(2,1)S(1)} %get-tuple-element.171), channel_id=1, source_target_pairs={{0,4},{2,6},{4,0},{6,2},{8,12},{10,14},{12,8},{14,10},{16,20},{18,... | collective-permute-start | bytes 786440 | tf_op jit(solution)/shard_map/ppermute | solution.py:1081
  330.4 26.4 %collective-permute-start.40 = (bf16[4,256,512]{2,1,0:T(8,128)(2,1)}, bf16[4,256,512]{2,1,0:T(8,128)(2,1)}, u32[]{:S(2)}, u32[]{:S(2)}) collective-permute-start(bf16[4,256,512]{2,1,0:T(8,128)(2,1)} %get-tuple-element.163), channel_id=1, source_target_pairs={{0,1},{1,0},{2,3},{3,2},{4,5},{5,4},{6,7},{7,6},{8,9},{9,8},{10,11... | collective-permute-start | bytes 3145736 | tf_op jit(solution)/shard_map/ppermute | solution.py:1077
  337.2 65.9 %collective-permute-start.16 = (bf16[512,768]{1,0:T(8,128)(2,1)}, bf16[512,768]{1,0:T(8,128)(2,1)}, u32[]{:S(2)}, u32[]{:S(2)}) collective-permute-start(bf16[512,768]{1,0:T(8,128)(2,1)} %get-tuple-element.130), channel_id=1, source_target_pairs={{0,1},{1,0},{2,3},{3,2},{4,5},{5,4},{6,7},{7,6},{8,9},{9,8},{10,11... | collective-permute-start | bytes 2359304 | tf_op jit(solution)/shard_map/ppermute | solution.py:1077
  343.1 34.4 %collective-permute-start.37 = (bf16[64,2048]{1,0:T(8,128)(2,1)S(1)}, bf16[64,2048]{1,0:T(8,128)(2,1)}, u32[]{:S(2)}, u32[]{:S(2)}) collective-permute-start(bf16[64,2048]{1,0:T(8,128)(2,1)S(1)} %get-tuple-element.167), channel_id=1, source_target_pairs={{0,8},{2,10},{4,12},{6,14},{8,0},{10,2},{12,4},{14,6},{16,24},{18,... | collective-permute-start | bytes 786440 | tf_op jit(solution)/shard_map/ppermute | solution.py:1081
  343.7 34.3 %collective-permute-start.38 = (bf16[64,2048]{1,0:T(8,128)(2,1)S(1)}, bf16[64,2048]{1,0:T(8,128)(2,1)}, u32[]{:S(2)}, u32[]{:S(2)}) collective-permute-start(bf16[64,2048]{1,0:T(8,128)(2,1)S(1)} %get-tuple-element.169), channel_id=1, source_target_pairs={{0,16},{2,18},{4,20},{6,22},{8,24},{10,26},{12,28},{14,30},{16,0},... | collective-permute-start | bytes 786440 | tf_op jit(solution)/shard_map/ppermute | solution.py:1081
  356.7 22.0 %collective-permute-start.39 = (bf16[64,2048]{1,0:T(8,128)(2,1)S(1)}, bf16[64,2048]{1,0:T(8,128)(2,1)}, u32[]{:S(2)}, u32[]{:S(2)}) collective-permute-start(bf16[64,2048]{1,0:T(8,128)(2,1)S(1)} %get-tuple-element.168), channel_id=1, source_target_pairs={{0,24},{2,26},{4,28},{6,30},{8,16},{10,18},{12,20},{14,22},{16,8},... | collective-permute-start | bytes 786440 | tf_op jit(solution)/shard_map/ppermute | solution.py:1081
  377.5 51.6 %collective-permute-start.10 = (bf16[512,1024]{1,0:T(8,128)(2,1)}, bf16[512,1024]{1,0:T(8,128)(2,1)S(1)}, u32[]{:S(2)}, u32[]{:S(2)}) collective-permute-start(bf16[512,1024]{1,0:T(8,128)(2,1)} %get-tuple-element.134), channel_id=1, source_target_pairs={{0,1},{1,0},{2,3},{3,2},{4,5},{5,4},{6,7},{7,6},{8,9},{9,8},{10,11... | collective-permute-start | bytes 3145736 | tf_op jit(solution)/shard_map/ppermute | solution.py:1077
  378.0 12.4 %collective-permute-start.41 = (bf16[256,512]{1,0:T(8,128)(2,1)S(1)}, bf16[256,512]{1,0:T(8,128)(2,1)S(1)}, u32[]{:S(2)}, u32[]{:S(2)}) collective-permute-start(bf16[256,512]{1,0:T(8,128)(2,1)S(1)} %get-tuple-element.164), channel_id=1, source_target_pairs={{0,8},{2,10},{4,12},{6,14},{8,0},{10,2},{12,4},{14,6},{16,24},{18,... | collective-permute-start | bytes 786440 | tf_op jit(solution)/shard_map/ppermute | solution.py:1081
  378.7 21.3 %collective-permute-start.42 = (bf16[256,512]{1,0:T(8,128)(2,1)S(1)}, bf16[256,512]{1,0:T(8,128)(2,1)S(1)}, u32[]{:S(2)}, u32[]{:S(2)}) collective-permute-start(bf16[256,512]{1,0:T(8,128)(2,1)S(1)} %get-tuple-element.166), channel_id=1, source_target_pairs={{0,16},{2,18},{4,20},{6,22},{8,24},{10,26},{12,28},{14,30},{16,0},... | collective-permute-start | bytes 786440 | tf_op jit(solution)/shard_map/ppermute | solution.py:1081
  380.0 20.1 %collective-permute-start.43 = (bf16[256,512]{1,0:T(8,128)(2,1)S(1)}, bf16[256,512]{1,0:T(8,128)(2,1)S(1)}, u32[]{:S(2)}, u32[]{:S(2)}) collective-permute-start(bf16[256,512]{1,0:T(8,128)(2,1)S(1)} %get-tuple-element.165), channel_id=1, source_target_pairs={{0,24},{2,26},{4,28},{6,30},{8,16},{10,18},{12,20},{14,22},{16,8},... | collective-permute-start | bytes 786440 | tf_op jit(solution)/shard_map/ppermute | solution.py:1081
  390.4 12.1 %collective-permute-start.12 = (f32[5,1024]{1,0:T(8,128)S(1)}, f32[5,1024]{1,0:T(8,128)S(1)}, u32[]{:S(2)}, u32[]{:S(2)}) collective-permute-start(f32[5,1024]{1,0:T(8,128)S(1)} %fusion.13), channel_id=1, source_target_pairs={{0,4},{2,6},{4,0},{6,2},{8,12},{10,14},{12,8},{14,10},{16,20},{18,... | collective-permute-start | bytes 61448 | tf_op jit(solution)/shard_map/ppermute | solution.py:1081
  401.0 31.8 %collective-permute-start.21 = (bf16[512,768]{1,0:T(8,128)(2,1)S(1)}, bf16[512,768]{1,0:T(8,128)(2,1)S(1)}, u32[]{:S(2)}, u32[]{:S(2)}) collective-permute-start(bf16[512,768]{1,0:T(8,128)(2,1)S(1)} %copy-done.33), channel_id=1, source_target_pairs={{0,1},{1,0},{2,3},{3,2},{4,5},{5,4},{6,7},{7,6},{8,9},{9,8},{10,11... | collective-permute-start | bytes 2359304 | tf_op jit(solution)/shard_map/ppermute | solution.py:1077
  402.5 18.3 %collective-permute-start.13 = (f32[5,1024]{1,0:T(8,128)S(1)}, f32[5,1024]{1,0:T(8,128)S(1)}, u32[]{:S(2)}, u32[]{:S(2)}) collective-permute-start(f32[5,1024]{1,0:T(8,128)S(1)} %add.201), channel_id=1, source_target_pairs={{0,1},{1,0},{2,3},{3,2},{4,5},{5,4},{6,7},{7,6},{8,9},{9,8},{10,11... | collective-permute-start | bytes 61448 | tf_op jit(solution)/shard_map/ppermute | solution.py:1077
  425.5 11.5 %collective-permute-start.17 = (bf16[4,64,768]{2,1,0:T(8,128)(2,1)S(1)}, bf16[4,64,768]{2,1,0:T(8,128)(2,1)S(1)}, u32[]{:S(2)}, u32[]{:S(2)}) collective-permute-start(bf16[4,64,768]{2,1,0:T(8,128)(2,1)S(1)} %dynamic-slice_bitcast_fusion.3), channel_id=1, source_target_pairs={{0,4},{2,6},{4,0},{6,2},{8,12},{10,14},{12,8},{14,10},{16,20},{18,... | collective-permute-start | bytes 1179656 | tf_op jit(solution)/shard_map/ppermute | solution.py:1081
  433.0 9.9 %collective-permute-start.22 = (bf16[4,64,768]{2,1,0:T(8,128)(2,1)S(1)}, bf16[4,64,768]{2,1,0:T(8,128)(2,1)S(1)}, u32[]{:S(2)}, u32[]{:S(2)}) collective-permute-start(bf16[4,64,768]{2,1,0:T(8,128)(2,1)S(1)} %dynamic-slice_bitcast_fusion.2), channel_id=1, source_target_pairs={{0,4},{2,6},{4,0},{6,2},{8,12},{10,14},{12,8},{14,10},{16,20},{18,... | collective-permute-start | bytes 1179656 | tf_op jit(solution)/shard_map/ppermute | solution.py:1081
  437.4 10.2 %collective-permute-start.19 = (bf16[64,768]{1,0:T(8,128)(2,1)S(1)}, bf16[64,768]{1,0:T(8,128)(2,1)S(1)}, u32[]{:S(2)}, u32[]{:S(2)}) collective-permute-start(bf16[64,768]{1,0:T(8,128)(2,1)S(1)} %get-tuple-element.174), channel_id=1, source_target_pairs={{0,16},{2,18},{4,20},{6,22},{8,24},{10,26},{12,28},{14,30},{16,0},... | collective-permute-start | bytes 294920 | tf_op jit(solution)/shard_map/ppermute | solution.py:1081
  438.8 8.8 %collective-permute-start.20 = (bf16[64,768]{1,0:T(8,128)(2,1)S(1)}, bf16[64,768]{1,0:T(8,128)(2,1)S(1)}, u32[]{:S(2)}, u32[]{:S(2)}) collective-permute-start(bf16[64,768]{1,0:T(8,128)(2,1)S(1)} %get-tuple-element.173), channel_id=1, source_target_pairs={{0,24},{2,26},{4,28},{6,30},{8,16},{10,18},{12,20},{14,22},{16,8},... | collective-permute-start | bytes 294920 | tf_op jit(solution)/shard_map/ppermute | solution.py:1081
  443.4 9.7 %collective-permute-start.24 = (bf16[64,768]{1,0:T(8,128)(2,1)S(1)}, bf16[64,768]{1,0:T(8,128)(2,1)S(1)}, u32[]{:S(2)}, u32[]{:S(2)}) collective-permute-start(bf16[64,768]{1,0:T(8,128)(2,1)S(1)} %get-tuple-element.177), channel_id=1, source_target_pairs={{0,16},{2,18},{4,20},{6,22},{8,24},{10,26},{12,28},{14,30},{16,0},... | collective-permute-start | bytes 294920 | tf_op jit(solution)/shard_map/ppermute | solution.py:1081
  (46 other events, 403.5 us)

commit v4 on v3

--- a/solution.py
+++ b/solution.py
@@ -49,6 +49,10 @@
 
 def params(mib=None, **more):
     return pltpu.CompilerParams(vmem_limit_bytes=(mib or 60) * 2**20, **more)
+
+
+def cost(flops, moved):
+    return pl.CostEstimate(flops=flops, bytes_accessed=moved, transcendentals=0)
 
 
 def whole(shape):
@@ -127,9 +131,7 @@
         ],
         input_output_aliases={6 + k: k for k in range(len(earlier))},
         compiler_params=params(),
-        cost_estimate=pl.CostEstimate(
-            flops=2 * n * d * 3 * d, bytes_accessed=6 * d * d + 10 * n * d, transcendentals=n
-        ),
+        cost_estimate=cost(2 * n * d * 3 * d, 6 * d * d + 10 * n * d),
     )(at, tok, gain, shift, w, bias, *earlier)
 
 
@@ -228,9 +230,7 @@
             jax.ShapeDtypeStruct((pairs, 4, 8, size), f32),
         ],
         compiler_params=params(),
-        cost_estimate=pl.CostEstimate(
-            flops=flops * 4, bytes_accessed=8 * half_len * wide, transcendentals=8 * half_len * half_len * pairs
-        ),
+        cost_estimate=cost(flops * 4, 8 * half_len * wide),
     )(tab, qkv, qkv, qkv, head_scale_row)
 
 
@@ -336,9 +336,7 @@
             jax.ShapeDtypeStruct((pairs, 8, LANES), f32),
         ],
         compiler_params=params(),
-        cost_estimate=pl.CostEstimate(
-            flops=flops * 10, bytes_accessed=8 * half_len * wide, transcendentals=8 * half_len * half_len * pairs
-        ),
+        cost_estimate=cost(flops * 10, 8 * half_len * wide),
     )(tab, qkv, qkv, qkv, heads_out, d_out, inv_scale_row, lse)
 
 
@@ -575,10 +573,8 @@
         ],
         input_output_aliases={9 + k: 4 + k for k in range(len(earlier))},
         compiler_params=params(62),
-        cost_estimate=pl.CostEstimate(
-            flops=8 * n * d * ff + 4 * n * d * d,
-            bytes_accessed=4 * d * ff + 2 * d * d + 4 * n * ff + 20 * n * d,
-            transcendentals=2 * n * ff,
+        cost_estimate=cost(
+            8 * n * d * ff + 4 * n * d * d, 4 * d * ff + 2 * d * d + 4 * n * ff + 20 * n * d
         ),
     )(at, ho, tok, cot, out_w, w1, w2, vec, vec4, *earlier)
 
@@ -631,9 +627,7 @@
             jax.ShapeDtypeStruct((8, d), f32),
         ],
         compiler_params=params(),
-        cost_estimate=pl.CostEstimate(
-            flops=6 * n * d * d, bytes_accessed=6 * d * d + 16 * n * d, transcendentals=n
-        ),
+        cost_estimate=cost(6 * n * d * d, 6 * d * d + 16 * n * d),
     )(at, even, odd, w, tok, grad_middle, gain)
 
 
@@ -641,117 +635,122 @@
     return lax.optimization_barrier((x,) + others)[0]
 
 
-def weight_grad_body(a_count, b_count, halves, received_too, tab, *refs):
-    def joined(parts, axis=1):
-        parts = [x[0] if len(x.shape) == 3 else x[...] for x in parts]
-        return parts[0] if len(parts) == 1 else jnp.concatenate(parts, axis=axis)
-
-    rhs = joined(refs[a_count : a_count + b_count], 0 if halves else 1)
-    total = mm(joined(refs[:a_count]), rhs, TN)
-    if not received_too:
-        refs[-1][0] = total.astype(bf16)
-        return
-    received, send, keep = refs[-3:]
-    total = (total + received[0].astype(f32)).astype(bf16)
-
-    @pl.when(pl.program_id(0) == 0)
-    def _():
-        send[...] = total
-
-    @pl.when(pl.program_id(0) == 1)
-    def _():
-        keep[...] = total
-
-
-def weight_grad(tab, a, b, a_blocks, b_blocks, out_block, shape, steps, received=None):
-    flops = 2 * a.shape[-2] * 2 * shape[0] * shape[1]
-    out_index = out_block[1]
-    halves = isinstance(b, tuple)
-    bs = b if halves else (b,) * len(b_blocks)
-    moved = 2 * (a.size + bs[0].size) + 4 * shape[0] * shape[1]
-    part = pl.BlockSpec((1,) + out_block[0], lambda s, i, t: (s,) + out_index(i))
-    in_specs = [pl.BlockSpec(*spec) for spec in (*a_blocks, *b_blocks)]
-    args = [tab] + [a] * len(a_blocks) + list(bs)
+def emit(at_low, low, high, received, outs):
+    send, keep = jnp.where(at_low, high, low), jnp.where(at_low, low, high)
     if received is None:
-        out_specs = part
-        out_shape = jax.ShapeDtypeStruct((2,) + shape, bf16)
+        outs[-1][0] = send.astype(bf16)
+        outs[-1][1] = keep.astype(bf16)
     else:
-        in_specs.append(part)
+        outs[-2][...] = (send + received[0].astype(f32)).astype(bf16)
+        outs[-1][...] = (keep + received[1].astype(f32)).astype(bf16)
+
+
+def tall_grad_body(received_too, tab, *refs):
+    runs, halves = refs[:2], refs[2:4]
+    a = jnp.concatenate([r[...] for r in runs], axis=1)
+    total = mm(a, jnp.concatenate([h[0] for h in halves], axis=0), TN)
+    wide = total.shape[1] // 2
+    emit(tab[2] == 0, total[:, :wide], total[:, wide:], refs[4] if received_too else None, refs)
+
+
+def tall_grad(tab, a, b, received=None):
+    n, wide = a.shape
+    d = b[0].shape[2]
+    tall = wide // 16
+    steps = 4
+
+    def run(k):
+        return pl.BlockSpec((n, tall), lambda i, t: (0, (2 * i + k) * 2 + t[0]))
+
+    in_specs = [
+        run(0),
+        run(1),
+        pl.BlockSpec((1, n // 2, d), lambda i, t: (t[2], 0, 0), pipeline_mode=pl.Buffered(1)),
+        pl.BlockSpec((1, n // 2, d), lambda i, t: (0, 0, 0), pipeline_mode=pl.Buffered(1)),
+    ]
+    both = pl.BlockSpec((2, 2 * tall, d // 2), lambda i, t: (0, i, 0))
+    one = pl.BlockSpec((2 * tall, d // 2), lambda i, t: (i, 0))
+    args = [tab, a, a, *b]
+    if received is not None:
+        in_specs.append(both)
         args.append(received)
-        last = steps - 1
-        out_specs = [
-            pl.BlockSpec(out_block[0], lambda s, i, t: out_index(jnp.where(s == 0, i, last))),
-            pl.BlockSpec(out_block[0], lambda s, i, t: out_index(jnp.where(s == 0, 0, i))),
-        ]
-        out_shape = [jax.ShapeDtypeStruct(shape, bf16)] * 2
+    shape = (wide // 2, d // 2)
     return pl.pallas_call(
-        partial(weight_grad_body, len(a_blocks), len(b_blocks), halves, received is not None),
-        name="weight_grad",
+        partial(tall_grad_body, received is not None),
+        name="tall_grad",
         grid_spec=pltpu.PrefetchScalarGridSpec(
-            num_scalar_prefetch=1, grid=(2, steps), in_specs=in_specs, out_specs=out_specs
+            num_scalar_prefetch=1,
+            grid=(steps,),
+            in_specs=in_specs,
+            out_specs=both if received is None else [one, one],
         ),
-        out_shape=out_shape,
+        out_shape=jax.ShapeDtypeStruct((2,) + shape, bf16)
+        if received is None
+        else [jax.ShapeDtypeStruct(shape, bf16)] * 2,
         compiler_params=params(),
-        cost_estimate=pl.CostEstimate(flops=flops, bytes_accessed=moved, transcendentals=0),
+        cost_estimate=cost(2 * n * wide * d // 2, n * wide + 2 * n * d + 8 * wide * d // 4),
     )(*args)
 
 
-def part_of(s, t, at):
-    return jnp.where(s == 0, 1 - t[at], t[at])
-
-
-def tall_how(n, d, ff):
-    tall = ff // 16
-
-    def run(k):
-        return ((n, tall), lambda s, i, t: (0, ((2 * i + k) * 2 + part_of(s, t, 1)) * 2 + t[0]))
-
-    return (
-        [run(0), run(1)],
-        [
-            ((1, n // 2, d), lambda s, i, t: (t[2], 0, 0)),
-            ((1, n // 2, d), lambda s, i, t: (0, 0, 0)),
-        ],
-        ((2 * tall, d), lambda i: (i, 0)),
-        (4 * tall, d),
-        2,
-    )
-
-
-def flat_how(n, d, width):
-    tn = d // 2
-    count = 2 if width > 2 * d else 1
-    steps = width // (2 * tn * count)
-
-    def columns(k):
-        return ((n, tn), lambda s, i, t: (0, (part_of(s, t, 2) * steps + i) * count + k))
-
-    return (
-        [((1, n, d // 2), lambda s, i, t: (t[0], 0, 0))],
-        [columns(k) for k in range(count)],
-        ((d // 2, tn * count), lambda i: (0, i)),
-        (d // 2, steps * tn * count),
-        steps,
-    )
-
-
-def qkv_how(n, d):
-    run = d // 4
-
-    def columns(k):
-        def index(s, i, t):
-            at = part_of(s, t, 2) * 3 + k
-            return at // 2, 0, at % 2
-
-        return ((1, n, run), index)
-
-    return (
-        [((1, n, d // 2), lambda s, i, t: (t[0], 0, 0))],
-        [columns(k) for k in range(3)],
-        ((d // 2, 3 * run), lambda i: (0, 0)),
-        (d // 2, 3 * run),
-        1,
-    )
+def flat_grad_body(counts, received_too, tab, *refs):
+    step = pl.program_id(0)
+    parts = len(counts)
+    lhs, rhs = refs[:parts], refs[parts : 2 * parts]
+    first = 0
+    for k, count in enumerate(counts):
+
+        @pl.when((step >= first) & (step < first + count))
+        def _(k=k):
+            b = rhs[k][0] if len(rhs[k].shape) == 3 else rhs[k][...]
+            total = mm(lhs[k][0], b, TN)
+            run = total.shape[0] // 8
+            low, high = (
+                jnp.concatenate([total[(2 * z + h) * run : (2 * z + h + 1) * run] for z in range(4)])
+                for h in range(2)
+            )
+            emit(tab[1] == 0, low, high, refs[2 * parts] if received_too else None, refs)
+
+        first += count
+
+
+def flat_grad(tab, pairs, tn, received=None):
+    counts = [b.shape[0] if b.ndim == 3 else b.shape[1] // tn for _, b in pairs]
+    steps = sum(counts)
+    n, wide = pairs[0][0].shape[1:]
+    in_specs = [
+        pl.BlockSpec((1, n, wide), lambda i, t: (t[0], 0, 0), pipeline_mode=pl.Buffered(1))
+    ] * len(pairs)
+    first = 0
+    for (_, b), count in zip(pairs, counts):
+        at = partial(lambda first, last, i: jnp.clip(i - first, 0, last), first, count - 1)
+        if b.ndim == 3:
+            in_specs.append(pl.BlockSpec((1, n, tn), lambda i, t, at=at: (at(i), 0, 0)))
+        else:
+            in_specs.append(pl.BlockSpec((n, tn), lambda i, t, at=at: (0, at(i))))
+        first += count
+    both = pl.BlockSpec((2, wide // 2, tn), lambda i, t: (0, 0, i))
+    one = pl.BlockSpec((wide // 2, tn), lambda i, t: (0, i))
+    args = [tab] + [a for a, _ in pairs] + [b for _, b in pairs]
+    if received is not None:
+        in_specs.append(both)
+        args.append(received)
+    shape = (wide // 2, steps * tn)
+    weight = 16 if pairs[0][1].ndim == 3 else 1
+    return pl.pallas_call(
+        partial(flat_grad_body, counts, received is not None),
+        name="flat_grad",
+        grid_spec=pltpu.PrefetchScalarGridSpec(
+            num_scalar_prefetch=1,
+            grid=(steps,),
+            in_specs=in_specs,
+            out_specs=both if received is None else [one, one],
+        ),
+        out_shape=jax.ShapeDtypeStruct((2,) + shape, bf16)
+        if received is None
+        else [jax.ShapeDtypeStruct(shape, bf16)] * 2,
+        compiler_params=params(),
+        cost_estimate=cost(2 * n * wide * shape[1] // weight, (2 * n * (wide + shape[1]) + 8 * wide * shape[1]) // weight),
+    )(*args)
 
 
 def running_sums(lengths):
@@ -1158,11 +1157,27 @@
     def fill(kept, back):
         return lax.dynamic_update_slice_in_dim(kept, back.astype(f32)[None], 1 - b, 0)
 
-    def z_stage(parts):
-        total = lax.dynamic_index_in_dim(parts, z, 0, keepdims=False).astype(f32)
-        for k in (1, 2, 3):
-            total = total + flip(lax.dynamic_index_in_dim(parts, z ^ k, 0, keepdims=False), 4 * k).astype(f32)
-        return total
+    def near_z(total):
+        total = total.astype(bf16).reshape((2, 2) + total.shape[1:])
+        odd = z % 2
+        return (
+            lax.dynamic_index_in_dim(total, 1 - odd, 1, keepdims=False),
+            lax.dynamic_index_in_dim(total, odd, 1, keepdims=False),
+        )
+
+    def far_z(total):
+        total = total.astype(bf16)
+        high = z // 2
+        return (
+            lax.dynamic_index_in_dim(total, 1 - high, 0, keepdims=False),
+            lax.dynamic_index_in_dim(total, high, 0, keepdims=False),
+        )
+
+    def add_z(move, send, keep):
+        return keep.astype(f32) + flip(send, move).astype(f32)
+
+    def held(parts, *others):
+        return parts[0], after(parts[1], *others)
 
     def rows_by_x(total):
         total = total.astype(bf16).reshape(4, 2, -1, total.shape[1])
@@ -1171,14 +1186,16 @@
             lax.dynamic_index_in_dim(total, x, 1, keepdims=False),
         )
 
-    def columns_by_y(total):
-        total = total.astype(bf16)
-        total = total.reshape(4, -1, total.shape[-1])
-        width = total.shape[2] // 2
-        return (
-            lax.dynamic_slice_in_dim(total, (1 - y) * width, width, 2),
-            lax.dynamic_slice_in_dim(total, y * width, width, 2),
-        )
+    def columns_by_y(total, *cuts):
+        total = total.astype(bf16).reshape(4, -1, total.shape[1])
+        out = []
+        for at in (1 - y, y):
+            groups = []
+            for first, last in zip((0,) + cuts, cuts + (total.shape[2],)):
+                width = (last - first) // 2
+                groups.append(lax.dynamic_slice_in_dim(total, first + at * width, width, 2))
+            out.append(jnp.concatenate(groups, axis=2) if cuts else groups[0])
+        return out
 
     def add_x(send, keep):
         return keep.astype(f32) + flip(send, 2).astype(f32)
@@ -1186,61 +1203,50 @@
     def add_y(send, keep):
         return keep.astype(f32) + exchange(send).astype(f32)
 
-    tall, flat4, flat1, qkv3 = (
-        tall_how(n, d, ff), flat_how(n, d, ff), flat_how(n, d, d), qkv_how(n, d)
-    )
     cots = (cotangent, cot_in)
-    fc2_theirs = weight_grad(theirs, mid_out, cots, *tall)
-    ffn_in = after(ffn_in, fc2_theirs)
-    fc1_theirs = weight_grad(theirs, ffn_in, grad_hidden, *flat4)
-    mid_out = after(mid_out, fc1_theirs)
-    fc2_parts = weight_grad(mine, mid_out, cots, *tall, flip(fc2_theirs, 1))
-    heads_in = after(heads_in, *fc2_parts)
-    out_theirs = weight_grad(theirs, heads_in, grad_proj, *flat1)
-    ffn_in = after(ffn_in, out_theirs)
-    fc1_parts = weight_grad(mine, ffn_in, grad_hidden, *flat4, flip(fc1_theirs, 1))
-
-    sums = jnp.concatenate([sums, sums4.reshape(8 * ff // d, d)[: 3 * ff // d]])
-    steps = (
-        (partial(flip, bit=1), fc2_theirs),
-        (partial(flip, bit=2), fc1_theirs),
-        (exchange, fc2_parts[0]),
-        (partial(flip, bit=4), fc1_parts[0]),
-    )
-    for move, done in steps:
-        sums = after(sums, done) + move(sums)
-
-    d_out = after(d_out, *fc1_parts)
+    output = fill(output, out_back)
+    wide_pairs = [(after(ffn_in, output), grad_hidden), (heads_in, grad_proj)]
+    wide_theirs = flat_grad(theirs, wide_pairs, d)
+    fc2_theirs = tall_grad(theirs, after(mid_out, wide_theirs), cots)
+    wide_pairs = [(after(ffn_in, fc2_theirs), grad_hidden), (heads_in, grad_proj)]
+    wide_parts = flat_grad(mine, wide_pairs, d, flip(wide_theirs, 1))
+    fc2_parts = tall_grad(mine, after(mid_out, *wide_parts), cots, flip(fc2_theirs, 1))
+    d_out = after(d_out, *fc2_parts)
     back_args = (1.0 / scale_row, logs, scale)
     even, dots_even = attend_back(tab, qkv, heads_out, d_out, *back_args, 0)
     even = even.reshape(3, n, d // 2)
-    sums = after(sums, even) + flip(sums, 8)
-    output = fill(after(output, even), out_back)
-    out_parts = weight_grad(mine, after(heads_in, even), grad_proj, *flat1, flip(out_theirs, 1))
-    even_theirs = weight_grad(theirs, after(attn_in, *out_parts), even, *qkv3)
-    fc2_parts = columns_by_y(add_x(fc2_parts[0], after(fc2_parts[1], even_theirs)))
-    fc1_parts = rows_by_x(add_y(fc1_parts[0], after(fc1_parts[1], even_theirs)))
-    d_out = after(d_out, even_theirs, *fc2_parts, *fc1_parts)
+    even_theirs = flat_grad(theirs, [(after(attn_in, even), even)], d // 2)
+    d_out = after(d_out, even_theirs)
     odd, dots_odd = attend_back(tab, qkv, heads_out, d_out, *back_args, 1)
     odd = odd.reshape(3, n, d // 2)
-    odd_theirs = weight_grad(theirs, attn_in, odd, *qkv3)
-    attn_in = after(attn_in, odd_theirs)
-    even_parts = weight_grad(mine, attn_in, even, *qkv3, flip(even_theirs, 1))
+    wide_parts = columns_by_y(add_x(*held(wide_parts, odd)), ff)
+    fc2_parts = rows_by_x(add_y(*held(fc2_parts, odd)))
+    odd_theirs = flat_grad(theirs, [(after(attn_in, *wide_parts, *fc2_parts), odd)], d // 2)
+    even_parts = flat_grad(mine, [(after(attn_in, odd_theirs), even)], d // 2, flip(even_theirs, 1))
     grad_sent, sums_sent = first_back(
         sent_at, after(even, *even_parts), odd, qkv_weight, tok_in, mid_sent, line(norm1_gain), 1, False
     )
     grad_back = exchange(grad_sent)
-    odd_parts = weight_grad(mine, after(attn_in, grad_sent), odd, *qkv3, flip(odd_theirs, 1))
+    fc2_parts = near_z(add_x(*held(fc2_parts, grad_sent)))
+    odd_parts = flat_grad(
+        mine, [(after(attn_in, grad_sent, *fc2_parts), odd)], d // 2, flip(odd_theirs, 1)
+    )
+    wide_parts = near_z(add_y(*held(wide_parts, *odd_parts)))
     tokens_grad, sums_kept = first_back(
-        kept_at, after(even, *odd_parts), odd, qkv_weight, tokens, mid_kept, line(norm1_gain), 0, True
-    )
-    fc2_weight_grad = z_stage(add_y(fc2_parts[0], after(fc2_parts[1], grad_sent)).astype(bf16))
-    fc1_weight_grad = z_stage(add_x(fc1_parts[0], after(fc1_parts[1], grad_sent)).astype(bf16))
-    out_parts = rows_by_x(add_y(out_parts[0], after(out_parts[1], odd)))
-    out_weight_grad = z_stage(add_x(out_parts[0], after(out_parts[1], grad_sent)).astype(bf16))
-    even_parts = rows_by_x(add_y(even_parts[0], after(even_parts[1], tokens_grad)))
-    odd_parts = rows_by_x(add_y(odd_parts[0], after(odd_parts[1], tokens_grad)))
-    even_grad, odd_grad = (z_stage(add_x(*parts).astype(bf16)) for parts in (even_parts, odd_parts))
+        kept_at, after(even, *wide_parts), odd, qkv_weight, tokens, mid_kept, line(norm1_gain), 0, True
+    )
+    fc2_parts = far_z(add_z(4, *held(fc2_parts, tokens_grad)))
+    even_parts = columns_by_y(add_x(*held(even_parts, tokens_grad)))
+    wide_parts = far_z(add_z(4, *held(wide_parts, *fc2_parts, *even_parts)))
+    tokens_grad = fill(tokens_grad, grad_back)
+    fc2_weight_grad = add_z(8, *fc2_parts)
+    odd_parts = columns_by_y(add_x(*odd_parts))
+    even_parts = near_z(add_y(*even_parts))
+    wide_grad = add_z(8, *wide_parts)
+    fc1_weight_grad, out_weight_grad = wide_grad[:, : ff // 2], wide_grad[:, ff // 2 :]
+    even_parts = far_z(add_z(4, *even_parts))
+    odd_parts = far_z(add_z(4, *near_z(add_y(*odd_parts))))
+    even_grad, odd_grad = (add_z(8, *parts) for parts in (even_parts, odd_parts))
     run = d // 4
     qkv_weight_grad = jnp.stack(
         [even_grad.reshape(-1, 3, run), odd_grad.reshape(-1, 3, run)], axis=2
@@ -1249,10 +1255,13 @@
     dots = jnp.stack([dots_even[:, 0].reshape(2, 4, head_dim), dots_odd[:, 0].reshape(2, 4, head_dim)], axis=1)
     head_scales_grad = jnp.sum(dots, axis=3).reshape(heads) / head_scales
     head_scales_grad = jnp.pad(head_scales_grad, (0, d - heads))
-    first_sums = jnp.concatenate([(sums_sent + sums_kept)[:4], head_scales_grad[None]])
-    for move in (partial(flip, bit=1), partial(flip, bit=2), exchange, partial(flip, bit=4), partial(flip, bit=8)):
-        first_sums = first_sums + move(first_sums)
-    sums4 = sums[8:].reshape(3, ff)
+    first_sums = (sums_sent + sums_kept)[:4]
+    total = jnp.concatenate(
+        [first_sums, head_scales_grad[None], sums[:6], sums4.reshape(8 * ff // d, d)[: 3 * ff // d]]
+    )
+    for move in (partial(flip, bit=1), partial(flip, bit=4), partial(flip, bit=8), partial(flip, bit=2), exchange):
+        total = total + move(total)
+    first_sums, sums, sums4 = total[:5], total[5:11], total[11:].reshape(3, ff)
     return (
         output,
         tokens_grad,

time: 462 us -> 395 us (0.85)
  waiting for transfers between devices: 78.7 us -> 45.6 us
  starting transfers between devices: 60.9 us -> 32.8 us
  Pallas kernels: 277 us -> 272 us
    ppermute x33 -> x20, starting transfers between devices: 46.3 us -> 22 us  [flip(): return lax.ppermute(x, 'dp', [(i, i ^ bit) for i in range(16)])]
    ppermute x11 -> x9, waiting for transfers between devices: 40.8 us -> 21.3 us  [exchange(): return lax.ppermute(x, 'blk', swap)]
    ppermute x33 -> x20, waiting for transfers between devices: 37.9 us -> 24.3 us  [flip(): return lax.ppermute(x, 'dp', [(i, i ^ bit) for i in range(16)])]
    pallas_call x10 -> x8, Pallas kernels: 74.5 us -> 68.8 us  [the longest x6 49.4 us: flat_grad(): pl.pallas_call(partial(flat_grad_body, counts, received is not None), nam...]
    convert_element_type x6 -> x11, other arithmetic: 6 us -> 10.3 us  [the longest x3 5.18 us: columns_by_y(): total = total.astype(bf16).reshape(4, -1, total.shape[1])]
    ppermute x11 -> x9, starting transfers between devices: 14.6 us -> 10.8 us  [exchange(): return lax.ppermute(x, 'blk', swap)]
  transfers between devices with their start and end apart: 44 -> 29, of which waited for: 16 -> 9; matrix products, arithmetic and copies ran while one was open for 7% -> 8% of each run, Pallas kernels for 37% -> 54%
where the time goes in v4:
time: 395 us; the launch traced here: 388 us
  Pallas kernels  272 us (69%)
  waiting for transfers between devices  45.6 us (12%)
  starting transfers between devices  32.8 us (8%)
  other arithmetic  22.3 us (6%)
  local copies, waits for them, and re-layouts  13.7 us (3%)
    pallas_call x2, Pallas kernels, middle_pass(): pl.pallas_call(middle_body, name='middle_pass', grid_spec=pltpu.PrefetchS...  102 us
    pallas_call x6, Pallas kernels, flat_grad(): pl.pallas_call(partial(flat_grad_body, counts, received is not None), nam...  49.4 us
    pallas_call x2, Pallas kernels, attend_back(): pl.pallas_call(partial(attend_back_body, scale), name='attend_back', grid...  39.4 us
    pallas_call x1, Pallas kernels, attend(): pl.pallas_call(attend_body, name='attend', grid_spec=pltpu.PrefetchScalar...  25 us
    ppermute x20, waiting for transfers between devices, flip(): return lax.ppermute(x, 'dp', [(i, i ^ bit) for i in range(16)])  24.3 us
    ppermute x20, starting transfers between devices, flip(): return lax.ppermute(x, 'dp', [(i, i ^ bit) for i in range(16)])  22 us
    ppermute x9, waiting for transfers between devices, exchange(): return lax.ppermute(x, 'blk', swap)  21.3 us
    pallas_call x2, Pallas kernels, tall_grad(): pl.pallas_call(partial(tall_grad_body, received is not None), name='tall_...  19.4 us
  transfers between devices with their start and end apart: 29, of which 9 were waited for; matrix products, arithmetic and copies ran while one was open for 8% of the time, Pallas kernels for 54%

profile of v4, /device:TPU:0, one launch (start us, length us, event | category | flops | bytes accessed | tf_op | source)
XLA Modules:
  0.0 387.8 jit_solution(2704633286565055511)
XLA Ops:
  2.2 3.0 collective-permute-start
  8.8 8.9 %project_qkv.2 = (bf16[2,1024,512]{2,1,0:T(8,128)(2,1)}, bf16[1024,3072]{1,0:T(8,128)(2,1)}) custom-call(s32[1]{0:T(128)} %bitcast.at, bf16[2,512,1024]{2,1,0:T(8,128)(2,1)} %tok.5, f32[1,1024]{1,0:T(1,128)} %bitcast.142, f32[1,1024]{1,0:T(1,128)} %bitcast.152, bf16[1024,3072]{1,0:T(8,128)(2,1)} %w.7, f32[1,3072]{1,0:T(1,128)} %bitcast.138), custom_call_target="tpu_custom_call" | custom-call | flops 3221225472 | bytes 11534336 | tf_op jit(solution)/shard_map/project_qkv/pallas_call | solution.py:104
  18.5 10.7 %collective-permute-done.tok = bf16[1,512,1024]{2,1,0:T(8,128)(2,1)S(1)} collective-permute-done((bf16[1,512,1024]{2,1,0:T(8,128)(2,1)S(1)}, bf16[1,512,1024]{2,1,0:T(8,128)(2,1)S(1)}, u32[]{:S(2)}, u32[]{:S(2)}) %collective-permute-start) | collective-permute-done | bytes 1048608 | tf_op jit(solution)/shard_map/ppermute | solution.py:1076
  30.2 8.9 %project_qkv.3 = (bf16[2,1024,512]{2,1,0:T(8,128)(2,1)}, bf16[1024,3072]{1,0:T(8,128)(2,1)}) custom-call(s32[1]{0:T(128)} %constant.138.clone.1.at, bf16[1,512,1024]{2,1,0:T(8,128)(2,1)} %copy-done.3, f32[1,1024]{1,0:T(1,128)} %bitcast.143, f32[1,1024]{1,0:T(1,128)} %bitcast.153, ...), custom_call_target="tpu_custom_call", output_to_operand_aliasing={{0}: (6, {}), {1}: (7, {})} | custom-call | flops 3221225472 | bytes 11534336 | tf_op jit(solution)/shard_map/project_qkv/pallas_call | solution.py:104
  39.1 25.0 %attend.1 = (bf16[2,512,1024]{2,1,0:T(8,128)(2,1)}, f32[8,4,8,256]{3,2,1,0:T(8,128)}) custom-call(s32[17]{0:T(128)} %pad_add_fusion.tab, bf16[2,512,3072]{2,1,0:T(8,128)(2,1)} %bitcast.119, bf16[2,512,3072]{2,1,0:T(8,128)(2,1)} %bitcast.120, bf16[2,512,3072]{2,1,0:T(8,128)(2,1)} %bitcast.121, f32[1,1024]{1,0:T(1,128)} %copy-done.9), custom_call_target="tpu_custom_call" | custom-call | flops 17179869184 | bytes 12582912 | tf_op jit(solution)/shard_map/attend/pallas_call | solution.py:210
  64.1 50.6 %middle_pass.2 = (bf16[512,1024]{1,0:T(8,128)(2,1)}, f32[512,1024]{1,0:T(8,128)}, f32[8,1024]{1,0:T(8,128)}, f32[8,4096]{1,0:T(8,128)}, bf16[2,1024,512]{2,1,0:T...) custom-call(s32[1]{0:T(128)} %constant.138.clone.1.at, ...), custom_call_target="tpu_custom_call" | custom-call | flops 19327352832 | bytes 37748736 | tf_op jit(solution)/shard_map/middle_pass/pallas_call | solution.py:519
  114.7 2.1 collective-permute-start.2
  116.8 51.0 %middle_pass.3 = (f32[2,512,1024]{2,1,0:T(8,128)}, f32[512,1024]{1,0:T(8,128)}, f32[8,1024]{1,0:T(8,128)}, f32[8,4096]{1,0:T(8,128)}, bf16[2,1024,512]{2,1,0:T(8...) custom-call(s32[1]{0:T(128)} %bitcast.at, ...), custom_call_target="tpu_custom_call", output_to_operand_aliasing={{4}: (9, {}), {5}: (10, {}), {6}: (11, {}), {7}: (12, {}), ... | custom-call | flops 19327352832 | bytes 37748736 | tf_op jit(solution)/shard_map/middle_pass/pallas_call | solution.py:519
  169.4 12.0 %flat_grad.6 = bf16[2,256,5120]{2,1,0:T(8,128)(2,1)} custom-call(s32[3]{0:T(128)} %add_add_fusion.1.tab, bf16[2,1024,512]{2,1,0:T(8,128)(2,1)} %get-tuple-element.101.refs_0_, bf16[2,1024,512]{2,1,0:T(8,128)(2,1)} %get-tuple-element.97.refs_1_, bf16[1024,4096]{1,0:T(8,128)(2,1)} %get-tuple-element.98.refs_2_, bf16[1024,1024]{1,0:T(8,128)(2,1)} %get-tuple-element.99.refs_3_), custom_call_target="tpu_custom_call" | custom-call | flops 5368709120 | bytes 32505856 | tf_op jit(solution)/shard_map/flat_grad/pallas_call | solution.py:739
  181.5 9.2 %tall_grad.2 = bf16[2,2048,512]{2,1,0:T(8,128)(2,1)} custom-call(s32[3]{0:T(128)} %add_add_fusion.1.tab, bf16[1024,4096]{1,0:T(8,128)(2,1)} %get-tuple-element.104.refs_0_.refs_1_, bf16[1024,4096]{1,0:T(8,128)(2,1)} %get-tuple-element.104.refs_0_.refs_1_, bf16[2,512,1024]{2,1,0:T(8,128)(2,1)} %refs_2_.3, bf16[1,512,1024]{2,1,0:T(8,128)(2,1)} %collective-permute-done.1.cot.refs_3_), custom_call_target="tpu_custom_call" | custom-call | flops 4294967296 | bytes 14680064 | tf_op jit(solution)/shard_map/tall_grad/pallas_call | solution.py:678
  192.4 12.7 %flat_grad.7 = (bf16[256,5120]{1,0:T(8,128)(2,1)}, bf16[256,5120]{1,0:T(8,128)(2,1)}) custom-call(s32[3]{0:T(128)} %add_add_fusion.tab, bf16[2,1024,512]{2,1,0:T(8,128)(2,1)} %get-tuple-element.101.refs_0_, bf16[2,1024,512]{2,1,0:T(8,128)(2,1)} %get-tuple-element.97.refs_1_, bf16[1024,4096]{1,0:T(8,128)(2,1)} %get-tuple-element.98.refs_2_, ...), custom_call_target="tpu_custom_call" | custom-call | flops 5368709120 | bytes 32505856 | tf_op jit(solution)/shard_map/flat_grad/pallas_call | solution.py:739
  206.6 10.1 %tall_grad.3 = (bf16[2048,512]{1,0:T(8,128)(2,1)}, bf16[2048,512]{1,0:T(8,128)(2,1)}) custom-call(s32[3]{0:T(128)} %add_add_fusion.tab, bf16[1024,4096]{1,0:T(8,128)(2,1)} %get-tuple-element.104.refs_0_.refs_1_, bf16[1024,4096]{1,0:T(8,128)(2,1)} %get-tuple-element.104.refs_0_.refs_1_, bf16[2,512,1024]{2,1,0:T(8,128)(2,1)} %refs_2_.3, ...), custom_call_target="tpu_custom_call" | custom-call | flops 4294967296 | bytes 14680064 | tf_op jit(solution)/shard_map/tall_grad/pallas_call | solution.py:678
  217.2 19.5 %attend_back.2 = (bf16[3,2,512,512]{3,2,1,0:T(8,128)(2,1)}, f32[4,8,128]{2,1,0:T(8,128)}) custom-call(s32[17]{0:T(128)} %pad_add_fusion.tab, bf16[2,512,3072]{2,1,0:T(8,128)(2,1)} %bitcast.122, bf16[2,512,3072]{2,1,0:T(8,128)(2,1)} %bitcast.123, bf16[2,512,3072]{2,1,0:T(8,128)(2,1)} %bitcast.124, bf16[2,512,1024]{2,1,0:T(8,128)(2,1)} %get-tuple-element.84.ho.heads_out, ...), custom_call_target="tpu_custom_call" | custom-call | flops 21474836480 | bytes 12582912 | tf_op jit(solution)/shard_map/attend_back/pallas_call | solution.py:312
  236.7 6.0 %flat_grad.8 = bf16[2,256,1536]{2,1,0:T(8,128)(2,1)} custom-call(s32[3]{0:T(128)} %add_add_fusion.1.tab, bf16[2,1024,512]{2,1,0:T(8,128)(2,1)} %get-tuple-element.124.refs_0_, bf16[3,1024,512]{2,1,0:T(8,128)(2,1)} %bitcast.108), custom_call_target="tpu_custom_call" | custom-call | flops 100663296 | bytes 655360 | tf_op jit(solution)/shard_map/flat_grad/pallas_call | solution.py:739
  242.7 19.9 %attend_back.3 = (bf16[3,2,512,512]{3,2,1,0:T(8,128)(2,1)}, f32[4,8,128]{2,1,0:T(8,128)}) custom-call(s32[17]{0:T(128)} %pad_add_fusion.tab, bf16[2,512,3072]{2,1,0:T(8,128)(2,1)} %bitcast.125, bf16[2,512,3072]{2,1,0:T(8,128)(2,1)} %bitcast.126, bf16[2,512,3072]{2,1,0:T(8,128)(2,1)} %bitcast.127, bf16[2,512,1024]{2,1,0:T(8,128)(2,1)} %get-tuple-element.84.ho.heads_out, ...), custom_call_target="tpu_custom_call" | custom-call | flops 21474836480 | bytes 12582912 | tf_op jit(solution)/shard_map/attend_back/pallas_call | solution.py:312
  264.3 2.3 add_convert_fusion.1
  268.7 2.4 add_convert_fusion
  273.2 6.1 %flat_grad.9 = bf16[2,256,1536]{2,1,0:T(8,128)(2,1)} custom-call(s32[3]{0:T(128)} %add_add_fusion.1.tab, bf16[2,1024,512]{2,1,0:T(8,128)(2,1)} %get-tuple-element.124.refs_0_, bf16[3,1024,512]{2,1,0:T(8,128)(2,1)} %bitcast.112), custom_call_target="tpu_custom_call" | custom-call | flops 100663296 | bytes 655360 | tf_op jit(solution)/shard_map/flat_grad/pallas_call | solution.py:739
  281.2 6.3 %flat_grad.10 = (bf16[256,1536]{1,0:T(8,128)(2,1)}, bf16[256,1536]{1,0:T(8,128)(2,1)}) custom-call(s32[3]{0:T(128)} %add_add_fusion.tab, bf16[2,1024,512]{2,1,0:T(8,128)(2,1)} %get-tuple-element.124.refs_0_, bf16[3,1024,512]{2,1,0:T(8,128)(2,1)} %bitcast.109, bf16[2,256,1536]{2,1,0:T(8,128)(2,1)} %collective-permute-done.7.refs_2_), custom_call_target="tpu_custom_call" | custom-call | flops 100663296 | bytes 655360 | tf_op jit(solution)/shard_map/flat_grad/pallas_call | solution.py:739
  288.7 9.2 %first_back.2 = (bf16[512,1024]{1,0:T(8,128)(2,1)}, f32[8,1024]{1,0:T(8,128)}) custom-call(s32[1]{0:T(128)} %constant.138.clone.1.at, bf16[3,1024,512]{2,1,0:T(8,128)(2,1)} %bitcast.110, bf16[3,1024,512]{2,1,0:T(8,128)(2,1)} %bitcast.113, bf16[1024,3072]{1,0:T(8,128)(2,1)} %w.7, bf16[1,512,1024]{2,1,0:T(8,128)(2,1)} %copy-done.3, ...), custom_call_target="tpu_custom_call" | custom-call | flops 3221225472 | bytes 14680064 | tf_op jit(solution)/shard_map/first_back/pallas_call | solution.py:616
  303.7 6.3 %flat_grad.11 = (bf16[256,1536]{1,0:T(8,128)(2,1)}, bf16[256,1536]{1,0:T(8,128)(2,1)}) custom-call(s32[3]{0:T(128)} %add_add_fusion.tab, bf16[2,1024,512]{2,1,0:T(8,128)(2,1)} %get-tuple-element.124.refs_0_, bf16[3,1024,512]{2,1,0:T(8,128)(2,1)} %bitcast.114, bf16[2,256,1536]{2,1,0:T(8,128)(2,1)} %collective-permute-done.9.refs_2_), custom_call_target="tpu_custom_call" | custom-call | flops 100663296 | bytes 655360 | tf_op jit(solution)/shard_map/flat_grad/pallas_call | solution.py:739
  313.2 9.7 %first_back.3 = (f32[2,512,1024]{2,1,0:T(8,128)}, f32[8,1024]{1,0:T(8,128)}) custom-call(s32[1]{0:T(128)} %bitcast.at, bf16[3,1024,512]{2,1,0:T(8,128)(2,1)} %bitcast.111, bf16[3,1024,512]{2,1,0:T(8,128)(2,1)} %bitcast.115, bf16[1024,3072]{1,0:T(8,128)(2,1)} %w.7, bf16[2,512,1024]{2,1,0:T(8,128)(2,1)} %tok.5, f32[512,1024]{1,0:T(8,128)} %get-tuple-element.129.grad_middle, ...), custom_call_target="tpu_custom_call" | custom-call | flops 3221225472 | bytes 14680064 | tf_op jit(solution)/shard_map/first_back/pallas_call | solution.py:616
  325.3 2.6 collective-permute-start.28
  331.9 5.0 %collective-permute-done.13 = f32[23,1024]{1,0:T(8,128)S(1)} collective-permute-done((f32[23,1024]{1,0:T(8,128)S(1)}, f32[23,1024]{1,0:T(8,128)S(1)}, u32[]{:S(2)}, u32[]{:S(2)}) %collective-permute-start.13) | collective-permute-done | bytes 94240 | tf_op jit(solution)/shard_map/ppermute | solution.py:1080
  337.0 3.6 collective-permute-start.14
  340.8 4.4 %collective-permute-done.14 = f32[23,1024]{1,0:T(8,128)S(1)} collective-permute-done((f32[23,1024]{1,0:T(8,128)S(1)}, f32[23,1024]{1,0:T(8,128)S(1)}, u32[]{:S(2)}, u32[]{:S(2)}) %collective-permute-start.14) | collective-permute-done | bytes 94240 | tf_op jit(solution)/shard_map/ppermute | solution.py:1080
  347.1 2.8 collective-permute-done.15
  351.1 3.5 collective-permute-done.16
  362.7 5.4 %collective-permute-done.22 = bf16[4,64,768]{2,1,0:T(8,128)(2,1)S(1)} collective-permute-done((bf16[4,64,768]{2,1,0:T(8,128)(2,1)S(1)}, bf16[4,64,768]{2,1,0:T(8,128)(2,1)S(1)}, u32[]{:S(2)}, u32[]{:S(2)}) %collective-permute-start.22) | collective-permute-done | bytes 393248 | tf_op jit(solution)/shard_map/ppermute | solution.py:1076
  368.2 2.7 collective-permute-start.23
  371.2 8.1 %collective-permute-done.23 = bf16[2,64,768]{2,1,0:T(8,128)(2,1)S(1)} collective-permute-done((bf16[2,64,768]{2,1,0:T(8,128)(2,1)S(1)}, bf16[2,64,768]{2,1,0:T(8,128)(2,1)S(1)}, u32[]{:S(2)}, u32[]{:S(2)}) %collective-permute-start.23) | collective-permute-done | bytes 196640 | tf_op jit(solution)/shard_map/ppermute | solution.py:1080
  381.7 4.0 %collective-permute-done.24 = bf16[64,768]{1,0:T(8,128)(2,1)S(1)} collective-permute-done((bf16[64,768]{1,0:T(8,128)(2,1)S(1)}, bf16[64,768]{1,0:T(8,128)(2,1)S(1)}, u32[]{:S(2)}, u32[]{:S(2)}) %collective-permute-start.24) | collective-permute-done | bytes 98336 | tf_op jit(solution)/shard_map/ppermute | solution.py:1080
  (185 shorter events, 51.7 us)
Async XLA Ops:
  2.2 27.0 %collective-permute-start = (bf16[1,512,1024]{2,1,0:T(8,128)(2,1)S(1)}, bf16[1,512,1024]{2,1,0:T(8,128)(2,1)S(1)}, u32[]{:S(2)}, u32[]{:S(2)}) collective-permute-start(bf16[1,512,1024]{2,1,0:T(8,128)(2,1)S(1)} %constant_dynamic-slice_fusion.8), channel_id=1, source_target_pairs={{0,1},{1,0},{2,3},{3,2},{4,5},{5,4},{6,7},{7,6},{8,9},{9,8},{10,11... | collective-permute-start | bytes 3145736 | tf_op jit(solution)/shard_map/ppermute | solution.py:1076
  5.3 58.7 %collective-permute-start.1 = (bf16[1,512,1024]{2,1,0:T(8,128)(2,1)S(1)}, bf16[1,512,1024]{2,1,0:T(8,128)(2,1)}, u32[]{:S(2)}, u32[]{:S(2)}) collective-permute-start(bf16[1,512,1024]{2,1,0:T(8,128)(2,1)S(1)} %constant_dynamic-slice_fusion.7), channel_id=1, source_target_pairs={{0,1},{1,0},{2,3},{3,2},{4,5},{5,4},{6,7},{7,6},{8,9},{9,8},{10,11... | collective-permute-start | bytes 3145736 | tf_op jit(solution)/shard_map/ppermute | solution.py:1076
  114.7 53.2 %collective-permute-start.2 = (bf16[512,1024]{1,0:T(8,128)(2,1)}, bf16[512,1024]{1,0:T(8,128)(2,1)S(1)}, u32[]{:S(2)}, u32[]{:S(2)}) collective-permute-start(bf16[512,1024]{1,0:T(8,128)(2,1)} %get-tuple-element.92), channel_id=1, source_target_pairs={{0,1},{1,0},{2,3},{3,2},{4,5},{5,4},{6,7},{7,6},{8,9},{9,8},{10,11... | collective-permute-start | bytes 3145736 | tf_op jit(solution)/shard_map/ppermute | solution.py:1076
  181.5 10.9 %collective-permute-start.3 = (bf16[2,256,5120]{2,1,0:T(8,128)(2,1)}, bf16[2,256,5120]{2,1,0:T(8,128)(2,1)}, u32[]{:S(2)}, u32[]{:S(2)}) collective-permute-start(bf16[2,256,5120]{2,1,0:T(8,128)(2,1)} %flat_grad.6), channel_id=1, source_target_pairs={{0,2},{2,0},{4,6},{6,4},{8,10},{10,8},{12,14},{14,12},{16,18},{18,... | collective-permute-start | bytes 15728648 | tf_op jit(solution)/shard_map/ppermute | solution.py:1080
  190.7 15.9 %collective-permute-start.4 = (bf16[2,2048,512]{2,1,0:T(8,128)(2,1)}, bf16[2,2048,512]{2,1,0:T(8,128)(2,1)}, u32[]{:S(2)}, u32[]{:S(2)}) collective-permute-start(bf16[2,2048,512]{2,1,0:T(8,128)(2,1)} %tall_grad.2), channel_id=1, source_target_pairs={{0,2},{2,0},{4,6},{6,4},{8,10},{10,8},{12,14},{14,12},{16,18},{18,... | collective-permute-start | bytes 12582920 | tf_op jit(solution)/shard_map/ppermute | solution.py:1080
  205.1 63.3 %collective-permute-start.5 = (bf16[256,5120]{1,0:T(8,128)(2,1)}, bf16[256,5120]{1,0:T(8,128)(2,1)}, u32[]{:S(2)}, u32[]{:S(2)}) collective-permute-start(bf16[256,5120]{1,0:T(8,128)(2,1)} %get-tuple-element.102), channel_id=1, source_target_pairs={{0,4},{2,6},{4,0},{6,2},{8,12},{10,14},{12,8},{14,10},{16,20},{18,... | collective-permute-start | bytes 7864328 | tf_op jit(solution)/shard_map/ppermute | solution.py:1080
  216.7 47.6 %collective-permute-start.6 = (bf16[2048,512]{1,0:T(8,128)(2,1)}, bf16[2048,512]{1,0:T(8,128)(2,1)}, u32[]{:S(2)}, u32[]{:S(2)}) collective-permute-start(bf16[2048,512]{1,0:T(8,128)(2,1)} %get-tuple-element.105), channel_id=1, source_target_pairs={{0,1},{1,0},{2,3},{3,2},{4,5},{5,4},{6,7},{7,6},{8,9},{9,8},{10,11... | collective-permute-start | bytes 6291464 | tf_op jit(solution)/shard_map/ppermute | solution.py:1076
  242.7 21.6 %copy-start.5 = (bf16[2048,512]{1,0:T(8,128)(2,1)S(1)}, bf16[2048,512]{1,0:T(8,128)(2,1)}, u32[]{:S(2)}) copy-start(bf16[2048,512]{1,0:T(8,128)(2,1)} %get-tuple-element.115) | copy-start | bytes 6291460
  262.6 18.6 %collective-permute-start.7 = (bf16[2,256,1536]{2,1,0:T(8,128)(2,1)}, bf16[2,256,1536]{2,1,0:T(8,128)(2,1)}, u32[]{:S(2)}, u32[]{:S(2)}) collective-permute-start(bf16[2,256,1536]{2,1,0:T(8,128)(2,1)} %flat_grad.8), channel_id=1, source_target_pairs={{0,2},{2,0},{4,6},{6,4},{8,10},{10,8},{12,14},{14,12},{16,18},{18,... | collective-permute-start | bytes 4718600 | tf_op jit(solution)/shard_map/ppermute | solution.py:1080
  267.8 31.6 %collective-permute-start.8 = (bf16[4,256,512]{2,1,0:T(8,128)(2,1)}, bf16[4,256,512]{2,1,0:T(8,128)(2,1)}, u32[]{:S(2)}, u32[]{:S(2)}) collective-permute-start(bf16[4,256,512]{2,1,0:T(8,128)(2,1)} %get-tuple-element.151), channel_id=1, source_target_pairs={{0,4},{2,6},{4,0},{6,2},{8,12},{10,14},{12,8},{14,10},{16,20},{18,... | collective-permute-start | bytes 3145736 | tf_op jit(solution)/shard_map/ppermute | solution.py:1080
  272.6 38.3 %collective-permute-start.10 = (bf16[4,64,2560]{2,1,0:T(8,128)(2,1)}, bf16[4,64,2560]{2,1,0:T(8,128)(2,1)}, u32[]{:S(2)}, u32[]{:S(2)}) collective-permute-start(bf16[4,64,2560]{2,1,0:T(8,128)(2,1)} %pad_maximum_fusion.1), channel_id=1, source_target_pairs={{0,1},{1,0},{2,3},{3,2},{4,5},{5,4},{6,7},{7,6},{8,9},{9,8},{10,11... | collective-permute-start | bytes 3932168 | tf_op jit(solution)/shard_map/ppermute | solution.py:1076
  279.3 24.4 %collective-permute-start.9 = (bf16[2,256,1536]{2,1,0:T(8,128)(2,1)}, bf16[2,256,1536]{2,1,0:T(8,128)(2,1)}, u32[]{:S(2)}, u32[]{:S(2)}) collective-permute-start(bf16[2,256,1536]{2,1,0:T(8,128)(2,1)} %flat_grad.9), channel_id=1, source_target_pairs={{0,2},{2,0},{4,6},{6,4},{8,10},{10,8},{12,14},{14,12},{16,18},{18,... | collective-permute-start | bytes 4718600 | tf_op jit(solution)/shard_map/ppermute | solution.py:1080
  287.6 37.8 %collective-permute-start.17 = (bf16[256,1536]{1,0:T(8,128)(2,1)}, bf16[256,1536]{1,0:T(8,128)(2,1)}, u32[]{:S(2)}, u32[]{:S(2)}) collective-permute-start(bf16[256,1536]{1,0:T(8,128)(2,1)} %get-tuple-element.118), channel_id=1, source_target_pairs={{0,4},{2,6},{4,0},{6,2},{8,12},{10,14},{12,8},{14,10},{16,20},{18,... | collective-permute-start | bytes 2359304 | tf_op jit(solution)/shard_map/ppermute | solution.py:1080
  298.0 32.1 %collective-permute-start.11 = (bf16[512,1024]{1,0:T(8,128)(2,1)}, bf16[512,1024]{1,0:T(8,128)(2,1)S(1)}, u32[]{:S(2)}, u32[]{:S(2)}) collective-permute-start(bf16[512,1024]{1,0:T(8,128)(2,1)} %get-tuple-element.122), channel_id=1, source_target_pairs={{0,1},{1,0},{2,3},{3,2},{4,5},{5,4},{6,7},{7,6},{8,9},{9,8},{10,11... | collective-permute-start | bytes 3145736 | tf_op jit(solution)/shard_map/ppermute | solution.py:1076
  302.1 21.7 %collective-permute-start.25 = (bf16[2,256,512]{2,1,0:T(8,128)(2,1)}, bf16[2,256,512]{2,1,0:T(8,128)(2,1)}, u32[]{:S(2)}, u32[]{:S(2)}) collective-permute-start(bf16[2,256,512]{2,1,0:T(8,128)(2,1)} %get-tuple-element.155), channel_id=1, source_target_pairs={{0,8},{2,10},{4,12},{6,14},{8,0},{10,2},{12,4},{14,6},{16,24},{18,... | collective-permute-start | bytes 1572872 | tf_op jit(solution)/shard_map/ppermute | solution.py:1080
  310.0 48.3 %collective-permute-start.21 = (bf16[256,1536]{1,0:T(8,128)(2,1)}, bf16[256,1536]{1,0:T(8,128)(2,1)}, u32[]{:S(2)}, u32[]{:S(2)}) collective-permute-start(bf16[256,1536]{1,0:T(8,128)(2,1)} %get-tuple-element.125), channel_id=1, source_target_pairs={{0,4},{2,6},{4,0},{6,2},{8,12},{10,14},{12,8},{14,10},{16,20},{18,... | collective-permute-start | bytes 2359304 | tf_op jit(solution)/shard_map/ppermute | solution.py:1080
  312.7 48.6 %collective-permute-start.26 = (bf16[2,64,2560]{2,1,0:T(8,128)(2,1)S(1)}, bf16[2,64,2560]{2,1,0:T(8,128)(2,1)S(1)}, u32[]{:S(2)}, u32[]{:S(2)}) collective-permute-start(bf16[2,64,2560]{2,1,0:T(8,128)(2,1)S(1)} %get-tuple-element.153), channel_id=1, source_target_pairs={{0,8},{2,10},{4,12},{6,14},{8,0},{10,2},{12,4},{14,6},{16,24},{18,... | collective-permute-start | bytes 1966088 | tf_op jit(solution)/shard_map/ppermute | solution.py:1080
  323.8 5.6 %collective-permute-start.12 = (f32[23,1024]{1,0:T(8,128)S(1)}, f32[23,1024]{1,0:T(8,128)S(1)}, u32[]{:S(2)}, u32[]{:S(2)}) collective-permute-start(f32[23,1024]{1,0:T(8,128)S(1)} %pad_maximum_fusion.3), channel_id=1, source_target_pairs={{0,2},{2,0},{4,6},{6,4},{8,10},{10,8},{12,14},{14,12},{16,18},{18,... | collective-permute-start | bytes 282632 | tf_op jit(solution)/shard_map/ppermute | solution.py:1080
  325.3 20.9 %collective-permute-start.28 = (bf16[256,512]{1,0:T(8,128)(2,1)S(1)}, bf16[256,512]{1,0:T(8,128)(2,1)S(1)}, u32[]{:S(2)}, u32[]{:S(2)}) collective-permute-start(bf16[256,512]{1,0:T(8,128)(2,1)S(1)} %dynamic-slice_bitcast_fusion.8), channel_id=1, source_target_pairs={{0,16},{2,18},{4,20},{6,22},{8,24},{10,26},{12,28},{14,30},{16,0},... | collective-permute-start | bytes 786440 | tf_op jit(solution)/shard_map/ppermute | solution.py:1080
  329.4 21.1 %collective-permute-start.18 = (bf16[4,64,768]{2,1,0:T(8,128)(2,1)S(1)}, bf16[4,64,768]{2,1,0:T(8,128)(2,1)S(1)}, u32[]{:S(2)}, u32[]{:S(2)}) collective-permute-start(bf16[4,64,768]{2,1,0:T(8,128)(2,1)S(1)} %constant_dynamic-slice_fusion.1), channel_id=1, source_target_pairs={{0,1},{1,0},{2,3},{3,2},{4,5},{5,4},{6,7},{7,6},{8,9},{9,8},{10,11... | collective-permute-start | bytes 1179656 | tf_op jit(solution)/shard_map/ppermute | solution.py:1076
  330.0 6.9 %collective-permute-start.13 = (f32[23,1024]{1,0:T(8,128)S(1)}, f32[23,1024]{1,0:T(8,128)S(1)}, u32[]{:S(2)}, u32[]{:S(2)}) collective-permute-start(f32[23,1024]{1,0:T(8,128)S(1)} %fusion.4), channel_id=1, source_target_pairs={{0,8},{2,10},{4,12},{6,14},{8,0},{10,2},{12,4},{14,6},{16,24},{18,... | collective-permute-start | bytes 282632 | tf_op jit(solution)/shard_map/ppermute | solution.py:1080
  337.0 8.2 %collective-permute-start.14 = (f32[23,1024]{1,0:T(8,128)S(1)}, f32[23,1024]{1,0:T(8,128)S(1)}, u32[]{:S(2)}, u32[]{:S(2)}) collective-permute-start(f32[23,1024]{1,0:T(8,128)S(1)} %add.194), channel_id=1, source_target_pairs={{0,16},{2,18},{4,20},{6,22},{8,24},{10,26},{12,28},{14,30},{16,0},... | collective-permute-start | bytes 282632 | tf_op jit(solution)/shard_map/ppermute | solution.py:1080
  340.8 16.3 %copy-start.29 = (f32[2,512,1024]{2,1,0:T(8,128)}, f32[2,512,1024]{2,1,0:T(8,128)S(1)}, u32[]{:S(2)}) copy-start(f32[2,512,1024]{2,1,0:T(8,128)S(1)} %convert_dynamic-update-slice_fusion) | copy-start | bytes 12582916
  345.2 13.1 %copy-start.7 = (bf16[256,1536]{1,0:T(8,128)(2,1)S(1)}, bf16[256,1536]{1,0:T(8,128)(2,1)}, u32[]{:S(2)}) copy-start(bf16[256,1536]{1,0:T(8,128)(2,1)} %get-tuple-element.126) | copy-start | bytes 2359300
  345.2 4.7 %collective-permute-start.15 = (f32[23,1024]{1,0:T(8,128)S(1)}, f32[23,1024]{1,0:T(8,128)S(1)}, u32[]{:S(2)}, u32[]{:S(2)}) collective-permute-start(f32[23,1024]{1,0:T(8,128)S(1)} %add.195), channel_id=1, source_target_pairs={{0,4},{2,6},{4,0},{6,2},{8,12},{10,14},{12,8},{14,10},{16,20},{18,... | collective-permute-start | bytes 282632 | tf_op jit(solution)/shard_map/ppermute | solution.py:1080
  349.9 4.7 %collective-permute-start.16 = (f32[23,1024]{1,0:T(8,128)S(1)}, f32[23,1024]{1,0:T(8,128)S(1)}, u32[]{:S(2)}, u32[]{:S(2)}) collective-permute-start(f32[23,1024]{1,0:T(8,128)S(1)} %add.196), channel_id=1, source_target_pairs={{0,1},{1,0},{2,3},{3,2},{4,5},{5,4},{6,7},{7,6},{8,9},{9,8},{10,11... | collective-permute-start | bytes 282632 | tf_op jit(solution)/shard_map/ppermute | solution.py:1076
  350.6 6.4 %collective-permute-start.19 = (bf16[2,64,768]{2,1,0:T(8,128)(2,1)S(1)}, bf16[2,64,768]{2,1,0:T(8,128)(2,1)S(1)}, u32[]{:S(2)}, u32[]{:S(2)}) collective-permute-start(bf16[2,64,768]{2,1,0:T(8,128)(2,1)S(1)} %dynamic-slice_bitcast_fusion.10), channel_id=1, source_target_pairs={{0,8},{2,10},{4,12},{6,14},{8,0},{10,2},{12,4},{14,6},{16,24},{18,... | collective-permute-start | bytes 589832 | tf_op jit(solution)/shard_map/ppermute | solution.py:1080
  357.1 13.8 %collective-permute-start.20 = (bf16[64,768]{1,0:T(8,128)(2,1)S(1)}, bf16[64,768]{1,0:T(8,128)(2,1)S(1)}, u32[]{:S(2)}, u32[]{:S(2)}) collective-permute-start(bf16[64,768]{1,0:T(8,128)(2,1)S(1)} %dynamic-slice_bitcast_fusion.12), channel_id=1, source_target_pairs={{0,16},{2,18},{4,20},{6,22},{8,24},{10,26},{12,28},{14,30},{16,0},... | collective-permute-start | bytes 294920 | tf_op jit(solution)/shard_map/ppermute | solution.py:1080
  359.7 8.4 %collective-permute-start.22 = (bf16[4,64,768]{2,1,0:T(8,128)(2,1)S(1)}, bf16[4,64,768]{2,1,0:T(8,128)(2,1)S(1)}, u32[]{:S(2)}, u32[]{:S(2)}) collective-permute-start(bf16[4,64,768]{2,1,0:T(8,128)(2,1)S(1)} %constant_dynamic-slice_fusion), channel_id=1, source_target_pairs={{0,1},{1,0},{2,3},{3,2},{4,5},{5,4},{6,7},{7,6},{8,9},{9,8},{10,11... | collective-permute-start | bytes 1179656 | tf_op jit(solution)/shard_map/ppermute | solution.py:1076
  361.5 18.7 %collective-permute-start.27 = (bf16[64,2560]{1,0:T(8,128)(2,1)S(1)}, bf16[64,2560]{1,0:T(8,128)(2,1)S(1)}, u32[]{:S(2)}, u32[]{:S(2)}) collective-permute-start(bf16[64,2560]{1,0:T(8,128)(2,1)S(1)} %dynamic-slice_bitcast_fusion.6), channel_id=1, source_target_pairs={{0,16},{2,18},{4,20},{6,22},{8,24},{10,26},{12,28},{14,30},{16,0},... | collective-permute-start | bytes 983048 | tf_op jit(solution)/shard_map/ppermute | solution.py:1080
  368.2 11.1 %collective-permute-start.23 = (bf16[2,64,768]{2,1,0:T(8,128)(2,1)S(1)}, bf16[2,64,768]{2,1,0:T(8,128)(2,1)S(1)}, u32[]{:S(2)}, u32[]{:S(2)}) collective-permute-start(bf16[2,64,768]{2,1,0:T(8,128)(2,1)S(1)} %dynamic-slice_bitcast_fusion.9), channel_id=1, source_target_pairs={{0,8},{2,10},{4,12},{6,14},{8,0},{10,2},{12,4},{14,6},{16,24},{18,... | collective-permute-start | bytes 589832 | tf_op jit(solution)/shard_map/ppermute | solution.py:1080
  379.4 6.4 %collective-permute-start.24 = (bf16[64,768]{1,0:T(8,128)(2,1)S(1)}, bf16[64,768]{1,0:T(8,128)(2,1)S(1)}, u32[]{:S(2)}, u32[]{:S(2)}) collective-permute-start(bf16[64,768]{1,0:T(8,128)(2,1)S(1)} %dynamic-slice_bitcast_fusion.11), channel_id=1, source_target_pairs={{0,16},{2,18},{4,20},{6,22},{8,24},{10,26},{12,28},{14,30},{16,0},... | collective-permute-start | bytes 294920 | tf_op jit(solution)/shard_map/ppermute | solution.py:1080
  (27 other events, 180.5 us)

commit v5 on v4

--- a/solution.py
+++ b/solution.py
@@ -363,7 +363,6 @@
     n, d = ho.shape
     chunks, _, fc = w1s.shape
     ff = fc * chunks
-    c = step % chunks
     ahead = 2
 
     def fetch(k):
@@ -407,59 +406,64 @@
 
         lax.fori_loop(0, strips, one, 0)
 
+    @pl.when(step == 0)
+    def _():
+        total[...] = jnp.zeros_like(total)
+
     @pl.when(step < chunks - ahead)
     def _():
         for copy in fetch(step + ahead):
             copy.start()
 
-    @pl.when(step < chunks)
-    def _():
-        for copy in fetch(step):
+    sub = 256
+
+    def first_phase(k):
+        for copy in fetch(k):
             copy.wait()
-        h = mm(d_out[...], w1s[c]) + vec4[0:1, :]
-        back[c] = mm(cot[...], w2s[c], NT).astype(back.dtype)
-        a, b = gelu_parts(h)
-        act[c] = a
-        slope[c] = b.astype(slope.dtype)
-
-    @pl.when(step == 0)
-    def _():
-        total[...] = jnp.zeros_like(total)
-
-    @pl.when(step < chunks)
-    def _():
-        total[...] += fold(act[c])
-
-    @pl.when(step == chunks)
-    def _():
-        mean = jnp.sum(total[...], axis=1, keepdims=True) * (1.0 / ff)
-
-        def one(k, t):
-            centered = act[k] - mean
-            return t + fold(centered * centered)
-
-        square = lax.fori_loop(0, chunks, one, jnp.zeros_like(total))
-        stats[:, 2:3] = mean
-        stats[:, 3:4] = lax.rsqrt(jnp.sum(square, axis=1, keepdims=True) * (1.0 / ff) + eps)
-        total[...] = jnp.zeros_like(total)
-        total_u[...] = jnp.zeros_like(total_u)
-
-    here = pl.ds(pl.multiple_of(c * fc, fc), fc)
-
-    @pl.when((step >= chunks) & (step < 2 * chunks))
-    def _():
-        u = (act[c] - stats[:, 2:3]) * stats[:, 3:4]
-        act[c] = u
+        for at in range(0, fc, sub):
+            cs = slice(at, at + sub)
+            h = mm(d_out[...], w1s[k, :, cs]) + vec4[0:1, cs]
+            a, b = gelu_parts(h)
+            act[k, :, cs] = a
+            slope[k, :, cs] = b.astype(slope.dtype)
+            total[...] += fold(a)
+            back[k, :, cs] = mm(cot[...], w2s[k, cs, :], NT).astype(back.dtype)
+
+    def second_phase(k):
+        here = slice(k * fc, (k + 1) * fc)
+        u = (act[k] - stats[:, 2:3]) * stats[:, 3:4]
+        act[k] = u
         gain = vec4[1:2, :]
         m = (u * gain + vec4[2:3, :]).astype(bf16)
         mid_out[...] = m
-        acc[...] += mm(m, w2s[c])
-        gm = back[c].astype(f32)
+        acc[...] += mm(m, w2s[k])
+        gm = back[k].astype(f32)
         gmu = gm * u
         sums4[1:2, here] = row_sum(gmu)
         sums4[2:3, here] = row_sum(gm)
         total[...] += fold(gm * gain)
         total_u[...] += fold(gmu * gain)
+
+    def third_phase(k):
+        here = slice(k * fc, (k + 1) * fc)
+        e = back[k].astype(f32) * vec4[1:2, :]
+        grad_act = stats[:, 3:4] * (e - stats[:, 4:5] - act[k] * stats[:, 5:6])
+        gh = (grad_act * slope[k].astype(f32)).astype(bf16)
+        grad_hidden[...] = gh
+        sums4[0:1, here] = row_sum(gh.astype(f32))
+        acc[...] += mm(gh, w1s[k], NT)
+
+    @pl.when(step == chunks)
+    def _():
+        mean = jnp.sum(total[...], axis=1, keepdims=True) * (1.0 / ff)
+        square = jnp.zeros_like(total)
+        for k in range(chunks):
+            centered = act[k] - mean
+            square = square + fold(centered * centered)
+        stats[:, 2:3] = mean
+        stats[:, 3:4] = lax.rsqrt(jnp.sum(square, axis=1, keepdims=True) * (1.0 / ff) + eps)
+        total[...] = jnp.zeros_like(total)
+        total_u[...] = jnp.zeros_like(total_u)
 
     @pl.when(step == 2 * chunks)
     def _():
@@ -468,14 +472,9 @@
         output[...] = acc[...].astype(output.dtype)
         acc[...] = jnp.zeros_like(acc)
 
-    @pl.when(step >= 2 * chunks)
-    def _():
-        e = back[c].astype(f32) * vec4[1:2, :]
-        grad_act = stats[:, 3:4] * (e - stats[:, 4:5] - act[c] * stats[:, 5:6])
-        gh = (grad_act * slope[c].astype(f32)).astype(bf16)
-        grad_hidden[...] = gh
-        sums4[0:1, here] = row_sum(gh.astype(f32))
-        acc[...] += mm(gh, w1s[c], NT)
+    for phase, body in enumerate((first_phase, second_phase, third_phase)):
+        for k in range(chunks):
+            pl.when(step == phase * chunks + k)(partial(body, k))
 
     @pl.when(step == 3 * chunks - 1)
     def _():
@@ -1118,7 +1117,17 @@
     kept_at = b[None]
     sent_at = jnp.zeros((1,), jnp.int32)
 
-    lengths = lax.dynamic_slice_in_dim(doc_lengths, b, 1, 0)
+    def line(v):
+        return v.reshape(1, -1)
+
+    qkv_bias = jnp.concatenate([query_bias, jnp.zeros_like(query_bias), value_bias])
+    first_args = (line(norm1_gain), line(norm1_shift), qkv_weight, line(qkv_bias), scale)
+    early = project_qkv(kept_at, tokens, *first_args, 0, n)
+
+    def later(v):
+        return after(v, early[0])
+
+    lengths = lax.dynamic_slice_in_dim(later(doc_lengths), b, 1, 0)
     ends = running_sums(lengths)[0]
     firsts = (half_len // 2) * jnp.arange(4, dtype=jnp.int32)
     starts = jnp.max(jnp.where(ends[None, :] <= firsts[:, None], ends[None, :], 0), axis=1)
@@ -1126,20 +1135,16 @@
     tab = jnp.concatenate([b[None], allowed.reshape(16)])
     theirs = jnp.stack([1 - core, x, y])
     mine = jnp.stack([core, x, y])
-
-    def line(v):
-        return v.reshape(1, -1)
-
+    head_scales = later(head_scales)
     scale_row = jnp.broadcast_to(head_scales[:, None], (heads, head_dim)).reshape(1, d)
     vec = jnp.stack(
-        [out_bias, attn_gain, attn_shift, norm2_gain, norm2_shift, fc2_bias, scale_row[0], out_bias]
-    )
+        [later(out_bias), attn_gain, attn_shift, norm2_gain, norm2_shift, fc2_bias, scale_row[0], out_bias]
+    )
+    fc1_bias = later(fc1_bias)
     vec4 = jnp.stack([fc1_bias, mid_gain, mid_shift, fc1_bias])
-    qkv_bias = jnp.concatenate([query_bias, jnp.zeros_like(query_bias), value_bias])
-
-    first_args = (line(norm1_gain), line(norm1_shift), qkv_weight, line(qkv_bias), scale)
-    early = project_qkv(kept_at, tokens, *first_args, 0, n)
-    attn_in, qkv = project_qkv(sent_at, tok_in, *first_args, 1, n, early)
+
+    made = after(sent_at, tab, theirs, mine, scale_row, vec, vec4)
+    attn_in, qkv = project_qkv(made, tok_in, *first_args, 1, n, early)
     qkv = qkv.reshape(2, half_len, 3 * d)
     heads_out, logs = attend(tab, qkv, scale_row)
 
@@ -1228,40 +1233,47 @@
     )
     grad_back = exchange(grad_sent)
     fc2_parts = near_z(add_x(*held(fc2_parts, grad_sent)))
-    odd_parts = flat_grad(
-        mine, [(after(attn_in, grad_sent, *fc2_parts), odd)], d // 2, flip(odd_theirs, 1)
-    )
-    wide_parts = near_z(add_y(*held(wide_parts, *odd_parts)))
+    wide_parts = near_z(add_y(*held(wide_parts, *fc2_parts)))
     tokens_grad, sums_kept = first_back(
         kept_at, after(even, *wide_parts), odd, qkv_weight, tokens, mid_kept, line(norm1_gain), 0, True
     )
+    odd_parts = flat_grad(
+        mine, [(after(attn_in, tokens_grad), odd)], d // 2, flip(odd_theirs, 1)
+    )
+    dots = jnp.stack([dots_even[:, 0].reshape(2, 4, head_dim), dots_odd[:, 0].reshape(2, 4, head_dim)], axis=1)
+    head_scales_grad = jnp.sum(dots, axis=3).reshape(heads) / head_scales
+    head_scales_grad = jnp.pad(head_scales_grad, (0, d - heads))
+    total = jnp.concatenate(
+        [
+            (sums_sent + sums_kept)[:4],
+            head_scales_grad[None],
+            sums[:6],
+            sums4.reshape(8 * ff // d, d)[: 3 * ff // d],
+        ]
+    )
     fc2_parts = far_z(add_z(4, *held(fc2_parts, tokens_grad)))
     even_parts = columns_by_y(add_x(*held(even_parts, tokens_grad)))
+    total = after(total, *odd_parts)
+    odd_parts = columns_by_y(add_x(*odd_parts))
     wide_parts = far_z(add_z(4, *held(wide_parts, *fc2_parts, *even_parts)))
     tokens_grad = fill(tokens_grad, grad_back)
+    for move in (partial(flip, bit=1), partial(flip, bit=4), partial(flip, bit=8)):
+        total = total + move(total)
+    total = after(total, *odd_parts)
+    for move in (partial(flip, bit=2), exchange):
+        total = total + move(total)
     fc2_weight_grad = add_z(8, *fc2_parts)
-    odd_parts = columns_by_y(add_x(*odd_parts))
     even_parts = near_z(add_y(*even_parts))
     wide_grad = add_z(8, *wide_parts)
     fc1_weight_grad, out_weight_grad = wide_grad[:, : ff // 2], wide_grad[:, ff // 2 :]
     even_parts = far_z(add_z(4, *even_parts))
     odd_parts = far_z(add_z(4, *near_z(add_y(*odd_parts))))
     even_grad, odd_grad = (add_z(8, *parts) for parts in (even_parts, odd_parts))
+    first_sums, sums, sums4 = total[:5], total[5:11], total[11:].reshape(3, ff)
     run = d // 4
     qkv_weight_grad = jnp.stack(
         [even_grad.reshape(-1, 3, run), odd_grad.reshape(-1, 3, run)], axis=2
     ).reshape(-1, 6 * run)
-    tokens_grad = fill(tokens_grad, grad_back)
-    dots = jnp.stack([dots_even[:, 0].reshape(2, 4, head_dim), dots_odd[:, 0].reshape(2, 4, head_dim)], axis=1)
-    head_scales_grad = jnp.sum(dots, axis=3).reshape(heads) / head_scales
-    head_scales_grad = jnp.pad(head_scales_grad, (0, d - heads))
-    first_sums = (sums_sent + sums_kept)[:4]
-    total = jnp.concatenate(
-        [first_sums, head_scales_grad[None], sums[:6], sums4.reshape(8 * ff // d, d)[: 3 * ff // d]]
-    )
-    for move in (partial(flip, bit=1), partial(flip, bit=4), partial(flip, bit=8), partial(flip, bit=2), exchange):
-        total = total + move(total)
-    first_sums, sums, sums4 = total[:5], total[5:11], total[11:].reshape(3, ff)
     return (
         output,
         tokens_grad,

time: 395 us -> 440 us (1.11)
  Pallas kernels: 272 us -> 316 us
  starting transfers between devices: 32.8 us -> 28.1 us
    pallas_call x2, Pallas kernels: 102 us -> 146 us  [middle_pass(): pl.pallas_call(middle_body, name='middle_pass', grid_spec=pltpu.PrefetchS...]
    ppermute x20, starting transfers between devices: 22 us -> 16.9 us  [flip(): return lax.ppermute(x, 'dp', [(i, i ^ bit) for i in range(16)])]
  transfers between devices with their start and end apart: 29 -> 29, of which waited for: 9 -> 11; matrix products, arithmetic and copies ran while one was open for 8% -> 8% of each run, Pallas kernels for 54% -> 54%
where the time goes in v5:
time: 440 us; the launch traced here: 433 us
  Pallas kernels  316 us (72%)
  waiting for transfers between devices  47.3 us (11%)
  starting transfers between devices  28.1 us (6%)
  other arithmetic  25.6 us (6%)
  local copies, waits for them, and re-layouts  14.7 us (3%)
    pallas_call x2, Pallas kernels, middle_pass(): pl.pallas_call(middle_body, name='middle_pass', grid_spec=pltpu.PrefetchS...  146 us
    pallas_call x6, Pallas kernels, flat_grad(): pl.pallas_call(partial(flat_grad_body, counts, received is not None), nam...  49.2 us
    pallas_call x2, Pallas kernels, attend_back(): pl.pallas_call(partial(attend_back_body, scale), name='attend_back', grid...  39.4 us
    pallas_call x1, Pallas kernels, attend(): pl.pallas_call(attend_body, name='attend', grid_spec=pltpu.PrefetchScalar...  25 us
    ppermute x9, waiting for transfers between devices, exchange(): return lax.ppermute(x, 'blk', swap)  24.6 us
    ppermute x20, waiting for transfers between devices, flip(): return lax.ppermute(x, 'dp', [(i, i ^ bit) for i in range(16)])  22.6 us
    pallas_call x2, Pallas kernels, tall_grad(): pl.pallas_call(partial(tall_grad_body, received is not None), name='tall_...  19.4 us
    pallas_call x2, Pallas kernels, first_back(): pl.pallas_call(first_back_body, name='first_back', grid_spec=pltpu.Prefet...  19 us
  transfers between devices with their start and end apart: 29, of which 11 were waited for; matrix products, arithmetic and copies ran while one was open for 8% of the time, Pallas kernels for 54%

profile of v5, /device:TPU:0, one launch (start us, length us, event | category | flops | bytes accessed | tf_op | source)
XLA Modules:
  0.0 433.0 jit_solution(5653429865401067191)
XLA Ops:
  2.2 3.0 collective-permute-start
  6.4 9.0 %project_qkv.2 = (bf16[2,1024,512]{2,1,0:T(8,128)(2,1)}, bf16[1024,3072]{1,0:T(8,128)(2,1)}) custom-call(s32[1]{0:T(128)} %bitcast.at, bf16[2,512,1024]{2,1,0:T(8,128)(2,1)} %tok.5, f32[1,1024]{1,0:T(1,128)} %bitcast.142, f32[1,1024]{1,0:T(1,128)} %bitcast.155, bf16[1024,3072]{1,0:T(8,128)(2,1)} %w.7, f32[1,3072]{1,0:T(1,128)} %bitcast.140), custom_call_target="tpu_custom_call" | custom-call | flops 3221225472 | bytes 11534336 | tf_op jit(solution)/shard_map/project_qkv/pallas_call | solution.py:104
  18.7 10.5 %collective-permute-done.tok = bf16[1,512,1024]{2,1,0:T(8,128)(2,1)S(1)} collective-permute-done((bf16[1,512,1024]{2,1,0:T(8,128)(2,1)S(1)}, bf16[1,512,1024]{2,1,0:T(8,128)(2,1)S(1)}, u32[]{:S(2)}, u32[]{:S(2)}) %collective-permute-start) | collective-permute-done | bytes 1048608 | tf_op jit(solution)/shard_map/ppermute | solution.py:1075
  30.1 8.9 %project_qkv.3 = (bf16[2,1024,512]{2,1,0:T(8,128)(2,1)}, bf16[1024,3072]{1,0:T(8,128)(2,1)}) custom-call(s32[1]{0:T(128)} %constant.139.clone.1.at, bf16[1,512,1024]{2,1,0:T(8,128)(2,1)} %copy-done.3, f32[1,1024]{1,0:T(1,128)} %bitcast.143, f32[1,1024]{1,0:T(1,128)} %bitcast.156, ...), custom_call_target="tpu_custom_call", output_to_operand_aliasing={{0}: (6, {}), {1}: (7, {})} | custom-call | flops 3221225472 | bytes 11534336 | tf_op jit(solution)/shard_map/project_qkv/pallas_call | solution.py:104
  39.0 25.0 %attend.1 = (bf16[2,512,1024]{2,1,0:T(8,128)(2,1)}, f32[8,4,8,256]{3,2,1,0:T(8,128)}) custom-call(s32[17]{0:T(128)} %pad_add_fusion.tab, bf16[2,512,3072]{2,1,0:T(8,128)(2,1)} %bitcast.121, bf16[2,512,3072]{2,1,0:T(8,128)(2,1)} %bitcast.122, bf16[2,512,3072]{2,1,0:T(8,128)(2,1)} %bitcast.123, f32[1,1024]{1,0:T(1,128)} %copy-done.10), custom_call_target="tpu_custom_call" | custom-call | flops 17179869184 | bytes 12582912 | tf_op jit(solution)/shard_map/attend/pallas_call | solution.py:210
  64.0 68.8 %middle_pass.2 = (bf16[512,1024]{1,0:T(8,128)(2,1)}, f32[512,1024]{1,0:T(8,128)}, f32[8,1024]{1,0:T(8,128)}, f32[8,4096]{1,0:T(8,128)}, bf16[2,1024,512]{2,1,0:T...) custom-call(s32[1]{0:T(128)} %constant.139.clone.1.at, ...), custom_call_target="tpu_custom_call" | custom-call | flops 19327352832 | bytes 37748736 | tf_op jit(solution)/shard_map/middle_pass/pallas_call | solution.py:518
  132.8 2.1 collective-permute-start.2
  134.9 77.0 %middle_pass.3 = (f32[2,512,1024]{2,1,0:T(8,128)}, f32[512,1024]{1,0:T(8,128)}, f32[8,1024]{1,0:T(8,128)}, f32[8,4096]{1,0:T(8,128)}, bf16[2,1024,512]{2,1,0:T(8...) custom-call(s32[1]{0:T(128)} %bitcast.at, ...), custom_call_target="tpu_custom_call", output_to_operand_aliasing={{4}: (9, {}), {5}: (10, {}), {6}: (11, {}), {7}: (12, {}), ... | custom-call | flops 19327352832 | bytes 37748736 | tf_op jit(solution)/shard_map/middle_pass/pallas_call | solution.py:518
  213.5 11.9 %flat_grad.6 = bf16[2,256,5120]{2,1,0:T(8,128)(2,1)} custom-call(s32[3]{0:T(128)} %get-tuple-element.185.tab, bf16[2,1024,512]{2,1,0:T(8,128)(2,1)} %get-tuple-element.113.refs_0_, bf16[2,1024,512]{2,1,0:T(8,128)(2,1)} %get-tuple-element.109.refs_1_, bf16[1024,4096]{1,0:T(8,128)(2,1)} %get-tuple-element.110.refs_2_, ...), custom_call_target="tpu_custom_call" | custom-call | flops 5368709120 | bytes 32505856 | tf_op jit(solution)/shard_map/flat_grad/pallas_call | solution.py:738
  225.5 9.2 %tall_grad.2 = bf16[2,2048,512]{2,1,0:T(8,128)(2,1)} custom-call(s32[3]{0:T(128)} %get-tuple-element.185.tab, bf16[1024,4096]{1,0:T(8,128)(2,1)} %get-tuple-element.116.refs_0_.refs_1_, bf16[1024,4096]{1,0:T(8,128)(2,1)} %get-tuple-element.116.refs_0_.refs_1_, bf16[2,512,1024]{2,1,0:T(8,128)(2,1)} %refs_2_.3, ...), custom_call_target="tpu_custom_call" | custom-call | flops 4294967296 | bytes 14680064 | tf_op jit(solution)/shard_map/tall_grad/pallas_call | solution.py:677
  237.1 12.7 %flat_grad.7 = (bf16[256,5120]{1,0:T(8,128)(2,1)}, bf16[256,5120]{1,0:T(8,128)(2,1)}) custom-call(s32[3]{0:T(128)} %get-tuple-element.186.tab, bf16[2,1024,512]{2,1,0:T(8,128)(2,1)} %get-tuple-element.113.refs_0_, bf16[2,1024,512]{2,1,0:T(8,128)(2,1)} %get-tuple-element.109.refs_1_, bf16[1024,4096]{1,0:T(8,128)(2,1)} %get-tuple-element.110.refs_2_, ...), custom_call_target="tpu_custom_call" | custom-call | flops 5368709120 | bytes 32505856 | tf_op jit(solution)/shard_map/flat_grad/pallas_call | solution.py:738
  251.3 10.1 %tall_grad.3 = (bf16[2048,512]{1,0:T(8,128)(2,1)}, bf16[2048,512]{1,0:T(8,128)(2,1)}) custom-call(s32[3]{0:T(128)} %get-tuple-element.186.tab, bf16[1024,4096]{1,0:T(8,128)(2,1)} %get-tuple-element.116.refs_0_.refs_1_, bf16[1024,4096]{1,0:T(8,128)(2,1)} %get-tuple-element.116.refs_0_.refs_1_, bf16[2,512,1024]{2,1,0:T(8,128)(2,1)} %refs_2_.3, ...), custom_call_target="tpu_custom_call" | custom-call | flops 4294967296 | bytes 14680064 | tf_op jit(solution)/shard_map/tall_grad/pallas_call | solution.py:677
  262.0 19.5 %attend_back.2 = (bf16[3,2,512,512]{3,2,1,0:T(8,128)(2,1)}, f32[4,8,128]{2,1,0:T(8,128)}) custom-call(s32[17]{0:T(128)} %pad_add_fusion.tab, bf16[2,512,3072]{2,1,0:T(8,128)(2,1)} %bitcast.124, bf16[2,512,3072]{2,1,0:T(8,128)(2,1)} %bitcast.125, bf16[2,512,3072]{2,1,0:T(8,128)(2,1)} %bitcast.126, bf16[2,512,1024]{2,1,0:T(8,128)(2,1)} %get-tuple-element.96.ho.heads_out, ...), custom_call_target="tpu_custom_call" | custom-call | flops 21474836480 | bytes 12582912 | tf_op jit(solution)/shard_map/attend_back/pallas_call | solution.py:312
  281.6 6.0 %flat_grad.8 = bf16[2,256,1536]{2,1,0:T(8,128)(2,1)} custom-call(s32[3]{0:T(128)} %get-tuple-element.185.tab, bf16[2,1024,512]{2,1,0:T(8,128)(2,1)} %get-tuple-element.148.refs_0_, bf16[3,1024,512]{2,1,0:T(8,128)(2,1)} %bitcast.114), custom_call_target="tpu_custom_call" | custom-call | flops 100663296 | bytes 655360 | tf_op jit(solution)/shard_map/flat_grad/pallas_call | solution.py:738
  287.5 19.9 %attend_back.3 = (bf16[3,2,512,512]{3,2,1,0:T(8,128)(2,1)}, f32[4,8,128]{2,1,0:T(8,128)}) custom-call(s32[17]{0:T(128)} %pad_add_fusion.tab, bf16[2,512,3072]{2,1,0:T(8,128)(2,1)} %bitcast.127, bf16[2,512,3072]{2,1,0:T(8,128)(2,1)} %bitcast.128, bf16[2,512,3072]{2,1,0:T(8,128)(2,1)} %bitcast.129, bf16[2,512,1024]{2,1,0:T(8,128)(2,1)} %get-tuple-element.96.ho.heads_out, ...), custom_call_target="tpu_custom_call" | custom-call | flops 21474836480 | bytes 12582912 | tf_op jit(solution)/shard_map/attend_back/pallas_call | solution.py:312
  309.1 2.3 add_convert_fusion.1
  313.5 2.4 add_convert_fusion
  321.5 6.0 %flat_grad.9 = bf16[2,256,1536]{2,1,0:T(8,128)(2,1)} custom-call(s32[3]{0:T(128)} %get-tuple-element.185.tab, bf16[2,1024,512]{2,1,0:T(8,128)(2,1)} %get-tuple-element.148.refs_0_, bf16[3,1024,512]{2,1,0:T(8,128)(2,1)} %bitcast.110), custom_call_target="tpu_custom_call" | custom-call | flops 100663296 | bytes 655360 | tf_op jit(solution)/shard_map/flat_grad/pallas_call | solution.py:738
  327.5 6.3 %flat_grad.10 = (bf16[256,1536]{1,0:T(8,128)(2,1)}, bf16[256,1536]{1,0:T(8,128)(2,1)}) custom-call(s32[3]{0:T(128)} %get-tuple-element.186.tab, bf16[2,1024,512]{2,1,0:T(8,128)(2,1)} %get-tuple-element.148.refs_0_, bf16[3,1024,512]{2,1,0:T(8,128)(2,1)} %bitcast.115, bf16[2,256,1536]{2,1,0:T(8,128)(2,1)} %collective-permute-done.7.refs_2_), custom_call_target="tpu_custom_call" | custom-call | flops 100663296 | bytes 655360 | tf_op jit(solution)/shard_map/flat_grad/pallas_call | solution.py:738
  335.0 9.3 %first_back.2 = (bf16[512,1024]{1,0:T(8,128)(2,1)}, f32[8,1024]{1,0:T(8,128)}) custom-call(s32[1]{0:T(128)} %constant.139.clone.1.at, bf16[3,1024,512]{2,1,0:T(8,128)(2,1)} %bitcast.116, bf16[3,1024,512]{2,1,0:T(8,128)(2,1)} %bitcast.111, bf16[1024,3072]{1,0:T(8,128)(2,1)} %w.7, bf16[1,512,1024]{2,1,0:T(8,128)(2,1)} %copy-done.3, ...), custom_call_target="tpu_custom_call" | custom-call | flops 3221225472 | bytes 14680064 | tf_op jit(solution)/shard_map/first_back/pallas_call | solution.py:615
  351.9 9.7 %first_back.3 = (f32[2,512,1024]{2,1,0:T(8,128)}, f32[8,1024]{1,0:T(8,128)}) custom-call(s32[1]{0:T(128)} %bitcast.at, bf16[3,1024,512]{2,1,0:T(8,128)(2,1)} %bitcast.117, bf16[3,1024,512]{2,1,0:T(8,128)(2,1)} %bitcast.112, bf16[1024,3072]{1,0:T(8,128)(2,1)} %w.7, bf16[2,512,1024]{2,1,0:T(8,128)(2,1)} %tok.5, f32[512,1024]{1,0:T(8,128)} %get-tuple-element.138.grad_middle, ...), custom_call_target="tpu_custom_call" | custom-call | flops 3221225472 | bytes 14680064 | tf_op jit(solution)/shard_map/first_back/pallas_call | solution.py:615
  363.6 2.7 collective-permute-start.28
  368.6 6.3 %flat_grad.11 = (bf16[256,1536]{1,0:T(8,128)(2,1)}, bf16[256,1536]{1,0:T(8,128)(2,1)}) custom-call(s32[3]{0:T(128)} %get-tuple-element.186.tab, bf16[2,1024,512]{2,1,0:T(8,128)(2,1)} %get-tuple-element.148.refs_0_, bf16[3,1024,512]{2,1,0:T(8,128)(2,1)} %bitcast.113, bf16[2,256,1536]{2,1,0:T(8,128)(2,1)} %collective-permute-done.11.refs_2_), custom_call_target="tpu_custom_call" | custom-call | flops 100663296 | bytes 655360 | tf_op jit(solution)/shard_map/flat_grad/pallas_call | solution.py:738
  375.0 2.9 convert_dynamic-update-slice_fusion
  380.9 3.4 collective-permute-done.13
  384.4 2.3 collective-permute-start.14
  388.5 3.2 collective-permute-done.14
  393.7 4.0 collective-permute-done.15
  399.9 8.8 %collective-permute-done.22 = bf16[4,64,768]{2,1,0:T(8,128)(2,1)S(1)} collective-permute-done((bf16[4,64,768]{2,1,0:T(8,128)(2,1)S(1)}, bf16[4,64,768]{2,1,0:T(8,128)(2,1)S(1)}, u32[]{:S(2)}, u32[]{:S(2)}) %collective-permute-start.22) | collective-permute-done | bytes 393248 | tf_op jit(solution)/shard_map/ppermute | solution.py:1075
  409.7 6.5 %collective-permute-done.27 = bf16[64,2560]{1,0:T(8,128)(2,1)S(1)} collective-permute-done((bf16[64,2560]{1,0:T(8,128)(2,1)S(1)}, bf16[64,2560]{1,0:T(8,128)(2,1)S(1)}, u32[]{:S(2)}, u32[]{:S(2)}) %collective-permute-start.27) | collective-permute-done | bytes 327712 | tf_op jit(solution)/shard_map/ppermute | solution.py:1079
  418.8 3.7 collective-permute-done.17
  427.6 3.4 collective-permute-done.24
  (186 shorter events, 54.5 us)
Async XLA Ops:
  2.2 27.0 %collective-permute-start = (bf16[1,512,1024]{2,1,0:T(8,128)(2,1)S(1)}, bf16[1,512,1024]{2,1,0:T(8,128)(2,1)S(1)}, u32[]{:S(2)}, u32[]{:S(2)}) collective-permute-start(bf16[1,512,1024]{2,1,0:T(8,128)(2,1)S(1)} %constant_dynamic-slice_fusion.9), channel_id=1, source_target_pairs={{0,1},{1,0},{2,3},{3,2},{4,5},{5,4},{6,7},{7,6},{8,9},{9,8},{10,11... | collective-permute-start | bytes 3145736 | tf_op jit(solution)/shard_map/ppermute | solution.py:1075
  5.3 58.8 %collective-permute-start.1 = (bf16[1,512,1024]{2,1,0:T(8,128)(2,1)S(1)}, bf16[1,512,1024]{2,1,0:T(8,128)(2,1)}, u32[]{:S(2)}, u32[]{:S(2)}) collective-permute-start(bf16[1,512,1024]{2,1,0:T(8,128)(2,1)S(1)} %constant_dynamic-slice_fusion.8), channel_id=1, source_target_pairs={{0,1},{1,0},{2,3},{3,2},{4,5},{5,4},{6,7},{7,6},{8,9},{9,8},{10,11... | collective-permute-start | bytes 3145736 | tf_op jit(solution)/shard_map/ppermute | solution.py:1075
  16.1 22.9 %copy-start.10 = (f32[1,1024]{1,0:T(1,128)}, f32[1,1024]{1,0:T(1,128)S(1)}, u32[]{:S(2)}) copy-start(f32[1,1024]{1,0:T(1,128)S(1)} %reshape.192.head_scale) | copy-start | bytes 12292
  132.8 79.1 %collective-permute-start.2 = (bf16[512,1024]{1,0:T(8,128)(2,1)}, bf16[512,1024]{1,0:T(8,128)(2,1)S(1)}, u32[]{:S(2)}, u32[]{:S(2)}) collective-permute-start(bf16[512,1024]{1,0:T(8,128)(2,1)} %get-tuple-element.104), channel_id=1, source_target_pairs={{0,1},{1,0},{2,3},{3,2},{4,5},{5,4},{6,7},{7,6},{8,9},{9,8},{10,11... | collective-permute-start | bytes 3145736 | tf_op jit(solution)/shard_map/ppermute | solution.py:1075
  225.4 11.7 %collective-permute-start.3 = (bf16[2,256,5120]{2,1,0:T(8,128)(2,1)}, bf16[2,256,5120]{2,1,0:T(8,128)(2,1)}, u32[]{:S(2)}, u32[]{:S(2)}) collective-permute-start(bf16[2,256,5120]{2,1,0:T(8,128)(2,1)} %flat_grad.6), channel_id=1, source_target_pairs={{0,2},{2,0},{4,6},{6,4},{8,10},{10,8},{12,14},{14,12},{16,18},{18,... | collective-permute-start | bytes 15728648 | tf_op jit(solution)/shard_map/ppermute | solution.py:1079
  234.7 16.6 %collective-permute-start.4 = (bf16[2,2048,512]{2,1,0:T(8,128)(2,1)}, bf16[2,2048,512]{2,1,0:T(8,128)(2,1)}, u32[]{:S(2)}, u32[]{:S(2)}) collective-permute-start(bf16[2,2048,512]{2,1,0:T(8,128)(2,1)} %tall_grad.2), channel_id=1, source_target_pairs={{0,2},{2,0},{4,6},{6,4},{8,10},{10,8},{12,14},{14,12},{16,18},{18,... | collective-permute-start | bytes 12582920 | tf_op jit(solution)/shard_map/ppermute | solution.py:1079
  249.8 63.3 %collective-permute-start.5 = (bf16[256,5120]{1,0:T(8,128)(2,1)}, bf16[256,5120]{1,0:T(8,128)(2,1)}, u32[]{:S(2)}, u32[]{:S(2)}) collective-permute-start(bf16[256,5120]{1,0:T(8,128)(2,1)} %get-tuple-element.114), channel_id=1, source_target_pairs={{0,4},{2,6},{4,0},{6,2},{8,12},{10,14},{12,8},{14,10},{16,20},{18,... | collective-permute-start | bytes 7864328 | tf_op jit(solution)/shard_map/ppermute | solution.py:1079
  261.4 47.6 %collective-permute-start.6 = (bf16[2048,512]{1,0:T(8,128)(2,1)}, bf16[2048,512]{1,0:T(8,128)(2,1)}, u32[]{:S(2)}, u32[]{:S(2)}) collective-permute-start(bf16[2048,512]{1,0:T(8,128)(2,1)} %get-tuple-element.117), channel_id=1, source_target_pairs={{0,1},{1,0},{2,3},{3,2},{4,5},{5,4},{6,7},{7,6},{8,9},{9,8},{10,11... | collective-permute-start | bytes 6291464 | tf_op jit(solution)/shard_map/ppermute | solution.py:1075
  287.5 21.5 %copy-start.5 = (bf16[2048,512]{1,0:T(8,128)(2,1)S(1)}, bf16[2048,512]{1,0:T(8,128)(2,1)}, u32[]{:S(2)}) copy-start(bf16[2048,512]{1,0:T(8,128)(2,1)} %get-tuple-element.127) | copy-start | bytes 6291460
  307.4 20.1 %collective-permute-start.7 = (bf16[2,256,1536]{2,1,0:T(8,128)(2,1)}, bf16[2,256,1536]{2,1,0:T(8,128)(2,1)}, u32[]{:S(2)}, u32[]{:S(2)}) collective-permute-start(bf16[2,256,1536]{2,1,0:T(8,128)(2,1)} %flat_grad.8), channel_id=1, source_target_pairs={{0,2},{2,0},{4,6},{6,4},{8,10},{10,8},{12,14},{14,12},{16,18},{18,... | collective-permute-start | bytes 4718600 | tf_op jit(solution)/shard_map/ppermute | solution.py:1079
  312.6 33.1 %collective-permute-start.8 = (bf16[4,256,512]{2,1,0:T(8,128)(2,1)}, bf16[4,256,512]{2,1,0:T(8,128)(2,1)}, u32[]{:S(2)}, u32[]{:S(2)}) collective-permute-start(bf16[4,256,512]{2,1,0:T(8,128)(2,1)} %get-tuple-element.167), channel_id=1, source_target_pairs={{0,4},{2,6},{4,0},{6,2},{8,12},{10,14},{12,8},{14,10},{16,20},{18,... | collective-permute-start | bytes 3145736 | tf_op jit(solution)/shard_map/ppermute | solution.py:1079
  318.0 30.9 %collective-permute-start.9 = (bf16[4,64,2560]{2,1,0:T(8,128)(2,1)}, bf16[4,64,2560]{2,1,0:T(8,128)(2,1)}, u32[]{:S(2)}, u32[]{:S(2)}) collective-permute-start(bf16[4,64,2560]{2,1,0:T(8,128)(2,1)} %pad_maximum_fusion.1), channel_id=1, source_target_pairs={{0,1},{1,0},{2,3},{3,2},{4,5},{5,4},{6,7},{7,6},{8,9},{9,8},{10,11... | collective-permute-start | bytes 3932168 | tf_op jit(solution)/shard_map/ppermute | solution.py:1075
  327.5 41.1 %collective-permute-start.11 = (bf16[2,256,1536]{2,1,0:T(8,128)(2,1)}, bf16[2,256,1536]{2,1,0:T(8,128)(2,1)}, u32[]{:S(2)}, u32[]{:S(2)}) collective-permute-start(bf16[2,256,1536]{2,1,0:T(8,128)(2,1)} %flat_grad.9), channel_id=1, source_target_pairs={{0,2},{2,0},{4,6},{6,4},{8,10},{10,8},{12,14},{14,12},{16,18},{18,... | collective-permute-start | bytes 4718600 | tf_op jit(solution)/shard_map/ppermute | solution.py:1079
  333.8 32.4 %collective-permute-start.18 = (bf16[256,1536]{1,0:T(8,128)(2,1)}, bf16[256,1536]{1,0:T(8,128)(2,1)}, u32[]{:S(2)}, u32[]{:S(2)}) collective-permute-start(bf16[256,1536]{1,0:T(8,128)(2,1)} %get-tuple-element.130), channel_id=1, source_target_pairs={{0,4},{2,6},{4,0},{6,2},{8,12},{10,14},{12,8},{14,10},{16,20},{18,... | collective-permute-start | bytes 2359304 | tf_op jit(solution)/shard_map/ppermute | solution.py:1079
  344.2 30.8 %collective-permute-start.10 = (bf16[512,1024]{1,0:T(8,128)(2,1)}, bf16[512,1024]{1,0:T(8,128)(2,1)}, u32[]{:S(2)}, u32[]{:S(2)}) collective-permute-start(bf16[512,1024]{1,0:T(8,128)(2,1)} %get-tuple-element.134), channel_id=1, source_target_pairs={{0,1},{1,0},{2,3},{3,2},{4,5},{5,4},{6,7},{7,6},{8,9},{9,8},{10,11... | collective-permute-start | bytes 3145736 | tf_op jit(solution)/shard_map/ppermute | solution.py:1075
  347.3 15.0 %collective-permute-start.25 = (bf16[2,256,512]{2,1,0:T(8,128)(2,1)S(1)}, bf16[2,256,512]{2,1,0:T(8,128)(2,1)}, u32[]{:S(2)}, u32[]{:S(2)}) collective-permute-start(bf16[2,256,512]{2,1,0:T(8,128)(2,1)S(1)} %get-tuple-element.171), channel_id=1, source_target_pairs={{0,8},{2,10},{4,12},{6,14},{8,0},{10,2},{12,4},{14,6},{16,24},{18,... | collective-permute-start | bytes 1572872 | tf_op jit(solution)/shard_map/ppermute | solution.py:1079
  350.8 41.6 %collective-permute-start.26 = (bf16[2,64,2560]{2,1,0:T(8,128)(2,1)S(1)}, bf16[2,64,2560]{2,1,0:T(8,128)(2,1)}, u32[]{:S(2)}, u32[]{:S(2)}) collective-permute-start(bf16[2,64,2560]{2,1,0:T(8,128)(2,1)S(1)} %get-tuple-element.169), channel_id=1, source_target_pairs={{0,8},{2,10},{4,12},{6,14},{8,0},{10,2},{12,4},{14,6},{16,24},{18,... | collective-permute-start | bytes 1966088 | tf_op jit(solution)/shard_map/ppermute | solution.py:1079
  363.6 23.1 %collective-permute-start.28 = (bf16[256,512]{1,0:T(8,128)(2,1)S(1)}, bf16[256,512]{1,0:T(8,128)(2,1)}, u32[]{:S(2)}, u32[]{:S(2)}) collective-permute-start(bf16[256,512]{1,0:T(8,128)(2,1)S(1)} %dynamic-slice_bitcast_fusion.8), channel_id=1, source_target_pairs={{0,16},{2,18},{4,20},{6,22},{8,24},{10,26},{12,28},{14,30},{16,0},... | collective-permute-start | bytes 786440 | tf_op jit(solution)/shard_map/ppermute | solution.py:1079
  367.6 12.5 %collective-permute-start.19 = (bf16[4,64,768]{2,1,0:T(8,128)(2,1)S(1)}, bf16[4,64,768]{2,1,0:T(8,128)(2,1)S(1)}, u32[]{:S(2)}, u32[]{:S(2)}) collective-permute-start(bf16[4,64,768]{2,1,0:T(8,128)(2,1)S(1)} %constant_dynamic-slice_fusion), channel_id=1, source_target_pairs={{0,1},{1,0},{2,3},{3,2},{4,5},{5,4},{6,7},{7,6},{8,9},{9,8},{10,11... | collective-permute-start | bytes 1179656 | tf_op jit(solution)/shard_map/ppermute | solution.py:1075
  374.9 3.7 collective-permute-start.12
  377.8 19.9 %collective-permute-start.15 = (bf16[256,1536]{1,0:T(8,128)(2,1)S(1)}, bf16[256,1536]{1,0:T(8,128)(2,1)S(1)}, u32[]{:S(2)}, u32[]{:S(2)}) collective-permute-start(bf16[256,1536]{1,0:T(8,128)(2,1)S(1)} %copy-done.30), channel_id=1, source_target_pairs={{0,4},{2,6},{4,0},{6,2},{8,12},{10,14},{12,8},{14,10},{16,20},{18,... | collective-permute-start | bytes 2359304 | tf_op jit(solution)/shard_map/ppermute | solution.py:1079
  378.6 5.7 %collective-permute-start.13 = (f32[23,1024]{1,0:T(8,128)S(1)}, f32[23,1024]{1,0:T(8,128)S(1)}, u32[]{:S(2)}, u32[]{:S(2)}) collective-permute-start(f32[23,1024]{1,0:T(8,128)S(1)} %add.192), channel_id=1, source_target_pairs={{0,8},{2,10},{4,12},{6,14},{8,0},{10,2},{12,4},{14,6},{16,24},{18,... | collective-permute-start | bytes 282632 | tf_op jit(solution)/shard_map/ppermute | solution.py:1079
  380.3 11.4 %collective-permute-start.20 = (bf16[2,64,768]{2,1,0:T(8,128)(2,1)S(1)}, bf16[2,64,768]{2,1,0:T(8,128)(2,1)S(1)}, u32[]{:S(2)}, u32[]{:S(2)}) collective-permute-start(bf16[2,64,768]{2,1,0:T(8,128)(2,1)S(1)} %dynamic-slice_bitcast_fusion.10), channel_id=1, source_target_pairs={{0,8},{2,10},{4,12},{6,14},{8,0},{10,2},{12,4},{14,6},{16,24},{18,... | collective-permute-start | bytes 589832 | tf_op jit(solution)/shard_map/ppermute | solution.py:1079
  384.4 7.3 %collective-permute-start.14 = (f32[23,1024]{1,0:T(8,128)S(1)}, f32[23,1024]{1,0:T(8,128)S(1)}, u32[]{:S(2)}, u32[]{:S(2)}) collective-permute-start(f32[23,1024]{1,0:T(8,128)S(1)} %add.193), channel_id=1, source_target_pairs={{0,16},{2,18},{4,20},{6,22},{8,24},{10,26},{12,28},{14,30},{16,0},... | collective-permute-start | bytes 282632 | tf_op jit(solution)/shard_map/ppermute | solution.py:1079
  391.8 7.9 %collective-permute-start.21 = (bf16[64,768]{1,0:T(8,128)(2,1)S(1)}, bf16[64,768]{1,0:T(8,128)(2,1)S(1)}, u32[]{:S(2)}, u32[]{:S(2)}) collective-permute-start(bf16[64,768]{1,0:T(8,128)(2,1)S(1)} %dynamic-slice_bitcast_fusion.12), channel_id=1, source_target_pairs={{0,16},{2,18},{4,20},{6,22},{8,24},{10,26},{12,28},{14,30},{16,0},... | collective-permute-start | bytes 294920 | tf_op jit(solution)/shard_map/ppermute | solution.py:1079
  398.0 10.7 %collective-permute-start.22 = (bf16[4,64,768]{2,1,0:T(8,128)(2,1)S(1)}, bf16[4,64,768]{2,1,0:T(8,128)(2,1)S(1)}, u32[]{:S(2)}, u32[]{:S(2)}) collective-permute-start(bf16[4,64,768]{2,1,0:T(8,128)(2,1)S(1)} %constant_dynamic-slice_fusion.3), channel_id=1, source_target_pairs={{0,1},{1,0},{2,3},{3,2},{4,5},{5,4},{6,7},{7,6},{8,9},{9,8},{10,11... | collective-permute-start | bytes 1179656 | tf_op jit(solution)/shard_map/ppermute | solution.py:1075
  399.2 17.0 %collective-permute-start.27 = (bf16[64,2560]{1,0:T(8,128)(2,1)S(1)}, bf16[64,2560]{1,0:T(8,128)(2,1)S(1)}, u32[]{:S(2)}, u32[]{:S(2)}) collective-permute-start(bf16[64,2560]{1,0:T(8,128)(2,1)S(1)} %dynamic-slice_bitcast_fusion.6), channel_id=1, source_target_pairs={{0,16},{2,18},{4,20},{6,22},{8,24},{10,26},{12,28},{14,30},{16,0},... | collective-permute-start | bytes 983048 | tf_op jit(solution)/shard_map/ppermute | solution.py:1079
  408.8 9.0 %collective-permute-start.16 = (f32[23,1024]{1,0:T(8,128)S(1)}, f32[23,1024]{1,0:T(8,128)S(1)}, u32[]{:S(2)}, u32[]{:S(2)}) collective-permute-start(f32[23,1024]{1,0:T(8,128)S(1)} %add.194), channel_id=1, source_target_pairs={{0,4},{2,6},{4,0},{6,2},{8,12},{10,14},{12,8},{14,10},{16,20},{18,... | collective-permute-start | bytes 282632 | tf_op jit(solution)/shard_map/ppermute | solution.py:1079
  417.8 14.8 %copy-start.1 = (s32[2,4]{1,0:T(2,128)S(1)}, s32[2,4]{1,0:T(2,128)}, u32[]{:S(2)}) copy-start(s32[2,4]{1,0:T(2,128)} %param.23) | copy-start | bytes 100
  417.8 4.7 %collective-permute-start.17 = (f32[23,1024]{1,0:T(8,128)S(1)}, f32[23,1024]{1,0:T(8,128)S(1)}, u32[]{:S(2)}, u32[]{:S(2)}) collective-permute-start(f32[23,1024]{1,0:T(8,128)S(1)} %add.198), channel_id=1, source_target_pairs={{0,1},{1,0},{2,3},{3,2},{4,5},{5,4},{6,7},{7,6},{8,9},{9,8},{10,11... | collective-permute-start | bytes 282632 | tf_op jit(solution)/shard_map/ppermute | solution.py:1075
  418.7 5.8 %collective-permute-start.23 = (bf16[2,64,768]{2,1,0:T(8,128)(2,1)S(1)}, bf16[2,64,768]{2,1,0:T(8,128)(2,1)S(1)}, u32[]{:S(2)}, u32[]{:S(2)}) collective-permute-start(bf16[2,64,768]{2,1,0:T(8,128)(2,1)S(1)} %dynamic-slice_bitcast_fusion.9), channel_id=1, source_target_pairs={{0,8},{2,10},{4,12},{6,14},{8,0},{10,2},{12,4},{14,6},{16,24},{18,... | collective-permute-start | bytes 589832 | tf_op jit(solution)/shard_map/ppermute | solution.py:1079
  424.6 6.4 %collective-permute-start.24 = (bf16[64,768]{1,0:T(8,128)(2,1)S(1)}, bf16[64,768]{1,0:T(8,128)(2,1)S(1)}, u32[]{:S(2)}, u32[]{:S(2)}) collective-permute-start(bf16[64,768]{1,0:T(8,128)(2,1)S(1)} %dynamic-slice_bitcast_fusion.11), channel_id=1, source_target_pairs={{0,16},{2,18},{4,20},{6,22},{8,24},{10,26},{12,28},{14,30},{16,0},... | collective-permute-start | bytes 294920 | tf_op jit(solution)/shard_map/ppermute | solution.py:1079
  (28 other events, 229.1 us)

commit v6 on v4

--- a/solution.py
+++ b/solution.py
@@ -1118,7 +1118,17 @@
     kept_at = b[None]
     sent_at = jnp.zeros((1,), jnp.int32)
 
-    lengths = lax.dynamic_slice_in_dim(doc_lengths, b, 1, 0)
+    def line(v):
+        return v.reshape(1, -1)
+
+    qkv_bias = jnp.concatenate([query_bias, jnp.zeros_like(query_bias), value_bias])
+    first_args = (line(norm1_gain), line(norm1_shift), qkv_weight, line(qkv_bias), scale)
+    early = project_qkv(kept_at, tokens, *first_args, 0, n)
+
+    def later(v):
+        return after(v, early[0])
+
+    lengths = lax.dynamic_slice_in_dim(later(doc_lengths), b, 1, 0)
     ends = running_sums(lengths)[0]
     firsts = (half_len // 2) * jnp.arange(4, dtype=jnp.int32)
     starts = jnp.max(jnp.where(ends[None, :] <= firsts[:, None], ends[None, :], 0), axis=1)
@@ -1126,20 +1136,16 @@
     tab = jnp.concatenate([b[None], allowed.reshape(16)])
     theirs = jnp.stack([1 - core, x, y])
     mine = jnp.stack([core, x, y])
-
-    def line(v):
-        return v.reshape(1, -1)
-
+    head_scales = later(head_scales)
     scale_row = jnp.broadcast_to(head_scales[:, None], (heads, head_dim)).reshape(1, d)
     vec = jnp.stack(
-        [out_bias, attn_gain, attn_shift, norm2_gain, norm2_shift, fc2_bias, scale_row[0], out_bias]
-    )
+        [later(out_bias), attn_gain, attn_shift, norm2_gain, norm2_shift, fc2_bias, scale_row[0], out_bias]
+    )
+    fc1_bias = later(fc1_bias)
     vec4 = jnp.stack([fc1_bias, mid_gain, mid_shift, fc1_bias])
-    qkv_bias = jnp.concatenate([query_bias, jnp.zeros_like(query_bias), value_bias])
-
-    first_args = (line(norm1_gain), line(norm1_shift), qkv_weight, line(qkv_bias), scale)
-    early = project_qkv(kept_at, tokens, *first_args, 0, n)
-    attn_in, qkv = project_qkv(sent_at, tok_in, *first_args, 1, n, early)
+
+    made = after(sent_at, tab, theirs, mine, scale_row, vec, vec4)
+    attn_in, qkv = project_qkv(made, tok_in, *first_args, 1, n, early)
     qkv = qkv.reshape(2, half_len, 3 * d)
     heads_out, logs = attend(tab, qkv, scale_row)
 
@@ -1235,33 +1241,41 @@
     tokens_grad, sums_kept = first_back(
         kept_at, after(even, *wide_parts), odd, qkv_weight, tokens, mid_kept, line(norm1_gain), 0, True
     )
+    dots = jnp.stack([dots_even[:, 0].reshape(2, 4, head_dim), dots_odd[:, 0].reshape(2, 4, head_dim)], axis=1)
+    head_scales_grad = jnp.sum(dots, axis=3).reshape(heads) / head_scales
+    head_scales_grad = jnp.pad(head_scales_grad, (0, d - heads))
+    total = jnp.concatenate(
+        [
+            (sums_sent + sums_kept)[:4],
+            head_scales_grad[None],
+            sums[:6],
+            sums4.reshape(8 * ff // d, d)[: 3 * ff // d],
+        ]
+    )
     fc2_parts = far_z(add_z(4, *held(fc2_parts, tokens_grad)))
     even_parts = columns_by_y(add_x(*held(even_parts, tokens_grad)))
-    wide_parts = far_z(add_z(4, *held(wide_parts, *fc2_parts, *even_parts)))
+    wide_parts = far_z(add_z(4, *held(wide_parts, tokens_grad)))
     tokens_grad = fill(tokens_grad, grad_back)
-    fc2_weight_grad = add_z(8, *fc2_parts)
     odd_parts = columns_by_y(add_x(*odd_parts))
     even_parts = near_z(add_y(*even_parts))
+    odd_parts = near_z(add_y(*odd_parts))
+    total = total + (partial(flip, bit=1))(total)
+    total = total + (partial(flip, bit=4))(total)
+    total = total + (partial(flip, bit=8))(total)
+    total = after(total, *odd_parts)
+    total = total + (partial(flip, bit=2))(total)
+    total = total + (exchange)(total)
+    even_parts = far_z(add_z(4, *even_parts))
+    odd_parts = far_z(add_z(4, *odd_parts))
+    fc2_weight_grad = add_z(8, *fc2_parts)
     wide_grad = add_z(8, *wide_parts)
     fc1_weight_grad, out_weight_grad = wide_grad[:, : ff // 2], wide_grad[:, ff // 2 :]
-    even_parts = far_z(add_z(4, *even_parts))
-    odd_parts = far_z(add_z(4, *near_z(add_y(*odd_parts))))
     even_grad, odd_grad = (add_z(8, *parts) for parts in (even_parts, odd_parts))
+    first_sums, sums, sums4 = total[:5], total[5:11], total[11:].reshape(3, ff)
     run = d // 4
     qkv_weight_grad = jnp.stack(
         [even_grad.reshape(-1, 3, run), odd_grad.reshape(-1, 3, run)], axis=2
     ).reshape(-1, 6 * run)
-    tokens_grad = fill(tokens_grad, grad_back)
-    dots = jnp.stack([dots_even[:, 0].reshape(2, 4, head_dim), dots_odd[:, 0].reshape(2, 4, head_dim)], axis=1)
-    head_scales_grad = jnp.sum(dots, axis=3).reshape(heads) / head_scales
-    head_scales_grad = jnp.pad(head_scales_grad, (0, d - heads))
-    first_sums = (sums_sent + sums_kept)[:4]
-    total = jnp.concatenate(
-        [first_sums, head_scales_grad[None], sums[:6], sums4.reshape(8 * ff // d, d)[: 3 * ff // d]]
-    )
-    for move in (partial(flip, bit=1), partial(flip, bit=4), partial(flip, bit=8), partial(flip, bit=2), exchange):
-        total = total + move(total)
-    first_sums, sums, sums4 = total[:5], total[5:11], total[11:].reshape(3, ff)
     return (
         output,
         tokens_grad,

time: 395 us -> 390 us (0.987)
  transfers between devices with their start and end apart: 29 -> 29, of which waited for: 9 -> 11; matrix products, arithmetic and copies ran while one was open for 8% -> 7% of each run, Pallas kernels for 54% -> 55%
where the time goes in v6:
time: 390 us; the launch traced here: 383 us
  Pallas kernels  272 us (70%)
  waiting for transfers between devices  46.1 us (12%)
  starting transfers between devices  30 us (8%)
  other arithmetic  20.3 us (5%)
  local copies, waits for them, and re-layouts  12.9 us (3%)
    pallas_call x2, Pallas kernels, middle_pass(): pl.pallas_call(middle_body, name='middle_pass', grid_spec=pltpu.PrefetchS...  102 us
    pallas_call x6, Pallas kernels, flat_grad(): pl.pallas_call(partial(flat_grad_body, counts, received is not None), nam...  49.5 us
    pallas_call x2, Pallas kernels, attend_back(): pl.pallas_call(partial(attend_back_body, scale), name='attend_back', grid...  39.4 us
    ppermute x20, waiting for transfers between devices, flip(): return lax.ppermute(x, 'dp', [(i, i ^ bit) for i in range(16)])  25.3 us
    pallas_call x1, Pallas kernels, attend(): pl.pallas_call(attend_body, name='attend', grid_spec=pltpu.PrefetchScalar...  25 us
    ppermute x20, starting transfers between devices, flip(): return lax.ppermute(x, 'dp', [(i, i ^ bit) for i in range(16)])  20.8 us
    ppermute x9, waiting for transfers between devices, exchange(): return lax.ppermute(x, 'blk', swap)  20.8 us
    pallas_call x2, Pallas kernels, tall_grad(): pl.pallas_call(partial(tall_grad_body, received is not None), name='tall_...  19.4 us
  transfers between devices with their start and end apart: 29, of which 11 were waited for; matrix products, arithmetic and copies ran while one was open for 7% of the time, Pallas kernels for 55%

profile of v6, /device:TPU:0, one launch (start us, length us, event | category | flops | bytes accessed | tf_op | source)
XLA Modules:
  0.0 382.8 jit_solution(3744318247513985008)
XLA Ops:
  2.2 3.0 collective-permute-start
  6.4 9.0 %project_qkv.2 = (bf16[2,1024,512]{2,1,0:T(8,128)(2,1)}, bf16[1024,3072]{1,0:T(8,128)(2,1)}) custom-call(s32[1]{0:T(128)} %bitcast.at, bf16[2,512,1024]{2,1,0:T(8,128)(2,1)} %tok.5, f32[1,1024]{1,0:T(1,128)} %bitcast.144, f32[1,1024]{1,0:T(1,128)} %bitcast.156, bf16[1024,3072]{1,0:T(8,128)(2,1)} %w.7, f32[1,3072]{1,0:T(1,128)} %bitcast.140), custom_call_target="tpu_custom_call" | custom-call | flops 3221225472 | bytes 11534336 | tf_op jit(solution)/shard_map/project_qkv/pallas_call | solution.py:104
  18.6 10.6 %collective-permute-done.tok = bf16[1,512,1024]{2,1,0:T(8,128)(2,1)S(1)} collective-permute-done((bf16[1,512,1024]{2,1,0:T(8,128)(2,1)S(1)}, bf16[1,512,1024]{2,1,0:T(8,128)(2,1)S(1)}, u32[]{:S(2)}, u32[]{:S(2)}) %collective-permute-start) | collective-permute-done | bytes 1048608 | tf_op jit(solution)/shard_map/ppermute | solution.py:1076
  30.1 8.9 %project_qkv.3 = (bf16[2,1024,512]{2,1,0:T(8,128)(2,1)}, bf16[1024,3072]{1,0:T(8,128)(2,1)}) custom-call(s32[1]{0:T(128)} %constant.139.clone.1.at, bf16[1,512,1024]{2,1,0:T(8,128)(2,1)} %copy-done.3, f32[1,1024]{1,0:T(1,128)} %bitcast.145, f32[1,1024]{1,0:T(1,128)} %bitcast.157, ...), custom_call_target="tpu_custom_call", output_to_operand_aliasing={{0}: (6, {}), {1}: (7, {})} | custom-call | flops 3221225472 | bytes 11534336 | tf_op jit(solution)/shard_map/project_qkv/pallas_call | solution.py:104
  39.0 25.0 %attend.1 = (bf16[2,512,1024]{2,1,0:T(8,128)(2,1)}, f32[8,4,8,256]{3,2,1,0:T(8,128)}) custom-call(s32[17]{0:T(128)} %pad_add_fusion.tab, bf16[2,512,3072]{2,1,0:T(8,128)(2,1)} %bitcast.121, bf16[2,512,3072]{2,1,0:T(8,128)(2,1)} %bitcast.122, bf16[2,512,3072]{2,1,0:T(8,128)(2,1)} %bitcast.123, f32[1,1024]{1,0:T(1,128)} %copy-done.8), custom_call_target="tpu_custom_call" | custom-call | flops 17179869184 | bytes 12582912 | tf_op jit(solution)/shard_map/attend/pallas_call | solution.py:210
  64.0 50.6 %middle_pass.2 = (bf16[512,1024]{1,0:T(8,128)(2,1)}, f32[512,1024]{1,0:T(8,128)}, f32[8,1024]{1,0:T(8,128)}, f32[8,4096]{1,0:T(8,128)}, bf16[2,1024,512]{2,1,0:T...) custom-call(s32[1]{0:T(128)} %constant.139.clone.1.at, ...), custom_call_target="tpu_custom_call" | custom-call | flops 19327352832 | bytes 37748736 | tf_op jit(solution)/shard_map/middle_pass/pallas_call | solution.py:519
  114.6 2.1 collective-permute-start.2
  116.7 51.0 %middle_pass.3 = (f32[2,512,1024]{2,1,0:T(8,128)}, f32[512,1024]{1,0:T(8,128)}, f32[8,1024]{1,0:T(8,128)}, f32[8,4096]{1,0:T(8,128)}, bf16[2,1024,512]{2,1,0:T(8...) custom-call(s32[1]{0:T(128)} %bitcast.at, ...), custom_call_target="tpu_custom_call", output_to_operand_aliasing={{4}: (9, {}), {5}: (10, {}), {6}: (11, {}), {7}: (12, {}), ... | custom-call | flops 19327352832 | bytes 37748736 | tf_op jit(solution)/shard_map/middle_pass/pallas_call | solution.py:519
  169.4 12.1 %flat_grad.6 = bf16[2,256,5120]{2,1,0:T(8,128)(2,1)} custom-call(s32[3]{0:T(128)} %get-tuple-element.179.tab, bf16[2,1024,512]{2,1,0:T(8,128)(2,1)} %get-tuple-element.112.refs_0_, bf16[2,1024,512]{2,1,0:T(8,128)(2,1)} %get-tuple-element.108.refs_1_, bf16[1024,4096]{1,0:T(8,128)(2,1)} %get-tuple-element.109.refs_2_, ...), custom_call_target="tpu_custom_call" | custom-call | flops 5368709120 | bytes 32505856 | tf_op jit(solution)/shard_map/flat_grad/pallas_call | solution.py:739
  181.4 9.3 %tall_grad.2 = bf16[2,2048,512]{2,1,0:T(8,128)(2,1)} custom-call(s32[3]{0:T(128)} %get-tuple-element.179.tab, bf16[1024,4096]{1,0:T(8,128)(2,1)} %get-tuple-element.115.refs_0_.refs_1_, bf16[1024,4096]{1,0:T(8,128)(2,1)} %get-tuple-element.115.refs_0_.refs_1_, bf16[2,512,1024]{2,1,0:T(8,128)(2,1)} %refs_2_.3, ...), custom_call_target="tpu_custom_call" | custom-call | flops 4294967296 | bytes 14680064 | tf_op jit(solution)/shard_map/tall_grad/pallas_call | solution.py:678
  191.8 12.7 %flat_grad.7 = (bf16[256,5120]{1,0:T(8,128)(2,1)}, bf16[256,5120]{1,0:T(8,128)(2,1)}) custom-call(s32[3]{0:T(128)} %get-tuple-element.180.tab, bf16[2,1024,512]{2,1,0:T(8,128)(2,1)} %get-tuple-element.112.refs_0_, bf16[2,1024,512]{2,1,0:T(8,128)(2,1)} %get-tuple-element.108.refs_1_, bf16[1024,4096]{1,0:T(8,128)(2,1)} %get-tuple-element.109.refs_2_, ...), custom_call_target="tpu_custom_call" | custom-call | flops 5368709120 | bytes 32505856 | tf_op jit(solution)/shard_map/flat_grad/pallas_call | solution.py:739
  206.0 10.1 %tall_grad.3 = (bf16[2048,512]{1,0:T(8,128)(2,1)}, bf16[2048,512]{1,0:T(8,128)(2,1)}) custom-call(s32[3]{0:T(128)} %get-tuple-element.180.tab, bf16[1024,4096]{1,0:T(8,128)(2,1)} %get-tuple-element.115.refs_0_.refs_1_, bf16[1024,4096]{1,0:T(8,128)(2,1)} %get-tuple-element.115.refs_0_.refs_1_, bf16[2,512,1024]{2,1,0:T(8,128)(2,1)} %refs_2_.3, ...), custom_call_target="tpu_custom_call" | custom-call | flops 4294967296 | bytes 14680064 | tf_op jit(solution)/shard_map/tall_grad/pallas_call | solution.py:678
  216.6 19.5 %attend_back.2 = (bf16[3,2,512,512]{3,2,1,0:T(8,128)(2,1)}, f32[4,8,128]{2,1,0:T(8,128)}) custom-call(s32[17]{0:T(128)} %pad_add_fusion.tab, bf16[2,512,3072]{2,1,0:T(8,128)(2,1)} %bitcast.124, bf16[2,512,3072]{2,1,0:T(8,128)(2,1)} %bitcast.125, bf16[2,512,3072]{2,1,0:T(8,128)(2,1)} %bitcast.126, bf16[2,512,1024]{2,1,0:T(8,128)(2,1)} %get-tuple-element.95.ho.heads_out, ...), custom_call_target="tpu_custom_call" | custom-call | flops 21474836480 | bytes 12582912 | tf_op jit(solution)/shard_map/attend_back/pallas_call | solution.py:312
  236.2 6.0 %flat_grad.8 = bf16[2,256,1536]{2,1,0:T(8,128)(2,1)} custom-call(s32[3]{0:T(128)} %get-tuple-element.179.tab, bf16[2,1024,512]{2,1,0:T(8,128)(2,1)} %get-tuple-element.135.refs_0_, bf16[3,1024,512]{2,1,0:T(8,128)(2,1)} %bitcast.110), custom_call_target="tpu_custom_call" | custom-call | flops 100663296 | bytes 655360 | tf_op jit(solution)/shard_map/flat_grad/pallas_call | solution.py:739
  242.1 19.9 %attend_back.3 = (bf16[3,2,512,512]{3,2,1,0:T(8,128)(2,1)}, f32[4,8,128]{2,1,0:T(8,128)}) custom-call(s32[17]{0:T(128)} %pad_add_fusion.tab, bf16[2,512,3072]{2,1,0:T(8,128)(2,1)} %bitcast.127, bf16[2,512,3072]{2,1,0:T(8,128)(2,1)} %bitcast.128, bf16[2,512,3072]{2,1,0:T(8,128)(2,1)} %bitcast.129, bf16[2,512,1024]{2,1,0:T(8,128)(2,1)} %get-tuple-element.95.ho.heads_out, ...), custom_call_target="tpu_custom_call" | custom-call | flops 21474836480 | bytes 12582912 | tf_op jit(solution)/shard_map/attend_back/pallas_call | solution.py:312
  263.8 2.3 add_convert_fusion.1
  267.9 2.4 add_convert_fusion
  272.3 6.1 %flat_grad.9 = bf16[2,256,1536]{2,1,0:T(8,128)(2,1)} custom-call(s32[3]{0:T(128)} %get-tuple-element.179.tab, bf16[2,1024,512]{2,1,0:T(8,128)(2,1)} %get-tuple-element.135.refs_0_, bf16[3,1024,512]{2,1,0:T(8,128)(2,1)} %bitcast.114), custom_call_target="tpu_custom_call" | custom-call | flops 100663296 | bytes 655360 | tf_op jit(solution)/shard_map/flat_grad/pallas_call | solution.py:739
  281.1 6.3 %flat_grad.10 = (bf16[256,1536]{1,0:T(8,128)(2,1)}, bf16[256,1536]{1,0:T(8,128)(2,1)}) custom-call(s32[3]{0:T(128)} %get-tuple-element.180.tab, bf16[2,1024,512]{2,1,0:T(8,128)(2,1)} %get-tuple-element.135.refs_0_, bf16[3,1024,512]{2,1,0:T(8,128)(2,1)} %bitcast.111, bf16[2,256,1536]{2,1,0:T(8,128)(2,1)} %collective-permute-done.7.refs_2_), custom_call_target="tpu_custom_call" | custom-call | flops 100663296 | bytes 655360 | tf_op jit(solution)/shard_map/flat_grad/pallas_call | solution.py:739
  287.9 9.3 %first_back.2 = (bf16[512,1024]{1,0:T(8,128)(2,1)}, f32[8,1024]{1,0:T(8,128)}) custom-call(s32[1]{0:T(128)} %constant.139.clone.1.at, bf16[3,1024,512]{2,1,0:T(8,128)(2,1)} %bitcast.112, bf16[3,1024,512]{2,1,0:T(8,128)(2,1)} %bitcast.115, bf16[1024,3072]{1,0:T(8,128)(2,1)} %w.7, bf16[1,512,1024]{2,1,0:T(8,128)(2,1)} %copy-done.3, ...), custom_call_target="tpu_custom_call" | custom-call | flops 3221225472 | bytes 14680064 | tf_op jit(solution)/shard_map/first_back/pallas_call | solution.py:616
  302.1 6.3 %flat_grad.11 = (bf16[256,1536]{1,0:T(8,128)(2,1)}, bf16[256,1536]{1,0:T(8,128)(2,1)}) custom-call(s32[3]{0:T(128)} %get-tuple-element.180.tab, bf16[2,1024,512]{2,1,0:T(8,128)(2,1)} %get-tuple-element.135.refs_0_, bf16[3,1024,512]{2,1,0:T(8,128)(2,1)} %bitcast.116, bf16[2,256,1536]{2,1,0:T(8,128)(2,1)} %collective-permute-done.9.refs_2_), custom_call_target="tpu_custom_call" | custom-call | flops 100663296 | bytes 655360 | tf_op jit(solution)/shard_map/flat_grad/pallas_call | solution.py:739
  310.7 9.7 %first_back.3 = (f32[2,512,1024]{2,1,0:T(8,128)}, f32[8,1024]{1,0:T(8,128)}) custom-call(s32[1]{0:T(128)} %bitcast.at, bf16[3,1024,512]{2,1,0:T(8,128)(2,1)} %bitcast.113, bf16[3,1024,512]{2,1,0:T(8,128)(2,1)} %bitcast.117, bf16[1024,3072]{1,0:T(8,128)(2,1)} %w.7, bf16[2,512,1024]{2,1,0:T(8,128)(2,1)} %tok.5, f32[512,1024]{1,0:T(8,128)} %get-tuple-element.140.grad_middle, ...), custom_call_target="tpu_custom_call" | custom-call | flops 3221225472 | bytes 14680064 | tf_op jit(solution)/shard_map/first_back/pallas_call | solution.py:616
  322.2 2.7 collective-permute-start.28
  330.1 6.0 %collective-permute-done.13 = f32[23,1024]{1,0:T(8,128)S(1)} collective-permute-done((f32[23,1024]{1,0:T(8,128)S(1)}, f32[23,1024]{1,0:T(8,128)S(1)}, u32[]{:S(2)}, u32[]{:S(2)}) %collective-permute-start.13) | collective-permute-done | bytes 94240 | tf_op jit(solution)/shard_map/ppermute | solution.py:1080
  336.1 2.7 collective-permute-start.14
  342.0 3.7 collective-permute-done.21
  347.7 2.1 collective-permute-start.26
  349.9 6.5 %collective-permute-done.16 = bf16[4,64,768]{2,1,0:T(8,128)(2,1)S(1)} collective-permute-done((bf16[4,64,768]{2,1,0:T(8,128)(2,1)S(1)}, bf16[4,64,768]{2,1,0:T(8,128)(2,1)S(1)}, u32[]{:S(2)}, u32[]{:S(2)}) %collective-permute-start.16) | collective-permute-done | bytes 393248 | tf_op jit(solution)/shard_map/ppermute | solution.py:1076
  357.9 2.9 collective-permute-done.22
  361.0 7.9 %collective-permute-done.23 = bf16[2,64,768]{2,1,0:T(8,128)(2,1)S(1)} collective-permute-done((bf16[2,64,768]{2,1,0:T(8,128)(2,1)S(1)}, bf16[2,64,768]{2,1,0:T(8,128)(2,1)S(1)}, u32[]{:S(2)}, u32[]{:S(2)}) %collective-permute-start.23) | collective-permute-done | bytes 196640 | tf_op jit(solution)/shard_map/ppermute | solution.py:1080
  372.2 2.4 collective-permute-done.17
  377.4 1.9 collective-permute-done.18
  (180 shorter events, 50.0 us)
Async XLA Ops:
  2.2 27.0 %collective-permute-start = (bf16[1,512,1024]{2,1,0:T(8,128)(2,1)S(1)}, bf16[1,512,1024]{2,1,0:T(8,128)(2,1)S(1)}, u32[]{:S(2)}, u32[]{:S(2)}) collective-permute-start(bf16[1,512,1024]{2,1,0:T(8,128)(2,1)S(1)} %constant_dynamic-slice_fusion.7), channel_id=1, source_target_pairs={{0,1},{1,0},{2,3},{3,2},{4,5},{5,4},{6,7},{7,6},{8,9},{9,8},{10,11... | collective-permute-start | bytes 3145736 | tf_op jit(solution)/shard_map/ppermute | solution.py:1076
  5.3 58.7 %collective-permute-start.1 = (bf16[1,512,1024]{2,1,0:T(8,128)(2,1)S(1)}, bf16[1,512,1024]{2,1,0:T(8,128)(2,1)}, u32[]{:S(2)}, u32[]{:S(2)}) collective-permute-start(bf16[1,512,1024]{2,1,0:T(8,128)(2,1)S(1)} %constant_dynamic-slice_fusion.6), channel_id=1, source_target_pairs={{0,1},{1,0},{2,3},{3,2},{4,5},{5,4},{6,7},{7,6},{8,9},{9,8},{10,11... | collective-permute-start | bytes 3145736 | tf_op jit(solution)/shard_map/ppermute | solution.py:1076
  16.0 23.0 %copy-start.8 = (f32[1,1024]{1,0:T(1,128)}, f32[1,1024]{1,0:T(1,128)S(1)}, u32[]{:S(2)}) copy-start(f32[1,1024]{1,0:T(1,128)S(1)} %reshape.192.head_scale) | copy-start | bytes 12292
  114.6 53.2 %collective-permute-start.2 = (bf16[512,1024]{1,0:T(8,128)(2,1)}, bf16[512,1024]{1,0:T(8,128)(2,1)S(1)}, u32[]{:S(2)}, u32[]{:S(2)}) collective-permute-start(bf16[512,1024]{1,0:T(8,128)(2,1)} %get-tuple-element.103), channel_id=1, source_target_pairs={{0,1},{1,0},{2,3},{3,2},{4,5},{5,4},{6,7},{7,6},{8,9},{9,8},{10,11... | collective-permute-start | bytes 3145736 | tf_op jit(solution)/shard_map/ppermute | solution.py:1076
  181.4 10.3 %collective-permute-start.3 = (bf16[2,256,5120]{2,1,0:T(8,128)(2,1)}, bf16[2,256,5120]{2,1,0:T(8,128)(2,1)}, u32[]{:S(2)}, u32[]{:S(2)}) collective-permute-start(bf16[2,256,5120]{2,1,0:T(8,128)(2,1)} %flat_grad.6), channel_id=1, source_target_pairs={{0,2},{2,0},{4,6},{6,4},{8,10},{10,8},{12,14},{14,12},{16,18},{18,... | collective-permute-start | bytes 15728648 | tf_op jit(solution)/shard_map/ppermute | solution.py:1080
  190.7 15.3 %collective-permute-start.4 = (bf16[2,2048,512]{2,1,0:T(8,128)(2,1)}, bf16[2,2048,512]{2,1,0:T(8,128)(2,1)}, u32[]{:S(2)}, u32[]{:S(2)}) collective-permute-start(bf16[2,2048,512]{2,1,0:T(8,128)(2,1)} %tall_grad.2), channel_id=1, source_target_pairs={{0,2},{2,0},{4,6},{6,4},{8,10},{10,8},{12,14},{14,12},{16,18},{18,... | collective-permute-start | bytes 12582920 | tf_op jit(solution)/shard_map/ppermute | solution.py:1080
  204.5 62.4 %collective-permute-start.5 = (bf16[256,5120]{1,0:T(8,128)(2,1)}, bf16[256,5120]{1,0:T(8,128)(2,1)}, u32[]{:S(2)}, u32[]{:S(2)}) collective-permute-start(bf16[256,5120]{1,0:T(8,128)(2,1)} %get-tuple-element.113), channel_id=1, source_target_pairs={{0,4},{2,6},{4,0},{6,2},{8,12},{10,14},{12,8},{14,10},{16,20},{18,... | collective-permute-start | bytes 7864328 | tf_op jit(solution)/shard_map/ppermute | solution.py:1080
  216.1 47.7 %collective-permute-start.6 = (bf16[2048,512]{1,0:T(8,128)(2,1)}, bf16[2048,512]{1,0:T(8,128)(2,1)}, u32[]{:S(2)}, u32[]{:S(2)}) collective-permute-start(bf16[2048,512]{1,0:T(8,128)(2,1)} %get-tuple-element.116), channel_id=1, source_target_pairs={{0,1},{1,0},{2,3},{3,2},{4,5},{5,4},{6,7},{7,6},{8,9},{9,8},{10,11... | collective-permute-start | bytes 6291464 | tf_op jit(solution)/shard_map/ppermute | solution.py:1076
  242.1 21.7 %copy-start.5 = (bf16[2048,512]{1,0:T(8,128)(2,1)S(1)}, bf16[2048,512]{1,0:T(8,128)(2,1)}, u32[]{:S(2)}) copy-start(bf16[2048,512]{1,0:T(8,128)(2,1)} %get-tuple-element.126) | copy-start | bytes 6291460
  262.0 19.1 %collective-permute-start.7 = (bf16[2,256,1536]{2,1,0:T(8,128)(2,1)}, bf16[2,256,1536]{2,1,0:T(8,128)(2,1)}, u32[]{:S(2)}, u32[]{:S(2)}) collective-permute-start(bf16[2,256,1536]{2,1,0:T(8,128)(2,1)} %flat_grad.8), channel_id=1, source_target_pairs={{0,2},{2,0},{4,6},{6,4},{8,10},{10,8},{12,14},{14,12},{16,18},{18,... | collective-permute-start | bytes 4718600 | tf_op jit(solution)/shard_map/ppermute | solution.py:1080
  266.3 32.5 %collective-permute-start.8 = (bf16[4,256,512]{2,1,0:T(8,128)(2,1)S(1)}, bf16[4,256,512]{2,1,0:T(8,128)(2,1)}, u32[]{:S(2)}, u32[]{:S(2)}) collective-permute-start(bf16[4,256,512]{2,1,0:T(8,128)(2,1)S(1)} %get-tuple-element.161), channel_id=1, source_target_pairs={{0,4},{2,6},{4,0},{6,2},{8,12},{10,14},{12,8},{14,10},{16,20},{18,... | collective-permute-start | bytes 3145736 | tf_op jit(solution)/shard_map/ppermute | solution.py:1080
  271.7 36.6 %collective-permute-start.10 = (bf16[4,64,2560]{2,1,0:T(8,128)(2,1)}, bf16[4,64,2560]{2,1,0:T(8,128)(2,1)}, u32[]{:S(2)}, u32[]{:S(2)}) collective-permute-start(bf16[4,64,2560]{2,1,0:T(8,128)(2,1)} %pad_maximum_fusion.1), channel_id=1, source_target_pairs={{0,1},{1,0},{2,3},{3,2},{4,5},{5,4},{6,7},{7,6},{8,9},{9,8},{10,11... | collective-permute-start | bytes 3932168 | tf_op jit(solution)/shard_map/ppermute | solution.py:1076
  278.4 23.7 %collective-permute-start.9 = (bf16[2,256,1536]{2,1,0:T(8,128)(2,1)}, bf16[2,256,1536]{2,1,0:T(8,128)(2,1)}, u32[]{:S(2)}, u32[]{:S(2)}) collective-permute-start(bf16[2,256,1536]{2,1,0:T(8,128)(2,1)} %flat_grad.9), channel_id=1, source_target_pairs={{0,2},{2,0},{4,6},{6,4},{8,10},{10,8},{12,14},{14,12},{16,18},{18,... | collective-permute-start | bytes 4718600 | tf_op jit(solution)/shard_map/ppermute | solution.py:1080
  287.4 37.5 %collective-permute-start.19 = (bf16[256,1536]{1,0:T(8,128)(2,1)}, bf16[256,1536]{1,0:T(8,128)(2,1)}, u32[]{:S(2)}, u32[]{:S(2)}) collective-permute-start(bf16[256,1536]{1,0:T(8,128)(2,1)} %get-tuple-element.129), channel_id=1, source_target_pairs={{0,4},{2,6},{4,0},{6,2},{8,12},{10,14},{12,8},{14,10},{16,20},{18,... | collective-permute-start | bytes 2359304 | tf_op jit(solution)/shard_map/ppermute | solution.py:1080
  297.2 29.8 %collective-permute-start.11 = (bf16[512,1024]{1,0:T(8,128)(2,1)}, bf16[512,1024]{1,0:T(8,128)(2,1)}, u32[]{:S(2)}, u32[]{:S(2)}) collective-permute-start(bf16[512,1024]{1,0:T(8,128)(2,1)} %get-tuple-element.133), channel_id=1, source_target_pairs={{0,1},{1,0},{2,3},{3,2},{4,5},{5,4},{6,7},{7,6},{8,9},{9,8},{10,11... | collective-permute-start | bytes 3145736 | tf_op jit(solution)/shard_map/ppermute | solution.py:1076
  300.4 21.5 %collective-permute-start.27 = (bf16[2,256,512]{2,1,0:T(8,128)(2,1)S(1)}, bf16[2,256,512]{2,1,0:T(8,128)(2,1)S(1)}, u32[]{:S(2)}, u32[]{:S(2)}) collective-permute-start(bf16[2,256,512]{2,1,0:T(8,128)(2,1)S(1)} %get-tuple-element.165), channel_id=1, source_target_pairs={{0,8},{2,10},{4,12},{6,14},{8,0},{10,2},{12,4},{14,6},{16,24},{18,... | collective-permute-start | bytes 1572872 | tf_op jit(solution)/shard_map/ppermute | solution.py:1080
  310.2 37.4 %collective-permute-start.25 = (bf16[2,64,2560]{2,1,0:T(8,128)(2,1)S(1)}, bf16[2,64,2560]{2,1,0:T(8,128)(2,1)S(1)}, u32[]{:S(2)}, u32[]{:S(2)}) collective-permute-start(bf16[2,64,2560]{2,1,0:T(8,128)(2,1)S(1)} %get-tuple-element.163), channel_id=1, source_target_pairs={{0,8},{2,10},{4,12},{6,14},{8,0},{10,2},{12,4},{14,6},{16,24},{18,... | collective-permute-start | bytes 1966088 | tf_op jit(solution)/shard_map/ppermute | solution.py:1080
  320.4 26.4 %collective-permute-start.15 = (bf16[256,1536]{1,0:T(8,128)(2,1)}, bf16[256,1536]{1,0:T(8,128)(2,1)S(1)}, u32[]{:S(2)}, u32[]{:S(2)}) collective-permute-start(bf16[256,1536]{1,0:T(8,128)(2,1)} %get-tuple-element.136), channel_id=1, source_target_pairs={{0,4},{2,6},{4,0},{6,2},{8,12},{10,14},{12,8},{14,10},{16,20},{18,... | collective-permute-start | bytes 2359304 | tf_op jit(solution)/shard_map/ppermute | solution.py:1080
  322.2 17.6 %collective-permute-start.28 = (bf16[256,512]{1,0:T(8,128)(2,1)S(1)}, bf16[256,512]{1,0:T(8,128)(2,1)S(1)}, u32[]{:S(2)}, u32[]{:S(2)}) collective-permute-start(bf16[256,512]{1,0:T(8,128)(2,1)S(1)} %dynamic-slice_bitcast_fusion.7), channel_id=1, source_target_pairs={{0,16},{2,18},{4,20},{6,22},{8,24},{10,26},{12,28},{14,30},{16,0},... | collective-permute-start | bytes 786440 | tf_op jit(solution)/shard_map/ppermute | solution.py:1080
  324.9 1.5 collective-permute-start.12
  326.4 12.4 %collective-permute-start.20 = (bf16[4,64,768]{2,1,0:T(8,128)(2,1)S(1)}, bf16[4,64,768]{2,1,0:T(8,128)(2,1)S(1)}, u32[]{:S(2)}, u32[]{:S(2)}) collective-permute-start(bf16[4,64,768]{2,1,0:T(8,128)(2,1)S(1)} %constant_dynamic-slice_fusion), channel_id=1, source_target_pairs={{0,1},{1,0},{2,3},{3,2},{4,5},{5,4},{6,7},{7,6},{8,9},{9,8},{10,11... | collective-permute-start | bytes 1179656 | tf_op jit(solution)/shard_map/ppermute | solution.py:1076
  327.0 9.1 %collective-permute-start.13 = (f32[23,1024]{1,0:T(8,128)S(1)}, f32[23,1024]{1,0:T(8,128)S(1)}, u32[]{:S(2)}, u32[]{:S(2)}) collective-permute-start(f32[23,1024]{1,0:T(8,128)S(1)} %fusion.3), channel_id=1, source_target_pairs={{0,8},{2,10},{4,12},{6,14},{8,0},{10,2},{12,4},{14,6},{16,24},{18,... | collective-permute-start | bytes 282632 | tf_op jit(solution)/shard_map/ppermute | solution.py:1080
  330.1 16.7 %copy-start.6 = (bf16[256,1536]{1,0:T(8,128)(2,1)S(1)}, bf16[256,1536]{1,0:T(8,128)(2,1)}, u32[]{:S(2)}) copy-start(bf16[256,1536]{1,0:T(8,128)(2,1)} %get-tuple-element.137) | copy-start | bytes 2359300
  336.1 6.0 %collective-permute-start.14 = (f32[23,1024]{1,0:T(8,128)S(1)}, f32[23,1024]{1,0:T(8,128)S(1)}, u32[]{:S(2)}, u32[]{:S(2)}) collective-permute-start(f32[23,1024]{1,0:T(8,128)S(1)} %add.193), channel_id=1, source_target_pairs={{0,16},{2,18},{4,20},{6,22},{8,24},{10,26},{12,28},{14,30},{16,0},... | collective-permute-start | bytes 282632 | tf_op jit(solution)/shard_map/ppermute | solution.py:1080
  338.9 6.9 %collective-permute-start.21 = (bf16[2,64,768]{2,1,0:T(8,128)(2,1)S(1)}, bf16[2,64,768]{2,1,0:T(8,128)(2,1)S(1)}, u32[]{:S(2)}, u32[]{:S(2)}) collective-permute-start(bf16[2,64,768]{2,1,0:T(8,128)(2,1)S(1)} %dynamic-slice_bitcast_fusion.8), channel_id=1, source_target_pairs={{0,8},{2,10},{4,12},{6,14},{8,0},{10,2},{12,4},{14,6},{16,24},{18,... | collective-permute-start | bytes 589832 | tf_op jit(solution)/shard_map/ppermute | solution.py:1080
  345.8 14.9 %collective-permute-start.22 = (bf16[64,768]{1,0:T(8,128)(2,1)S(1)}, bf16[64,768]{1,0:T(8,128)(2,1)S(1)}, u32[]{:S(2)}, u32[]{:S(2)}) collective-permute-start(bf16[64,768]{1,0:T(8,128)(2,1)S(1)} %dynamic-slice_bitcast_fusion.12), channel_id=1, source_target_pairs={{0,16},{2,18},{4,20},{6,22},{8,24},{10,26},{12,28},{14,30},{16,0},... | collective-permute-start | bytes 294920 | tf_op jit(solution)/shard_map/ppermute | solution.py:1080
  347.1 9.3 %collective-permute-start.16 = (bf16[4,64,768]{2,1,0:T(8,128)(2,1)S(1)}, bf16[4,64,768]{2,1,0:T(8,128)(2,1)S(1)}, u32[]{:S(2)}, u32[]{:S(2)}) collective-permute-start(bf16[4,64,768]{2,1,0:T(8,128)(2,1)S(1)} %constant_dynamic-slice_fusion.1), channel_id=1, source_target_pairs={{0,1},{1,0},{2,3},{3,2},{4,5},{5,4},{6,7},{7,6},{8,9},{9,8},{10,11... | collective-permute-start | bytes 1179656 | tf_op jit(solution)/shard_map/ppermute | solution.py:1076
  347.7 22.8 %collective-permute-start.26 = (bf16[64,2560]{1,0:T(8,128)(2,1)S(1)}, bf16[64,2560]{1,0:T(8,128)(2,1)S(1)}, u32[]{:S(2)}, u32[]{:S(2)}) collective-permute-start(bf16[64,2560]{1,0:T(8,128)(2,1)S(1)} %dynamic-slice_bitcast_fusion.6), channel_id=1, source_target_pairs={{0,16},{2,18},{4,20},{6,22},{8,24},{10,26},{12,28},{14,30},{16,0},... | collective-permute-start | bytes 983048 | tf_op jit(solution)/shard_map/ppermute | solution.py:1080
  356.5 12.4 %collective-permute-start.23 = (bf16[2,64,768]{2,1,0:T(8,128)(2,1)S(1)}, bf16[2,64,768]{2,1,0:T(8,128)(2,1)S(1)}, u32[]{:S(2)}, u32[]{:S(2)}) collective-permute-start(bf16[2,64,768]{2,1,0:T(8,128)(2,1)S(1)} %dynamic-slice_bitcast_fusion.10), channel_id=1, source_target_pairs={{0,8},{2,10},{4,12},{6,14},{8,0},{10,2},{12,4},{14,6},{16,24},{18,... | collective-permute-start | bytes 589832 | tf_op jit(solution)/shard_map/ppermute | solution.py:1080
  369.0 6.7 %collective-permute-start.24 = (bf16[64,768]{1,0:T(8,128)(2,1)S(1)}, bf16[64,768]{1,0:T(8,128)(2,1)S(1)}, u32[]{:S(2)}, u32[]{:S(2)}) collective-permute-start(bf16[64,768]{1,0:T(8,128)(2,1)S(1)} %dynamic-slice_bitcast_fusion.11), channel_id=1, source_target_pairs={{0,16},{2,18},{4,20},{6,22},{8,24},{10,26},{12,28},{14,30},{16,0},... | collective-permute-start | bytes 294920 | tf_op jit(solution)/shard_map/ppermute | solution.py:1080
  370.0 4.6 %collective-permute-start.17 = (f32[23,1024]{1,0:T(8,128)S(1)}, f32[23,1024]{1,0:T(8,128)S(1)}, u32[]{:S(2)}, u32[]{:S(2)}) collective-permute-start(f32[23,1024]{1,0:T(8,128)S(1)} %add.194), channel_id=1, source_target_pairs={{0,4},{2,6},{4,0},{6,2},{8,12},{10,14},{12,8},{14,10},{16,20},{18,... | collective-permute-start | bytes 282632 | tf_op jit(solution)/shard_map/ppermute | solution.py:1080
  374.6 4.7 %collective-permute-start.18 = (f32[23,1024]{1,0:T(8,128)S(1)}, f32[23,1024]{1,0:T(8,128)S(1)}, u32[]{:S(2)}, u32[]{:S(2)}) collective-permute-start(f32[23,1024]{1,0:T(8,128)S(1)} %add.199), channel_id=1, source_target_pairs={{0,1},{1,0},{2,3},{3,2},{4,5},{5,4},{6,7},{7,6},{8,9},{9,8},{10,11... | collective-permute-start | bytes 282632 | tf_op jit(solution)/shard_map/ppermute | solution.py:1076
  (25 other events, 203.9 us)
